TPU v7x, 32 devices: a whole 2x2x4 slice. The times are simulated.
32 devices in a mesh: seq: 8 (over y, x, core), tensor: 4 (over z).
Axes of the slice: x: 2, y: 2, z: 4, core: 2. Of those that a mesh axis runs over, the one named last changes fastest.
Arguments:
- tokens: bfloat16 [8192, 1024], P('seq', 'tensor'), may hold values from -6 to 6
- segment_ids: int32 [8192], P('seq'), may hold values from 0 to 4, as said below
- out_grad: bfloat16 [8192, 1024], P('seq', 'tensor'), may hold values from -6 to 6
- ln1_gain: bfloat16 [1024], P('tensor'), may hold values from 0.099609375 to 1.8984375
- ln1_bias: bfloat16 [1024], P('tensor'), may hold values from -3 to 3
- w_qkv: bfloat16 [1024, 16, 192], P(None, 'tensor'), may hold values from -0.1875 to 0.1875
- b_qv: bfloat16 [16, 128], P('tensor'), may hold values from -3 to 3
- w_out: bfloat16 [16, 64, 1024], P('tensor'), may hold values from -2 to 2
- b_out: bfloat16 [1024], P('tensor'), may hold values from -3 to 3
- ln2_gain: bfloat16 [1024], P('tensor'), may hold values from 0.099609375 to 1.8984375
- ln2_bias: bfloat16 [1024], P('tensor'), may hold values from -3 to 3
- w_up: bfloat16 [1024, 4096], P(None, 'tensor'), may hold values from -0.1875 to 0.1875
- b_up: bfloat16 [4096], P('tensor'), may hold values from -3 to 3
- w_down: bfloat16 [4096, 1024], P('tensor'), may hold values from -0.09375 to 0.09375
- b_down: bfloat16 [1024], P('tensor'), may hold values from -3 to 3
- prefix_embed: bfloat16 [10, 1024], replicated, may hold values from -6 to 6
- reparam_in: bfloat16 [1024, 512], replicated, may hold values from -0.1875 to 0.1875
- reparam_in_bias: bfloat16 [512], replicated, may hold values from -3 to 3
- reparam_out: bfloat16 [512, 16, 128], P(None, 'tensor'), may hold values from -0.25 to 0.25
- reparam_out_bias: bfloat16 [16, 128], P('tensor'), may hold values from -3 to 3
Outputs:
- output_act: bfloat16 [8192, 1024], P('seq', 'tensor')
- input_grad: bfloat16 [8192, 1024], P('seq', 'tensor')
- grad_ln1_gain: float32 [1024], P('tensor')
- grad_ln1_bias: float32 [1024], P('tensor')
- grad_w_qkv: float32 [1024, 16, 192], P(None, 'tensor')
- grad_b_qv: float32 [16, 128], P('tensor')
- grad_w_out: float32 [16, 64, 1024], P('tensor')
- grad_b_out: float32 [1024], P('tensor')
- grad_ln2_gain: float32 [1024], P('tensor')
- grad_ln2_bias: float32 [1024], P('tensor')
- grad_w_up: float32 [1024, 4096], P(None, 'tensor')
- grad_b_up: float32 [4096], P('tensor')
- grad_w_down: float32 [4096, 1024], P('tensor')
- grad_b_down: float32 [1024], P('tensor')
- grad_prefix_embed: float32 [10, 1024], replicated
- grad_reparam_in: float32 [1024, 512], replicated
- grad_reparam_in_bias: float32 [512], replicated
- grad_reparam_out: float32 [512, 16, 128], P(None, 'tensor')
- grad_reparam_out_bias: float32 [16, 128], P('tensor')
Inputs may be any that keep to these rules, and one draw needn't show every extreme that they name: `segment_ids`: never falling along the tokens; every document has 1 or more tokens; document 2 has exactly 7168 tokens and starts within the first 1024 tokens.
All inputs are finite; a program needn't handle non-finite values.
Results may differ from a plain program's by a relative error of at most 0.024.
Values may be sent and summed in bfloat16 or wider, within the bound.
No kernel may reach another device: no remote copies, remote signals or barrier semaphores. Data moves between devices by JAX's collectives and lax.ppermute only.
A program may use at most 128 MiB of HBM per device.

v0:
```python
import math

import jax
import jax.numpy as jnp
from jax import lax
from jax.sharding import PartitionSpec as P

D = 1024


EPS = 1e-05
NEGATIVE = -1e30
HIGHEST = lax.Precision.HIGHEST


def shifted(array, axis, by):
    length = lax.axis_size(axis)
    pairs = [(i, i + by) for i in range(length) if 0 <= i + by < length]
    return lax.ppermute(array, axis, pairs)


def from_behind(value, axis, steps):
    count = lax.axis_size(axis)
    pairs = [(source, (source + steps) % count) for source in range(count)]
    return lax.ppermute(value, axis, pairs)


def gelu_tanh(values):
    return jax.nn.gelu(values, approximate=True)


def row_stats(first, second):
    return lax.psum((first, second), "tensor")


def feature_rows(values):
    return lax.all_gather(values, "tensor", axis=1, tiled=True)


def feature_sums(values):
    return lax.psum_scatter(
        values.astype(jnp.bfloat16), "tensor", scatter_dimension=1, tiled=True
    ).astype(jnp.float32)


def norm_forward(values, gain, shift, width):
    total, squares = row_stats(jnp.sum(values, 1), jnp.sum(values * values, 1))
    mean = total / width
    inverse = lax.rsqrt(squares / width - mean * mean + EPS)
    normed = (values - mean[:, None]) * inverse[:, None]
    return (normed, inverse, normed * gain + shift)


def norm_backward(grad, normed, inverse, gain, width):
    scaled = grad * gain
    first, second = row_stats(jnp.sum(scaled, 1), jnp.sum(scaled * normed, 1))
    back = inverse[:, None] * (scaled - first[:, None] / width - normed * second[:, None] / width)
    return (back, jnp.sum(grad * normed, 0), jnp.sum(grad, 0))


def key_mask(query_docs, query_places, key_docs, key_start):
    key_places = key_start + lax.iota(jnp.int32, key_docs.shape[0])
    valid = key_start >= 0
    return (
        (query_docs[:, None] == key_docs[None, :])
        & (key_places[None, :] <= query_places[:, None])
        & valid
    )


def attend_update(carry, query, key_block, value_block, mask, scale):
    peak, total, accum = carry
    scores = (
        jnp.einsum("qhd,khd->hqk", query, key_block, preferred_element_type=jnp.float32) * scale
    )
    scores = jnp.where(mask[None], scores, NEGATIVE)
    new_peak = jnp.maximum(peak, jnp.max(scores, -1))
    factor = jnp.exp(peak - new_peak)
    weights = jnp.where(mask[None], jnp.exp(scores - new_peak[..., None]), 0.0)
    total = total * factor + jnp.sum(weights, -1)
    accum = accum * factor[..., None] + jnp.einsum(
        "hqk,khd->hqd",
        weights.astype(jnp.bfloat16),
        value_block,
        preferred_element_type=jnp.float32,
    )
    return (new_peak, total, accum)


def attend_back(query, grad_out, log_total, delta, key_block, value_block, mask, scale):
    scores = (
        jnp.einsum("qhd,khd->hqk", query, key_block, preferred_element_type=jnp.float32) * scale
    )
    probs = jnp.where(mask[None], jnp.exp(scores - log_total[..., None]), 0.0)
    grad_probs = jnp.einsum(
        "hqd,khd->hqk", grad_out, value_block, preferred_element_type=jnp.float32
    )
    grad_scores = (probs * (grad_probs - delta[..., None])).astype(jnp.bfloat16)
    grad_query = (
        jnp.einsum("hqk,khd->qhd", grad_scores, key_block, preferred_element_type=jnp.float32)
        * scale
    )
    grad_key = (
        jnp.einsum("hqk,qhd->khd", grad_scores, query, preferred_element_type=jnp.float32) * scale
    )
    grad_value = jnp.einsum(
        "hqk,hqd->khd", probs.astype(jnp.bfloat16), grad_out, preferred_element_type=jnp.float32
    )
    return (grad_query, grad_key, grad_value)


def fold_keys(carry, piece, start, query, query_docs, query_places, all_docs, scale):
    key_all, value_all = piece
    size = math.gcd(key_all.shape[0], 1024)

    def step(number, inner):
        begin = number * size
        key_start = start + begin
        key_docs = lax.dynamic_slice_in_dim(all_docs, jnp.maximum(key_start, 0), size, 0)
        mask = key_mask(query_docs, query_places, key_docs, key_start)
        return attend_update(inner, query, key_all, value_all, mask, scale)

    return lax.fori_loop(0, key_all.shape[0] // size, step, carry)


def cycle_back(
    query,
    grad_out,
    log_total,
    delta,
    key_rows,
    value_rows,
    query_docs,
    query_places,
    all_docs,
    scale,
):
    count = key_rows.shape[0]
    devices = lax.axis_size("seq")
    place = lax.axis_index("seq")

    def turn(step, state):
        key_block, value_block, grad_key, grad_value, grad_query = state
        anchor = (place - step) % devices
        key_start = anchor * count
        key_docs = lax.dynamic_slice_in_dim(all_docs, key_start, count, 0)
        mask = key_mask(query_docs, query_places, key_docs, key_start)
        grads = (grad_query, grad_key, grad_value)
        add_query, add_key, add_value = attend_back(
            query, grad_out, log_total, delta, key_block, value_block, mask, scale
        )
        grads = (grads[0] + add_query, grads[1] + add_key, grads[2] + add_value)
        key_block, value_block = shifted((key_block, value_block), "seq", 1)
        grad_key, grad_value = (
            from_behind(grads[1].astype(jnp.bfloat16), "seq", 1).astype(jnp.float32),
            from_behind(grads[2].astype(jnp.bfloat16), "seq", 1).astype(jnp.float32),
        )
        return (key_block, value_block, grad_key, grad_value, grads[0])

    zeros = jnp.zeros(key_rows.shape, jnp.float32)
    start_state = (key_rows, value_rows, zeros, zeros, jnp.zeros(query.shape, jnp.float32))
    final = lax.fori_loop(0, devices, turn, start_state)
    return (final[4], final[2], final[3])


def on_device(
    tokens,
    segment_ids,
    out_grad,
    ln1_gain,
    ln1_bias,
    w_qkv,
    b_qv,
    w_out,
    b_out,
    ln2_gain,
    ln2_bias,
    w_up,
    b_up,
    w_down,
    b_down,
    prefix_embed,
    reparam_in,
    reparam_in_bias,
    reparam_out,
    reparam_out_bias,
):
    rows = tokens.shape[0]
    heads = w_qkv.shape[1]
    head_size = w_qkv.shape[2] // 3
    scale = head_size ** (-0.5)
    place = lax.axis_index("seq")
    all_docs = lax.all_gather(segment_ids, "seq", axis=0, tiled=True)
    positions = place * rows + lax.iota(jnp.int32, rows)
    resid = tokens.astype(jnp.float32)
    gain1 = ln1_gain.astype(jnp.float32)
    gain2 = ln2_gain.astype(jnp.float32)
    normed1, inverse1, out1 = norm_forward(resid, gain1, ln1_bias.astype(jnp.float32), D)
    full1 = feature_rows(out1.astype(jnp.bfloat16))
    mixed = jnp.einsum("td,dhe->the", full1, w_qkv, preferred_element_type=jnp.float32)
    bias_pair = b_qv.astype(jnp.float32)
    query = (mixed[..., :head_size] + bias_pair[:, :head_size]).astype(jnp.bfloat16)
    key_rows = mixed[..., head_size : 2 * head_size].astype(jnp.bfloat16)
    value_rows = (mixed[..., 2 * head_size :] + bias_pair[:, head_size:]).astype(jnp.bfloat16)
    embed_float = prefix_embed.astype(jnp.float32)
    reparam_in_float = reparam_in.astype(jnp.float32)
    reparam_out_float = reparam_out.astype(jnp.float32)
    prefix_hidden = jnp.tanh(
        jnp.dot(prefix_embed, reparam_in, preferred_element_type=jnp.float32)
        + reparam_in_bias.astype(jnp.float32)
    )
    prefix_pair = jnp.einsum("pa,ahe->phe", prefix_hidden, reparam_out_float, precision=HIGHEST)
    prefix_pair = (prefix_pair + reparam_out_bias.astype(jnp.float32)).astype(jnp.bfloat16)
    prefix_keys = prefix_pair[..., :head_size]
    prefix_values = prefix_pair[..., head_size:]
    prefix_mask = jnp.ones((rows, prefix_pair.shape[0]), bool)
    start_carry = (
        jnp.full((heads, rows), NEGATIVE, jnp.float32),
        jnp.zeros((heads, rows), jnp.float32),
        jnp.zeros((heads, rows, head_size), jnp.float32),
    )
    carry = attend_update(start_carry, query, prefix_keys, prefix_values, prefix_mask, scale)

    def fold_piece(state, piece, start):
        return fold_keys(state, piece, start, query, segment_ids, positions, all_docs, scale)

    carry = fold_piece(carry, (key_rows, value_rows), place * rows)

    def forward_turn(step, state):
        inner, keys_now, values_now = state
        keys_now, values_now = shifted((keys_now, values_now), "seq", 1)
        inner = fold_piece(inner, (keys_now, values_now), (place - step) * rows)
        return (inner, keys_now, values_now)

    carry = lax.fori_loop(1, lax.axis_size("seq"), forward_turn, (carry, key_rows, value_rows))[0]
    peak, total, accum = carry
    attended_heads = accum / total[..., None]
    log_total = peak + jnp.log(total)
    attended_low = attended_heads.astype(jnp.bfloat16)
    branch = feature_sums(
        jnp.einsum("hte,hed->td", attended_low, w_out, preferred_element_type=jnp.float32)
    )
    middle = resid + branch + b_out.astype(jnp.float32)
    normed2, inverse2, out2 = norm_forward(middle, gain2, ln2_bias.astype(jnp.float32), D)
    full2 = feature_rows(out2.astype(jnp.bfloat16))
    hidden_pre = jnp.dot(full2, w_up, preferred_element_type=jnp.float32) + b_up.astype(jnp.float32)
    hidden_act, gelu_back = jax.vjp(gelu_tanh, hidden_pre)
    hidden_low = hidden_act.astype(jnp.bfloat16)
    mlp_out = feature_sums(jnp.dot(hidden_low, w_down, preferred_element_type=jnp.float32))
    output_act = (middle + mlp_out + b_down.astype(jnp.float32)).astype(jnp.bfloat16)
    grad_top = out_grad.astype(jnp.float32)
    grad_b_down = jnp.sum(grad_top, 0)
    full_grad = feature_rows(out_grad)
    grad_w_down = jnp.einsum("tf,td->fd", hidden_low, full_grad, preferred_element_type=jnp.float32)
    grad_hidden = jnp.einsum("td,fd->tf", full_grad, w_down, preferred_element_type=jnp.float32)
    grad_pre = gelu_back(grad_hidden)[0].astype(jnp.bfloat16)
    grad_b_up = jnp.sum(grad_pre.astype(jnp.float32), 0)
    grad_w_up = jnp.einsum("td,tf->df", full2, grad_pre, preferred_element_type=jnp.float32)
    grad_normed2 = feature_sums(
        jnp.einsum("tf,df->td", grad_pre, w_up, preferred_element_type=jnp.float32)
    )
    back2, grad_ln2_gain, grad_ln2_bias = norm_backward(grad_normed2, normed2, inverse2, gain2, D)
    grad_middle = grad_top + back2
    grad_b_out = jnp.sum(grad_middle, 0)
    full_branch = feature_rows(grad_middle.astype(jnp.bfloat16))
    grad_w_out = jnp.einsum(
        "hte,td->hed", attended_low, full_branch, preferred_element_type=jnp.float32
    )
    grad_attended = jnp.einsum(
        "td,hed->hte", full_branch, w_out, preferred_element_type=jnp.float32
    ).astype(jnp.bfloat16)
    delta = jnp.sum(grad_attended.astype(jnp.float32) * attended_heads, -1)
    prefix_query, prefix_key_grad, prefix_value_grad = attend_back(
        query, grad_attended, log_total, delta, prefix_keys, prefix_values, prefix_mask, scale
    )
    grad_query, grad_key, grad_value = cycle_back(
        query,
        grad_attended,
        log_total,
        delta,
        key_rows,
        value_rows,
        segment_ids,
        positions,
        all_docs,
        scale,
    )
    query_low = (grad_query + prefix_query).astype(jnp.bfloat16)
    value_low = grad_value.astype(jnp.bfloat16)
    grad_mixed = jnp.concatenate([query_low, grad_key.astype(jnp.bfloat16), value_low], -1)
    grad_w_qkv = jnp.einsum("td,the->dhe", full1, grad_mixed, preferred_element_type=jnp.float32)
    grad_b_qv = jnp.concatenate(
        [jnp.sum(query_low.astype(jnp.float32), 0), jnp.sum(value_low.astype(jnp.float32), 0)], -1
    )
    grad_normed1 = feature_sums(
        jnp.einsum("the,dhe->td", grad_mixed, w_qkv, preferred_element_type=jnp.float32)
    )
    back1, grad_ln1_gain, grad_ln1_bias = norm_backward(grad_normed1, normed1, inverse1, gain1, D)
    input_grad = (grad_middle + back1).astype(jnp.bfloat16)
    prefix_part = jnp.concatenate([prefix_key_grad, prefix_value_grad], -1)
    summed = (
        lax.psum(grad_w_qkv.astype(jnp.bfloat16), "seq").astype(jnp.float32),
        lax.psum(grad_b_qv.astype(jnp.bfloat16), "seq").astype(jnp.float32),
        lax.psum(grad_w_out.astype(jnp.bfloat16), "seq").astype(jnp.float32),
        lax.psum(grad_b_out.astype(jnp.bfloat16), "seq").astype(jnp.float32),
        lax.psum(grad_w_up.astype(jnp.bfloat16), "seq").astype(jnp.float32),
        lax.psum(grad_b_up.astype(jnp.bfloat16), "seq").astype(jnp.float32),
        lax.psum(grad_w_down.astype(jnp.bfloat16), "seq").astype(jnp.float32),
        lax.psum(grad_b_down.astype(jnp.bfloat16), "seq").astype(jnp.float32),
        lax.psum(grad_ln1_gain.astype(jnp.bfloat16), "seq").astype(jnp.float32),
        lax.psum(grad_ln1_bias.astype(jnp.bfloat16), "seq").astype(jnp.float32),
        lax.psum(grad_ln2_gain.astype(jnp.bfloat16), "seq").astype(jnp.float32),
        lax.psum(grad_ln2_bias.astype(jnp.bfloat16), "seq").astype(jnp.float32),
        lax.psum(prefix_part.astype(jnp.bfloat16), "seq").astype(jnp.float32),
    )
    prefix_grad_low = summed[12].astype(jnp.bfloat16)
    prefix_grad = prefix_grad_low.astype(jnp.float32)
    grad_reparam_out = jnp.einsum("pa,phe->ahe", prefix_hidden, prefix_grad, precision=HIGHEST)
    grad_reparam_out_bias = jnp.sum(prefix_grad, 0)
    hidden_part = jnp.einsum(
        "phe,ahe->pa", prefix_grad_low, reparam_out, preferred_element_type=jnp.float32
    )
    hidden_grad = lax.psum(hidden_part, "tensor")
    grad_prefix_pre = hidden_grad * (1.0 - prefix_hidden * prefix_hidden)
    grad_reparam_in_bias = jnp.sum(grad_prefix_pre, 0)
    grad_reparam_in = jnp.einsum("pd,pa->da", embed_float, grad_prefix_pre, precision=HIGHEST)
    grad_prefix_embed = jnp.einsum(
        "pa,da->pd", grad_prefix_pre, reparam_in_float, precision=HIGHEST
    )
    return (
        output_act,
        input_grad,
        summed[8],
        summed[9],
        summed[0],
        summed[1],
        summed[2],
        summed[3],
        summed[10],
        summed[11],
        summed[4],
        summed[5],
        summed[6],
        summed[7],
        grad_prefix_embed,
        grad_reparam_in,
        grad_reparam_in_bias,
        grad_reparam_out,
        grad_reparam_out_bias,
    )


def solution(mesh):
    placed = (
        P("seq", "tensor"),
        P("seq"),
        P("seq", "tensor"),
        P("tensor"),
        P("tensor"),
        P(None, "tensor", None),
        P("tensor", None),
        P("tensor", None, None),
        P("tensor"),
        P("tensor"),
        P("tensor"),
        P(None, "tensor"),
        P("tensor"),
        P("tensor", None),
        P("tensor"),
        P(),
        P(),
        P(),
        P(None, "tensor", None),
        P("tensor", None),
    )
    return jax.shard_map(
        on_device,
        mesh=mesh,
        in_specs=placed,
        out_specs=(
            P("seq", "tensor"),
            P("seq", "tensor"),
            P("tensor"),
            P("tensor"),
            P(None, "tensor", None),
            P("tensor", None),
            P("tensor", None, None),
            P("tensor"),
            P("tensor"),
            P("tensor"),
            P(None, "tensor"),
            P("tensor"),
            P("tensor", None),
            P("tensor"),
            P(),
            P(),
            P(),
            P(None, "tensor", None),
            P("tensor", None),
        ),
        check_vma=False,
    )
```

profile of v0, /device:TPU:1, one launch (start us, length us, event | category | flops | bytes accessed | tf_op | source)
XLA Modules:
  0.0 1209.9 jit_solution(17123283654889361772)
XLA Ops:
  10.1 10.9 all-reduce.3
  24.7 11.9 all_gather.16
  43.1 26.3 %all-gather.5.cloned.1.call-done = bf16[1024,1024]{1,0:T(8,128)(2,1)} async-done(((bf16[1024,256]{1,0:T(8,128)(2,1)}), bf16[1024,1024]{1,0:T(8,128)(2,1)}) %all-gather.5.cloned.1.call-update) | async-done | bytes 2097168 | tf_op jit(solution)/shard_map/all_gather | solution.py:37
  82.3 4.7 fusion.39
  89.4 194.7 %while.68 = (s32[]{:T(128)}, f32[4,1024]{1,0:T(4,128)S(1)}, f32[4,1024]{1,0:T(4,128)S(1)}, f32[4,1024,64]{1,2,0:T(8,128)}, bf16[1024,4,64]{0,2,1:T(8,128)(2,1)},...) while((s32[]{:T(128)}, f32[4,1024]{1,0:T(4,128)S(1)}, ...), condition=%wide.region_11.12_spmd.clone, body=%wide.region_8.11_spmd.clone.sunk | while | flops 1132996608 | bytes 73171272 | solution.py:235
  110.8 5.8 fusion.210
  138.5 5.8 fusion.210
  166.1 5.8 fusion.210
  193.8 5.8 fusion.210
  221.4 5.8 fusion.210
  249.1 5.8 fusion.210
  255.8 4.9 collective-permute-start
  260.7 5.0 collective-permute-start.1
  277.3 5.8 fusion.210
  287.7 47.4 %reduce-scatter.5.cloned.1.call-done = bf16[1024,256]{1,0:T(8,128)(2,1)} async-done(((bf16[1024,1024]{1,0:T(8,128)(2,1)}), bf16[1024,256]{1,0:T(8,128)(2,1)}) %reduce-scatter.5.cloned.1.call-update) | async-done | bytes 524304 | tf_op jit(solution)/shard_map/reduce_scatter | solution.py:41
  336.5 8.4 all-reduce.2
  347.8 45.2 %all-gather.7.cloned.1.call-done = bf16[1024,1024]{1,0:T(8,128)(2,1)} async-done(((bf16[1024,256]{1,0:T(8,128)(2,1)}), bf16[1024,1024]{1,0:T(8,128)(2,1)}) %all-gather.7.cloned.1.call-update) | async-done | bytes 2097168 | tf_op jit(solution)/shard_map/all_gather | solution.py:37
  393.0 6.6 fusion.138
  399.5 39.4 %all-gather.9.cloned.1.call-done = bf16[1024,1024]{1,0:T(8,128)(2,1)} async-done(((bf16[1024,256]{1,0:T(8,128)(2,1)}), bf16[1024,1024]{1,0:T(8,128)(2,1)}) %all-gather.9.cloned.1.call-update) | async-done | bytes 2097168 | tf_op jit(solution)/shard_map/all_gather | solution.py:37
  439.0 8.2 fusion.127
  452.3 6.3 convolution_convert_fusion.3
  458.7 36.3 %reduce-scatter.9.cloned.1.call-done = bf16[1024,256]{1,0:T(8,128)(2,1)} async-done(((bf16[1024,1024]{1,0:T(8,128)(2,1)}), bf16[1024,256]{1,0:T(8,128)(2,1)}) %reduce-scatter.9.cloned.1.call-update) | async-done | bytes 524304 | tf_op jit(solution)/shard_map/reduce_scatter | solution.py:41
  497.5 8.4 all-reduce.1
  505.9 35.1 %reduce-scatter.7.cloned.1.call-done = bf16[1024,256]{1,0:T(8,128)(2,1)} async-done(((bf16[1024,1024]{1,0:T(8,128)(2,1)}), bf16[1024,256]{1,0:T(8,128)(2,1)}) %reduce-scatter.7.cloned.1.call-update) | async-done | bytes 524304 | tf_op jit(solution)/shard_map/reduce_scatter | solution.py:41
  545.5 6.1 convolution_convert_fusion.1
  556.0 34.4 %all-gather.11.cloned.1.call-done = bf16[1024,1024]{1,0:T(8,128)(2,1)} async-done(((bf16[1024,256]{1,0:T(8,128)(2,1)}), bf16[1024,1024]{1,0:T(8,128)(2,1)}) %all-gather.11.cloned.1.call-update) | async-done | bytes 2097168 | tf_op jit(solution)/shard_map/all_gather | solution.py:37
  594.2 394.3 %while.69 = (s32[]{:T(128)}, bf16[1024,4,64]{0,2,1:T(8,128)(2,1)S(1)}, bf16[1024,4,64]{0,2,1:T(8,128)(2,1)S(1)}, f32[1024,4,64]{0,2,1:T(8,128)}, f32[1024,4,64]{...) while((s32[]{:T(128)}, ...), condition=%wide.region_25.26_spmd.clone, body=%wide.region_24.25_spmd.clone.sunk | while | flops 2733639680 | bytes 145310352 | solution.py:162
  601.9 8.1 fusion.221
  611.3 9.6 multiply_convert_fusion.5
  625.9 8.6 fusion.223
  634.6 6.1 fusion.224
  651.3 8.1 fusion.221
  660.7 9.6 multiply_convert_fusion.5
  675.4 8.6 fusion.223
  684.0 6.1 fusion.224
  699.9 8.1 fusion.221
  709.3 9.6 multiply_convert_fusion.5
  723.9 8.6 fusion.223
  732.6 6.1 fusion.224
  749.3 8.1 fusion.221
  758.7 9.6 multiply_convert_fusion.5
  773.4 8.6 fusion.223
  782.0 6.1 fusion.224
  797.8 8.1 fusion.221
  807.2 9.6 multiply_convert_fusion.5
  821.9 8.6 fusion.223
  830.5 6.1 fusion.224
  847.3 8.1 fusion.221
  856.7 9.6 multiply_convert_fusion.5
  871.3 8.6 fusion.223
  880.0 6.1 fusion.224
  895.8 8.1 fusion.221
  905.2 9.6 multiply_convert_fusion.5
  919.9 8.6 fusion.223
  928.5 6.1 fusion.224
  945.3 8.1 fusion.221
  954.7 9.6 multiply_convert_fusion.5
  969.3 8.6 fusion.223
  978.0 6.1 fusion.224
  998.0 5.0 bitcast_convert_fusion
  1004.0 95.9 %all-reduce.8.cloned.1.call-done = (bf16[1024,4,192]{0,2,1:T(8,128)(2,1)}, bf16[4,64,1024]{2,1,0:T(8,128)(2,1)}, bf16[1024,1024]{1,0:T(8,128)(2,1)}, bf16[1024,1024]{1,0:T(8,128)(2,1)}) async-done(((bf16[1024,4,192]{0,2,1:T(8,128)(2,1)}, bf16[4,64,1024]{2,1,0:T(8,128)(2,1)}, bf16[1024,1024]{1,0:T(8,128)(2,1)}, bf16[1024,1024]{1,0:T(8,128)(2,1)}), (bf16[1024,4,192]{0,2,1:T(8,128)(2,1)}, ...) | async-done | bytes 6291472 | tf_op jit(solution)/shard_map/psum | solution.py:302
  1110.7 36.0 %reduce-scatter.11.cloned.1.call-done = bf16[1024,256]{1,0:T(8,128)(2,1)} async-done(((bf16[1024,1024]{1,0:T(8,128)(2,1)}), bf16[1024,256]{1,0:T(8,128)(2,1)}) %reduce-scatter.11.cloned.1.call-update) | async-done | bytes 524304 | tf_op jit(solution)/shard_map/reduce_scatter | solution.py:41
  1149.7 21.6 %all-reduce.4 = (bf16[10,4,128]{2,0,1:T(8,128)(2,1)S(1)}, bf16[256]{0:T(256)(128)(2,1)S(1)}, bf16[256]{0:T(256)(128)(2,1)S(1)}, bf16[4,128]{1,0:T(4,128)(2,1)S(1...) all-reduce(bf16[10,4,128]{2,0,1:T(8,128)(2,1)S(1)} %pad_maximum_fus, ...), channel_id=1, replica_groups=mesh['seq'=8,'tensor'=4] {'seq'}, use_global_device_ids=true, to_apply=%region_52.53 | all-reduce | flops 8192 | bytes 32768 | tf_op jit(solution)/shard_map/psum | solution.py:314
  1172.1 14.2 %all-reduce = (f32[1024]{0:T(1024)S(1)}, f32[1024]{0:T(1024)S(1)}, f32[10,512]{1,0:T(8,128)S(1)}) all-reduce(f32[1024]{0:T(1024)S(1)} %get-tuple-element.754, f32[1024]{0:T(1024)S(1)} %get-tuple-element.757, f32[10,512]{1,0:T(8,128)S(1)} %convolution_bitcast_fusion.1), channel_id=1, replica_groups=mesh['seq'=8,'tensor'=4] {'tensor'}, use_global_device_ids=true, to_apply=%region_30.31 | all-reduce | flops 7168 | bytes 57344 | tf_op jit(solution)/shard_map/psum | solution.py:33
  (535 shorter events, 373.9 us)
Async XLA Ops:
  7.2 431.8 %copy-start = (bf16[1024,1024]{1,0:T(8,128)(2,1)S(1)}, bf16[1024,1024]{1,0:T(8,128)(2,1)}, u32[]{:S(2)}) copy-start(bf16[1024,1024]{1,0:T(8,128)(2,1)} %param.37) | copy-start | bytes 6291460
  7.2 62.2 %all-gather.5.cloned.1.call-start = ((), (), s32[]{:S(2)}) async-start(), calls=%async_computation.4 | async-start | bytes 2621440 | tf_op jit(solution)/shard_map/all_gather | solution.py:37
  23.3 311.8 %reduce-scatter.5.cloned.1.call-start = ((), (), s32[]{:S(2)}) async-start(), calls=%async_computation.5 | async-start | bytes 2621440 | tf_op jit(solution)/shard_map/reduce_scatter | solution.py:41
  89.8 10.8 collective-permute-start
  94.2 14.7 %collective-permute-start.1 = (bf16[1024,4,64]{0,2,1:T(8,128)(2,1)}, bf16[1024,4,64]{0,2,1:T(8,128)(2,1)}, u32[]{:S(2)}, u32[]{:S(2)}) collective-permute-start(bf16[1024,4,64]{0,2,1:T(8,128)(2,1)} %get-tuple-element.1050), channel_id=1, source_target_pairs={{0,4},{4,8},{8,12},{12,16},{16,20},{20,24},{24,28},{1,5},{5,9},{9,... | collective-permute-start | bytes 1572872 | tf_op jit(solution)/shard_map/while/body/eval_jaxpr/ppermute | solution.py:19
  117.6 10.7 collective-permute-start
  121.9 14.7 %collective-permute-start.1 = (bf16[1024,4,64]{0,2,1:T(8,128)(2,1)}, bf16[1024,4,64]{0,2,1:T(8,128)(2,1)}, u32[]{:S(2)}, u32[]{:S(2)}) collective-permute-start(bf16[1024,4,64]{0,2,1:T(8,128)(2,1)} %get-tuple-element.1050), channel_id=1, source_target_pairs={{0,4},{4,8},{8,12},{12,16},{16,20},{20,24},{24,28},{1,5},{5,9},{9,... | collective-permute-start | bytes 1572872 | tf_op jit(solution)/shard_map/while/body/eval_jaxpr/ppermute | solution.py:19
  145.2 10.7 collective-permute-start
  149.5 14.7 %collective-permute-start.1 = (bf16[1024,4,64]{0,2,1:T(8,128)(2,1)}, bf16[1024,4,64]{0,2,1:T(8,128)(2,1)}, u32[]{:S(2)}, u32[]{:S(2)}) collective-permute-start(bf16[1024,4,64]{0,2,1:T(8,128)(2,1)} %get-tuple-element.1050), channel_id=1, source_target_pairs={{0,4},{4,8},{8,12},{12,16},{16,20},{20,24},{24,28},{1,5},{5,9},{9,... | collective-permute-start | bytes 1572872 | tf_op jit(solution)/shard_map/while/body/eval_jaxpr/ppermute | solution.py:19
  172.9 10.7 collective-permute-start
  177.2 14.7 %collective-permute-start.1 = (bf16[1024,4,64]{0,2,1:T(8,128)(2,1)}, bf16[1024,4,64]{0,2,1:T(8,128)(2,1)}, u32[]{:S(2)}, u32[]{:S(2)}) collective-permute-start(bf16[1024,4,64]{0,2,1:T(8,128)(2,1)} %get-tuple-element.1050), channel_id=1, source_target_pairs={{0,4},{4,8},{8,12},{12,16},{16,20},{20,24},{24,28},{1,5},{5,9},{9,... | collective-permute-start | bytes 1572872 | tf_op jit(solution)/shard_map/while/body/eval_jaxpr/ppermute | solution.py:19
  200.5 10.7 collective-permute-start
  204.8 14.7 %collective-permute-start.1 = (bf16[1024,4,64]{0,2,1:T(8,128)(2,1)}, bf16[1024,4,64]{0,2,1:T(8,128)(2,1)}, u32[]{:S(2)}, u32[]{:S(2)}) collective-permute-start(bf16[1024,4,64]{0,2,1:T(8,128)(2,1)} %get-tuple-element.1050), channel_id=1, source_target_pairs={{0,4},{4,8},{8,12},{12,16},{16,20},{20,24},{24,28},{1,5},{5,9},{9,... | collective-permute-start | bytes 1572872 | tf_op jit(solution)/shard_map/while/body/eval_jaxpr/ppermute | solution.py:19
  228.2 10.7 collective-permute-start
  232.5 14.7 %collective-permute-start.1 = (bf16[1024,4,64]{0,2,1:T(8,128)(2,1)}, bf16[1024,4,64]{0,2,1:T(8,128)(2,1)}, u32[]{:S(2)}, u32[]{:S(2)}) collective-permute-start(bf16[1024,4,64]{0,2,1:T(8,128)(2,1)} %get-tuple-element.1050), channel_id=1, source_target_pairs={{0,4},{4,8},{8,12},{12,16},{16,20},{20,24},{24,28},{1,5},{5,9},{9,... | collective-permute-start | bytes 1572872 | tf_op jit(solution)/shard_map/while/body/eval_jaxpr/ppermute | solution.py:19
  255.8 11.3 collective-permute-start
  260.7 14.7 %collective-permute-start.1 = (bf16[1024,4,64]{0,2,1:T(8,128)(2,1)}, bf16[1024,4,64]{0,2,1:T(8,128)(2,1)}, u32[]{:S(2)}, u32[]{:S(2)}) collective-permute-start(bf16[1024,4,64]{0,2,1:T(8,128)(2,1)} %get-tuple-element.1050), channel_id=1, source_target_pairs={{0,4},{4,8},{8,12},{12,16},{16,20},{20,24},{24,28},{1,5},{5,9},{9,... | collective-permute-start | bytes 1572872 | tf_op jit(solution)/shard_map/while/body/eval_jaxpr/ppermute | solution.py:19
  284.1 306.4 %copy-start.34 = (f32[4,1024]{1,0:T(4,128)}, f32[4,1024]{1,0:T(4,128)S(1)}, u32[]{:S(2)}) copy-start(f32[4,1024]{1,0:T(4,128)S(1)} %get-tuple-element.635) | copy-start | bytes 49156
  287.6 60.2 %copy-start.49 = (bf16[1024]{0:T(1024)(128)(2,1)S(1)}, bf16[1024]{0:T(1024)(128)(2,1)}, u32[]{:S(2)}) copy-start(bf16[1024]{0:T(1024)(128)(2,1)} %param.36) | copy-start | bytes 6148
  287.6 105.4 %all-gather.7.cloned.1.call-start = ((), (), s32[]{:S(2)}) async-start(), calls=%async_computation.6 | async-start | bytes 2621440 | tf_op jit(solution)/shard_map/all_gather | solution.py:37
  347.1 91.8 %all-gather.9.cloned.1.call-start = ((), (), s32[]{:S(2)}) async-start(), calls=%async_computation.8 | async-start | bytes 2621440 | tf_op jit(solution)/shard_map/all_gather | solution.py:37
  347.7 147.3 %reduce-scatter.9.cloned.1.call-start = ((), (), s32[]{:S(2)}) async-start(), calls=%async_computation.9 | async-start | bytes 2621440 | tf_op jit(solution)/shard_map/reduce_scatter | solution.py:41
  452.2 88.8 %reduce-scatter.7.cloned.1.call-start = ((), (), s32[]{:S(2)}) async-start(), calls=%async_computation.7 | async-start | bytes 2621440 | tf_op jit(solution)/shard_map/reduce_scatter | solution.py:41
  458.6 131.8 %all-gather.11.cloned.1.call-start = ((), (), s32[]{:S(2)}) async-start(), calls=%async_computation.10 | async-start | bytes 2621440 | tf_op jit(solution)/shard_map/all_gather | solution.py:37
  545.2 554.6 %all-reduce.8.cloned.1.call-start = ((), (), s32[]{:S(2)}) async-start(), calls=%async_computation.12 | async-start | bytes 12582912 | tf_op jit(solution)/shard_map/psum | solution.py:302
  594.2 397.2 %copy-start.29 = (bf16[4,1024,10]{1,2,0:T(8,128)(2,1)S(1)}, bf16[4,1024,10]{1,2,0:T(8,128)(2,1)}, u32[]{:S(2)}) copy-start(bf16[4,1024,10]{1,2,0:T(8,128)(2,1)} %fusion.74) | copy-start | bytes 245764
  594.2 397.2 %copy-start.39 = (bf16[10,4,128]{2,0,1:T(8,128)(2,1)S(1)}, bf16[10,4,128]{2,0,1:T(8,128)(2,1)}, u32[]{:S(2)}) copy-start(bf16[10,4,128]{2,0,1:T(8,128)(2,1)} %copy-done.37) | copy-start | bytes 30724
  595.5 49.6 %collective-permute-start.3 = (bf16[1024,4,64]{0,2,1:T(8,128)(2,1)}, bf16[1024,4,64]{0,2,1:T(8,128)(2,1)S(1)}, u32[]{:S(2)}, u32[]{:S(2)}) collective-permute-start(bf16[1024,4,64]{0,2,1:T(8,128)(2,1)} %copy.83), channel_id=1, source_target_pairs={{0,4},{4,8},{8,12},{12,16},{16,20},{20,24},{24,28},{1,5},{5,9},{9,... | collective-permute-start | bytes 1572872 | tf_op jit(solution)/shard_map/while/body/eval_jaxpr/ppermute | solution.py:19
  599.9 45.2 %collective-permute-start.2 = (bf16[1024,4,64]{0,2,1:T(8,128)(2,1)S(1)}, bf16[1024,4,64]{0,2,1:T(8,128)(2,1)S(1)}, u32[]{:S(2)}, u32[]{:S(2)}) collective-permute-start(bf16[1024,4,64]{0,2,1:T(8,128)(2,1)S(1)} %copy.82), channel_id=1, source_target_pairs={{0,4},{4,8},{8,12},{12,16},{16,20},{20,24},{24,28},{1,5},{5,9},{9,... | collective-permute-start | bytes 1572872 | tf_op jit(solution)/shard_map/while/body/eval_jaxpr/ppermute | solution.py:19
  624.4 16.4 %collective-permute-start.4 = (bf16[1024,4,64]{0,2,1:T(8,128)(2,1)}, bf16[1024,4,64]{0,2,1:T(8,128)(2,1)}, u32[]{:S(2)}, u32[]{:S(2)}) collective-permute-start(bf16[1024,4,64]{0,2,1:T(8,128)(2,1)} %fusion.222), channel_id=1, source_target_pairs={{0,4},{4,8},{8,12},{12,16},{16,20},{20,24},{24,28},{28,0},{1,5},{5... | collective-permute-start | bytes 1572872 | tf_op jit(solution)/shard_map/while/body/eval_jaxpr/ppermute | solution.py:25
  634.6 8.3 collective-permute-start.5
  645.8 48.6 %collective-permute-start.3 = (bf16[1024,4,64]{0,2,1:T(8,128)(2,1)}, bf16[1024,4,64]{0,2,1:T(8,128)(2,1)S(1)}, u32[]{:S(2)}, u32[]{:S(2)}) collective-permute-start(bf16[1024,4,64]{0,2,1:T(8,128)(2,1)} %copy.83), channel_id=1, source_target_pairs={{0,4},{4,8},{8,12},{12,16},{16,20},{20,24},{24,28},{1,5},{5,9},{9,... | collective-permute-start | bytes 1572872 | tf_op jit(solution)/shard_map/while/body/eval_jaxpr/ppermute | solution.py:19
  649.3 45.1 %collective-permute-start.2 = (bf16[1024,4,64]{0,2,1:T(8,128)(2,1)S(1)}, bf16[1024,4,64]{0,2,1:T(8,128)(2,1)S(1)}, u32[]{:S(2)}, u32[]{:S(2)}) collective-permute-start(bf16[1024,4,64]{0,2,1:T(8,128)(2,1)S(1)} %copy.82), channel_id=1, source_target_pairs={{0,4},{4,8},{8,12},{12,16},{16,20},{20,24},{24,28},{1,5},{5,9},{9,... | collective-permute-start | bytes 1572872 | tf_op jit(solution)/shard_map/while/body/eval_jaxpr/ppermute | solution.py:19
  673.8 16.3 %collective-permute-start.4 = (bf16[1024,4,64]{0,2,1:T(8,128)(2,1)}, bf16[1024,4,64]{0,2,1:T(8,128)(2,1)}, u32[]{:S(2)}, u32[]{:S(2)}) collective-permute-start(bf16[1024,4,64]{0,2,1:T(8,128)(2,1)} %fusion.222), channel_id=1, source_target_pairs={{0,4},{4,8},{8,12},{12,16},{16,20},{20,24},{24,28},{28,0},{1,5},{5... | collective-permute-start | bytes 1572872 | tf_op jit(solution)/shard_map/while/body/eval_jaxpr/ppermute | solution.py:25
  684.0 8.3 collective-permute-start.5
  695.2 47.7 %collective-permute-start.3 = (bf16[1024,4,64]{0,2,1:T(8,128)(2,1)}, bf16[1024,4,64]{0,2,1:T(8,128)(2,1)S(1)}, u32[]{:S(2)}, u32[]{:S(2)}) collective-permute-start(bf16[1024,4,64]{0,2,1:T(8,128)(2,1)} %copy.83), channel_id=1, source_target_pairs={{0,4},{4,8},{8,12},{12,16},{16,20},{20,24},{24,28},{1,5},{5,9},{9,... | collective-permute-start | bytes 1572872 | tf_op jit(solution)/shard_map/while/body/eval_jaxpr/ppermute | solution.py:19
  697.9 45.1 %collective-permute-start.2 = (bf16[1024,4,64]{0,2,1:T(8,128)(2,1)S(1)}, bf16[1024,4,64]{0,2,1:T(8,128)(2,1)S(1)}, u32[]{:S(2)}, u32[]{:S(2)}) collective-permute-start(bf16[1024,4,64]{0,2,1:T(8,128)(2,1)S(1)} %copy.82), channel_id=1, source_target_pairs={{0,4},{4,8},{8,12},{12,16},{16,20},{20,24},{24,28},{1,5},{5,9},{9,... | collective-permute-start | bytes 1572872 | tf_op jit(solution)/shard_map/while/body/eval_jaxpr/ppermute | solution.py:19
  722.4 16.3 %collective-permute-start.4 = (bf16[1024,4,64]{0,2,1:T(8,128)(2,1)}, bf16[1024,4,64]{0,2,1:T(8,128)(2,1)}, u32[]{:S(2)}, u32[]{:S(2)}) collective-permute-start(bf16[1024,4,64]{0,2,1:T(8,128)(2,1)} %fusion.222), channel_id=1, source_target_pairs={{0,4},{4,8},{8,12},{12,16},{16,20},{20,24},{24,28},{28,0},{1,5},{5... | collective-permute-start | bytes 1572872 | tf_op jit(solution)/shard_map/while/body/eval_jaxpr/ppermute | solution.py:25
  732.5 8.3 collective-permute-start.5
  743.8 48.6 %collective-permute-start.3 = (bf16[1024,4,64]{0,2,1:T(8,128)(2,1)}, bf16[1024,4,64]{0,2,1:T(8,128)(2,1)S(1)}, u32[]{:S(2)}, u32[]{:S(2)}) collective-permute-start(bf16[1024,4,64]{0,2,1:T(8,128)(2,1)} %copy.83), channel_id=1, source_target_pairs={{0,4},{4,8},{8,12},{12,16},{16,20},{20,24},{24,28},{1,5},{5,9},{9,... | collective-permute-start | bytes 1572872 | tf_op jit(solution)/shard_map/while/body/eval_jaxpr/ppermute | solution.py:19
  747.3 45.1 %collective-permute-start.2 = (bf16[1024,4,64]{0,2,1:T(8,128)(2,1)S(1)}, bf16[1024,4,64]{0,2,1:T(8,128)(2,1)S(1)}, u32[]{:S(2)}, u32[]{:S(2)}) collective-permute-start(bf16[1024,4,64]{0,2,1:T(8,128)(2,1)S(1)} %copy.82), channel_id=1, source_target_pairs={{0,4},{4,8},{8,12},{12,16},{16,20},{20,24},{24,28},{1,5},{5,9},{9,... | collective-permute-start | bytes 1572872 | tf_op jit(solution)/shard_map/while/body/eval_jaxpr/ppermute | solution.py:19
  771.8 16.3 %collective-permute-start.4 = (bf16[1024,4,64]{0,2,1:T(8,128)(2,1)}, bf16[1024,4,64]{0,2,1:T(8,128)(2,1)}, u32[]{:S(2)}, u32[]{:S(2)}) collective-permute-start(bf16[1024,4,64]{0,2,1:T(8,128)(2,1)} %fusion.222), channel_id=1, source_target_pairs={{0,4},{4,8},{8,12},{12,16},{16,20},{20,24},{24,28},{28,0},{1,5},{5... | collective-permute-start | bytes 1572872 | tf_op jit(solution)/shard_map/while/body/eval_jaxpr/ppermute | solution.py:25
  782.0 8.3 collective-permute-start.5
  793.2 47.7 %collective-permute-start.3 = (bf16[1024,4,64]{0,2,1:T(8,128)(2,1)}, bf16[1024,4,64]{0,2,1:T(8,128)(2,1)S(1)}, u32[]{:S(2)}, u32[]{:S(2)}) collective-permute-start(bf16[1024,4,64]{0,2,1:T(8,128)(2,1)} %copy.83), channel_id=1, source_target_pairs={{0,4},{4,8},{8,12},{12,16},{16,20},{20,24},{24,28},{1,5},{5,9},{9,... | collective-permute-start | bytes 1572872 | tf_op jit(solution)/shard_map/while/body/eval_jaxpr/ppermute | solution.py:19
  795.9 45.1 %collective-permute-start.2 = (bf16[1024,4,64]{0,2,1:T(8,128)(2,1)S(1)}, bf16[1024,4,64]{0,2,1:T(8,128)(2,1)S(1)}, u32[]{:S(2)}, u32[]{:S(2)}) collective-permute-start(bf16[1024,4,64]{0,2,1:T(8,128)(2,1)S(1)} %copy.82), channel_id=1, source_target_pairs={{0,4},{4,8},{8,12},{12,16},{16,20},{20,24},{24,28},{1,5},{5,9},{9,... | collective-permute-start | bytes 1572872 | tf_op jit(solution)/shard_map/while/body/eval_jaxpr/ppermute | solution.py:19
  820.3 16.3 %collective-permute-start.4 = (bf16[1024,4,64]{0,2,1:T(8,128)(2,1)}, bf16[1024,4,64]{0,2,1:T(8,128)(2,1)}, u32[]{:S(2)}, u32[]{:S(2)}) collective-permute-start(bf16[1024,4,64]{0,2,1:T(8,128)(2,1)} %fusion.222), channel_id=1, source_target_pairs={{0,4},{4,8},{8,12},{12,16},{16,20},{20,24},{24,28},{28,0},{1,5},{5... | collective-permute-start | bytes 1572872 | tf_op jit(solution)/shard_map/while/body/eval_jaxpr/ppermute | solution.py:25
  830.5 8.3 collective-permute-start.5
  841.8 48.7 %collective-permute-start.3 = (bf16[1024,4,64]{0,2,1:T(8,128)(2,1)}, bf16[1024,4,64]{0,2,1:T(8,128)(2,1)S(1)}, u32[]{:S(2)}, u32[]{:S(2)}) collective-permute-start(bf16[1024,4,64]{0,2,1:T(8,128)(2,1)} %copy.83), channel_id=1, source_target_pairs={{0,4},{4,8},{8,12},{12,16},{16,20},{20,24},{24,28},{1,5},{5,9},{9,... | collective-permute-start | bytes 1572872 | tf_op jit(solution)/shard_map/while/body/eval_jaxpr/ppermute | solution.py:19
  845.3 45.1 %collective-permute-start.2 = (bf16[1024,4,64]{0,2,1:T(8,128)(2,1)S(1)}, bf16[1024,4,64]{0,2,1:T(8,128)(2,1)S(1)}, u32[]{:S(2)}, u32[]{:S(2)}) collective-permute-start(bf16[1024,4,64]{0,2,1:T(8,128)(2,1)S(1)} %copy.82), channel_id=1, source_target_pairs={{0,4},{4,8},{8,12},{12,16},{16,20},{20,24},{24,28},{1,5},{5,9},{9,... | collective-permute-start | bytes 1572872 | tf_op jit(solution)/shard_map/while/body/eval_jaxpr/ppermute | solution.py:19
  869.8 16.3 %collective-permute-start.4 = (bf16[1024,4,64]{0,2,1:T(8,128)(2,1)}, bf16[1024,4,64]{0,2,1:T(8,128)(2,1)}, u32[]{:S(2)}, u32[]{:S(2)}) collective-permute-start(bf16[1024,4,64]{0,2,1:T(8,128)(2,1)} %fusion.222), channel_id=1, source_target_pairs={{0,4},{4,8},{8,12},{12,16},{16,20},{20,24},{24,28},{28,0},{1,5},{5... | collective-permute-start | bytes 1572872 | tf_op jit(solution)/shard_map/while/body/eval_jaxpr/ppermute | solution.py:25
  880.0 8.3 collective-permute-start.5
  891.2 47.7 %collective-permute-start.3 = (bf16[1024,4,64]{0,2,1:T(8,128)(2,1)}, bf16[1024,4,64]{0,2,1:T(8,128)(2,1)S(1)}, u32[]{:S(2)}, u32[]{:S(2)}) collective-permute-start(bf16[1024,4,64]{0,2,1:T(8,128)(2,1)} %copy.83), channel_id=1, source_target_pairs={{0,4},{4,8},{8,12},{12,16},{16,20},{20,24},{24,28},{1,5},{5,9},{9,... | collective-permute-start | bytes 1572872 | tf_op jit(solution)/shard_map/while/body/eval_jaxpr/ppermute | solution.py:19
  893.9 45.1 %collective-permute-start.2 = (bf16[1024,4,64]{0,2,1:T(8,128)(2,1)S(1)}, bf16[1024,4,64]{0,2,1:T(8,128)(2,1)S(1)}, u32[]{:S(2)}, u32[]{:S(2)}) collective-permute-start(bf16[1024,4,64]{0,2,1:T(8,128)(2,1)S(1)} %copy.82), channel_id=1, source_target_pairs={{0,4},{4,8},{8,12},{12,16},{16,20},{20,24},{24,28},{1,5},{5,9},{9,... | collective-permute-start | bytes 1572872 | tf_op jit(solution)/shard_map/while/body/eval_jaxpr/ppermute | solution.py:19
  918.3 16.3 %collective-permute-start.4 = (bf16[1024,4,64]{0,2,1:T(8,128)(2,1)}, bf16[1024,4,64]{0,2,1:T(8,128)(2,1)}, u32[]{:S(2)}, u32[]{:S(2)}) collective-permute-start(bf16[1024,4,64]{0,2,1:T(8,128)(2,1)} %fusion.222), channel_id=1, source_target_pairs={{0,4},{4,8},{8,12},{12,16},{16,20},{20,24},{24,28},{28,0},{1,5},{5... | collective-permute-start | bytes 1572872 | tf_op jit(solution)/shard_map/while/body/eval_jaxpr/ppermute | solution.py:25
  928.5 8.3 collective-permute-start.5
  939.7 48.7 %collective-permute-start.3 = (bf16[1024,4,64]{0,2,1:T(8,128)(2,1)}, bf16[1024,4,64]{0,2,1:T(8,128)(2,1)S(1)}, u32[]{:S(2)}, u32[]{:S(2)}) collective-permute-start(bf16[1024,4,64]{0,2,1:T(8,128)(2,1)} %copy.83), channel_id=1, source_target_pairs={{0,4},{4,8},{8,12},{12,16},{16,20},{20,24},{24,28},{1,5},{5,9},{9,... | collective-permute-start | bytes 1572872 | tf_op jit(solution)/shard_map/while/body/eval_jaxpr/ppermute | solution.py:19
  943.3 45.1 %collective-permute-start.2 = (bf16[1024,4,64]{0,2,1:T(8,128)(2,1)S(1)}, bf16[1024,4,64]{0,2,1:T(8,128)(2,1)S(1)}, u32[]{:S(2)}, u32[]{:S(2)}) collective-permute-start(bf16[1024,4,64]{0,2,1:T(8,128)(2,1)S(1)} %copy.82), channel_id=1, source_target_pairs={{0,4},{4,8},{8,12},{12,16},{16,20},{20,24},{24,28},{1,5},{5,9},{9,... | collective-permute-start | bytes 1572872 | tf_op jit(solution)/shard_map/while/body/eval_jaxpr/ppermute | solution.py:19
  967.8 16.3 %collective-permute-start.4 = (bf16[1024,4,64]{0,2,1:T(8,128)(2,1)}, bf16[1024,4,64]{0,2,1:T(8,128)(2,1)}, u32[]{:S(2)}, u32[]{:S(2)}) collective-permute-start(bf16[1024,4,64]{0,2,1:T(8,128)(2,1)} %fusion.222), channel_id=1, source_target_pairs={{0,4},{4,8},{8,12},{12,16},{16,20},{20,24},{24,28},{28,0},{1,5},{5... | collective-permute-start | bytes 1572872 | tf_op jit(solution)/shard_map/while/body/eval_jaxpr/ppermute | solution.py:25
  978.0 8.3 collective-permute-start.5
  997.9 148.7 %reduce-scatter.11.cloned.1.call-start = ((), (), s32[]{:S(2)}) async-start(), calls=%async_computation.11 | async-start | bytes 2621440 | tf_op jit(solution)/shard_map/reduce_scatter | solution.py:41
  1108.1 63.7 %copy-start.21 = (bf16[512,4,128]{2,1,0:T(4,128)(2,1)S(1)}, bf16[512,4,128]{2,1,0:T(4,128)(2,1)}, u32[]{:S(2)}) copy-start(bf16[512,4,128]{2,1,0:T(4,128)(2,1)} %param.42) | copy-start | bytes 1572868
  1108.2 78.1 %copy-start.28 = (f32[10,512]{1,0:T(8,128)S(1)}, f32[10,512]{1,0:T(8,128)}, u32[]{:S(2)}) copy-start(f32[10,512]{1,0:T(8,128)} %copy-done.27) | copy-start | bytes 61444
  1108.2 78.7 %copy-start.18 = (bf16[1024,512]{1,0:T(8,128)(2,1)S(1)}, bf16[1024,512]{1,0:T(8,128)(2,1)}, u32[]{:S(2)}) copy-start(bf16[1024,512]{1,0:T(8,128)(2,1)} %param.40) | copy-start | bytes 3145732
  1108.2 80.9 %copy-start.40 = (bf16[10,1024]{1,0:T(8,128)(2,1)S(1)}, bf16[10,1024]{1,0:T(8,128)(2,1)}, u32[]{:S(2)}) copy-start(bf16[10,1024]{1,0:T(8,128)(2,1)} %param.39) | copy-start | bytes 61444
  (92 other events, 1016.6 us)
Sparse Core Ops, SparseCore 0:
  23.4 45.9 all-gather.4
  287.7 47.3 reduce-scatter.4
  347.2 45.6 all-gather.6
  394.5 44.4 all-gather.8
  452.3 42.6 reduce-scatter.8
  497.7 43.2 reduce-scatter.6
  545.4 45.0 all-gather.10
  998.0 101.8 all-reduce.7
  1102.7 43.8 reduce-scatter.10
where the time goes:
time: 1230 us; the launch traced here: 1210 us
  matrix products  420 us (34%)
  waiting for transfers between devices  410 us (33%)
  other arithmetic  133 us (11%)
  starting transfers between devices  107 us (9%)
  blocking collectives  75.3 us (6%)
  local copies, waits for them, and re-layouts  46.8 us (4%)
  between operations  14.8 us (1%)
    reduce_scatter x4, waiting for transfers between devices, feature_sums(): lax.psum_scatter(values.astype(jnp.bfloat16), 'tensor', scatter_dimension...  155 us
    all_gather x4, waiting for transfers between devices, feature_rows(): return lax.all_gather(values, 'tensor', axis=1, tiled=True)  145 us
    psum x1, waiting for transfers between devices, on_device(): lax.psum(grad_w_qkv.astype(jnp.bfloat16), 'seq').astype(jnp.float32)  95.9 us
    ppermute x30, starting transfers between devices, shifted(): return lax.ppermute(array, axis, pairs)  94.5 us
    dot_general x9, matrix products, attend_back(): jnp.einsum('hqd,khd->hqk', grad_out, value_block, preferred_element_type=...  77.5 us
    dot_general x9, matrix products, attend_back(): jnp.einsum('hqk,hqd->khd', probs.astype(jnp.bfloat16), grad_out, preferre...  69.3 us
    dot_general x8, matrix products, attend_back(): jnp.einsum('qhd,khd->hqk', query, key_block, preferred_element_type=jnp.f...  65 us
    dot_general x9, matrix products, attend_back(): jnp.einsum('hqk,khd->qhd', grad_scores, key_block, preferred_element_type...  49.6 us
  transfers between devices with their start and end apart: 55, of which 15 were waited for; matrix products, arithmetic and copies ran while one was open for 37% of the time, Pallas kernels for 0%

commit v1 on v0

v1 whole, which is shorter than its diff:
```python
import functools

import jax
import jax.numpy as jnp
from jax import lax
from jax.experimental import pallas as pl
from jax.experimental.pallas import tpu as pltpu
from jax.sharding import PartitionSpec as P

EPS = 1e-05
NEGATIVE = -1e30
HIGHEST = lax.Precision.HIGHEST
F32 = jnp.float32
BF16 = jnp.bfloat16
LANES = 128
PAD = 16
WEAK = 1e-24
DOCS = 5

VM = pl.BlockSpec(memory_space=pltpu.VMEM)
SM = pl.BlockSpec(memory_space=pltpu.SMEM)


def gelu_tanh(values):
    return jax.nn.gelu(values, approximate=True)


def contract(first, second, first_dim, second_dim):
    return lax.dot_general(
        first, second, (((first_dim,), (second_dim,)), ((), ())), preferred_element_type=F32
    )


def work(queries, keys, products):
    pairs = queries * keys // 2
    return pl.CostEstimate(
        flops=2 * 256 * products * pairs, bytes_accessed=8 * 2**20, transcendentals=pairs
    )


def after(values, other):
    return lax.optimization_barrier((values, other))[0]


def document_start(meta, place):
    found = jnp.zeros_like(place) if getattr(place, "shape", ()) else jnp.int32(0)
    for number in range(DOCS - 1):
        begin = meta[number]
        found = jnp.where(place >= begin, jnp.maximum(found, begin), found)
    return found


def query_places(meta, index, base, chunk, group):
    return base + (index // chunk) * (chunk * group) + meta[DOCS - 1] * chunk + index % chunk


def tile_bounds(meta, base, count, chunk, group):
    rank = meta[DOCS - 1]
    first = base + rank * chunk
    last = base + (count // chunk - 1) * (chunk * group) + rank * chunk + chunk - 1
    return first, last, document_start(meta, first), document_start(meta, last)


def one_row(rows, columns):
    return lax.broadcasted_iota(jnp.int32, (rows, columns), 0) == 0


def over_keys(bounds, keys, block):
    first, last, low, low_last = bounds

    def step(number, _):
        clear = (number * keys >= low_last) & ((number + 1) * keys - 1 <= first)

        @pl.when(clear)
        def _():
            block(number, False)

        @pl.when(jnp.logical_not(clear))
        def _():
            block(number, True)

        return 0

    lax.fori_loop(low // keys, last // keys + 1, step, 0)


def allowed(meta, number, keys, places):
    key = number * keys + lax.broadcasted_iota(jnp.int32, (keys, 1), 0)
    return (key <= places) & (key >= document_start(meta, places))


def forward_kernel(
    meta, query, key, value, pre_key, pre_value,
    out_low, out_full, log_total,
    key_rows, value_ones, accum, peak,
    *, tile, keys, prefix, chunk, group,
):
    sources, size, length = key.shape
    blocks, _, width = query.shape
    per, parts = width // tile, length // keys
    scale = size**-0.5
    padded = pre_key.shape[1]

    def extended(values, count, total):
        ones = jnp.where(one_row(PAD, count), 1.0, 0.0).astype(BF16)
        rest = total - size - PAD
        tail = [jnp.zeros((rest, count), BF16)] if rest else []
        return jnp.concatenate([values, ones] + tail, 0)

    def longest(values):
        wide = values.astype(F32)
        return jnp.max(jnp.sum(wide * wide, 0, keepdims=True), 1, keepdims=True)

    def prepare(source, most):
        rows = pl.ds(pl.multiple_of(source * length, length), length)
        key_rows[rows, :] = extended(key[source], length, LANES).astype(F32).T.astype(BF16)
        value_ones[source] = extended(value[source], length, size + PAD)
        return jnp.maximum(most, longest(key[source]))

    most = jnp.sqrt(lax.fori_loop(0, sources, prepare, longest(pre_key[...])))
    pre_key_ones = extended(pre_key[...], padded, LANES)
    pre_value_ones = extended(pre_value[...], padded, size + PAD)
    pre_row = lax.broadcasted_iota(jnp.int32, (padded, tile), 0)

    def query_tile(number, _):
        source, part = number // per, number % per
        base = number * tile * group
        columns = pl.ds(pl.multiple_of(part * tile, tile), tile)
        scaled = query[source, :, columns].astype(F32) * scale
        limit = jnp.sqrt(jnp.sum(scaled * scaled, 0, keepdims=True)) * most
        limit = limit.astype(BF16).astype(F32)
        shifted = jnp.concatenate(
            [
                scaled,
                jnp.where(one_row(PAD, tile), -limit, 0.0),
                jnp.zeros((LANES - size - PAD, tile), F32),
            ],
            0,
        ).astype(BF16)
        index = lax.broadcasted_iota(jnp.int32, (1, tile), 1)
        places = query_places(meta, index, base, chunk, group)
        bounds = tile_bounds(meta, base, tile, chunk, group)

        weights = jnp.where(pre_row < prefix, jnp.exp(contract(pre_key_ones, shifted, 0, 0)), 0.0)
        accum[...] = contract(pre_value_ones, weights.astype(BF16), 1, 0)

        def block(number, masked):
            rows = pl.ds(pl.multiple_of(number * keys, keys), keys)
            lanes = pl.ds(pl.multiple_of((number % parts) * keys, keys), keys)
            weights = jnp.exp(contract(key_rows[rows, :], shifted, 1, 0))
            if masked:
                weights = jnp.where(allowed(meta, number, keys, places), weights, 0.0)
            accum[...] += contract(value_ones[number // parts, :, lanes], weights.astype(BF16), 1, 0)

        over_keys(bounds, keys, block)
        peak[...] = limit

        @pl.when(jnp.min(accum[size : size + 1, :]) < WEAK)
        def _():
            plain = scaled.astype(BF16)

            def fold(scores, mask, values):
                scores = jnp.where(mask, scores, NEGATIVE)
                new = jnp.maximum(peak[...], jnp.max(scores, 0, keepdims=True))
                weights = jnp.where(mask, jnp.exp(scores - new), 0.0).astype(BF16)
                accum[...] = accum[...] * jnp.exp(peak[...] - new) + contract(values, weights, 1, 0)
                peak[...] = new

            peak[...] = jnp.full(peak.shape, NEGATIVE, F32)
            accum[...] = jnp.zeros(accum.shape, F32)
            fold(contract(pre_key[...], plain, 0, 0), pre_row < prefix, pre_value_ones)

            def slow(number, masked):
                rows = pl.ds(pl.multiple_of(number * keys, keys), keys)
                lanes = pl.ds(pl.multiple_of((number % parts) * keys, keys), keys)
                scores = contract(key_rows[rows, :][:, :size], plain, 1, 0)
                fold(
                    scores,
                    allowed(meta, number, keys, places),
                    value_ones[number // parts, :, lanes],
                )

            def step(number, _):
                slow(number, True)
                return 0

            lax.fori_loop(bounds[2] // keys, bounds[1] // keys + 1, step, 0)

        total = accum[size : size + 1, :]
        result = accum[:size, :] / total
        log_total[number] = peak[...] + jnp.log(total)
        for part in range(tile // LANES):
            piece = result[:, part * LANES : (part + 1) * LANES]
            out_full[number * (tile // LANES) + part] = piece
            out_low[number * (tile // LANES) + part] = piece.astype(BF16)
        return 0

    lax.fori_loop(0, blocks * per, query_tile, 0)


def attend_forward(meta, query, key, value, pre_key, pre_value, tile, keys, prefix, chunk, group):
    sources, size, length = key.shape
    count = query.shape[0] * query.shape[2]
    return pl.pallas_call(
        functools.partial(
            forward_kernel, tile=tile, keys=keys, prefix=prefix, chunk=chunk, group=group
        ),
        out_shape=(
            jax.ShapeDtypeStruct((count // LANES, size, LANES), BF16),
            jax.ShapeDtypeStruct((count // LANES, size, LANES), F32),
            jax.ShapeDtypeStruct((count // tile, 1, tile), F32),
        ),
        in_specs=[SM] + [VM] * 5,
        out_specs=(VM, VM, VM),
        scratch_shapes=[
            pltpu.VMEM((sources * length, LANES), BF16),
            pltpu.VMEM((sources, size + PAD, length), BF16),
            pltpu.VMEM((size + PAD, tile), F32),
            pltpu.VMEM((1, tile), F32),
        ],
        compiler_params=pltpu.CompilerParams(vmem_limit_bytes=48 * 2**20),
        cost_estimate=work(count, sources * length, 2),
        name="attend_forward",
    )(meta, query, key, value, pre_key, pre_value)


def backward_kernel(
    meta, query, key, value, pre_key, pre_value, grad_out, out_full, log_total,
    grad_query, grad_keep, grad_prefix,
    key_rows, value_rows, key_sum, value_sum, query_sum,
    *, tile, keys, prefix, chunk, group,
):
    sources, size, length = key.shape
    blocks, _, width = query.shape
    per, parts = width // tile, length // keys
    scale = size**-0.5
    count = tile // LANES
    rank = meta[DOCS - 1]

    def prepare(source, _):
        rows = pl.ds(pl.multiple_of(source * length, length), length)
        key_rows[rows, :] = key[source].astype(F32).T.astype(BF16)
        value_rows[rows, :] = value[source].astype(F32).T.astype(BF16)
        key_sum[rows, :] = jnp.zeros((length, size), F32)
        value_sum[rows, :] = jnp.zeros((length, size), F32)
        return 0

    lax.fori_loop(0, sources, prepare, 0)
    grad_prefix[...] = jnp.zeros(grad_prefix.shape, F32)
    pre_row = lax.broadcasted_iota(jnp.int32, (pre_key.shape[0], tile), 0)

    def query_tile(number, _):
        source, part = number // per, number % per
        base = number * tile * group
        columns = pl.ds(pl.multiple_of(part * tile, tile), tile)
        scaled = (query[source, :, columns].astype(F32) * scale).astype(BF16)
        pieces = [number * count + piece for piece in range(count)]
        grad = jnp.concatenate([grad_out[piece] for piece in pieces], 1)
        full = jnp.concatenate([out_full[piece] for piece in pieces], 1)
        delta = jnp.sum(grad.astype(F32) * full, 0, keepdims=True)
        level = log_total[number]
        index = lax.broadcasted_iota(jnp.int32, (1, tile), 1)
        places = query_places(meta, index, base, chunk, group)
        bounds = tile_bounds(meta, base, tile, chunk, group)

        probs = jnp.exp(contract(pre_key[...], scaled, 1, 0) - level)
        probs = jnp.where(pre_row < prefix, probs, 0.0)
        slope = (probs * (contract(pre_value[...], grad, 1, 0) - delta)).astype(BF16)
        grad_prefix[0] += contract(slope, scaled, 1, 1)
        grad_prefix[1] += contract(probs.astype(BF16), grad, 1, 1)
        query_sum[...] = contract(pre_key[...], slope, 0, 0)

        def block(number, masked):
            rows = pl.ds(pl.multiple_of(number * keys, keys), keys)
            lanes = pl.ds(pl.multiple_of((number % parts) * keys, keys), keys)
            probs = jnp.exp(contract(key_rows[rows, :], scaled, 1, 0) - level)
            if masked:
                probs = jnp.where(allowed(meta, number, keys, places), probs, 0.0)
            slope = contract(value_rows[rows, :], grad, 1, 0)
            slope = (probs * (slope - delta)).astype(BF16)
            value_sum[rows, :] += contract(probs.astype(BF16), grad, 1, 1)
            key_sum[rows, :] += contract(slope, scaled, 1, 1)
            query_sum[...] += contract(key[number // parts, :, lanes], slope, 1, 0)

        over_keys(bounds, keys, block)
        grad_query[source, :, columns] = (query_sum[...] * scale).astype(BF16)
        return 0

    lax.fori_loop(0, blocks * per, query_tile, 0)
    key_slot = rank if group == 2 else 0
    value_slot = 1 - rank if group == 2 else 1

    def flush(source, _):
        rows = pl.ds(pl.multiple_of(source * length, length), length)
        grad_keep[key_slot, source] = key_sum[rows, :].T.astype(BF16)
        grad_keep[value_slot, source] = value_sum[rows, :].T.astype(BF16)
        return 0

    lax.fori_loop(0, sources, flush, 0)


def attend_backward(
    meta, query, key, value, pre_key, pre_value, grad_out, out_full, log_total,
    tile, keys, prefix, chunk, group,
):
    sources, size, length = key.shape
    return pl.pallas_call(
        functools.partial(
            backward_kernel, tile=tile, keys=keys, prefix=prefix, chunk=chunk, group=group
        ),
        out_shape=(
            jax.ShapeDtypeStruct(query.shape, BF16),
            jax.ShapeDtypeStruct((2,) + key.shape, BF16),
            jax.ShapeDtypeStruct((2,) + pre_key.shape, F32),
        ),
        in_specs=[SM] + [VM] * 8,
        out_specs=(VM, VM, VM),
        scratch_shapes=[
            pltpu.VMEM((sources * length, size), BF16),
            pltpu.VMEM((sources * length, size), BF16),
            pltpu.VMEM((sources * length, size), F32),
            pltpu.VMEM((sources * length, size), F32),
            pltpu.VMEM((size, tile), F32),
        ],
        compiler_params=pltpu.CompilerParams(vmem_limit_bytes=56 * 2**20),
        cost_estimate=work(query.shape[0] * query.shape[2], sources * length, 5),
        name="attend_backward",
    )(meta, query, key, value, pre_key, pre_value, grad_out, out_full, log_total)


def turn_kernel(*refs):
    count = len(refs) // 2
    for source, target in zip(refs[:count], refs[count:]):
        target[...] = source[...].astype(F32).T.astype(BF16)


def turned(*arrays):
    return pl.pallas_call(
        turn_kernel,
        out_shape=tuple(jax.ShapeDtypeStruct(a.shape[::-1], BF16) for a in arrays),
        in_specs=[VM] * len(arrays),
        out_specs=(VM,) * len(arrays),
        compiler_params=pltpu.CompilerParams(vmem_limit_bytes=32 * 2**20),
        name="turned",
    )(*arrays)


def project_kernel(rows, columns, weight, bias, full, sent, stats, *, heads, size, step):
    length = rows.shape[1]
    pieces = length // step
    half = step // 2
    width = length // 2
    for piece in range(pieces):
        lanes = slice(piece * step, (piece + 1) * step)
        values = rows[:, lanes].astype(F32)
        mean = jnp.mean(values, 0, keepdims=True)
        centered = values - mean
        inverse = lax.rsqrt(jnp.mean(centered * centered, 0, keepdims=True) + EPS)
        stats[0:1, lanes] = mean
        stats[1:2, lanes] = inverse
        low = (centered * inverse * columns[:, 0:1] + columns[:, 1:2]).astype(BF16)
        full[:, lanes] = low
        mixed = (contract(weight[...], low, 1, 0) + bias[...]).astype(BF16)
        for head in range(heads):
            part = mixed[head * 3 * size : (head + 1) * 3 * size]
            spot = slice(piece * half, (piece + 1) * half)
            sent[2 * head, :, spot] = part[:size, :half]
            sent[2 * head + 1, :, spot] = part[:size, half:]
            spot = slice(width + piece * step, width + (piece + 1) * step)
            sent[2 * head, :, spot] = part[size : 2 * size]
            sent[2 * head + 1, :, spot] = part[2 * size :]


def project(rows, columns, weight, bias, heads, size, step):
    width, length = rows.shape
    return pl.pallas_call(
        functools.partial(project_kernel, heads=heads, size=size, step=step),
        out_shape=(
            jax.ShapeDtypeStruct((width, length), BF16),
            jax.ShapeDtypeStruct((2 * heads, size, length // 2 * 3), BF16),
            jax.ShapeDtypeStruct((2, length), F32),
        ),
        in_specs=[VM] * 4,
        out_specs=(VM, VM, VM),
        compiler_params=pltpu.CompilerParams(vmem_limit_bytes=40 * 2**20),
        name="project",
    )(rows, columns, weight, bias)


def unproject_kernel(
    slot, came, weight, rows, stats, columns, own_grad,
    flat, part, row_sums, sums, head_sums,
    *, heads, size, step,
):
    length = rows.shape[1]
    half = step // 2
    width = length // 2
    gain = columns[:, 0:1]
    sums[...] = jnp.zeros(sums.shape, F32)
    head_sums[...] = jnp.zeros(head_sums.shape, F32)
    for piece in range(length // step):
        lanes = slice(piece * step, (piece + 1) * step)
        spot = slice(piece * half, (piece + 1) * half)
        pair = slice(width + piece * step, width + (piece + 1) * step)
        pieces = []
        for head in range(heads):
            first, second = came[2 * head], came[2 * head + 1]
            pieces.append(jnp.concatenate([first[:, spot], second[:, spot]], 1))
            pieces += [first[:, pair], second[:, pair]]
        grads = jnp.concatenate(pieces, 0)
        flat[:, lanes] = grads
        head_sums[...] += jnp.sum(grads.astype(F32), 1, keepdims=True)
        back = contract(weight[...], grads, 1, 0)
        part[:, lanes] = back.astype(BF16)

        @pl.when(slot[0] == piece)
        def _():
            part[:, lanes] = (back + own_grad[...] / (stats[1:2, lanes] * gain)).astype(BF16)

        normed = (rows[:, lanes].astype(F32) - stats[0:1, lanes]) * stats[1:2, lanes]
        scaled = back * gain
        row_sums[0:1, lanes] = jnp.sum(scaled, 0, keepdims=True)
        row_sums[1:2, lanes] = jnp.sum(scaled * normed, 0, keepdims=True)
        sums[:, 0:1] += jnp.sum(back * normed, 1, keepdims=True)
        sums[:, 1:2] += jnp.sum(back, 1, keepdims=True)


def unproject(slot, came, weight, rows, stats, columns, own_grad, heads, size, step):
    width, length = rows.shape
    return pl.pallas_call(
        functools.partial(unproject_kernel, heads=heads, size=size, step=step),
        out_shape=(
            jax.ShapeDtypeStruct((3 * heads * size, length), BF16),
            jax.ShapeDtypeStruct((width, length), BF16),
            jax.ShapeDtypeStruct((2, length), F32),
            jax.ShapeDtypeStruct((width, 2), F32),
            jax.ShapeDtypeStruct((3 * heads * size, 1), F32),
        ),
        in_specs=[SM] + [VM] * 6,
        out_specs=(VM,) * 5,
        compiler_params=pltpu.CompilerParams(vmem_limit_bytes=40 * 2**20),
        name="unproject",
    )(slot, came, weight, rows, stats, columns, own_grad)


def finish_kernel(up, down, own_up, own_down, rows, gain, stats, row_sums, grad):
    half = up.shape[0]
    mean, inverse = stats[0:1], stats[1:2]
    first, second = row_sums[0:1], row_sums[1:2]
    for start, came, own in ((0, up, own_up), (half, down, own_down)):
        spot = slice(start, start + half)
        total = came[...].astype(F32) + own[...].astype(F32)
        normed = (rows[spot].astype(F32) - mean) * inverse
        back = inverse * (gain[spot] * total - first - normed * second)
        grad[:, spot] = back.T.astype(BF16)


def finish(up, down, own_up, own_down, rows, gain, stats, row_sums):
    return pl.pallas_call(
        finish_kernel,
        out_shape=jax.ShapeDtypeStruct(rows.shape[::-1], BF16),
        in_specs=[VM] * 8,
        out_specs=VM,
        compiler_params=pltpu.CompilerParams(vmem_limit_bytes=32 * 2**20),
        name="finish",
    )(up, down, own_up, own_down, rows, gain, stats, row_sums)


def feed_kernel(rows, grads, up_turned, up, down, bias, hidden, grad_pre, part):
    pre = contract(up_turned[...], rows[0], 1, 0) + bias[...]
    act, pull = jax.vjp(gelu_tanh, pre)
    hidden[0] = act.astype(BF16)
    low = pull(contract(down[...], grads[0], 1, 0))[0].astype(BF16)
    grad_pre[0] = low
    part[0] = contract(up[...], low, 1, 0).astype(BF16)


def feed(rows, grads, up_turned, up, down, bias):
    blocks, width, count = rows.shape
    inner = down.shape[0]

    def whole(shape):
        return pl.BlockSpec(shape, lambda i: (0,) * len(shape), pipeline_mode=pl.Buffered(1))

    def block(size):
        return pl.BlockSpec((1, size, count), lambda i: (i, 0, 0))

    return pl.pallas_call(
        feed_kernel,
        grid=(blocks,),
        out_shape=(
            jax.ShapeDtypeStruct((blocks, inner, count), BF16),
            jax.ShapeDtypeStruct((blocks, inner, count), BF16),
            jax.ShapeDtypeStruct((blocks, width, count), BF16),
        ),
        in_specs=[
            block(width),
            block(width),
            whole((inner, width)),
            whole((width, inner)),
            whole((inner, width)),
            whole((inner, 1)),
        ],
        out_specs=(block(inner), block(inner), block(width)),
        compiler_params=pltpu.CompilerParams(vmem_limit_bytes=32 * 2**20),
        cost_estimate=pl.CostEstimate(
            flops=6 * blocks * width * inner * count, bytes_accessed=2**24, transcendentals=0
        ),
        name="feed",
    )(rows, grads, up_turned, up, down, bias)


def feed_rest_kernel(
    slot, rows, grads, hidden, grad_pre, down_turned, middle, columns,
    weights, bias, out, *, square,
):
    blocks, width, _ = rows.shape
    inner = hidden.shape[1]
    features = out.shape[2]
    step = min(256, inner)
    pairs = [(hidden, grads), (rows, grad_pre) if square else (grad_pre, rows)]
    for which, (first, second) in enumerate(pairs):
        for start in range(0, inner, step):
            spot = slice(start, start + step)
            weights[which, spot] = sum(
                contract(first[n, spot], second[n], 1, 1) for n in range(blocks)
            ).astype(BF16)
    bias[...] = sum(jnp.sum(grad_pre[n].astype(F32), 1, keepdims=True) for n in range(blocks))
    for n in range(blocks):
        result = contract(down_turned[...], hidden[n], 1, 0)

        def put(values):
            for block in range(out.shape[0]):
                out[block, n] = values[block * features : (block + 1) * features].astype(BF16)

        put(result)

        @pl.when(slot[0] == n)
        def _():
            put(result + middle[...] + columns[:, 5:6])


def feed_rest(slot, rows, grads, hidden, grad_pre, down_turned, middle, columns):
    blocks, width, count = rows.shape
    inner = hidden.shape[1]
    return pl.pallas_call(
        functools.partial(feed_rest_kernel, square=inner == width),
        out_shape=(
            jax.ShapeDtypeStruct((2, inner, width), BF16),
            jax.ShapeDtypeStruct((inner, 1), F32),
            jax.ShapeDtypeStruct((blocks, blocks, width // blocks, count), BF16),
        ),
        in_specs=[SM] + [VM] * 7,
        out_specs=(VM,) * 3,
        compiler_params=pltpu.CompilerParams(vmem_limit_bytes=48 * 2**20),
        cost_estimate=pl.CostEstimate(
            flops=6 * blocks * width * inner * count, bytes_accessed=2**24, transcendentals=0
        ),
        name="feed_rest",
    )(slot, rows, grads, hidden, grad_pre, down_turned, middle, columns)


def spread(values, axis):
    count = lax.axis_size(axis)
    copies = jnp.broadcast_to(values[None], (count,) + values.shape)
    return lax.all_to_all(copies, axis, 0, 0, tiled=True)


def small_sum(values, axis):
    return jnp.sum(spread(values, axis), 0)


def ring(axis, by):
    count = lax.axis_size(axis)
    return [(source, (source + by) % count) for source in range(count)]


def ring_gather(values, axis):
    count, place = lax.axis_size(axis), lax.axis_index(axis)
    half = values.shape[0] // 2
    up, down = values[:half], values[half:]
    out = jnp.zeros((count,) + values.shape, values.dtype)
    out = lax.dynamic_update_slice_in_dim(out, values[None], place, 0)
    zeros = (0,) * (values.ndim - 1)
    for step in range(1, count):
        up = lax.ppermute(up, axis, ring(axis, 1))
        down = lax.ppermute(down, axis, ring(axis, -1))
        out = lax.dynamic_update_slice(out, up[None], ((place - step) % count, 0) + zeros)
        out = lax.dynamic_update_slice(out, down[None], ((place + step) % count, half) + zeros)
    return out


def ring_terms(blocks, axis):
    count, place = lax.axis_size(axis), lax.axis_index(axis)
    half = blocks.shape[1] // 2

    def own(offset, upper):
        block = lax.dynamic_index_in_dim(blocks, (place + offset) % count, 0, keepdims=False)
        return block[half:] if upper else block[:half]

    up, down = own(-1, False), own(1, True)
    for step in range(1, count):
        up = lax.ppermute(up, axis, ring(axis, 1))
        down = lax.ppermute(down, axis, ring(axis, -1))
        if step < count - 1:
            up = (up.astype(F32) + own(-1 - step, False).astype(F32)).astype(BF16)
            down = (down.astype(F32) + own(1 + step, True).astype(F32)).astype(BF16)
    return up, down, own(0, False), own(0, True)


def ring_sum(blocks, axis):
    up, down, own_up, own_down = [a.astype(F32) for a in ring_terms(blocks, axis)]
    return jnp.concatenate([up + own_up, down + own_down], 0)


def swapped(values):
    pairs = [(source, source ^ 1) for source in range(lax.axis_size("seq"))]
    return lax.ppermute(values, "seq", pairs)


def chip_groups():
    chips = lax.axis_size("seq") // 2
    return [[2 * chip + core for chip in range(chips)] for core in range(2)]


def core_halves(values):
    core = lax.axis_index("seq") % 2
    halves = values.reshape(2, values.shape[0] // 2, values.shape[1])
    mine = lax.dynamic_index_in_dim(halves, core, 0, keepdims=False)
    other = lax.dynamic_index_in_dim(halves, 1 - core, 0, keepdims=False)
    return (mine.astype(F32) + swapped(other).astype(F32)).astype(BF16)


def chip_parts(half):
    chips = lax.axis_size("seq") // 2
    blocks = half.reshape(chips, half.shape[0] // chips, half.shape[1])
    return lax.all_to_all(blocks, "seq", 0, 0, axis_index_groups=chip_groups(), tiled=True)


def chip_gather(parts):
    part = jnp.sum(parts.astype(F32), 0).astype(BF16)
    copies = jnp.broadcast_to(part[None], parts.shape)
    half = lax.all_to_all(copies, "seq", 0, 0, axis_index_groups=chip_groups(), tiled=True)
    return half.reshape(-1, half.shape[2])


def core_gather(half):
    core = lax.axis_index("seq") % 2
    other = swapped(half)
    first = jnp.where(core == 0, half, other)
    second = jnp.where(core == 0, other, half)
    return first, second


def regrouped(values, width):
    count, size, columns = values.shape
    if width == columns:
        return values
    if width > columns:
        merged = values.reshape(-1, width // columns, size, columns).transpose(0, 2, 1, 3)
        return merged.reshape(-1, size, width)
    cut = values.reshape(count, size, columns // width, width).transpose(0, 2, 1, 3)
    return cut.reshape(-1, size, width)


def group_gather(pieces, group):
    if group == 2:
        rank = lax.axis_index("seq") % 2
        other = swapped(pieces)
        return jnp.stack([jnp.where(rank == 0, pieces, other), jnp.where(rank == 0, other, pieces)])
    count = lax.axis_size("seq")
    groups = [[first + i for i in range(group)] for first in range(0, count, group)]
    return lax.all_gather(pieces, "seq", axis_index_groups=groups)


def on_device(
    tokens,
    segment_ids,
    out_grad,
    ln1_gain,
    ln1_bias,
    w_qkv,
    b_qv,
    w_out,
    b_out,
    ln2_gain,
    ln2_bias,
    w_up,
    b_up,
    w_down,
    b_down,
    prefix_embed,
    reparam_in,
    reparam_in_bias,
    reparam_out,
    reparam_out_bias,
):
    rows, features = tokens.shape
    heads = w_qkv.shape[1]
    size = w_qkv.shape[2] // 3
    inner = w_up.shape[1]
    seqs, tensors = lax.axis_size("seq"), lax.axis_size("tensor")
    width = features * tensors
    own_rows = rows // tensors
    group = seqs // heads
    chunk = own_rows // group
    place, slot = lax.axis_index("seq"), lax.axis_index("tensor")
    head, rank = place // group, place % group
    prefix = prefix_embed.shape[0]
    tokens_head = rows // group
    query_width = max(tokens_head, LANES)
    forward_tile = min(512, query_width)
    backward_tile = min(256, query_width)
    forward_keys, backward_keys = 512, 1024
    both = ("seq", "tensor")
    paired = group == 2 and chunk == LANES

    own_tokens, own_grads = turned(tokens, out_grad)
    full_tokens = ring_gather(own_tokens, "tensor").reshape(width, rows)
    numbers = jnp.arange(1, DOCS, dtype=jnp.int32)
    before = jnp.sum((segment_ids[None, :] < numbers[:, None]).astype(jnp.int32), 1)
    starts = small_sum(jnp.broadcast_to(before[:, None], (DOCS - 1, LANES)), "seq")[:, 0]
    meta = jnp.concatenate([starts, rank[None].astype(jnp.int32)])
    vectors = jnp.stack([ln1_gain, ln1_bias, ln2_gain, ln2_bias, b_out, b_down])
    share_rows = heads * size // seqs
    out_share = w_out.reshape(seqs, share_rows, width)
    out_share = lax.dynamic_index_in_dim(out_share, place, 0, keepdims=False)
    extra = -(-vectors.size // width)
    vectors = jnp.pad(vectors.reshape(-1), (0, extra * width - vectors.size))
    out_share = jnp.concatenate([out_share, vectors.reshape(extra, width)], 0)
    out_share = spread(out_share, "tensor")
    vectors = out_share[:, share_rows:].reshape(tensors, -1)[:, : 6 * features]
    columns = vectors.reshape(tensors, 6, features).transpose(0, 2, 1).reshape(width, 6).astype(F32)
    full_tokens, columns, meta, out_share = lax.optimization_barrier(
        (full_tokens, columns, meta, out_share[:, :share_rows])
    )
    out_share = spread(out_share, "seq")
    w_out_full = out_share.transpose(1, 0, 2, 3).reshape(width, width)
    gain2, shift2, bias_out = [columns[:, i : i + 1] for i in (2, 3, 4)]
    where_slot = slot[None].astype(jnp.int32)

    embed_float = prefix_embed.astype(F32)
    prefix_hidden = jnp.tanh(
        jnp.dot(prefix_embed, reparam_in, preferred_element_type=F32)
        + reparam_in_bias.astype(F32)
    )
    prefix_pair = jnp.einsum(
        "pa,ahe->phe", prefix_hidden, reparam_out.astype(F32), precision=HIGHEST
    )
    prefix_pair = (prefix_pair + reparam_out_bias.astype(F32)).astype(BF16)
    own_pair = lax.dynamic_index_in_dim(prefix_pair, head, 1, keepdims=False)
    own_pair = jnp.pad(own_pair, ((0, LANES - prefix), (0, 0)))
    pre_key, pre_value = own_pair[:, :size], own_pair[:, size:]

    w_flat = w_qkv.reshape(width, heads * 3 * size)
    bias_pair = b_qv.astype(F32)
    bias_three = jnp.stack(
        [bias_pair[:, :size], jnp.zeros((heads, size), F32), bias_pair[:, size:]], 1
    ).reshape(-1, 1)
    if paired:
        full1, sent, stats = project(
            full_tokens, columns, w_flat.T, bias_three, heads, size, own_rows
        )
    else:
        wide = full_tokens.astype(F32)
        mean = jnp.mean(wide, 0, keepdims=True)
        inverse = lax.rsqrt(jnp.mean((wide - mean) ** 2, 0, keepdims=True) + EPS)
        stats = jnp.concatenate([mean, inverse], 0)
        full1 = ((wide - mean) * inverse * columns[:, 0:1] + columns[:, 1:2]).astype(BF16)
        mixed = (contract(w_flat, full1, 0, 0) + bias_three).astype(BF16)
        mixed = mixed.reshape(heads, 3, size, rows)
        query_part = mixed[:, 0].reshape(heads, size, tensors, group, chunk)
        query_part = query_part.transpose(0, 3, 1, 2, 4).reshape(seqs, size, tokens_head)
        pair_part = mixed[:, 1:].transpose(0, 2, 1, 3).reshape(heads, size, group, 2 * tokens_head)
        pair_part = pair_part.transpose(0, 2, 1, 3).reshape(seqs, size, 2 * tokens_head)
        sent = jnp.concatenate([query_part, pair_part], 2)
    came = lax.all_to_all(sent, "seq", 0, 0, tiled=True)
    query, pair = came[:, :, :tokens_head], came[:, :, tokens_head:]
    query = regrouped(query, query_width)
    pair = group_gather(pair, group)
    if group == 2:
        key, value = pair[0], pair[1]
    else:
        pair = pair.transpose(1, 2, 0, 3).reshape(seqs, size, 2, rows)
        key, value = pair[:, :, 0], pair[:, :, 1]
    full_grad = lax.all_gather(after(own_grads, full_tokens), "tensor", axis=0, tiled=True)
    out_low, out_full, log_total = attend_forward(
        meta, query, key, value, pre_key.T, pre_value.T,
        forward_tile, forward_keys, prefix, chunk, group,
    )
    out_low, full_grad = lax.optimization_barrier((out_low, full_grad))

    came = lax.all_to_all(regrouped(out_low, chunk), both, 0, 0, tiled=True)
    came = came.reshape(heads, group, tensors, size, chunk).transpose(2, 0, 3, 1, 4)
    attended = came.reshape(width, own_rows)
    branch = contract(w_out_full, attended, 0, 0)
    own_block = lax.dynamic_slice_in_dim(full_tokens, slot * own_rows, own_rows, 1)
    middle = own_block.astype(F32) + branch + bias_out
    mean2 = jnp.mean(middle, 0, keepdims=True)
    centered = middle - mean2
    inverse2 = lax.rsqrt(jnp.mean(centered * centered, 0, keepdims=True) + EPS)
    normed2 = centered * inverse2
    out2 = (normed2 * gain2 + shift2).astype(BF16)

    full2 = ring_gather(out2, "tensor")
    grads = full_grad.reshape(width, tensors, own_rows).transpose(1, 0, 2)
    hidden, grad_pre, part = feed(
        full2, grads, w_up.T, w_up, w_down, b_up.astype(F32)[:, None]
    )
    feed_weights, grad_b_up, mlp_out = feed_rest(
        where_slot, full2, grads, hidden, grad_pre, w_down.T, middle, columns
    )
    core = place % 2
    feed_mine = lax.dynamic_index_in_dim(feed_weights, core, 0, keepdims=False)
    feed_other = lax.dynamic_index_in_dim(feed_weights, 1 - core, 0, keepdims=False)
    feed_half = (feed_mine.astype(F32) + swapped(feed_other).astype(F32)).astype(BF16)
    feed_parts = chip_parts(feed_half)
    grad_normed2 = ring_sum(part, "tensor")
    grad_normed2, feed_parts = lax.optimization_barrier((grad_normed2, feed_parts))

    scaled = grad_normed2 * gain2
    first = jnp.mean(scaled, 0, keepdims=True)
    second = jnp.mean(scaled * normed2, 0, keepdims=True)
    own_grad = lax.dynamic_index_in_dim(grads, slot, 0, keepdims=False)
    grad_middle = own_grad.astype(F32) + inverse2 * (scaled - first - normed2 * second)
    grad_branch = grad_middle.astype(BF16)
    grad_attended = contract(w_out_full, grad_branch, 1, 0).astype(BF16)
    sent = grad_attended.reshape(tensors, heads, size, group, chunk).transpose(1, 3, 0, 2, 4)
    came = lax.all_to_all(sent.reshape(seqs * tensors, size, chunk), both, 0, 0, tiled=True)
    grad_out = regrouped(came, LANES)

    token_sums = jnp.stack(
        [
            jnp.sum(grad_normed2 * normed2, 1),
            jnp.sum(grad_normed2, 1),
            jnp.sum(grad_middle, 1),
        ]
    )
    grad_w_out = contract(attended, grad_branch, 1, 1).astype(BF16)
    grad_out, mlp_out, grad_w_out, feed_parts = lax.optimization_barrier(
        (grad_out, mlp_out, grad_w_out, feed_parts)
    )
    feed_half = chip_gather(feed_parts)
    output_act = lax.psum_scatter(mlp_out, "tensor", scatter_dimension=0, tiled=True)
    grad_w_out = lax.psum_scatter(grad_w_out, "tensor", scatter_dimension=0, tiled=True)

    levels = log_total.reshape(-1, 1, backward_tile)
    grad_query, grad_pair, grad_prefix = attend_backward(
        meta, query, key, value, pre_key[:PAD], pre_value[:PAD], grad_out, out_full, levels,
        backward_tile, backward_keys, prefix, chunk, group,
    )
    grad_pair, output_act, grad_w_out, feed_half = lax.optimization_barrier(
        (grad_pair, output_act, grad_w_out, feed_half)
    )
    if group == 2:
        grad_share = (grad_pair[0].astype(F32) + swapped(grad_pair[1]).astype(F32)).astype(BF16)
    else:
        groups = [[first + i for i in range(group)] for first in range(0, seqs, group)]
        shares = grad_pair.transpose(1, 2, 0, 3).reshape(seqs, size, group, 2 * tokens_head)
        grad_share = lax.psum_scatter(
            shares.transpose(2, 0, 1, 3), "seq", axis_index_groups=groups
        )
    prefix_part = grad_prefix.transpose(2, 0, 1).reshape(size, 2 * PAD).astype(BF16)
    prefix_part = jnp.pad(prefix_part, ((0, 0), (0, LANES - 2 * PAD)))
    prefix_part = jnp.broadcast_to(prefix_part[None], (seqs, size, LANES))
    sent = jnp.concatenate([regrouped(grad_query, tokens_head), grad_share, prefix_part], 2)
    came = lax.all_to_all(sent, "seq", 0, 0, tiled=True)
    if paired:
        grad_flat, grad_part, row_sums, sums1, head_sums = unproject(
            where_slot, came, w_flat, full_tokens, stats, columns, grad_middle, heads, size, own_rows
        )
    else:
        query_part = came[:, :, :tokens_head].reshape(heads, group, size, tensors, chunk)
        query_part = query_part.transpose(0, 2, 3, 1, 4).reshape(heads, 1, size, rows)
        pair_part = came[:, :, tokens_head : 3 * tokens_head]
        pair_part = pair_part.reshape(heads, group, size, 2 * tokens_head).transpose(0, 2, 1, 3)
        pair_part = pair_part.reshape(heads, size, 2, rows).transpose(0, 2, 1, 3)
        grad_flat = jnp.concatenate([query_part, pair_part], 1).reshape(heads * 3 * size, rows)
        back = contract(w_flat, grad_flat, 1, 0)
        normed1 = (full_tokens.astype(F32) - stats[0]) * stats[1]
        scaled = back * columns[:, 0:1]
        row_sums = jnp.stack([jnp.sum(scaled, 0), jnp.sum(scaled * normed1, 0)])
        sums1 = jnp.stack([jnp.sum(back * normed1, 1), jnp.sum(back, 1)], 1)
        head_sums = jnp.sum(grad_flat.astype(F32), 1)
        own_inverse = lax.dynamic_slice_in_dim(stats[1:2], slot * own_rows, own_rows, 1)
        own_part = lax.dynamic_slice_in_dim(back, slot * own_rows, own_rows, 1)
        own_part = own_part + grad_middle / (own_inverse * columns[:, 0:1])
        back = lax.dynamic_update_slice_in_dim(back, own_part, slot * own_rows, 1)
        grad_part = back.astype(BF16)
    last_terms = ring_terms(grad_part.reshape(tensors, features, rows), "tensor")

    prefix_low = came[:, :, 3 * tokens_head : 3 * tokens_head + 2 * PAD].astype(F32)
    prefix_low = jnp.sum(prefix_low.reshape(heads, group, size, 2, PAD), 1)[..., :prefix]
    prefix_low = prefix_low.transpose(3, 0, 2, 1).reshape(prefix, heads, 2 * size).astype(BF16)
    prefix_grad = prefix_low.astype(F32)
    hidden_part = jnp.einsum("phe,ahe->pa", prefix_low, reparam_out, preferred_element_type=F32)
    owned = jnp.concatenate([sums1.T, token_sums], 0)
    owned = owned.reshape(-1, tensors, features).transpose(1, 0, 2).reshape(tensors, -1)
    shared = jnp.concatenate([row_sums.reshape(-1), hidden_part.reshape(-1)])
    shared = jnp.broadcast_to(shared[None], (tensors, shared.shape[0]))
    small = jnp.concatenate([owned, shared], 1)[:, None, :]
    small = jnp.sum(lax.all_to_all(small, "tensor", 0, 0, tiled=True), 0)[0]
    owned, row_sums = small[: 5 * features], small[5 * features : 5 * features + 2 * rows]
    hidden_grad = small[5 * features + 2 * rows :].reshape(prefix_hidden.shape)
    input_grad = finish(
        *last_terms, own_tokens, ln1_gain.astype(F32)[:, None], stats,
        row_sums.reshape(2, rows) / width,
    )
    output_act = output_act[0].transpose(0, 2, 1).reshape(rows, features)

    first_half, second_half = core_gather(feed_half)
    out_w_down = first_half.astype(F32)
    out_w_up = (second_half if inner == width else second_half.T).astype(F32)
    grad_w_qkv = contract(grad_flat, full1, 1, 1).astype(BF16)
    rest = jnp.concatenate([grad_w_qkv, grad_w_out], 0)
    rest_half = chip_gather(chip_parts(core_halves(rest)))
    rest = jnp.concatenate(core_gather(rest_half), 0).astype(F32)
    mixed_rows = heads * 3 * size
    out_w_qkv = rest[:mixed_rows].reshape(heads, 3 * size, width).transpose(2, 0, 1)
    out_w_out = rest[mixed_rows:].reshape(heads, size, width)

    grad_b_down = jnp.sum(out_grad.astype(F32), 0)
    head_sums = head_sums.reshape(heads, 3, size)
    late = jnp.concatenate(
        [
            owned,
            grad_b_down,
            grad_b_up.reshape(-1),
            head_sums[:, 0].reshape(-1),
            head_sums[:, 2].reshape(-1),
        ]
    )
    late = small_sum(late[None], "seq")[0]
    out_ln1_gain, out_ln1_bias, out_ln2_gain, out_ln2_bias, out_b_out, out_b_down = [
        late[i * features : (i + 1) * features] for i in range(6)
    ]
    late = late[6 * features :]
    out_b_up = late[:inner]
    pair_sums = late[inner:].reshape(2, heads, size)
    out_b_qv = jnp.concatenate([pair_sums[0], pair_sums[1]], 1)

    grad_reparam_out = jnp.einsum("pa,phe->ahe", prefix_hidden, prefix_grad, precision=HIGHEST)
    grad_reparam_out_bias = jnp.sum(prefix_grad, 0)
    grad_prefix_pre = hidden_grad * (1.0 - prefix_hidden * prefix_hidden)
    grad_reparam_in_bias = jnp.sum(grad_prefix_pre, 0)
    grad_reparam_in = jnp.einsum("pd,pa->da", embed_float, grad_prefix_pre, precision=HIGHEST)
    grad_prefix_embed = jnp.einsum(
        "pa,da->pd", grad_prefix_pre, reparam_in.astype(F32), precision=HIGHEST
    )
    return (
        output_act,
        input_grad,
        out_ln1_gain,
        out_ln1_bias,
        out_w_qkv,
        out_b_qv,
        out_w_out,
        out_b_out,
        out_ln2_gain,
        out_ln2_bias,
        out_w_up,
        out_b_up,
        out_w_down,
        out_b_down,
        grad_prefix_embed,
        grad_reparam_in,
        grad_reparam_in_bias,
        grad_reparam_out,
        grad_reparam_out_bias,
    )


def solution(mesh):
    placed = (
        P("seq", "tensor"),
        P("seq"),
        P("seq", "tensor"),
        P("tensor"),
        P("tensor"),
        P(None, "tensor", None),
        P("tensor", None),
        P("tensor", None, None),
        P("tensor"),
        P("tensor"),
        P("tensor"),
        P(None, "tensor"),
        P("tensor"),
        P("tensor", None),
        P("tensor"),
        P(),
        P(),
        P(),
        P(None, "tensor", None),
        P("tensor", None),
    )
    return jax.shard_map(
        on_device,
        mesh=mesh,
        in_specs=placed,
        out_specs=(
            P("seq", "tensor"),
            P("seq", "tensor"),
            P("tensor"),
            P("tensor"),
            P(None, "tensor", None),
            P("tensor", None),
            P("tensor", None, None),
            P("tensor"),
            P("tensor"),
            P("tensor"),
            P(None, "tensor"),
            P("tensor"),
            P("tensor", None),
            P("tensor"),
            P(),
            P(),
            P(),
            P(None, "tensor", None),
            P("tensor", None),
        ),
        check_vma=False,
    )
```

time: 1230 us -> 612 us (0.50)
  matrix products: 420 us -> 17.9 us
  waiting for transfers between devices: 410 us -> 158 us
  Pallas kernels: 0 us -> 141 us
  other arithmetic: 133 us -> 47.3 us
  blocking collectives: 75.3 us -> 0 us
  local copies, waits for them, and re-layouts: 46.8 us -> 120 us
    dot_general x76 -> x8, matrix products: 411 us -> 14.9 us  [the longest x4 11.5 us: contract(): lax.dot_general(first, second, (((first_dim,), (second_dim,)), ((), ())),...]
    all_gather x4 -> x1, waiting for transfers between devices: 145 us -> 0.01 us  [on_device(): lax.all_gather(after(own_grads, full_tokens), 'tensor', axis=0, tiled=True)]
    reduce_scatter x4 -> x2, waiting for transfers between devices: 155 us -> 14 us  [the longest x1 13.9 us: on_device(): lax.psum_scatter(grad_w_out, 'tensor', scatter_dimension=0, tiled=True)]
    pallas_call x0 -> x8, Pallas kernels: none -> 141 us  [the longest x1 62.8 us: attend_backward(): pl.pallas_call(functools.partial(backward_kernel, tile=tile, keys=keys, p...]
    psum x1 -> x0, waiting for transfers between devices: 95.9 us -> none  [on_device(): lax.psum(grad_w_qkv.astype(jnp.bfloat16), 'seq').astype(jnp.float32)]
    all_to_all x0 -> x13, waiting for transfers between devices: none -> 71.9 us  [the longest x2 22.2 us: on_device(): came = lax.all_to_all(sent, 'seq', 0, 0, tiled=True)]
    ppermute x46 -> x30, starting transfers between devices: 107 us -> 42.4 us  [the longest x6 14.1 us: ring_terms(): down = lax.ppermute(down, axis, ring(axis, -1))]
    psum x5 -> x0, blocking collectives: 63.5 us -> none  [the longest x4 41.9 us: row_stats(): return lax.psum((first, second), 'tensor')]
  transfers between devices with their start and end apart: 55 -> 46, of which waited for: 15 -> 24; matrix products, arithmetic and copies ran while one was open for 37% -> 21% of each run, Pallas kernels for 0% -> 17%
where the time goes in v1:
time: 612 us; the launch traced here: 603 us
  waiting for transfers between devices  158 us (26%)
  Pallas kernels  141 us (23%)
  local copies, waits for them, and re-layouts  120 us (20%)
  starting transfers between devices  104 us (17%)
  other arithmetic  47.3 us (8%)
  matrix products  17.9 us (3%)
  between operations  15.3 us (2%)
    pallas_call x1, Pallas kernels, attend_backward(): pl.pallas_call(functools.partial(backward_kernel, tile=tile, keys=keys, p...  62.8 us
    unnamed x151, local copies, waits for them, and re-layouts  44.4 us
    pallas_call x1, Pallas kernels, attend_forward(): pl.pallas_call(functools.partial(forward_kernel, tile=tile, keys=keys, pr...  39.3 us
    ppermute x6, waiting for transfers between devices, ring_terms(): up = lax.ppermute(up, axis, ring(axis, 1))  22.4 us
    all_to_all x2, waiting for transfers between devices, on_device(): came = lax.all_to_all(sent, 'seq', 0, 0, tiled=True)  22.2 us
    ppermute x6, waiting for transfers between devices, ring_terms(): down = lax.ppermute(down, axis, ring(axis, -1))  20.4 us
    all_to_all x4, starting transfers between devices, spread(): return lax.all_to_all(copies, axis, 0, 0, tiled=True)  18.1 us
    pallas_call x1, Pallas kernels, feed_rest(): pl.pallas_call(functools.partial(feed_rest_kernel, square=inner == width)...  15.7 us
  transfers between devices with their start and end apart: 46, of which 24 were waited for; matrix products, arithmetic and copies ran while one was open for 21% of the time, Pallas kernels for 17%

profile of v1, /device:TPU:1, one launch (start us, length us, event | category | flops | bytes accessed | tf_op | source)
XLA Modules:
  0.0 602.9 jit_solution(2669834820094637366)
XLA Ops:
  15.8 4.9 all-to-all-start.1
  27.0 4.1 all-to-all-start
  37.9 9.3 %all-to-all-done = bf16[4,34,1024]{2,1,0:T(8,128)(2,1)} async-done(((bf16[4,34,1024]{2,1,0:T(8,128)(2,1)}), bf16[4,34,1024]{2,1,0:T(8,128)(2,1)}, u32[]{:S(2)}, u32[]{:S(2)}) %all-to-all-start) | async-done | bytes 278560 | tf_op jit(solution)/shard_map/all_to_all | solution.py:566
  53.6 3.3 collective-permute-start.5
  58.8 3.3 collective-permute-done.4
  62.2 3.8 collective-permute-done.5
  66.0 3.2 project.1
  71.6 6.4 %all-to-all-start.2 = ((bf16[8,64,1536]{2,1,0:T(8,128)(2,1)}), bf16[8,64,1536]{2,1,0:T(8,128)(2,1)}, u32[]{:S(2)}, u32[]{:S(2)}) async-start(bf16[8,64,1536]{2,1,0:T(8,128)(2,1)} %copy-done.24), calls=%async_computation.2 | async-start | bytes 3145728 | tf_op jit(solution)/shard_map/all_to_all | solution.py:777
  78.8 16.8 %all-to-all-done.2 = bf16[8,64,1536]{2,1,0:T(8,128)(2,1)} async-done(((bf16[8,64,1536]{2,1,0:T(8,128)(2,1)}), bf16[8,64,1536]{2,1,0:T(8,128)(2,1)}, u32[]{:S(2)}, u32[]{:S(2)}) %all-to-all-start.2) | async-done | bytes 1572896 | tf_op jit(solution)/shard_map/all_to_all | solution.py:777
  97.9 3.6 collective-permute-start.6
  106.0 4.3 all-to-all-start.3
  113.4 39.3 %attend_forward.1 = (bf16[32,64,128]{2,1,0:T(8,128)(2,1)S(1)}, f32[32,64,128]{2,1,0:T(8,128)S(1)}, f32[8,1,512]{2,1,0:T(1,128)S(1)}) custom-call(s32[5]{0:T(128)S(1)} %pad_add_fusion.meta, bf16[8,64,512]{2,1,0:T(8,128)(2,1)S(1)} %slice.303.query, bf16[8,64,1024]{2,1,0:T(8,128)(2,1)S(1)} %get-tuple-element.248.key, ...), custom_call_target="tpu_custom_call" | custom-call | flops 17179869184 | bytes 8388608 | tf_op jit(solution)/shard_map/attend_forward/pallas_call | solution.py:204
  157.1 5.4 all-to-all-start.4
  165.0 3.2 copy.207
  168.2 9.5 %all-to-all-done.4 = bf16[32,64,128]{2,1,0:T(8,128)(2,1)} async-done(((bf16[32,64,128]{2,1,0:T(8,128)(2,1)}), bf16[32,64,128]{2,1,0:T(8,128)(2,1)}, u32[]{:S(2)}, u32[]{:S(2)}) %all-to-all-start.4) | async-done | bytes 524320 | tf_op jit(solution)/shard_map/all_to_all | solution.py:793
  179.3 2.6 fusion.38
  185.0 3.3 collective-permute-start.8
  188.3 4.0 copy.214
  193.3 3.9 copy.216
  197.2 3.9 copy.210
  201.2 3.9 copy.211
  207.0 3.1 collective-permute-start.10
  211.8 3.5 collective-permute-done.9
  216.1 5.0 collective-permute-done.10
  221.8 4.9 collective-permute-done.11
  227.4 5.1 collective-permute-done.12
  239.5 11.7 %feed.1 = (bf16[4,1024,256]{2,1,0:T(8,128)(2,1)S(1)}, bf16[4,1024,256]{2,1,0:T(8,128)(2,1)S(1)}, bf16[4,1024,256]{2,1,0:T(8,128)(2,1)S(1)}) custom-call(bf16[4,1024,256]{2,1,0:T(8,128)(2,1)S(1)} %copy-done.17, bf16[4,1024,256]{2,1,0:T(8,128)(2,1)S(1)} %bitcast.238, bf16[1024,1024]{1,0:T(8,128)(2,1)S(1)} %bitcast.242, bf16[1024,1024]{1,0:T(8,128)(2,1)S(1)} %copy-done.18, ...), custom_call_target="tpu_custom_call" | custom-call | flops 6442450944 | bytes 16777216 | tf_op jit(solution)/shard_map/feed/pallas_call | solution.py:488
  255.3 15.7 %feed_rest.1 = (bf16[2,1024,1024]{2,1,0:T(8,128)(2,1)}, f32[1024,1]{1,0:T(8,128)S(1)}, bf16[4,4,256,256]{3,2,1,0:T(8,128)(2,1)S(1)}) custom-call(s32[1]{0:T(128)} %bitcast.46.slot, bf16[4,1024,256]{2,1,0:T(8,128)(2,1)} %bitcast_dynamic-update-slice_fusion.2.rows, bf16[4,1024,256]{2,1,0:T(8,128)(2,1)} %bitcast.237, bf16[4,1024,256]{2,1,0:T(8,128)(2,1)} %copy-done.40, ...), custom_call_target="tpu_custom_call" | custom-call | flops 6442450944 | bytes 16777216 | tf_op jit(solution)/shard_map/feed_rest/pallas_call | solution.py:546
  271.0 4.1 dynamic-slice_bitcast_fusion
  277.6 3.1 collective-permute-start.16
  280.7 6.8 %collective-permute-done.13 = bf16[512,256]{1,0:T(8,128)(2,1)} collective-permute-done((bf16[512,256]{1,0:T(8,128)(2,1)}, bf16[512,256]{1,0:T(8,128)(2,1)}, u32[]{:S(2)}, u32[]{:S(2)}) %collective-permute-start.13) | collective-permute-done | bytes 262176 | tf_op jit(solution)/shard_map/ppermute | solution.py:603
  289.3 4.6 fusion
  293.9 4.5 all-to-all-start.5
  300.5 3.3 collective-permute-start.17
  303.8 5.0 collective-permute-done.15
  308.8 3.6 collective-permute-done.17
  315.9 8.4 %collective-permute-done.18 = bf16[512,256]{1,0:T(8,128)(2,1)S(1)} collective-permute-done((bf16[512,256]{1,0:T(8,128)(2,1)S(1)}, bf16[512,256]{1,0:T(8,128)(2,1)S(1)}, u32[]{:S(2)}, u32[]{:S(2)}) %collective-permute-start.18) | collective-permute-done | bytes 262176 | tf_op jit(solution)/shard_map/ppermute | solution.py:604
  336.8 6.1 %all-to-all-start.6 = ((bf16[32,64,128]{2,1,0:T(8,128)(2,1)}), bf16[32,64,128]{2,1,0:T(8,128)(2,1)}, u32[]{:S(2)}, u32[]{:S(2)}) async-start(bf16[32,64,128]{2,1,0:T(8,128)(2,1)} %bitcast.257), calls=%async_computation.6 | async-start | bytes 1048576 | tf_op jit(solution)/shard_map/all_to_all | solution.py:829
  342.9 3.5 convolution_convert_fusion
  346.4 11.8 %all-to-all-done.6.grad_out = bf16[32,64,128]{2,1,0:T(8,128)(2,1)} async-done(((bf16[32,64,128]{2,1,0:T(8,128)(2,1)}), bf16[32,64,128]{2,1,0:T(8,128)(2,1)}, u32[]{:S(2)}, u32[]{:S(2)}) %all-to-all-start.6) | async-done | bytes 524320 | tf_op jit(solution)/shard_map/all_to_all | solution.py:829
  359.6 2.9 reduce_sum.173
  362.6 2.7 broadcast_in_dim.139
  365.3 4.4 all-to-all-start.7
  369.7 62.8 %attend_backward.1 = (bf16[8,64,512]{2,1,0:T(8,128)(2,1)}, bf16[2,8,64,1024]{3,2,1,0:T(8,128)(2,1)}, f32[2,16,64]{2,1,0:T(8,128)}) custom-call(s32[5]{0:T(128)} %copy-done.39, bf16[8,64,512]{2,1,0:T(8,128)(2,1)} %copy-done.30, bf16[8,64,1024]{2,1,0:T(8,128)(2,1)} %copy-done.26, bf16[8,64,1024]{2,1,0:T(8,128)(2,1)} %copy-done.25, ...), custom_call_target="tpu_custom_call" | custom-call | flops 42949672960 | bytes 8388608 | tf_op jit(solution)/shard_map/attend_backward/pallas_call | solution.py:307
  432.6 13.9 %reduce-scatter.5.cloned.1.call-done = bf16[256,1024]{1,0:T(8,128)(2,1)} async-done(((bf16[1024,1024]{1,0:T(8,128)(2,1)}), bf16[256,1024]{1,0:T(8,128)(2,1)}) %reduce-scatter.5.cloned.1.call-update) | async-done | bytes 524304 | tf_op jit(solution)/shard_map/reduce_scatter | solution.py:845
  455.6 4.9 all-to-all-start.8
  460.5 2.6 copy.220.weight
  467.8 6.2 %select_convert_fusion = (f32[1024,1024]{1,0:T(8,128)}, f32[1024,1024]{1,0:T(8,128)}) fusion(bf16[1024,1024]{1,0:T(8,128)(2,1)} %bitcast.54, bf16[1024,1024]{1,0:T(8,128)(2,1)} %collective-permute-done.29, pred[]{:T(512)S(6)} %eq.43), kind=kLoop, calls=%fused_computation.8 | loop fusion | flops 4194304 | bytes 12582913 | tf_op jit(solution)/shard_map/convert_element_type | solution.py:912
  473.9 5.5 all-to-all-done.8.came
  483.1 6.3 %unproject.1 = (bf16[768,1024]{1,0:T(8,128)(2,1)S(1)}, bf16[1024,1024]{1,0:T(8,128)(2,1)S(1)}, f32[2,1024]{1,0:T(2,128)S(1)}, f32[1024,2]{1,0:T(8,128)S(1)}, f32[768,1]{1,0:T(8,128)S(1)}) custom-call(s32[1]{0:T(128)} %bitcast.46.slot, bf16[8,64,1664]{2,1,0:T(8,128)(2,1)} %all-to-all-done.8.came, bf16[1024,768]{1,0:T(8,128)(2,1)S(1)} %copy-done.10, ...), custom_call_target="tpu_custom_call" | custom-call | tf_op jit(solution)/shard_map/unproject/pallas_call | solution.py:430
  497.5 3.9 convolution_convert_fusion.1
  503.0 4.3 collective-permute-start.27
  508.1 4.2 all-to-all-start.9
  512.5 2.9 fusion.1
  517.1 3.5 all-to-all-start.11
  524.1 9.6 %all-to-all-done.11 = bf16[4,128,1024]{2,1,0:T(8,128)(2,1)S(1)} async-done(((bf16[4,128,1024]{2,1,0:T(8,128)(2,1)}), bf16[4,128,1024]{2,1,0:T(8,128)(2,1)S(1)}, u32[]{:S(2)}, u32[]{:S(2)}) %all-to-all-start.11) | async-done | bytes 1048608 | tf_op jit(solution)/shard_map/all_to_all | solution.py:637
  535.0 3.8 all-to-all-start.12
  541.2 2.9 copy.232
  544.1 7.7 %all-to-all-done.12 = bf16[4,128,1024]{2,1,0:T(8,128)(2,1)S(1)} async-done(((bf16[4,128,1024]{2,1,0:T(8,128)(2,1)}), bf16[4,128,1024]{2,1,0:T(8,128)(2,1)S(1)}, u32[]{:S(2)}, u32[]{:S(2)}) %all-to-all-start.12) | async-done | bytes 1048608 | tf_op jit(solution)/shard_map/all_to_all | solution.py:643
  552.6 4.7 all-to-all-start.10
  564.8 2.8 collective-permute-done.25
  567.7 6.6 %collective-permute-done.22 = bf16[128,1024]{1,0:T(8,128)(2,1)S(1)} collective-permute-done((bf16[128,1024]{1,0:T(8,128)(2,1)S(1)}, bf16[128,1024]{1,0:T(8,128)(2,1)S(1)}, u32[]{:S(2)}, u32[]{:S(2)}) %collective-permute-start.22) | collective-permute-done | bytes 262176 | tf_op jit(solution)/shard_map/ppermute | solution.py:603
  580.2 4.1 collective-permute-done.23.up
  584.2 5.5 collective-permute-done.26.down
  (344 shorter events, 153.1 us)
Async XLA Ops:
  7.2 94.3 %copy-start = (bf16[1024,512]{1,0:T(8,128)(2,1)S(1)}, bf16[1024,512]{1,0:T(8,128)(2,1)}, u32[]{:S(2)}) copy-start(bf16[1024,512]{1,0:T(8,128)(2,1)} %param.36) | copy-start | bytes 3145732
  9.4 11.3 %copy-start.65 = (bf16[256]{0:T(256)(128)(2,1)S(1)}, bf16[256]{0:T(256)(128)(2,1)}, u32[]{:S(2)}) copy-start(bf16[256]{0:T(256)(128)(2,1)} %param.28) | copy-start | bytes 1540
  9.4 11.4 %copy-start.66 = (bf16[256]{0:T(256)(128)(2,1)S(1)}, bf16[256]{0:T(256)(128)(2,1)}, u32[]{:S(2)}) copy-start(bf16[256]{0:T(256)(128)(2,1)} %param.34) | copy-start | bytes 1540
  9.4 11.4 %copy-start.59 = (bf16[4,128]{1,0:T(4,128)(2,1)S(1)}, bf16[4,128]{1,0:T(4,128)(2,1)}, u32[]{:S(2)}) copy-start(bf16[4,128]{1,0:T(4,128)(2,1)} %param.26) | copy-start | bytes 3076
  10.7 21.9 %collective-permute-start = (bf16[128,1024]{1,0:T(8,128)(2,1)}, bf16[128,1024]{1,0:T(8,128)(2,1)}, u32[]{:S(2)}, u32[]{:S(2)}) collective-permute-start(bf16[128,1024]{1,0:T(8,128)(2,1)} %get-tuple-element.268), channel_id=1, source_target_pairs={{0,1},{1,2},{2,3},{3,0},{4,5},{5,6},{6,7},{7,4},{8,9},{9,10},{10,1... | collective-permute-start | bytes 786440 | tf_op jit(solution)/shard_map/ppermute | solution.py:586
  12.9 21.2 %collective-permute-start.1 = (bf16[128,1024]{1,0:T(8,128)(2,1)}, bf16[128,1024]{1,0:T(8,128)(2,1)}, u32[]{:S(2)}, u32[]{:S(2)}) collective-permute-start(bf16[128,1024]{1,0:T(8,128)(2,1)} %get-tuple-element.267), channel_id=1, source_target_pairs={{0,3},{1,0},{2,1},{3,2},{4,7},{5,4},{6,5},{7,6},{8,11},{9,8},{10,9... | collective-permute-start | bytes 786440 | tf_op jit(solution)/shard_map/ppermute | solution.py:587
  15.8 9.6 %all-to-all-start.1 = ((s32[8,4,128]{2,1,0:T(4,128)}), s32[8,4,128]{2,1,0:T(4,128)S(1)}, u32[]{:S(2)}, u32[]{:S(2)}) async-start(s32[8,4,128]{2,1,0:T(4,128)} %broadcast_in_dim_broadcast_in_dim_broadcast_in_dim.2), calls=%async_computation.1 | async-start | bytes 32768 | tf_op jit(solution)/shard_map/all_to_all | solution.py:566
  27.0 20.1 %all-to-all-start = ((bf16[4,34,1024]{2,1,0:T(8,128)(2,1)}), bf16[4,34,1024]{2,1,0:T(8,128)(2,1)}, u32[]{:S(2)}, u32[]{:S(2)}) async-start(bf16[4,34,1024]{2,1,0:T(8,128)(2,1)} %broadcast_in_dim.125), calls=%async_computation | async-start | bytes 655360 | tf_op jit(solution)/shard_map/all_to_all | solution.py:566
  32.6 80.7 %copy-start.39 = (s32[5]{0:T(128)}, s32[5]{0:T(128)S(1)}, u32[]{:S(2)}) copy-start(s32[5]{0:T(128)S(1)} %pad_add_fusion.meta) | copy-start | bytes 64
  32.6 21.0 %collective-permute-start.2 = (bf16[128,1024]{1,0:T(8,128)(2,1)}, bf16[128,1024]{1,0:T(8,128)(2,1)}, u32[]{:S(2)}, u32[]{:S(2)}) collective-permute-start(bf16[128,1024]{1,0:T(8,128)(2,1)} %collective-permute-done), channel_id=1, source_target_pairs={{0,1},{1,2},{2,3},{3,0},{4,5},{5,6},{6,7},{7,4},{8,9},{9,10},{10,1... | collective-permute-start | bytes 786440 | tf_op jit(solution)/shard_map/ppermute | solution.py:586
  34.0 19.6 %collective-permute-start.3 = (bf16[128,1024]{1,0:T(8,128)(2,1)}, bf16[128,1024]{1,0:T(8,128)(2,1)}, u32[]{:S(2)}, u32[]{:S(2)}) collective-permute-start(bf16[128,1024]{1,0:T(8,128)(2,1)} %collective-permute-done.1), channel_id=1, source_target_pairs={{0,3},{1,0},{2,1},{3,2},{4,7},{5,4},{6,5},{7,6},{8,11},{9,8},{10,9... | collective-permute-start | bytes 786440 | tf_op jit(solution)/shard_map/ppermute | solution.py:587
  51.8 14.2 %copy-start.1 = (f32[4,256,6]{2,1,0:T(8,128)S(1)}, f32[4,256,6]{2,1,0:T(8,128)}, u32[]{:S(2)}) copy-start(f32[4,256,6]{2,1,0:T(8,128)} %copy.202) | copy-start | bytes 73732
  51.8 14.2 %copy-start.9 = (bf16[1024,4,192]{0,2,1:T(8,128)(2,1)S(1)}, bf16[1024,4,192]{0,2,1:T(8,128)(2,1)}, u32[]{:S(2)}) copy-start(bf16[1024,4,192]{0,2,1:T(8,128)(2,1)} %param.25) | copy-start | bytes 4718596
  53.6 8.5 %collective-permute-start.4 = (bf16[128,1024]{1,0:T(8,128)(2,1)}, bf16[128,1024]{1,0:T(8,128)(2,1)S(1)}, u32[]{:S(2)}, u32[]{:S(2)}) collective-permute-start(bf16[128,1024]{1,0:T(8,128)(2,1)} %collective-permute-done.2), channel_id=1, source_target_pairs={{0,1},{1,2},{2,3},{3,0},{4,5},{5,6},{6,7},{7,4},{8,9},{9,10},{10,1... | collective-permute-start | bytes 786440 | tf_op jit(solution)/shard_map/ppermute | solution.py:586
  53.6 12.3 %collective-permute-start.5 = (bf16[128,1024]{1,0:T(8,128)(2,1)}, bf16[128,1024]{1,0:T(8,128)(2,1)S(1)}, u32[]{:S(2)}, u32[]{:S(2)}) collective-permute-start(bf16[128,1024]{1,0:T(8,128)(2,1)} %collective-permute-done.3), channel_id=1, source_target_pairs={{0,3},{1,0},{2,1},{3,2},{4,7},{5,4},{6,5},{7,6},{8,11},{9,8},{10,9... | collective-permute-start | bytes 786440 | tf_op jit(solution)/shard_map/ppermute | solution.py:587
  71.6 24.0 %all-to-all-start.2 = ((bf16[8,64,1536]{2,1,0:T(8,128)(2,1)}), bf16[8,64,1536]{2,1,0:T(8,128)(2,1)}, u32[]{:S(2)}, u32[]{:S(2)}) async-start(bf16[8,64,1536]{2,1,0:T(8,128)(2,1)} %copy-done.24), calls=%async_computation.2 | async-start | bytes 3145728 | tf_op jit(solution)/shard_map/all_to_all | solution.py:777
  78.1 23.4 %copy-start.60 = (bf16[512]{0:T(512)(128)(2,1)S(1)}, bf16[512]{0:T(512)(128)(2,1)}, u32[]{:S(2)}) copy-start(bf16[512]{0:T(512)(128)(2,1)} %param.37) | copy-start | bytes 3076
  78.1 23.4 %copy-start.61 = (bf16[4,128]{1,0:T(4,128)(2,1)S(1)}, bf16[4,128]{1,0:T(4,128)(2,1)}, u32[]{:S(2)}) copy-start(bf16[4,128]{1,0:T(4,128)(2,1)} %param.39) | copy-start | bytes 3076
  78.1 23.5 %copy-start.52 = (bf16[10,1024]{1,0:T(8,128)(2,1)S(1)}, bf16[10,1024]{1,0:T(8,128)(2,1)}, u32[]{:S(2)}) copy-start(bf16[10,1024]{1,0:T(8,128)(2,1)} %param.35) | copy-start | bytes 61444
  78.1 79.0 %all-gather.2.cloned.1.call-start = ((), (), s32[]{:S(2)}) async-start(), calls=%async_computation.15 | async-start | bytes 2621440 | tf_op jit(solution)/shard_map/all_gather | solution.py:786
  97.9 13.6 %collective-permute-start.6 = (bf16[8,64,1024]{2,1,0:T(8,128)(2,1)}, bf16[8,64,1024]{2,1,0:T(8,128)(2,1)}, u32[]{:S(2)}, u32[]{:S(2)}) collective-permute-start(bf16[8,64,1024]{2,1,0:T(8,128)(2,1)} %slice.304), channel_id=1, source_target_pairs={{0,4},{4,0},{8,12},{12,8},{16,20},{20,16},{24,28},{28,24},{1,5},{5... | collective-permute-start | bytes 3145736 | tf_op jit(solution)/shard_map/ppermute | solution.py:618
  106.0 51.1 %all-to-all-start.3 = ((bf16[8,4,32,1024]{3,2,1,0:T(8,128)(2,1)}), bf16[8,4,32,1024]{3,2,1,0:T(8,128)(2,1)}, u32[]{:S(2)}, u32[]{:S(2)}) async-start(bf16[8,4,32,1024]{3,2,1,0:T(8,128)(2,1)} %broadcast_in_dim.127), calls=%async_computation.3 | async-start | bytes 4194304 | tf_op jit(solution)/shard_map/all_to_all | solution.py:566
  157.1 20.6 %all-to-all-start.4 = ((bf16[32,64,128]{2,1,0:T(8,128)(2,1)}), bf16[32,64,128]{2,1,0:T(8,128)(2,1)}, u32[]{:S(2)}, u32[]{:S(2)}) async-start(bf16[32,64,128]{2,1,0:T(8,128)(2,1)} %copy-done.32), calls=%async_computation.4 | async-start | bytes 1048576 | tf_op jit(solution)/shard_map/all_to_all | solution.py:793
  185.0 20.1 %collective-permute-start.7 = (bf16[512,256]{1,0:T(8,128)(2,1)}, bf16[512,256]{1,0:T(8,128)(2,1)}, u32[]{:S(2)}, u32[]{:S(2)}) collective-permute-start(bf16[512,256]{1,0:T(8,128)(2,1)} %get-tuple-element.266), channel_id=1, source_target_pairs={{0,1},{1,2},{2,3},{3,0},{4,5},{5,6},{6,7},{7,4},{8,9},{9,10},{10,1... | collective-permute-start | bytes 786440 | tf_op jit(solution)/shard_map/ppermute | solution.py:586
  185.0 22.0 %collective-permute-start.8 = (bf16[512,256]{1,0:T(8,128)(2,1)}, bf16[512,256]{1,0:T(8,128)(2,1)}, u32[]{:S(2)}, u32[]{:S(2)}) collective-permute-start(bf16[512,256]{1,0:T(8,128)(2,1)} %get-tuple-element.265), channel_id=1, source_target_pairs={{0,3},{1,0},{2,1},{3,2},{4,7},{5,4},{6,5},{7,6},{8,11},{9,8},{10,9... | collective-permute-start | bytes 786440 | tf_op jit(solution)/shard_map/ppermute | solution.py:587
  205.1 28.1 %copy-start.14 = (bf16[1024,4,256]{2,0,1:T(8,128)(2,1)S(1)}, bf16[1024,4,256]{2,0,1:T(8,128)(2,1)}, u32[]{:S(2)}) copy-start(bf16[1024,4,256]{2,0,1:T(8,128)(2,1)} %copy.211) | copy-start | bytes 6291460
  205.1 28.1 %copy-start.31 = (f32[1024,1]{1,0:T(8,128)S(1)}, f32[1024,1]{1,0:T(8,128)}, u32[]{:S(2)}) copy-start(f32[1024,1]{1,0:T(8,128)} %copy.215.bias) | copy-start | bytes 12292
  205.1 10.2 %collective-permute-start.9 = (bf16[512,256]{1,0:T(8,128)(2,1)}, bf16[512,256]{1,0:T(8,128)(2,1)S(1)}, u32[]{:S(2)}, u32[]{:S(2)}) collective-permute-start(bf16[512,256]{1,0:T(8,128)(2,1)} %collective-permute-done.7), channel_id=1, source_target_pairs={{0,1},{1,2},{2,3},{3,0},{4,5},{5,6},{6,7},{7,4},{8,9},{9,10},{10,1... | collective-permute-start | bytes 786440 | tf_op jit(solution)/shard_map/ppermute | solution.py:586
  207.0 14.0 %collective-permute-start.10 = (bf16[512,256]{1,0:T(8,128)(2,1)}, bf16[512,256]{1,0:T(8,128)(2,1)S(1)}, u32[]{:S(2)}, u32[]{:S(2)}) collective-permute-start(bf16[512,256]{1,0:T(8,128)(2,1)} %collective-permute-done.8), channel_id=1, source_target_pairs={{0,3},{1,0},{2,1},{3,2},{4,7},{5,4},{6,5},{7,6},{8,11},{9,8},{10,9... | collective-permute-start | bytes 786440 | tf_op jit(solution)/shard_map/ppermute | solution.py:587
  215.3 11.3 %collective-permute-start.11 = (bf16[512,256]{1,0:T(8,128)(2,1)S(1)}, bf16[512,256]{1,0:T(8,128)(2,1)S(1)}, u32[]{:S(2)}, u32[]{:S(2)}) collective-permute-start(bf16[512,256]{1,0:T(8,128)(2,1)S(1)} %collective-permute-done.9), channel_id=1, source_target_pairs={{0,1},{1,2},{2,3},{3,0},{4,5},{5,6},{6,7},{7,4},{8,9},{9,10},{10,1... | collective-permute-start | bytes 786440 | tf_op jit(solution)/shard_map/ppermute | solution.py:586
  221.0 11.4 %collective-permute-start.12 = (bf16[512,256]{1,0:T(8,128)(2,1)S(1)}, bf16[512,256]{1,0:T(8,128)(2,1)S(1)}, u32[]{:S(2)}, u32[]{:S(2)}) collective-permute-start(bf16[512,256]{1,0:T(8,128)(2,1)S(1)} %collective-permute-done.10), channel_id=1, source_target_pairs={{0,3},{1,0},{2,1},{3,2},{4,7},{5,4},{6,5},{7,6},{8,11},{9,8},{10,9... | collective-permute-start | bytes 786440 | tf_op jit(solution)/shard_map/ppermute | solution.py:587
  239.5 15.7 %copy-start.2 = (f32[4,256,6]{2,1,0:T(8,128)S(1)}, f32[4,256,6]{2,1,0:T(8,128)}, u32[]{:S(2)}) copy-start(f32[4,256,6]{2,1,0:T(8,128)} %copy.202) | copy-start | bytes 73732
  239.5 15.7 %copy-start.5 = (f32[1024,256]{1,0:T(8,128)S(1)}, f32[1024,256]{1,0:T(8,128)}, u32[]{:S(2)}) copy-start(f32[1024,256]{1,0:T(8,128)} %copy-done.4) | copy-start | bytes 3145732
  275.1 14.2 %collective-permute-start.19 = (bf16[1024,1024]{1,0:T(8,128)(2,1)}, bf16[1024,1024]{1,0:T(8,128)(2,1)}, u32[]{:S(2)}, u32[]{:S(2)}) collective-permute-start(bf16[1024,1024]{1,0:T(8,128)(2,1)} %dynamic-slice_bitcast_fusion), channel_id=1, source_target_pairs={{0,4},{4,0},{8,12},{12,8},{16,20},{20,16},{24,28},{28,24},{1,5},{5... | collective-permute-start | bytes 6291464 | tf_op jit(solution)/shard_map/ppermute | solution.py:618
  277.4 10.1 %collective-permute-start.13 = (bf16[512,256]{1,0:T(8,128)(2,1)}, bf16[512,256]{1,0:T(8,128)(2,1)}, u32[]{:S(2)}, u32[]{:S(2)}) collective-permute-start(bf16[512,256]{1,0:T(8,128)(2,1)} %get-tuple-element.263), channel_id=1, source_target_pairs={{0,1},{1,2},{2,3},{3,0},{4,5},{5,6},{6,7},{7,4},{8,9},{9,10},{10,1... | collective-permute-start | bytes 786440 | tf_op jit(solution)/shard_map/ppermute | solution.py:603
  277.6 20.7 %collective-permute-start.16 = (bf16[512,256]{1,0:T(8,128)(2,1)}, bf16[512,256]{1,0:T(8,128)(2,1)}, u32[]{:S(2)}, u32[]{:S(2)}) collective-permute-start(bf16[512,256]{1,0:T(8,128)(2,1)} %get-tuple-element.264), channel_id=1, source_target_pairs={{0,3},{1,0},{2,1},{3,2},{4,7},{5,4},{6,5},{7,6},{8,11},{9,8},{10,9... | collective-permute-start | bytes 786440 | tf_op jit(solution)/shard_map/ppermute | solution.py:604
  289.3 9.1 %collective-permute-start.14 = (bf16[512,256]{1,0:T(8,128)(2,1)}, bf16[512,256]{1,0:T(8,128)(2,1)}, u32[]{:S(2)}, u32[]{:S(2)}) collective-permute-start(bf16[512,256]{1,0:T(8,128)(2,1)} %fusion.14), channel_id=1, source_target_pairs={{0,1},{1,2},{2,3},{3,0},{4,5},{5,6},{6,7},{7,4},{8,9},{9,10},{10,1... | collective-permute-start | bytes 786440 | tf_op jit(solution)/shard_map/ppermute | solution.py:603
  293.9 32.5 %all-to-all-start.5 = ((bf16[4,256,1024]{2,1,0:T(8,128)(2,1)}), bf16[4,256,1024]{2,1,0:T(8,128)(2,1)}, u32[]{:S(2)}, u32[]{:S(2)}) async-start(bf16[4,256,1024]{2,1,0:T(8,128)(2,1)} %bitcast.246), calls=%async_computation.5 | async-start | bytes 4194304 | tf_op jit(solution)/shard_map/all_to_all | solution.py:637
  300.5 8.3 %collective-permute-start.15 = (bf16[512,256]{1,0:T(8,128)(2,1)}, bf16[512,256]{1,0:T(8,128)(2,1)}, u32[]{:S(2)}, u32[]{:S(2)}) collective-permute-start(bf16[512,256]{1,0:T(8,128)(2,1)} %get-tuple-element.261), channel_id=1, source_target_pairs={{0,1},{1,2},{2,3},{3,0},{4,5},{5,6},{6,7},{7,4},{8,9},{9,10},{10,1... | collective-permute-start | bytes 786440 | tf_op jit(solution)/shard_map/ppermute | solution.py:603
  300.5 11.9 %collective-permute-start.17 = (bf16[512,256]{1,0:T(8,128)(2,1)}, bf16[512,256]{1,0:T(8,128)(2,1)}, u32[]{:S(2)}, u32[]{:S(2)}) collective-permute-start(bf16[512,256]{1,0:T(8,128)(2,1)} %get-tuple-element.262), channel_id=1, source_target_pairs={{0,3},{1,0},{2,1},{3,2},{4,7},{5,4},{6,5},{7,6},{8,11},{9,8},{10,9... | collective-permute-start | bytes 786440 | tf_op jit(solution)/shard_map/ppermute | solution.py:604
  313.7 10.7 %collective-permute-start.18 = (bf16[512,256]{1,0:T(8,128)(2,1)S(1)}, bf16[512,256]{1,0:T(8,128)(2,1)S(1)}, u32[]{:S(2)}, u32[]{:S(2)}) collective-permute-start(bf16[512,256]{1,0:T(8,128)(2,1)S(1)} %get-tuple-element.260), channel_id=1, source_target_pairs={{0,3},{1,0},{2,1},{3,2},{4,7},{5,4},{6,5},{7,6},{8,11},{9,8},{10,9... | collective-permute-start | bytes 786440 | tf_op jit(solution)/shard_map/ppermute | solution.py:604
  336.8 21.4 %all-to-all-start.6 = ((bf16[32,64,128]{2,1,0:T(8,128)(2,1)}), bf16[32,64,128]{2,1,0:T(8,128)(2,1)}, u32[]{:S(2)}, u32[]{:S(2)}) async-start(bf16[32,64,128]{2,1,0:T(8,128)(2,1)} %bitcast.257), calls=%async_computation.6 | async-start | bytes 1048576 | tf_op jit(solution)/shard_map/all_to_all | solution.py:829
  342.9 89.7 %reduce-scatter.3.cloned.1.call-start = ((), (), s32[]{:S(2)}) async-start(), calls=%async_computation.16 | async-start | bytes 2621440 | tf_op jit(solution)/shard_map/reduce_scatter | solution.py:844
  358.2 88.3 %reduce-scatter.5.cloned.1.call-start = ((), (), s32[]{:S(2)}) async-start(), calls=%async_computation.17 | async-start | bytes 2621440 | tf_op jit(solution)/shard_map/reduce_scatter | solution.py:845
  365.3 67.3 %all-to-all-start.7 = ((bf16[4,256,1024]{2,1,0:T(8,128)(2,1)}), bf16[4,256,1024]{2,1,0:T(8,128)(2,1)}, u32[]{:S(2)}, u32[]{:S(2)}) async-start(bf16[4,256,1024]{2,1,0:T(8,128)(2,1)} %broadcast_in_dim.139), calls=%async_computation.9 | async-start | bytes 4194304 | tf_op jit(solution)/shard_map/all_to_all | solution.py:643
  432.6 17.0 %copy-start.55 = (f32[2,16,64]{2,1,0:T(8,128)S(1)}, f32[2,16,64]{2,1,0:T(8,128)}, u32[]{:S(2)}) copy-start(f32[2,16,64]{2,1,0:T(8,128)} %get-tuple-element.86) | copy-start | bytes 24580
  448.8 3.4 collective-permute-start.20
  449.6 18.2 %collective-permute-start.29 = (bf16[1024,1024]{1,0:T(8,128)(2,1)}, bf16[1024,1024]{1,0:T(8,128)(2,1)}, u32[]{:S(2)}, u32[]{:S(2)}) collective-permute-start(bf16[1024,1024]{1,0:T(8,128)(2,1)} %bitcast.54), channel_id=1, source_target_pairs={{0,4},{4,0},{8,12},{12,8},{16,20},{20,16},{24,28},{28,24},{1,5},{5... | collective-permute-start | bytes 6291464 | tf_op jit(solution)/shard_map/ppermute | solution.py:618
  455.6 23.8 %all-to-all-start.8 = ((bf16[8,64,1664]{2,1,0:T(8,128)(2,1)}), bf16[8,64,1664]{2,1,0:T(8,128)(2,1)}, u32[]{:S(2)}, u32[]{:S(2)}) async-start(bf16[8,64,1664]{2,1,0:T(8,128)(2,1)} %pad_maximum_fusion.1), calls=%async_computation.10 | async-start | bytes 3407872 | tf_op jit(solution)/shard_map/all_to_all | solution.py:867
  492.7 64.8 %collective-permute-start.24 = (bf16[128,1024]{1,0:T(8,128)(2,1)}, bf16[128,1024]{1,0:T(8,128)(2,1)}, u32[]{:S(2)}, u32[]{:S(2)}) collective-permute-start(bf16[128,1024]{1,0:T(8,128)(2,1)} %get-tuple-element.253), channel_id=1, source_target_pairs={{0,3},{1,0},{2,1},{3,2},{4,7},{5,4},{6,5},{7,6},{8,11},{9,8},{10,9... | collective-permute-start | bytes 786440 | tf_op jit(solution)/shard_map/ppermute | solution.py:604
  493.8 63.7 %collective-permute-start.21 = (bf16[128,1024]{1,0:T(8,128)(2,1)}, bf16[128,1024]{1,0:T(8,128)(2,1)}, u32[]{:S(2)}, u32[]{:S(2)}) collective-permute-start(bf16[128,1024]{1,0:T(8,128)(2,1)} %get-tuple-element.254), channel_id=1, source_target_pairs={{0,1},{1,2},{2,3},{3,0},{4,5},{5,6},{6,7},{7,4},{8,9},{9,10},{10,1... | collective-permute-start | bytes 786440 | tf_op jit(solution)/shard_map/ppermute | solution.py:603
  503.0 9.5 %collective-permute-start.27 = (bf16[512,1024]{1,0:T(8,128)(2,1)S(1)}, bf16[512,1024]{1,0:T(8,128)(2,1)}, u32[]{:S(2)}, u32[]{:S(2)}) collective-permute-start(bf16[512,1024]{1,0:T(8,128)(2,1)S(1)} %dynamic-slice_bitcast_fusion.1), channel_id=1, source_target_pairs={{0,4},{4,0},{8,12},{12,8},{16,20},{20,16},{24,28},{28,24},{1,5},{5... | collective-permute-start | bytes 3145736 | tf_op jit(solution)/shard_map/ppermute | solution.py:618
  508.1 9.1 %all-to-all-start.9 = ((f32[4,1,8448]{2,1,0:T(1,128)}), f32[4,1,8448]{2,1,0:T(1,128)S(1)}, u32[]{:S(2)}, u32[]{:S(2)}) async-start(f32[4,1,8448]{2,1,0:T(1,128)} %broadcast_in_dim.144), calls=%async_computation.11 | async-start | bytes 270336 | tf_op jit(solution)/shard_map/all_to_all | solution.py:902
  517.1 16.6 %all-to-all-start.11 = ((bf16[4,128,1024]{2,1,0:T(8,128)(2,1)}), bf16[4,128,1024]{2,1,0:T(8,128)(2,1)S(1)}, u32[]{:S(2)}, u32[]{:S(2)}) async-start(bf16[4,128,1024]{2,1,0:T(8,128)(2,1)} %bitcast.89), calls=%async_computation.13 | async-start | bytes 2097152 | tf_op jit(solution)/shard_map/all_to_all | solution.py:637
  524.1 14.7 %copy-start.53 = (bf16[10,1024]{1,0:T(8,128)(2,1)S(1)}, bf16[10,1024]{1,0:T(8,128)(2,1)}, u32[]{:S(2)}) copy-start(bf16[10,1024]{1,0:T(8,128)(2,1)} %param.35) | copy-start | bytes 61444
  535.0 16.8 %all-to-all-start.12 = ((bf16[4,128,1024]{2,1,0:T(8,128)(2,1)}), bf16[4,128,1024]{2,1,0:T(8,128)(2,1)S(1)}, u32[]{:S(2)}, u32[]{:S(2)}) async-start(bf16[4,128,1024]{2,1,0:T(8,128)(2,1)} %broadcast_in_dim.146), calls=%async_computation.14 | async-start | bytes 2097152 | tf_op jit(solution)/shard_map/all_to_all | solution.py:643
  552.6 11.5 %all-to-all-start.10 = ((f32[8,1,3072]{2,1,0:T(1,128)}), f32[8,1,3072]{2,1,0:T(1,128)S(1)}, u32[]{:S(2)}, u32[]{:S(2)}) async-start(f32[8,1,3072]{2,1,0:T(1,128)} %broadcast_in_dim.145), calls=%async_computation.12 | async-start | bytes 196608 | tf_op jit(solution)/shard_map/all_to_all | solution.py:566
  557.4 32.4 %copy-start.13 = (bf16[256,1024]{1,0:T(8,128)(2,1)S(1)}, bf16[256,1024]{1,0:T(8,128)(2,1)}, u32[]{:S(2)}) copy-start(bf16[256,1024]{1,0:T(8,128)(2,1)} %copy-done.11) | copy-start | bytes 1572868
  557.4 33.7 %collective-permute-start.28 = (bf16[512,1024]{1,0:T(8,128)(2,1)}, bf16[512,1024]{1,0:T(8,128)(2,1)}, u32[]{:S(2)}, u32[]{:S(2)}) collective-permute-start(bf16[512,1024]{1,0:T(8,128)(2,1)} %bitcast.250), channel_id=1, source_target_pairs={{0,4},{4,0},{8,12},{12,8},{16,20},{20,16},{24,28},{28,24},{1,5},{5... | collective-permute-start | bytes 3145736 | tf_op jit(solution)/shard_map/ppermute | solution.py:618
  559.7 8.0 %collective-permute-start.25 = (bf16[128,1024]{1,0:T(8,128)(2,1)}, bf16[128,1024]{1,0:T(8,128)(2,1)S(1)}, u32[]{:S(2)}, u32[]{:S(2)}) collective-permute-start(bf16[128,1024]{1,0:T(8,128)(2,1)} %get-tuple-element.257), channel_id=1, source_target_pairs={{0,3},{1,0},{2,1},{3,2},{4,7},{5,4},{6,5},{7,6},{8,11},{9,8},{10,9... | collective-permute-start | bytes 786440 | tf_op jit(solution)/shard_map/ppermute | solution.py:604
  562.0 12.2 %collective-permute-start.22 = (bf16[128,1024]{1,0:T(8,128)(2,1)S(1)}, bf16[128,1024]{1,0:T(8,128)(2,1)S(1)}, u32[]{:S(2)}, u32[]{:S(2)}) collective-permute-start(bf16[128,1024]{1,0:T(8,128)(2,1)S(1)} %get-tuple-element.258), channel_id=1, source_target_pairs={{0,1},{1,2},{2,3},{3,0},{4,5},{5,6},{6,7},{7,4},{8,9},{9,10},{10,1... | collective-permute-start | bytes 786440 | tf_op jit(solution)/shard_map/ppermute | solution.py:603
  575.4 8.8 %collective-permute-start.23 = (bf16[128,1024]{1,0:T(8,128)(2,1)S(1)}, bf16[128,1024]{1,0:T(8,128)(2,1)S(1)}, u32[]{:S(2)}, u32[]{:S(2)}) collective-permute-start(bf16[128,1024]{1,0:T(8,128)(2,1)S(1)} %get-tuple-element.256), channel_id=1, source_target_pairs={{0,1},{1,2},{2,3},{3,0},{4,5},{5,6},{6,7},{7,4},{8,9},{9,10},{10,1... | collective-permute-start | bytes 786440 | tf_op jit(solution)/shard_map/ppermute | solution.py:603
  576.7 13.1 %collective-permute-start.26 = (bf16[128,1024]{1,0:T(8,128)(2,1)S(1)}, bf16[128,1024]{1,0:T(8,128)(2,1)S(1)}, u32[]{:S(2)}, u32[]{:S(2)}) collective-permute-start(bf16[128,1024]{1,0:T(8,128)(2,1)S(1)} %get-tuple-element.255), channel_id=1, source_target_pairs={{0,3},{1,0},{2,1},{3,2},{4,7},{5,4},{6,5},{7,6},{8,11},{9,8},{10,9... | collective-permute-start | bytes 786440 | tf_op jit(solution)/shard_map/ppermute | solution.py:604
  579.5 11.5 %copy-start.46 = (bf16[4,128,1024]{2,1,0:T(8,128)(2,1)S(1)}, bf16[4,128,1024]{2,1,0:T(8,128)(2,1)}, u32[]{:S(2)}) copy-start(bf16[4,128,1024]{2,1,0:T(8,128)(2,1)} %copy-done.45) | copy-start | bytes 3145732
  (51 other events, 178.1 us)
Sparse Core Ops, SparseCore 0:
  81.1 45.7 all-gather.1
  358.3 41.8 reduce-scatter.2
  403.2 43.3 reduce-scatter.4

commit v2 on v1

--- a/solution.py
+++ b/solution.py
@@ -97,7 +97,7 @@
 ):
     sources, size, length = key.shape
     blocks, _, width = query.shape
-    per, parts = width // tile, length // keys
+    per = width // tile
     scale = size**-0.5
     padded = pre_key.shape[1]
 
@@ -114,7 +114,7 @@
     def prepare(source, most):
         rows = pl.ds(pl.multiple_of(source * length, length), length)
         key_rows[rows, :] = extended(key[source], length, LANES).astype(F32).T.astype(BF16)
-        value_ones[source] = extended(value[source], length, size + PAD)
+        value_ones[:, rows] = extended(value[source], length, size + PAD)
         return jnp.maximum(most, longest(key[source]))
 
     most = jnp.sqrt(lax.fori_loop(0, sources, prepare, longest(pre_key[...])))
@@ -146,11 +146,10 @@
 
         def block(number, masked):
             rows = pl.ds(pl.multiple_of(number * keys, keys), keys)
-            lanes = pl.ds(pl.multiple_of((number % parts) * keys, keys), keys)
             weights = jnp.exp(contract(key_rows[rows, :], shifted, 1, 0))
             if masked:
                 weights = jnp.where(allowed(meta, number, keys, places), weights, 0.0)
-            accum[...] += contract(value_ones[number // parts, :, lanes], weights.astype(BF16), 1, 0)
+            accum[...] += contract(value_ones[:, rows], weights.astype(BF16), 1, 0)
 
         over_keys(bounds, keys, block)
         peak[...] = limit
@@ -172,13 +171,8 @@
 
             def slow(number, masked):
                 rows = pl.ds(pl.multiple_of(number * keys, keys), keys)
-                lanes = pl.ds(pl.multiple_of((number % parts) * keys, keys), keys)
                 scores = contract(key_rows[rows, :][:, :size], plain, 1, 0)
-                fold(
-                    scores,
-                    allowed(meta, number, keys, places),
-                    value_ones[number // parts, :, lanes],
-                )
+                fold(scores, allowed(meta, number, keys, places), value_ones[:, rows])
 
             def step(number, _):
                 slow(number, True)
@@ -214,7 +208,7 @@
         out_specs=(VM, VM, VM),
         scratch_shapes=[
             pltpu.VMEM((sources * length, LANES), BF16),
-            pltpu.VMEM((sources, size + PAD, length), BF16),
+            pltpu.VMEM((size + PAD, sources * length), BF16),
             pltpu.VMEM((size + PAD, tile), F32),
             pltpu.VMEM((1, tile), F32),
         ],
@@ -224,25 +218,39 @@
     )(meta, query, key, value, pre_key, pre_value)
 
 
+def in_three(values):
+    high = values.astype(BF16).astype(F32)
+    middle = (values - high).astype(BF16).astype(F32)
+    low = values - high - middle
+    row = lax.broadcasted_iota(jnp.int32, (PAD, values.shape[1]), 0)
+    return jnp.where(row == 0, high, jnp.where(row == 1, middle, jnp.where(row == 2, low, 0.0)))
+
+
 def backward_kernel(
     meta, query, key, value, pre_key, pre_value, grad_out, out_full, log_total,
-    grad_query, grad_keep, grad_prefix,
-    key_rows, value_rows, key_sum, value_sum, query_sum,
+    grad_query, grad_keep, grad_send, grad_prefix,
+    key_rows, value_rows, key_columns, sums, query_sum,
     *, tile, keys, prefix, chunk, group,
 ):
     sources, size, length = key.shape
     blocks, _, width = query.shape
-    per, parts = width // tile, length // keys
+    per = width // tile
     scale = size**-0.5
     count = tile // LANES
     rank = meta[DOCS - 1]
 
+    def extended(values):
+        ones = jnp.where(
+            lax.broadcasted_iota(jnp.int32, (LANES - size, values.shape[1]), 0) < 3, 1.0, 0.0
+        )
+        return jnp.concatenate([values.astype(F32), ones], 0)
+
     def prepare(source, _):
         rows = pl.ds(pl.multiple_of(source * length, length), length)
-        key_rows[rows, :] = key[source].astype(F32).T.astype(BF16)
-        value_rows[rows, :] = value[source].astype(F32).T.astype(BF16)
-        key_sum[rows, :] = jnp.zeros((length, size), F32)
-        value_sum[rows, :] = jnp.zeros((length, size), F32)
+        key_rows[rows, :] = extended(key[source]).T.astype(BF16)
+        value_rows[rows, :] = extended(value[source]).T.astype(BF16)
+        key_columns[:, rows] = key[source]
+        sums[rows, :] = jnp.zeros((length, LANES), F32)
         return 0
 
     lax.fori_loop(0, sources, prepare, 0)
@@ -262,6 +270,13 @@
         index = lax.broadcasted_iota(jnp.int32, (1, tile), 1)
         places = query_places(meta, index, base, chunk, group)
         bounds = tile_bounds(meta, base, tile, chunk, group)
+        rest = jnp.zeros((LANES - size - PAD, tile), BF16)
+        scaled_less = jnp.concatenate([scaled, in_three(-level).astype(BF16), rest], 0)
+        grad_less = jnp.concatenate([grad, in_three(-delta).astype(BF16), rest], 0)
+        none = jnp.zeros((size, tile), BF16)
+        pair = jnp.concatenate(
+            [jnp.concatenate([grad, none], 1), jnp.concatenate([none, scaled], 1)], 0
+        )
 
         probs = jnp.exp(contract(pre_key[...], scaled, 1, 0) - level)
         probs = jnp.where(pre_row < prefix, probs, 0.0)
@@ -272,31 +287,42 @@
 
         def block(number, masked):
             rows = pl.ds(pl.multiple_of(number * keys, keys), keys)
-            lanes = pl.ds(pl.multiple_of((number % parts) * keys, keys), keys)
-            probs = jnp.exp(contract(key_rows[rows, :], scaled, 1, 0) - level)
+            probs = jnp.exp(contract(key_rows[rows, :], scaled_less, 1, 0))
             if masked:
                 probs = jnp.where(allowed(meta, number, keys, places), probs, 0.0)
-            slope = contract(value_rows[rows, :], grad, 1, 0)
-            slope = (probs * (slope - delta)).astype(BF16)
-            value_sum[rows, :] += contract(probs.astype(BF16), grad, 1, 1)
-            key_sum[rows, :] += contract(slope, scaled, 1, 1)
-            query_sum[...] += contract(key[number // parts, :, lanes], slope, 1, 0)
+            slope = (probs * contract(value_rows[rows, :], grad_less, 1, 0)).astype(BF16)
+            both = jnp.concatenate([probs.astype(BF16), slope], 1)
+            sums[rows, :] += contract(both, pair, 1, 1)
+            query_sum[...] += contract(key_columns[:, rows], slope, 1, 0)
 
         over_keys(bounds, keys, block)
         grad_query[source, :, columns] = (query_sum[...] * scale).astype(BF16)
         return 0
 
     lax.fori_loop(0, blocks * per, query_tile, 0)
-    key_slot = rank if group == 2 else 0
-    value_slot = 1 - rank if group == 2 else 1
-
-    def flush(source, _):
-        rows = pl.ds(pl.multiple_of(source * length, length), length)
-        grad_keep[key_slot, source] = key_sum[rows, :].T.astype(BF16)
-        grad_keep[value_slot, source] = value_sum[rows, :].T.astype(BF16)
-        return 0
-
-    lax.fori_loop(0, sources, flush, 0)
+
+    def flush(keys_target, values_target):
+        def step(source, _):
+            rows = pl.ds(pl.multiple_of(source * length, length), length)
+            turned = sums[rows, :].T.astype(BF16)
+            values_target[source] = turned[:size]
+            keys_target[source] = turned[size:]
+            return 0
+
+        lax.fori_loop(0, sources, step, 0)
+
+    if group == 2:
+
+        @pl.when(rank == 0)
+        def _():
+            flush(grad_keep, grad_send)
+
+        @pl.when(rank == 1)
+        def _():
+            flush(grad_send, grad_keep)
+
+    else:
+        flush(grad_keep, grad_send)
 
 
 def attend_backward(
@@ -310,16 +336,17 @@
         ),
         out_shape=(
             jax.ShapeDtypeStruct(query.shape, BF16),
-            jax.ShapeDtypeStruct((2,) + key.shape, BF16),
+            jax.ShapeDtypeStruct(key.shape, BF16),
+            jax.ShapeDtypeStruct(key.shape, BF16),
             jax.ShapeDtypeStruct((2,) + pre_key.shape, F32),
         ),
         in_specs=[SM] + [VM] * 8,
-        out_specs=(VM, VM, VM),
+        out_specs=(VM,) * 4,
         scratch_shapes=[
-            pltpu.VMEM((sources * length, size), BF16),
-            pltpu.VMEM((sources * length, size), BF16),
-            pltpu.VMEM((sources * length, size), F32),
-            pltpu.VMEM((sources * length, size), F32),
+            pltpu.VMEM((sources * length, LANES), BF16),
+            pltpu.VMEM((sources * length, LANES), BF16),
+            pltpu.VMEM((size, sources * length), BF16),
+            pltpu.VMEM((sources * length, LANES), F32),
             pltpu.VMEM((size, tile), F32),
         ],
         compiler_params=pltpu.CompilerParams(vmem_limit_bytes=56 * 2**20),
@@ -388,32 +415,21 @@
 
 
 def unproject_kernel(
-    slot, came, weight, rows, stats, columns, own_grad,
-    flat, part, row_sums, sums, head_sums,
-    *, heads, size, step,
+    spot, flat, weight, rows, stats, columns, own_grad,
+    part, row_sums, sums, head_sums,
+    *, step,
 ):
-    length = rows.shape[1]
-    half = step // 2
-    width = length // 2
     gain = columns[:, 0:1]
     sums[...] = jnp.zeros(sums.shape, F32)
     head_sums[...] = jnp.zeros(head_sums.shape, F32)
-    for piece in range(length // step):
+    for piece in range(rows.shape[1] // step):
         lanes = slice(piece * step, (piece + 1) * step)
-        spot = slice(piece * half, (piece + 1) * half)
-        pair = slice(width + piece * step, width + (piece + 1) * step)
-        pieces = []
-        for head in range(heads):
-            first, second = came[2 * head], came[2 * head + 1]
-            pieces.append(jnp.concatenate([first[:, spot], second[:, spot]], 1))
-            pieces += [first[:, pair], second[:, pair]]
-        grads = jnp.concatenate(pieces, 0)
-        flat[:, lanes] = grads
+        grads = flat[:, lanes]
         head_sums[...] += jnp.sum(grads.astype(F32), 1, keepdims=True)
         back = contract(weight[...], grads, 1, 0)
         part[:, lanes] = back.astype(BF16)
 
-        @pl.when(slot[0] == piece)
+        @pl.when(spot[0] == piece)
         def _():
             part[:, lanes] = (back + own_grad[...] / (stats[1:2, lanes] * gain)).astype(BF16)
 
@@ -425,22 +441,24 @@
         sums[:, 1:2] += jnp.sum(back, 1, keepdims=True)
 
 
-def unproject(slot, came, weight, rows, stats, columns, own_grad, heads, size, step):
+def unproject(spot, flat, weight, rows, stats, columns, own_grad, step):
     width, length = rows.shape
     return pl.pallas_call(
-        functools.partial(unproject_kernel, heads=heads, size=size, step=step),
+        functools.partial(unproject_kernel, step=step),
         out_shape=(
-            jax.ShapeDtypeStruct((3 * heads * size, length), BF16),
             jax.ShapeDtypeStruct((width, length), BF16),
             jax.ShapeDtypeStruct((2, length), F32),
             jax.ShapeDtypeStruct((width, 2), F32),
-            jax.ShapeDtypeStruct((3 * heads * size, 1), F32),
+            jax.ShapeDtypeStruct((flat.shape[0], 1), F32),
         ),
         in_specs=[SM] + [VM] * 6,
-        out_specs=(VM,) * 5,
+        out_specs=(VM,) * 4,
         compiler_params=pltpu.CompilerParams(vmem_limit_bytes=40 * 2**20),
+        cost_estimate=pl.CostEstimate(
+            flops=4 * flat.shape[0] * width * length, bytes_accessed=2**23, transcendentals=0
+        ),
         name="unproject",
-    )(slot, came, weight, rows, stats, columns, own_grad)
+    )(spot, flat, weight, rows, stats, columns, own_grad)
 
 
 def finish_kernel(up, down, own_up, own_down, rows, gain, stats, row_sums, grad):
@@ -470,7 +488,8 @@
     pre = contract(up_turned[...], rows[0], 1, 0) + bias[...]
     act, pull = jax.vjp(gelu_tanh, pre)
     hidden[0] = act.astype(BF16)
-    low = pull(contract(down[...], grads[0], 1, 0))[0].astype(BF16)
+    given = grads[...] if len(grads.shape) == 2 else grads[0]
+    low = pull(contract(down[...], given, 1, 0))[0].astype(BF16)
     grad_pre[0] = low
     part[0] = contract(up[...], low, 1, 0).astype(BF16)
 
@@ -484,6 +503,9 @@
 
     def block(size):
         return pl.BlockSpec((1, size, count), lambda i: (i, 0, 0))
+
+    if count % LANES:
+        grads = grads.reshape(width, blocks, count).transpose(1, 0, 2)
 
     return pl.pallas_call(
         feed_kernel,
@@ -495,7 +517,7 @@
         ),
         in_specs=[
             block(width),
-            block(width),
+            block(width) if count % LANES else pl.BlockSpec((width, count), lambda i: (0, i)),
             whole((inner, width)),
             whole((width, inner)),
             whole((inner, width)),
@@ -511,20 +533,36 @@
 
 
 def feed_rest_kernel(
-    slot, rows, grads, hidden, grad_pre, down_turned, middle, columns,
-    weights, bias, out, *, square,
+    spot, rows, grads, hidden, grad_pre, down_turned, middle, columns,
+    mine, other, bias, out,
+    *, square,
 ):
-    blocks, width, _ = rows.shape
+    blocks, width, count = rows.shape
     inner = hidden.shape[1]
     features = out.shape[2]
-    step = min(256, inner)
-    pairs = [(hidden, grads), (rows, grad_pre) if square else (grad_pre, rows)]
-    for which, (first, second) in enumerate(pairs):
-        for start in range(0, inner, step):
-            spot = slice(start, start + step)
-            weights[which, spot] = sum(
-                contract(first[n, spot], second[n], 1, 1) for n in range(blocks)
-            ).astype(BF16)
+
+    def lanes(n):
+        return slice(n * count, (n + 1) * count)
+
+    def weights(target, first, second, columns):
+        step = min(256, columns)
+        whole = jnp.concatenate([first(n) for n in range(blocks)], 1)
+        for start in range(0, columns, step):
+            tile = slice(start, start + step)
+            turned = jnp.concatenate([second(n, tile) for n in range(blocks)], 1)
+            target[:, tile] = contract(whole, turned, 1, 1).astype(BF16)
+
+    def down(target):
+        weights(target, lambda n: hidden[n], lambda n, tile: grads[tile, lanes(n)], width)
+
+    def up(target):
+        if square:
+            weights(target, lambda n: rows[n], lambda n, tile: grad_pre[n, tile], inner)
+        else:
+            weights(target, lambda n: grad_pre[n], lambda n, tile: rows[n, tile], width)
+
+    down(mine)
+    up(other)
     bias[...] = sum(jnp.sum(grad_pre[n].astype(F32), 1, keepdims=True) for n in range(blocks))
     for n in range(blocks):
         result = contract(down_turned[...], hidden[n], 1, 0)
@@ -535,29 +573,116 @@
 
         put(result)
 
-        @pl.when(slot[0] == n)
+        @pl.when(spot[0] == n)
         def _():
             put(result + middle[...] + columns[:, 5:6])
 
 
-def feed_rest(slot, rows, grads, hidden, grad_pre, down_turned, middle, columns):
+def feed_rest(spot, rows, grads, hidden, grad_pre, down_turned, middle, columns):
     blocks, width, count = rows.shape
     inner = hidden.shape[1]
     return pl.pallas_call(
         functools.partial(feed_rest_kernel, square=inner == width),
         out_shape=(
-            jax.ShapeDtypeStruct((2, inner, width), BF16),
+            jax.ShapeDtypeStruct((inner, width), BF16),
+            jax.ShapeDtypeStruct((inner, width), BF16),
             jax.ShapeDtypeStruct((inner, 1), F32),
             jax.ShapeDtypeStruct((blocks, blocks, width // blocks, count), BF16),
         ),
         in_specs=[SM] + [VM] * 7,
-        out_specs=(VM,) * 3,
+        out_specs=(VM,) * 4,
         compiler_params=pltpu.CompilerParams(vmem_limit_bytes=48 * 2**20),
         cost_estimate=pl.CostEstimate(
             flops=6 * blocks * width * inner * count, bytes_accessed=2**24, transcendentals=0
         ),
         name="feed_rest",
-    )(slot, rows, grads, hidden, grad_pre, down_turned, middle, columns)
+    )(spot, rows, grads, hidden, grad_pre, down_turned, middle, columns)
+
+
+def rest_kernel(spot, came, full, out, flat, mine, other, *, heads, size, step):
+    width, length = full.shape
+    half = step // 2
+    past = length // 2
+    for piece in range(length // step):
+        lanes = slice(piece * step, (piece + 1) * step)
+        place = slice(piece * half, (piece + 1) * half)
+        pair = slice(past + piece * step, past + (piece + 1) * step)
+        for head in range(heads):
+            first, second = 2 * head, 2 * head + 1
+            row = 3 * size * head
+            flat[row : row + size, lanes] = jnp.concatenate(
+                [came[first, :, place], came[second, :, place]], 1
+            )
+            flat[row + size : row + 2 * size, lanes] = came[first, :, pair]
+            flat[row + 2 * size : row + 3 * size, lanes] = came[second, :, pair]
+    split = mine.shape[0]
+    step = min(256, width)
+    for start in range(0, width, step):
+        tile = slice(start, start + step)
+        result = contract(flat[...], full[tile], 1, 1).astype(BF16)
+        first = result[:split]
+        second = jnp.concatenate([result[split:], out[:, tile]], 0)
+
+        @pl.when(spot[1] == 0)
+        def _():
+            mine[:, tile] = first
+            other[:, tile] = second
+
+        @pl.when(spot[1] == 1)
+        def _():
+            mine[:, tile] = second
+            other[:, tile] = first
+
+
+def rest_halves(spot, came, full, out, heads, size, step):
+    width, length = full.shape
+    rows = 3 * heads * size
+    half = (rows + out.shape[0]) // 2
+    return pl.pallas_call(
+        functools.partial(rest_kernel, heads=heads, size=size, step=step),
+        out_shape=(
+            jax.ShapeDtypeStruct((rows, length), BF16),
+            jax.ShapeDtypeStruct((half, width), BF16),
+            jax.ShapeDtypeStruct((half, width), BF16),
+        ),
+        in_specs=[SM] + [VM] * 3,
+        out_specs=(VM,) * 3,
+        compiler_params=pltpu.CompilerParams(vmem_limit_bytes=32 * 2**20),
+        name="rest_halves",
+    )(spot, came, full, out)
+
+
+def rest_whole_kernel(spot, half, other, mixed, out):
+    rows = half.shape[0]
+    extra = mixed.shape[0] - rows
+
+    def write(first, second):
+        mixed[:rows] = first[...].astype(F32)
+        mixed[rows:] = second[:extra].astype(F32)
+        out[...] = second[extra:].astype(F32)
+
+    @pl.when(spot[1] == 0)
+    def _():
+        write(half, other)
+
+    @pl.when(spot[1] == 1)
+    def _():
+        write(other, half)
+
+
+def rest_whole(spot, half, other, rows):
+    width = half.shape[1]
+    return pl.pallas_call(
+        rest_whole_kernel,
+        out_shape=(
+            jax.ShapeDtypeStruct((rows, width), F32),
+            jax.ShapeDtypeStruct((2 * half.shape[0] - rows, width), F32),
+        ),
+        in_specs=[SM, VM, VM],
+        out_specs=(VM, VM),
+        compiler_params=pltpu.CompilerParams(vmem_limit_bytes=32 * 2**20),
+        name="rest_whole",
+    )(spot, half, other)
 
 
 def spread(values, axis):
@@ -575,22 +700,26 @@
     return [(source, (source + by) % count) for source in range(count)]
 
 
-def ring_gather(values, axis):
+def ring_gather(values, axis, beside=()):
     count, place = lax.axis_size(axis), lax.axis_index(axis)
     half = values.shape[0] // 2
     up, down = values[:half], values[half:]
     out = jnp.zeros((count,) + values.shape, values.dtype)
     out = lax.dynamic_update_slice_in_dim(out, values[None], place, 0)
     zeros = (0,) * (values.ndim - 1)
+    results = []
     for step in range(1, count):
         up = lax.ppermute(up, axis, ring(axis, 1))
         down = lax.ppermute(down, axis, ring(axis, -1))
+        if step <= len(beside) and beside[step - 1]:
+            up, down, result = lax.optimization_barrier((up, down, beside[step - 1]()))
+            results.append(result)
         out = lax.dynamic_update_slice(out, up[None], ((place - step) % count, 0) + zeros)
         out = lax.dynamic_update_slice(out, down[None], ((place + step) % count, half) + zeros)
-    return out
-
-
-def ring_terms(blocks, axis):
+    return (out, results) if beside else out
+
+
+def ring_terms(blocks, axis, beside=()):
     count, place = lax.axis_size(axis), lax.axis_index(axis)
     half = blocks.shape[1] // 2
 
@@ -599,18 +728,19 @@
         return block[half:] if upper else block[:half]
 
     up, down = own(-1, False), own(1, True)
+    state = None
     for step in range(1, count):
         up = lax.ppermute(up, axis, ring(axis, 1))
         down = lax.ppermute(down, axis, ring(axis, -1))
+        if step <= len(beside):
+            state = beside[step - 1](state)
+            up, down, state = lax.optimization_barrier((up, down, state))
         if step < count - 1:
             up = (up.astype(F32) + own(-1 - step, False).astype(F32)).astype(BF16)
             down = (down.astype(F32) + own(1 + step, True).astype(F32)).astype(BF16)
-    return up, down, own(0, False), own(0, True)
-
-
-def ring_sum(blocks, axis):
-    up, down, own_up, own_down = [a.astype(F32) for a in ring_terms(blocks, axis)]
-    return jnp.concatenate([up + own_up, down + own_down], 0)
+    for other in beside[count - 1 :]:
+        state = other(state)
+    return (up, down, own(0, False), own(0, True)), state
 
 
 def swapped(values):
@@ -623,11 +753,7 @@
     return [[2 * chip + core for chip in range(chips)] for core in range(2)]
 
 
-def core_halves(values):
-    core = lax.axis_index("seq") % 2
-    halves = values.reshape(2, values.shape[0] // 2, values.shape[1])
-    mine = lax.dynamic_index_in_dim(halves, core, 0, keepdims=False)
-    other = lax.dynamic_index_in_dim(halves, 1 - core, 0, keepdims=False)
+def core_sum(mine, other):
     return (mine.astype(F32) + swapped(other).astype(F32)).astype(BF16)
 
 
@@ -637,11 +763,24 @@
     return lax.all_to_all(blocks, "seq", 0, 0, axis_index_groups=chip_groups(), tiled=True)
 
 
-def chip_gather(parts):
+def chip_copies(parts):
     part = jnp.sum(parts.astype(F32), 0).astype(BF16)
-    copies = jnp.broadcast_to(part[None], parts.shape)
+    return jnp.broadcast_to(part[None], parts.shape)
+
+
+def chip_gather(copies):
     half = lax.all_to_all(copies, "seq", 0, 0, axis_index_groups=chip_groups(), tiled=True)
     return half.reshape(-1, half.shape[2])
+
+
+def spread_direct(values, axis):
+    count, place = lax.axis_size(axis), lax.axis_index(axis)
+    out = jnp.zeros((count,) + values.shape, values.dtype)
+    out = lax.dynamic_update_slice_in_dim(out, values[None], place, 0)
+    for step in range(1, count):
+        came = lax.ppermute(values, axis, ring(axis, step))
+        out = lax.dynamic_update_slice_in_dim(out, came[None], (place - step) % count, 0)
+    return out
 
 
 def core_gather(half):
@@ -711,33 +850,33 @@
     query_width = max(tokens_head, LANES)
     forward_tile = min(512, query_width)
     backward_tile = min(256, query_width)
-    forward_keys, backward_keys = 512, 1024
+    forward_keys, backward_keys = 1024, 1024
     both = ("seq", "tensor")
     paired = group == 2 and chunk == LANES
 
     own_tokens, own_grads = turned(tokens, out_grad)
-    full_tokens = ring_gather(own_tokens, "tensor").reshape(width, rows)
     numbers = jnp.arange(1, DOCS, dtype=jnp.int32)
-    before = jnp.sum((segment_ids[None, :] < numbers[:, None]).astype(jnp.int32), 1)
-    starts = small_sum(jnp.broadcast_to(before[:, None], (DOCS - 1, LANES)), "seq")[:, 0]
-    meta = jnp.concatenate([starts, rank[None].astype(jnp.int32)])
-    vectors = jnp.stack([ln1_gain, ln1_bias, ln2_gain, ln2_bias, b_out, b_down])
-    share_rows = heads * size // seqs
-    out_share = w_out.reshape(seqs, share_rows, width)
+
+    def document_starts():
+        before = jnp.sum((segment_ids[None, :] < numbers[:, None]).astype(jnp.int32), 1)
+        return spread(jnp.broadcast_to(before[:, None], (DOCS - 1, LANES)), "seq")
+
+    def whole_vectors():
+        return spread(
+            jnp.stack([ln1_gain, ln1_bias, ln2_gain, ln2_bias, b_out, b_down]), "tensor"
+        )
+
+    full_tokens, (vectors, starts) = ring_gather(
+        own_tokens, "tensor", (None, whole_vectors, document_starts)
+    )
+    full_tokens = full_tokens.reshape(width, rows)
+    meta = jnp.concatenate([jnp.sum(starts, 0)[:, 0], rank[None].astype(jnp.int32)])
+    columns = vectors.transpose(0, 2, 1).reshape(width, 6).astype(F32)
+    out_share = w_out.reshape(seqs, heads * size // seqs, width)
     out_share = lax.dynamic_index_in_dim(out_share, place, 0, keepdims=False)
-    extra = -(-vectors.size // width)
-    vectors = jnp.pad(vectors.reshape(-1), (0, extra * width - vectors.size))
-    out_share = jnp.concatenate([out_share, vectors.reshape(extra, width)], 0)
-    out_share = spread(out_share, "tensor")
-    vectors = out_share[:, share_rows:].reshape(tensors, -1)[:, : 6 * features]
-    columns = vectors.reshape(tensors, 6, features).transpose(0, 2, 1).reshape(width, 6).astype(F32)
-    full_tokens, columns, meta, out_share = lax.optimization_barrier(
-        (full_tokens, columns, meta, out_share[:, :share_rows])
-    )
-    out_share = spread(out_share, "seq")
-    w_out_full = out_share.transpose(1, 0, 2, 3).reshape(width, width)
     gain2, shift2, bias_out = [columns[:, i : i + 1] for i in (2, 3, 4)]
-    where_slot = slot[None].astype(jnp.int32)
+    core = place % 2
+    spot = jnp.stack([slot, core]).astype(jnp.int32)
 
     embed_float = prefix_embed.astype(F32)
     prefix_hidden = jnp.tanh(
@@ -774,7 +913,12 @@
         pair_part = mixed[:, 1:].transpose(0, 2, 1, 3).reshape(heads, size, group, 2 * tokens_head)
         pair_part = pair_part.transpose(0, 2, 1, 3).reshape(seqs, size, 2 * tokens_head)
         sent = jnp.concatenate([query_part, pair_part], 2)
+    out_share = spread_direct(after(out_share, sent), "tensor")
     came = lax.all_to_all(sent, "seq", 0, 0, tiled=True)
+    out_share = jnp.broadcast_to(out_share[None], (seqs,) + out_share.shape)
+    came, out_share = lax.optimization_barrier((came, out_share))
+    out_share = lax.all_to_all(out_share, "seq", 0, 0, tiled=True)
+    w_out_full = out_share.transpose(1, 0, 2, 3).reshape(width, width)
     query, pair = came[:, :, :tokens_head], came[:, :, tokens_head:]
     query = regrouped(query, query_width)
     pair = group_gather(pair, group)
@@ -788,9 +932,14 @@
         meta, query, key, value, pre_key.T, pre_value.T,
         forward_tile, forward_keys, prefix, chunk, group,
     )
-    out_low, full_grad = lax.optimization_barrier((out_low, full_grad))
+    out_low, full_grad, late_up, late_down = lax.optimization_barrier(
+        (out_low, full_grad, w_up, w_down)
+    )
 
     came = lax.all_to_all(regrouped(out_low, chunk), both, 0, 0, tiled=True)
+    came, up_turned, down_turned, w_out_full = lax.optimization_barrier(
+        (came, late_up.T, late_down.T, w_out_full)
+    )
     came = came.reshape(heads, group, tensors, size, chunk).transpose(2, 0, 3, 1, 4)
     attended = came.reshape(width, own_rows)
     branch = contract(w_out_full, attended, 0, 0)
@@ -803,25 +952,26 @@
     out2 = (normed2 * gain2 + shift2).astype(BF16)
 
     full2 = ring_gather(out2, "tensor")
-    grads = full_grad.reshape(width, tensors, own_rows).transpose(1, 0, 2)
     hidden, grad_pre, part = feed(
-        full2, grads, w_up.T, w_up, w_down, b_up.astype(F32)[:, None]
-    )
-    feed_weights, grad_b_up, mlp_out = feed_rest(
-        where_slot, full2, grads, hidden, grad_pre, w_down.T, middle, columns
-    )
-    core = place % 2
-    feed_mine = lax.dynamic_index_in_dim(feed_weights, core, 0, keepdims=False)
-    feed_other = lax.dynamic_index_in_dim(feed_weights, 1 - core, 0, keepdims=False)
-    feed_half = (feed_mine.astype(F32) + swapped(feed_other).astype(F32)).astype(BF16)
-    feed_parts = chip_parts(feed_half)
-    grad_normed2 = ring_sum(part, "tensor")
-    grad_normed2, feed_parts = lax.optimization_barrier((grad_normed2, feed_parts))
+        full2, full_grad, up_turned, w_up, w_down, b_up.astype(F32)[:, None]
+    )
+
+    def weights_here(_):
+        return feed_rest(
+            spot, full2, full_grad, hidden, grad_pre, down_turned, middle, columns
+        )
+
+    terms, (grad_w_down, grad_w_up, grad_b_up, mlp_out) = ring_terms(
+        part, "tensor", (weights_here,)
+    )
+    feed_sums = lax.psum((grad_w_down, grad_w_up), "seq")
+    up, down, own_up, own_down = [a.astype(F32) for a in terms]
+    grad_normed2 = jnp.concatenate([up + own_up, down + own_down], 0)
 
     scaled = grad_normed2 * gain2
     first = jnp.mean(scaled, 0, keepdims=True)
     second = jnp.mean(scaled * normed2, 0, keepdims=True)
-    own_grad = lax.dynamic_index_in_dim(grads, slot, 0, keepdims=False)
+    own_grad = lax.dynamic_slice_in_dim(full_grad, slot * own_rows, own_rows, 1)
     grad_middle = own_grad.astype(F32) + inverse2 * (scaled - first - normed2 * second)
     grad_branch = grad_middle.astype(BF16)
     grad_attended = contract(w_out_full, grad_branch, 1, 0).astype(BF16)
@@ -837,24 +987,19 @@
         ]
     )
     grad_w_out = contract(attended, grad_branch, 1, 1).astype(BF16)
-    grad_out, mlp_out, grad_w_out, feed_parts = lax.optimization_barrier(
-        (grad_out, mlp_out, grad_w_out, feed_parts)
-    )
-    feed_half = chip_gather(feed_parts)
-    output_act = lax.psum_scatter(mlp_out, "tensor", scatter_dimension=0, tiled=True)
+    grad_out, mlp_out, grad_w_out = lax.optimization_barrier((grad_out, mlp_out, grad_w_out))
+    output_act = lax.all_to_all(mlp_out, "tensor", 0, 0, tiled=True)
     grad_w_out = lax.psum_scatter(grad_w_out, "tensor", scatter_dimension=0, tiled=True)
 
     levels = log_total.reshape(-1, 1, backward_tile)
-    grad_query, grad_pair, grad_prefix = attend_backward(
+    grad_query, grad_keep, grad_send, grad_prefix = attend_backward(
         meta, query, key, value, pre_key[:PAD], pre_value[:PAD], grad_out, out_full, levels,
         backward_tile, backward_keys, prefix, chunk, group,
     )
-    grad_pair, output_act, grad_w_out, feed_half = lax.optimization_barrier(
-        (grad_pair, output_act, grad_w_out, feed_half)
-    )
     if group == 2:
-        grad_share = (grad_pair[0].astype(F32) + swapped(grad_pair[1]).astype(F32)).astype(BF16)
+        grad_share = (grad_keep.astype(F32) + swapped(grad_send).astype(F32)).astype(BF16)
     else:
+        grad_pair = jnp.stack([grad_keep, grad_send])
         groups = [[first + i for i in range(group)] for first in range(0, seqs, group)]
         shares = grad_pair.transpose(1, 2, 0, 3).reshape(seqs, size, group, 2 * tokens_head)
         grad_share = lax.psum_scatter(
@@ -864,10 +1009,15 @@
     prefix_part = jnp.pad(prefix_part, ((0, 0), (0, LANES - 2 * PAD)))
     prefix_part = jnp.broadcast_to(prefix_part[None], (seqs, size, LANES))
     sent = jnp.concatenate([regrouped(grad_query, tokens_head), grad_share, prefix_part], 2)
+    sent, output_act, feed_sums = lax.optimization_barrier((sent, output_act, feed_sums))
     came = lax.all_to_all(sent, "seq", 0, 0, tiled=True)
+    output_act = jnp.sum(output_act.astype(F32), 0).astype(BF16)
+    output_act = output_act.transpose(0, 2, 1).reshape(rows, features)
+    came, output_act, grad_w_out = lax.optimization_barrier((came, output_act, grad_w_out))
     if paired:
-        grad_flat, grad_part, row_sums, sums1, head_sums = unproject(
-            where_slot, came, w_flat, full_tokens, stats, columns, grad_middle, heads, size, own_rows
+        grad_flat, mine, other = rest_halves(spot, came, full1, grad_w_out, heads, size, own_rows)
+        grad_part, row_sums, sums1, head_sums = unproject(
+            spot, grad_flat, w_flat, full_tokens, stats, columns, grad_middle, own_rows
         )
     else:
         query_part = came[:, :, :tokens_head].reshape(heads, group, size, tensors, chunk)
@@ -876,6 +1026,11 @@
         pair_part = pair_part.reshape(heads, group, size, 2 * tokens_head).transpose(0, 2, 1, 3)
         pair_part = pair_part.reshape(heads, size, 2, rows).transpose(0, 2, 1, 3)
         grad_flat = jnp.concatenate([query_part, pair_part], 1).reshape(heads * 3 * size, rows)
+        grad_w_qkv = contract(grad_flat, full1, 1, 1).astype(BF16)
+        rest = jnp.concatenate([grad_w_qkv, grad_w_out], 0)
+        halves = rest.reshape(2, rest.shape[0] // 2, width)
+        mine = lax.dynamic_index_in_dim(halves, core, 0, keepdims=False)
+        other = lax.dynamic_index_in_dim(halves, 1 - core, 0, keepdims=False)
         back = contract(w_flat, grad_flat, 1, 0)
         normed1 = (full_tokens.astype(F32) - stats[0]) * stats[1]
         scaled = back * columns[:, 0:1]
@@ -887,7 +1042,8 @@
         own_part = own_part + grad_middle / (own_inverse * columns[:, 0:1])
         back = lax.dynamic_update_slice_in_dim(back, own_part, slot * own_rows, 1)
         grad_part = back.astype(BF16)
-    last_terms = ring_terms(grad_part.reshape(tensors, features, rows), "tensor")
+    rest_half = core_sum(mine, other)
+    grad_part, rest_half = lax.optimization_barrier((grad_part, rest_half))
 
     prefix_low = came[:, :, 3 * tokens_head : 3 * tokens_head + 2 * PAD].astype(F32)
     prefix_low = jnp.sum(prefix_low.reshape(heads, group, size, 2, PAD), 1)[..., :prefix]
@@ -899,31 +1055,28 @@
     shared = jnp.concatenate([row_sums.reshape(-1), hidden_part.reshape(-1)])
     shared = jnp.broadcast_to(shared[None], (tensors, shared.shape[0]))
     small = jnp.concatenate([owned, shared], 1)[:, None, :]
-    small = jnp.sum(lax.all_to_all(small, "tensor", 0, 0, tiled=True), 0)[0]
-    owned, row_sums = small[: 5 * features], small[5 * features : 5 * features + 2 * rows]
-    hidden_grad = small[5 * features + 2 * rows :].reshape(prefix_hidden.shape)
-    input_grad = finish(
-        *last_terms, own_tokens, ln1_gain.astype(F32)[:, None], stats,
-        row_sums.reshape(2, rows) / width,
-    )
-    output_act = output_act[0].transpose(0, 2, 1).reshape(rows, features)
-
-    first_half, second_half = core_gather(feed_half)
-    out_w_down = first_half.astype(F32)
-    out_w_up = (second_half if inner == width else second_half.T).astype(F32)
-    grad_w_qkv = contract(grad_flat, full1, 1, 1).astype(BF16)
-    rest = jnp.concatenate([grad_w_qkv, grad_w_out], 0)
-    rest_half = chip_gather(chip_parts(core_halves(rest)))
-    rest = jnp.concatenate(core_gather(rest_half), 0).astype(F32)
-    mixed_rows = heads * 3 * size
-    out_w_qkv = rest[:mixed_rows].reshape(heads, 3 * size, width).transpose(2, 0, 1)
-    out_w_out = rest[mixed_rows:].reshape(heads, size, width)
 
     grad_b_down = jnp.sum(out_grad.astype(F32), 0)
     head_sums = head_sums.reshape(heads, 3, size)
+
+    def rest_parts(_):
+        return chip_parts(rest_half)
+
+    def small_here(parts):
+        return chip_copies(parts), lax.all_to_all(small, "tensor", 0, 0, tiled=True)
+
+    def rest_back(state):
+        return chip_gather(state[0]), state[1]
+
+    last_terms, (rest_half, small) = ring_terms(
+        grad_part.reshape(tensors, features, rows),
+        "tensor",
+        (rest_parts, small_here) + (lambda state: state,) * (tensors - 4) + (rest_back,),
+    )
+    small = jnp.sum(small, 0)[0]
     late = jnp.concatenate(
         [
-            owned,
+            small[: 5 * features],
             grad_b_down,
             grad_b_up.reshape(-1),
             head_sums[:, 0].reshape(-1),
@@ -931,6 +1084,23 @@
         ]
     )
     late = small_sum(late[None], "seq")[0]
+    row_sums = small[5 * features : 5 * features + 2 * rows]
+    hidden_grad = small[5 * features + 2 * rows :].reshape(prefix_hidden.shape)
+    input_grad = finish(
+        *last_terms, own_tokens, ln1_gain.astype(F32)[:, None], stats,
+        row_sums.reshape(2, rows) / width,
+    )
+    mixed_rows = heads * 3 * size
+    if paired:
+        out_w_qkv, out_w_out = rest_whole(spot, rest_half, swapped(rest_half), mixed_rows)
+    else:
+        rest = jnp.concatenate(core_gather(rest_half), 0).astype(F32)
+        out_w_qkv, out_w_out = rest[:mixed_rows], rest[mixed_rows:]
+    out_w_qkv = out_w_qkv.reshape(heads, 3 * size, width).transpose(2, 0, 1)
+    out_w_out = out_w_out.reshape(heads, size, width)
+    out_w_down = feed_sums[0].astype(F32)
+    out_w_up = (feed_sums[1] if inner == width else feed_sums[1].T).astype(F32)
+
     out_ln1_gain, out_ln1_bias, out_ln2_gain, out_ln2_bias, out_b_out, out_b_down = [
         late[i * features : (i + 1) * features] for i in range(6)
     ]

time: 612 us -> 553 us (0.904)
  waiting for transfers between devices: 158 us -> 122 us
  local copies, waits for them, and re-layouts: 120 us -> 101 us
  starting transfers between devices: 104 us -> 116 us
  Pallas kernels: 141 us -> 132 us
    pallas_call x1, Pallas kernels: 39.3 us -> 25.5 us  [attend_forward(): pl.pallas_call(functools.partial(forward_kernel, tile=tile, keys=keys, pr...]
    all_to_all x2 -> x1, waiting for transfers between devices: 9.58 us -> 0.01 us  [chip_parts(): lax.all_to_all(blocks, 'seq', 0, 0, axis_index_groups=chip_groups(), tile...]
    all_to_all x4 -> x3, waiting for transfers between devices: 9.31 us -> 0.01 us  [spread(): return lax.all_to_all(copies, axis, 0, 0, tiled=True)]
    pallas_call x1 -> x3, Pallas kernels: 6.27 us -> 14.8 us  [the longest x1 6 us: rest_halves(): pl.pallas_call(functools.partial(rest_kernel, heads=heads, size=size, ste...]
    all_to_all x1 -> x3, starting transfers between devices: 4.16 us -> 12.1 us  [the longest x1 4.45 us: on_device(): output_act = lax.all_to_all(mlp_out, 'tensor', 0, 0, tiled=True)]
    all_to_all x2 -> x1, waiting for transfers between devices: 7.72 us -> 0.01 us  [chip_gather(): lax.all_to_all(copies, 'seq', 0, 0, axis_index_groups=chip_groups(), tile...]
    reduce_scatter x1, waiting for transfers between devices: 13.9 us -> 7.2 us  [on_device(): lax.psum_scatter(grad_w_out, 'tensor', scatter_dimension=0, tiled=True)]
    ppermute x6, waiting for transfers between devices: 11.7 us -> 18.4 us  [ring_gather(): up = lax.ppermute(up, axis, ring(axis, 1))]
  transfers between devices with their start and end apart: 46 -> 46, of which waited for: 24 -> 27; matrix products, arithmetic and copies ran while one was open for 21% -> 18% of each run, Pallas kernels for 17% -> 19%
where the time goes in v2:
time: 553 us; the launch traced here: 543 us
  Pallas kernels  132 us (24%)
  waiting for transfers between devices  122 us (22%)
  starting transfers between devices  116 us (21%)
  local copies, waits for them, and re-layouts  101 us (18%)
  other arithmetic  44 us (8%)
  between operations  15.3 us (3%)
  matrix products  12.6 us (2%)
    pallas_call x1, Pallas kernels, attend_backward(): pl.pallas_call(functools.partial(backward_kernel, tile=tile, keys=keys, p...  57.2 us
    unnamed x163, local copies, waits for them, and re-layouts  44.1 us
    pallas_call x1, Pallas kernels, attend_forward(): pl.pallas_call(functools.partial(forward_kernel, tile=tile, keys=keys, pr...  25.5 us
    ppermute x6, waiting for transfers between devices, ring_terms(): down = lax.ppermute(down, axis, ring(axis, -1))  20.7 us
    ppermute x6, waiting for transfers between devices, ring_gather(): up = lax.ppermute(up, axis, ring(axis, 1))  18.4 us
    ppermute x6, waiting for transfers between devices, ring_gather(): down = lax.ppermute(down, axis, ring(axis, -1))  17.7 us
    ppermute x6, waiting for transfers between devices, ring_terms(): up = lax.ppermute(up, axis, ring(axis, 1))  16.9 us
    all_to_all x2, waiting for transfers between devices, on_device(): came = lax.all_to_all(sent, 'seq', 0, 0, tiled=True)  16 us
  transfers between devices with their start and end apart: 46, of which 27 were waited for; matrix products, arithmetic and copies ran while one was open for 18% of the time, Pallas kernels for 19%

profile of v2, /device:TPU:1, one launch (start us, length us, event | category | flops | bytes accessed | tf_op | source)
XLA Modules:
  0.0 542.5 jit_solution(11682361871312156151)
XLA Ops:
  17.1 3.3 all-to-all-start
  24.3 3.6 collective-permute-done.2
  32.6 6.8 %all-to-all-start.1 = ((s32[8,4,128]{2,1,0:T(4,128)}), s32[8,4,128]{2,1,0:T(4,128)}, u32[]{:S(2)}, u32[]{:S(2)}) async-start(s32[8,4,128]{2,1,0:T(4,128)} %broadcast_in_dim_broadcast_in_dim_broadcast_in_dim.2), calls=%async_computation.1 | async-start | bytes 32768 | tf_op jit(solution)/shard_map/all_to_all | solution.py:691
  40.6 3.2 collective-permute-start.5
  50.1 2.9 collective-permute-done.5
  57.9 3.2 project.1
  63.6 6.2 %all-to-all-start.2 = ((bf16[8,64,1536]{2,1,0:T(8,128)(2,1)}), bf16[8,64,1536]{2,1,0:T(8,128)(2,1)S(1)}, u32[]{:S(2)}, u32[]{:S(2)}) async-start(bf16[8,64,1536]{2,1,0:T(8,128)(2,1)} %copy-done.22), calls=%async_computation.2 | async-start | bytes 3145728 | tf_op jit(solution)/shard_map/all_to_all | solution.py:917
  78.2 9.2 %all-to-all-done.2 = bf16[8,64,1536]{2,1,0:T(8,128)(2,1)S(1)} async-done(((bf16[8,64,1536]{2,1,0:T(8,128)(2,1)}), bf16[8,64,1536]{2,1,0:T(8,128)(2,1)S(1)}, u32[]{:S(2)}, u32[]{:S(2)}) %all-to-all-start.2) | async-done | bytes 1572896 | tf_op jit(solution)/shard_map/all_to_all | solution.py:917
  90.2 3.5 collective-permute-start.9
  96.6 4.3 all-to-all-start.4
  102.7 25.5 %attend_forward.1 = (bf16[32,64,128]{2,1,0:T(8,128)(2,1)}, f32[32,64,128]{2,1,0:T(8,128)S(1)}, f32[8,1,512]{2,1,0:T(1,128)S(1)}) custom-call(s32[5]{0:T(128)S(1)} %pad_add_fusion.meta, bf16[8,64,512]{2,1,0:T(8,128)(2,1)S(1)} %slice.215.query, bf16[8,64,1024]{2,1,0:T(8,128)(2,1)S(1)} %get-tuple-element.320.key, ...), custom_call_target="tpu_custom_call" | custom-call | flops 17179869184 | bytes 8388608 | tf_op jit(solution)/shard_map/attend_forward/pallas_call | solution.py:198
  131.7 9.6 %all-to-all-start.3 = ((bf16[32,64,128]{2,1,0:T(8,128)(2,1)}), bf16[32,64,128]{2,1,0:T(8,128)(2,1)S(1)}, u32[]{:S(2)}, u32[]{:S(2)}) async-start(bf16[32,64,128]{2,1,0:T(8,128)(2,1)} %get-tuple-element.107), calls=%async_computation.3 | async-start | bytes 1048576 | tf_op jit(solution)/shard_map/all_to_all | solution.py:939
  142.7 3.9 copy.190
  146.7 3.9 copy.191
  150.6 3.2 copy.192
  153.8 2.8 all-to-all-done.3
  157.1 2.7 fusion.36
  163.4 3.3 collective-permute-start.11
  167.0 6.6 %collective-permute-done.10 = bf16[512,256]{1,0:T(8,128)(2,1)} collective-permute-done((bf16[512,256]{1,0:T(8,128)(2,1)}, bf16[512,256]{1,0:T(8,128)(2,1)}, u32[]{:S(2)}, u32[]{:S(2)}) %collective-permute-start.10) | collective-permute-done | bytes 262176 | tf_op jit(solution)/shard_map/ppermute | solution.py:712
  175.8 2.8 collective-permute-start.13
  179.3 5.5 %collective-permute-done.12 = bf16[512,256]{1,0:T(8,128)(2,1)S(1)} collective-permute-done((bf16[512,256]{1,0:T(8,128)(2,1)}, bf16[512,256]{1,0:T(8,128)(2,1)S(1)}, u32[]{:S(2)}, u32[]{:S(2)}) %collective-permute-start.12) | collective-permute-done | bytes 262176 | tf_op jit(solution)/shard_map/ppermute | solution.py:712
  185.6 4.8 collective-permute-done.13
  191.1 5.1 collective-permute-done.14
  196.9 4.8 collective-permute-done.15
  207.1 12.9 %feed.1 = (bf16[4,1024,256]{2,1,0:T(8,128)(2,1)S(1)}, bf16[4,1024,256]{2,1,0:T(8,128)(2,1)S(1)}, bf16[4,1024,256]{2,1,0:T(8,128)(2,1)S(1)}) custom-call(bf16[4,1024,256]{2,1,0:T(8,128)(2,1)} %bitcast_dynamic-update-slice_fusion.2.rows, bf16[1024,1024]{1,0:T(8,128)(2,1)S(1)} %copy-done.40, bf16[1024,1024]{1,0:T(8,128)(2,1)S(1)} %bitcast.218, ...), custom_call_target="tpu_custom_call" | custom-call | flops 6442450944 | bytes 16777216 | tf_op jit(solution)/shard_map/feed/pallas_call | solution.py:510
  223.1 3.0 collective-permute-start.17
  226.1 15.8 %feed_rest.1 = (bf16[1024,1024]{1,0:T(8,128)(2,1)S(1)}, bf16[1024,1024]{1,0:T(8,128)(2,1)}, f32[1024,1]{1,0:T(8,128)S(1)}, bf16[4,4,256,256]{3,2,1,0:T(8,128)(2,1)}) custom-call(s32[2]{0:T(128)S(1)} %pad_add_fusion.1.spot, bf16[4,1024,256]{2,1,0:T(8,128)(2,1)} %bitcast_dynamic-update-slice_fusion.2.rows, ...), custom_call_target="tpu_custom_call" | custom-call | flops 6442450944 | bytes 16777216 | tf_op jit(solution)/shard_map/feed_rest/pallas_call | solution.py:584
  245.9 8.5 %collective-permute-done.18 = bf16[512,256]{1,0:T(8,128)(2,1)S(1)} collective-permute-done((bf16[512,256]{1,0:T(8,128)(2,1)S(1)}, bf16[512,256]{1,0:T(8,128)(2,1)S(1)}, u32[]{:S(2)}, u32[]{:S(2)}) %collective-permute-start.18) | collective-permute-done | bytes 262176 | tf_op jit(solution)/shard_map/ppermute | solution.py:733
  255.7 3.3 collective-permute-start.20
  258.9 4.4 collective-permute-done.19
  263.3 3.9 collective-permute-done.20
  271.3 3.3 collective-permute-done.21
  275.6 2.2 multiply_reduce_fusion
  277.8 2.3 fusion.32
  286.7 9.0 %all-to-all-start.5 = ((bf16[32,64,128]{2,1,0:T(8,128)(2,1)}), bf16[32,64,128]{2,1,0:T(8,128)(2,1)}, u32[]{:S(2)}, u32[]{:S(2)}) async-start(bf16[32,64,128]{2,1,0:T(8,128)(2,1)} %bitcast.229), calls=%async_computation.5 | async-start | bytes 1048576 | tf_op jit(solution)/shard_map/all_to_all | solution.py:979
  298.4 12.7 %all-to-all-done.5.grad_out = bf16[32,64,128]{2,1,0:T(8,128)(2,1)} async-done(((bf16[32,64,128]{2,1,0:T(8,128)(2,1)}), bf16[32,64,128]{2,1,0:T(8,128)(2,1)}, u32[]{:S(2)}, u32[]{:S(2)}) %all-to-all-start.5) | async-done | bytes 524320 | tf_op jit(solution)/shard_map/all_to_all | solution.py:979
  311.1 4.4 all-to-all-start.6
  316.3 57.2 %attend_backward.1 = (bf16[8,64,512]{2,1,0:T(8,128)(2,1)}, bf16[8,64,1024]{2,1,0:T(8,128)(2,1)}, bf16[8,64,1024]{2,1,0:T(8,128)(2,1)}, f32[2,16,64]{2,1,0:T(8,128)}) custom-call(s32[5]{0:T(128)} %copy-done.44, bf16[8,64,512]{2,1,0:T(8,128)(2,1)} %copy-done.32, bf16[8,64,1024]{2,1,0:T(8,128)(2,1)} %copy-done.25, bf16[8,64,1024]{2,1,0:T(8,128)(2,1)} %copy-done.24, ...), custom_call_target="tpu_custom_call" | custom-call | flops 42949672960 | bytes 8388608 | tf_op jit(solution)/shard_map/attend_backward/pallas_call | solution.py:333
  373.5 5.0 collective-permute-start.22
  385.3 3.9 all-to-all-start.7
  389.2 2.8 reduce_sum.173
  394.1 7.2 %reduce-scatter.2.cloned.1.call-done.out = bf16[256,1024]{1,0:T(8,128)(2,1)} async-done(((bf16[1024,1024]{1,0:T(8,128)(2,1)}), bf16[256,1024]{1,0:T(8,128)(2,1)}) %reduce-scatter.2.cloned.1.call-update) | async-done | bytes 524304 | tf_op jit(solution)/shard_map/reduce_scatter | solution.py:992
  401.3 6.8 %all-to-all-done.7.came = bf16[8,64,1664]{2,1,0:T(8,128)(2,1)S(1)} async-done(((bf16[8,64,1664]{2,1,0:T(8,128)(2,1)}), bf16[8,64,1664]{2,1,0:T(8,128)(2,1)S(1)}, u32[]{:S(2)}, u32[]{:S(2)}) %all-to-all-start.7) | async-done | bytes 1703968 | tf_op jit(solution)/shard_map/all_to_all | solution.py:1013
  410.7 6.0 %rest_halves.1 = (bf16[768,1024]{1,0:T(8,128)(2,1)S(1)}, bf16[512,1024]{1,0:T(8,128)(2,1)S(1)}, bf16[512,1024]{1,0:T(8,128)(2,1)}) custom-call(s32[2]{0:T(128)S(1)} %pad_add_fusion.1.spot, bf16[8,64,1664]{2,1,0:T(8,128)(2,1)S(1)} %all-to-all-done.7.came, bf16[1024,1024]{1,0:T(8,128)(2,1)S(1)} %copy-done.16, bf16[256,1024]{1,0:T(8,128)(2,1)S(1)} %copy-done.29), custom_call_target="tpu_custom_call" | custom-call | tf_op jit(solution)/shard_map/rest_halves/pallas_call | solution.py:641
  418.9 3.5 collective-permute-start.23
  422.3 2.6 copy.198.weight
  430.7 5.3 unproject.1
  437.3 2.9 add_convert_fusion
  440.2 4.4 all-to-all-start.8
  448.2 2.2 collective-permute-start.24
  455.7 2.8 collective-permute-done.24
  458.5 5.8 %collective-permute-done.25 = bf16[128,1024]{1,0:T(8,128)(2,1)} collective-permute-done((bf16[128,1024]{1,0:T(8,128)(2,1)}, bf16[128,1024]{1,0:T(8,128)(2,1)}, u32[]{:S(2)}, u32[]{:S(2)}) %collective-permute-start.25) | collective-permute-done | bytes 262176 | tf_op jit(solution)/shard_map/ppermute | solution.py:734
  466.7 3.0 collective-permute-start.27
  471.2 3.3 all-to-all-start.9
  476.0 5.9 %all-to-all-done.9 = f32[4,1,8448]{2,1,0:T(1,128)S(1)} async-done(((f32[4,1,8448]{2,1,0:T(1,128)}), f32[4,1,8448]{2,1,0:T(1,128)S(1)}, u32[]{:S(2)}, u32[]{:S(2)}) %all-to-all-start.9) | async-done | bytes 135200 | tf_op jit(solution)/shard_map/all_to_all | solution.py:1066
  483.1 3.5 all-to-all-start.10
  488.2 4.2 convert_element_type.285
  492.4 2.5 convert_element_type.286
  495.4 2.2 fusion.4
  505.2 7.7 %collective-permute-done.29.down = bf16[128,1024]{1,0:T(8,128)(2,1)S(1)} collective-permute-done((bf16[128,1024]{1,0:T(8,128)(2,1)}, bf16[128,1024]{1,0:T(8,128)(2,1)S(1)}, u32[]{:S(2)}, u32[]{:S(2)}) %collective-permute-start.29) | collective-permute-done | bytes 262176 | tf_op jit(solution)/shard_map/ppermute | solution.py:734
  514.0 5.1 all-to-all-start.11
  519.2 2.4 convolution_bitcast_fusion
  521.6 3.0 copy.210
  532.0 3.5 rest_whole.1
  (347 shorter events, 146.1 us)
Async XLA Ops:
  7.2 86.5 %copy-start = (bf16[1024,512]{1,0:T(8,128)(2,1)S(1)}, bf16[1024,512]{1,0:T(8,128)(2,1)}, u32[]{:S(2)}) copy-start(bf16[1024,512]{1,0:T(8,128)(2,1)} %param.36) | copy-start | bytes 3145732
  9.4 7.0 %copy-start.73 = (bf16[256]{0:T(256)(128)(2,1)S(1)}, bf16[256]{0:T(256)(128)(2,1)}, u32[]{:S(2)}) copy-start(bf16[256]{0:T(256)(128)(2,1)} %param.28) | copy-start | bytes 1540
  9.4 7.0 %copy-start.74 = (bf16[256]{0:T(256)(128)(2,1)S(1)}, bf16[256]{0:T(256)(128)(2,1)}, u32[]{:S(2)}) copy-start(bf16[256]{0:T(256)(128)(2,1)} %param.34) | copy-start | bytes 1540
  9.4 11.0 %copy-start.67 = (bf16[4,128]{1,0:T(4,128)(2,1)S(1)}, bf16[4,128]{1,0:T(4,128)(2,1)}, u32[]{:S(2)}) copy-start(bf16[4,128]{1,0:T(4,128)(2,1)} %param.26) | copy-start | bytes 3076
  9.4 11.2 %copy-start.65 = (s32[1024]{0:T(1024)S(1)}, s32[1024]{0:T(1024)}, u32[]{:S(2)}) copy-start(s32[1024]{0:T(1024)} %param.21) | copy-start | bytes 12292
  12.2 10.6 %collective-permute-start = (bf16[128,1024]{1,0:T(8,128)(2,1)}, bf16[128,1024]{1,0:T(8,128)(2,1)}, u32[]{:S(2)}, u32[]{:S(2)}) collective-permute-start(bf16[128,1024]{1,0:T(8,128)(2,1)} %get-tuple-element.338), channel_id=1, source_target_pairs={{0,1},{1,2},{2,3},{3,0},{4,5},{5,6},{6,7},{7,4},{8,9},{9,10},{10,1... | collective-permute-start | bytes 786440 | tf_op jit(solution)/shard_map/ppermute | solution.py:712
  14.3 13.5 %collective-permute-start.2 = (bf16[128,1024]{1,0:T(8,128)(2,1)}, bf16[128,1024]{1,0:T(8,128)(2,1)}, u32[]{:S(2)}, u32[]{:S(2)}) collective-permute-start(bf16[128,1024]{1,0:T(8,128)(2,1)} %get-tuple-element.337), channel_id=1, source_target_pairs={{0,3},{1,0},{2,1},{3,2},{4,7},{5,4},{6,5},{7,6},{8,11},{9,8},{10,9... | collective-permute-start | bytes 786440 | tf_op jit(solution)/shard_map/ppermute | solution.py:713
  17.1 14.1 %all-to-all-start = ((bf16[4,6,256]{2,1,0:T(8,128)(2,1)}), bf16[4,6,256]{2,1,0:T(8,128)(2,1)S(1)}, u32[]{:S(2)}, u32[]{:S(2)}) async-start(bf16[4,6,256]{2,1,0:T(8,128)(2,1)} %broadcast_in_dim.123), calls=%async_computation | async-start | bytes 32768 | tf_op jit(solution)/shard_map/all_to_all | solution.py:691
  22.8 16.6 %collective-permute-start.1 = (bf16[128,1024]{1,0:T(8,128)(2,1)}, bf16[128,1024]{1,0:T(8,128)(2,1)}, u32[]{:S(2)}, u32[]{:S(2)}) collective-permute-start(bf16[128,1024]{1,0:T(8,128)(2,1)} %collective-permute-done), channel_id=1, source_target_pairs={{0,1},{1,2},{2,3},{3,0},{4,5},{5,6},{6,7},{7,4},{8,9},{9,10},{10,1... | collective-permute-start | bytes 786440 | tf_op jit(solution)/shard_map/ppermute | solution.py:712
  27.9 12.7 %collective-permute-start.3 = (bf16[128,1024]{1,0:T(8,128)(2,1)}, bf16[128,1024]{1,0:T(8,128)(2,1)}, u32[]{:S(2)}, u32[]{:S(2)}) collective-permute-start(bf16[128,1024]{1,0:T(8,128)(2,1)} %collective-permute-done.2), channel_id=1, source_target_pairs={{0,3},{1,0},{2,1},{3,2},{4,7},{5,4},{6,5},{7,6},{8,11},{9,8},{10,9... | collective-permute-start | bytes 786440 | tf_op jit(solution)/shard_map/ppermute | solution.py:713
  32.6 16.3 %all-to-all-start.1 = ((s32[8,4,128]{2,1,0:T(4,128)}), s32[8,4,128]{2,1,0:T(4,128)}, u32[]{:S(2)}, u32[]{:S(2)}) async-start(s32[8,4,128]{2,1,0:T(4,128)} %broadcast_in_dim_broadcast_in_dim_broadcast_in_dim.2), calls=%async_computation.1 | async-start | bytes 32768 | tf_op jit(solution)/shard_map/all_to_all | solution.py:691
  40.6 9.5 %collective-permute-start.4 = (bf16[128,1024]{1,0:T(8,128)(2,1)}, bf16[128,1024]{1,0:T(8,128)(2,1)}, u32[]{:S(2)}, u32[]{:S(2)}) collective-permute-start(bf16[128,1024]{1,0:T(8,128)(2,1)} %collective-permute-done.1), channel_id=1, source_target_pairs={{0,1},{1,2},{2,3},{3,0},{4,5},{5,6},{6,7},{7,4},{8,9},{9,10},{10,1... | collective-permute-start | bytes 786440 | tf_op jit(solution)/shard_map/ppermute | solution.py:712
  40.6 12.4 %collective-permute-start.5 = (bf16[128,1024]{1,0:T(8,128)(2,1)}, bf16[128,1024]{1,0:T(8,128)(2,1)}, u32[]{:S(2)}, u32[]{:S(2)}) collective-permute-start(bf16[128,1024]{1,0:T(8,128)(2,1)} %collective-permute-done.3), channel_id=1, source_target_pairs={{0,3},{1,0},{2,1},{3,2},{4,7},{5,4},{6,5},{7,6},{8,11},{9,8},{10,9... | collective-permute-start | bytes 786440 | tf_op jit(solution)/shard_map/ppermute | solution.py:713
  47.7 8.6 %copy-start.4 = (bf16[1024,4,192]{0,2,1:T(8,128)(2,1)S(1)}, bf16[1024,4,192]{0,2,1:T(8,128)(2,1)}, u32[]{:S(2)}) copy-start(bf16[1024,4,192]{0,2,1:T(8,128)(2,1)} %param.25) | copy-start | bytes 4718596
  63.6 23.8 %all-to-all-start.2 = ((bf16[8,64,1536]{2,1,0:T(8,128)(2,1)}), bf16[8,64,1536]{2,1,0:T(8,128)(2,1)S(1)}, u32[]{:S(2)}, u32[]{:S(2)}) async-start(bf16[8,64,1536]{2,1,0:T(8,128)(2,1)} %copy-done.22), calls=%async_computation.2 | async-start | bytes 3145728 | tf_op jit(solution)/shard_map/all_to_all | solution.py:917
  69.8 61.9 %all-gather.2.cloned.1.call-start = ((), (), s32[]{:S(2)}) async-start(), calls=%async_computation.13 | async-start | bytes 2621440 | tf_op jit(solution)/shard_map/all_gather | solution.py:930
  70.7 5.6 %collective-permute-start.6 = (bf16[32,1024]{1,0:T(8,128)(2,1)S(1)}, bf16[32,1024]{1,0:T(8,128)(2,1)}, u32[]{:S(2)}, u32[]{:S(2)}) collective-permute-start(bf16[32,1024]{1,0:T(8,128)(2,1)S(1)} %dynamic-slice_bitcast_fusion.16), channel_id=1, source_target_pairs={{0,1},{1,2},{2,3},{3,0},{4,5},{5,6},{6,7},{7,4},{8,9},{9,10},{10,1... | collective-permute-start | bytes 196616 | tf_op jit(solution)/shard_map/ppermute | solution.py:781
  70.7 6.4 %collective-permute-start.7 = (bf16[32,1024]{1,0:T(8,128)(2,1)S(1)}, bf16[32,1024]{1,0:T(8,128)(2,1)}, u32[]{:S(2)}, u32[]{:S(2)}) collective-permute-start(bf16[32,1024]{1,0:T(8,128)(2,1)S(1)} %dynamic-slice_bitcast_fusion.16), channel_id=1, source_target_pairs={{0,2},{1,3},{2,0},{3,1},{4,6},{5,7},{6,4},{7,5},{8,10},{9,11},{10,... | collective-permute-start | bytes 196616 | tf_op jit(solution)/shard_map/ppermute | solution.py:781
  72.8 5.4 collective-permute-start.8
  78.2 15.5 %copy-start.62 = (bf16[10,1024]{1,0:T(8,128)(2,1)S(1)}, bf16[10,1024]{1,0:T(8,128)(2,1)}, u32[]{:S(2)}) copy-start(bf16[10,1024]{1,0:T(8,128)(2,1)} %param.35) | copy-start | bytes 61444
  90.2 10.7 %collective-permute-start.9 = (bf16[8,64,1024]{2,1,0:T(8,128)(2,1)}, bf16[8,64,1024]{2,1,0:T(8,128)(2,1)}, u32[]{:S(2)}, u32[]{:S(2)}) collective-permute-start(bf16[8,64,1024]{2,1,0:T(8,128)(2,1)} %slice.216), channel_id=1, source_target_pairs={{0,4},{4,0},{8,12},{12,8},{16,20},{20,16},{24,28},{28,24},{1,5},{5... | collective-permute-start | bytes 3145736 | tf_op jit(solution)/shard_map/ppermute | solution.py:748
  95.5 7.2 %copy-start.44 = (s32[5]{0:T(128)}, s32[5]{0:T(128)S(1)}, u32[]{:S(2)}) copy-start(s32[5]{0:T(128)S(1)} %pad_add_fusion.meta) | copy-start | bytes 64
  96.6 35.1 %all-to-all-start.4 = ((bf16[8,4,32,1024]{3,2,1,0:T(8,128)(2,1)}), bf16[8,4,32,1024]{3,2,1,0:T(8,128)(2,1)}, u32[]{:S(2)}, u32[]{:S(2)}) async-start(bf16[8,4,32,1024]{3,2,1,0:T(8,128)(2,1)} %broadcast_in_dim.138), calls=%async_computation.4 | async-start | bytes 4194304 | tf_op jit(solution)/shard_map/all_to_all | solution.py:920
  131.7 24.9 %all-to-all-start.3 = ((bf16[32,64,128]{2,1,0:T(8,128)(2,1)}), bf16[32,64,128]{2,1,0:T(8,128)(2,1)S(1)}, u32[]{:S(2)}, u32[]{:S(2)}) async-start(bf16[32,64,128]{2,1,0:T(8,128)(2,1)} %get-tuple-element.107), calls=%async_computation.3 | async-start | bytes 1048576 | tf_op jit(solution)/shard_map/all_to_all | solution.py:939
  141.3 244.0 %all-reduce.5.cloned.1.call-start = ((), (), s32[]{:S(2)}) async-start(), calls=%async_computation.15 | async-start | bytes 8388608 | tf_op jit(solution)/shard_map/psum | solution.py:967
  163.4 10.2 %collective-permute-start.10 = (bf16[512,256]{1,0:T(8,128)(2,1)}, bf16[512,256]{1,0:T(8,128)(2,1)}, u32[]{:S(2)}, u32[]{:S(2)}) collective-permute-start(bf16[512,256]{1,0:T(8,128)(2,1)} %get-tuple-element.336), channel_id=1, source_target_pairs={{0,1},{1,2},{2,3},{3,0},{4,5},{5,6},{6,7},{7,4},{8,9},{9,10},{10,1... | collective-permute-start | bytes 786440 | tf_op jit(solution)/shard_map/ppermute | solution.py:712
  163.4 12.3 %collective-permute-start.11 = (bf16[512,256]{1,0:T(8,128)(2,1)}, bf16[512,256]{1,0:T(8,128)(2,1)S(1)}, u32[]{:S(2)}, u32[]{:S(2)}) collective-permute-start(bf16[512,256]{1,0:T(8,128)(2,1)} %get-tuple-element.335), channel_id=1, source_target_pairs={{0,3},{1,0},{2,1},{3,2},{4,7},{5,4},{6,5},{7,6},{8,11},{9,8},{10,9... | collective-permute-start | bytes 786440 | tf_op jit(solution)/shard_map/ppermute | solution.py:713
  167.0 35.4 %copy-start.13 = (bf16[1024,1024]{1,0:T(8,128)(2,1)S(1)}, bf16[1024,1024]{1,0:T(8,128)(2,1)}, u32[]{:S(2)}) copy-start(bf16[1024,1024]{1,0:T(8,128)(2,1)} %up.1) | copy-start | bytes 6291460
  173.6 11.2 %collective-permute-start.12 = (bf16[512,256]{1,0:T(8,128)(2,1)}, bf16[512,256]{1,0:T(8,128)(2,1)S(1)}, u32[]{:S(2)}, u32[]{:S(2)}) collective-permute-start(bf16[512,256]{1,0:T(8,128)(2,1)} %collective-permute-done.10), channel_id=1, source_target_pairs={{0,1},{1,2},{2,3},{3,0},{4,5},{5,6},{6,7},{7,4},{8,9},{9,10},{10,1... | collective-permute-start | bytes 786440 | tf_op jit(solution)/shard_map/ppermute | solution.py:712
  175.8 14.6 %collective-permute-start.13 = (bf16[512,256]{1,0:T(8,128)(2,1)S(1)}, bf16[512,256]{1,0:T(8,128)(2,1)S(1)}, u32[]{:S(2)}, u32[]{:S(2)}) collective-permute-start(bf16[512,256]{1,0:T(8,128)(2,1)S(1)} %collective-permute-done.11), channel_id=1, source_target_pairs={{0,3},{1,0},{2,1},{3,2},{4,7},{5,4},{6,5},{7,6},{8,11},{9,8},{10,9... | collective-permute-start | bytes 786440 | tf_op jit(solution)/shard_map/ppermute | solution.py:713
  184.9 11.3 %collective-permute-start.14 = (bf16[512,256]{1,0:T(8,128)(2,1)S(1)}, bf16[512,256]{1,0:T(8,128)(2,1)S(1)}, u32[]{:S(2)}, u32[]{:S(2)}) collective-permute-start(bf16[512,256]{1,0:T(8,128)(2,1)S(1)} %collective-permute-done.12), channel_id=1, source_target_pairs={{0,1},{1,2},{2,3},{3,0},{4,5},{5,6},{6,7},{7,4},{8,9},{9,10},{10,1... | collective-permute-start | bytes 786440 | tf_op jit(solution)/shard_map/ppermute | solution.py:712
  190.4 11.3 %collective-permute-start.15 = (bf16[512,256]{1,0:T(8,128)(2,1)S(1)}, bf16[512,256]{1,0:T(8,128)(2,1)S(1)}, u32[]{:S(2)}, u32[]{:S(2)}) collective-permute-start(bf16[512,256]{1,0:T(8,128)(2,1)S(1)} %collective-permute-done.13), channel_id=1, source_target_pairs={{0,3},{1,0},{2,1},{3,2},{4,7},{5,4},{6,5},{7,6},{8,11},{9,8},{10,9... | collective-permute-start | bytes 786440 | tf_op jit(solution)/shard_map/ppermute | solution.py:713
  222.7 21.3 %collective-permute-start.16 = (bf16[512,256]{1,0:T(8,128)(2,1)S(1)}, bf16[512,256]{1,0:T(8,128)(2,1)S(1)}, u32[]{:S(2)}, u32[]{:S(2)}) collective-permute-start(bf16[512,256]{1,0:T(8,128)(2,1)S(1)} %get-tuple-element.334), channel_id=1, source_target_pairs={{0,1},{1,2},{2,3},{3,0},{4,5},{5,6},{6,7},{7,4},{8,9},{9,10},{10,1... | collective-permute-start | bytes 786440 | tf_op jit(solution)/shard_map/ppermute | solution.py:733
  223.1 20.9 %collective-permute-start.17 = (bf16[512,256]{1,0:T(8,128)(2,1)S(1)}, bf16[512,256]{1,0:T(8,128)(2,1)S(1)}, u32[]{:S(2)}, u32[]{:S(2)}) collective-permute-start(bf16[512,256]{1,0:T(8,128)(2,1)S(1)} %get-tuple-element.333), channel_id=1, source_target_pairs={{0,3},{1,0},{2,1},{3,2},{4,7},{5,4},{6,5},{7,6},{8,11},{9,8},{10,9... | collective-permute-start | bytes 786440 | tf_op jit(solution)/shard_map/ppermute | solution.py:734
  245.8 8.6 %collective-permute-start.18 = (bf16[512,256]{1,0:T(8,128)(2,1)S(1)}, bf16[512,256]{1,0:T(8,128)(2,1)S(1)}, u32[]{:S(2)}, u32[]{:S(2)}) collective-permute-start(bf16[512,256]{1,0:T(8,128)(2,1)S(1)} %fusion.11), channel_id=1, source_target_pairs={{0,1},{1,2},{2,3},{3,0},{4,5},{5,6},{6,7},{7,4},{8,9},{9,10},{10,1... | collective-permute-start | bytes 786440 | tf_op jit(solution)/shard_map/ppermute | solution.py:733
  255.6 7.8 %collective-permute-start.19 = (bf16[512,256]{1,0:T(8,128)(2,1)S(1)}, bf16[512,256]{1,0:T(8,128)(2,1)S(1)}, u32[]{:S(2)}, u32[]{:S(2)}) collective-permute-start(bf16[512,256]{1,0:T(8,128)(2,1)S(1)} %get-tuple-element.331), channel_id=1, source_target_pairs={{0,1},{1,2},{2,3},{3,0},{4,5},{5,6},{6,7},{7,4},{8,9},{9,10},{10,1... | collective-permute-start | bytes 786440 | tf_op jit(solution)/shard_map/ppermute | solution.py:733
  255.7 11.6 %collective-permute-start.20 = (bf16[512,256]{1,0:T(8,128)(2,1)S(1)}, bf16[512,256]{1,0:T(8,128)(2,1)}, u32[]{:S(2)}, u32[]{:S(2)}) collective-permute-start(bf16[512,256]{1,0:T(8,128)(2,1)S(1)} %get-tuple-element.332), channel_id=1, source_target_pairs={{0,3},{1,0},{2,1},{3,2},{4,7},{5,4},{6,5},{7,6},{8,11},{9,8},{10,9... | collective-permute-start | bytes 786440 | tf_op jit(solution)/shard_map/ppermute | solution.py:734
  269.3 5.3 collective-permute-start.21
  282.7 13.7 %copy-start.9 = (f32[1024,256]{1,0:T(8,128)S(1)}, f32[1024,256]{1,0:T(8,128)}, u32[]{:S(2)}) copy-start(f32[1024,256]{1,0:T(8,128)} %copy-done.8) | copy-start | bytes 3145732
  282.7 13.7 %copy-start.52 = (bf16[4,2,4,64,128]{4,1,3,0,2:T(2,128)(2,1)S(1)}, bf16[4,2,4,64,128]{4,1,3,0,2:T(2,128)(2,1)}, u32[]{:S(2)}) copy-start(bf16[4,2,4,64,128]{4,1,3,0,2:T(2,128)(2,1)} %copy-done.51) | copy-start | bytes 1572868
  286.7 24.4 %all-to-all-start.5 = ((bf16[32,64,128]{2,1,0:T(8,128)(2,1)}), bf16[32,64,128]{2,1,0:T(8,128)(2,1)}, u32[]{:S(2)}, u32[]{:S(2)}) async-start(bf16[32,64,128]{2,1,0:T(8,128)(2,1)} %bitcast.229), calls=%async_computation.5 | async-start | bytes 1048576 | tf_op jit(solution)/shard_map/all_to_all | solution.py:979
  311.1 74.2 %all-to-all-start.6 = ((bf16[4,4,256,256]{3,2,1,0:T(8,128)(2,1)}), bf16[4,4,256,256]{3,2,1,0:T(8,128)(2,1)}, u32[]{:S(2)}, u32[]{:S(2)}) async-start(bf16[4,4,256,256]{3,2,1,0:T(8,128)(2,1)} %get-tuple-element.133), calls=%async_computation.6 | async-start | bytes 4194304 | tf_op jit(solution)/shard_map/all_to_all | solution.py:991
  315.6 85.7 %reduce-scatter.2.cloned.1.call-start = ((), (), s32[]{:S(2)}) async-start(), calls=%async_computation.14 | async-start | bytes 2621440 | tf_op jit(solution)/shard_map/reduce_scatter | solution.py:992
  373.5 10.4 %copy-start.58 = (bf16[8,64,512]{2,1,0:T(8,128)(2,1)S(1)}, bf16[8,64,512]{2,1,0:T(8,128)(2,1)}, u32[]{:S(2)}) copy-start(bf16[8,64,512]{2,1,0:T(8,128)(2,1)} %get-tuple-element.129) | copy-start | bytes 1572868
  373.5 7.5 %collective-permute-start.22 = (bf16[8,64,1024]{2,1,0:T(8,128)(2,1)}, bf16[8,64,1024]{2,1,0:T(8,128)(2,1)S(1)}, u32[]{:S(2)}, u32[]{:S(2)}) collective-permute-start(bf16[8,64,1024]{2,1,0:T(8,128)(2,1)} %get-tuple-element.131), channel_id=1, source_target_pairs={{0,4},{4,0},{8,12},{12,8},{16,20},{20,16},{24,28},{28,24},{1,5},{5... | collective-permute-start | bytes 3145736 | tf_op jit(solution)/shard_map/ppermute | solution.py:748
  385.3 22.8 %all-to-all-start.7 = ((bf16[8,64,1664]{2,1,0:T(8,128)(2,1)}), bf16[8,64,1664]{2,1,0:T(8,128)(2,1)S(1)}, u32[]{:S(2)}, u32[]{:S(2)}) async-start(bf16[8,64,1664]{2,1,0:T(8,128)(2,1)} %pad_maximum_fusion), calls=%async_computation.7 | async-start | bytes 3407872 | tf_op jit(solution)/shard_map/all_to_all | solution.py:1013
  418.9 18.4 %collective-permute-start.23 = (bf16[512,1024]{1,0:T(8,128)(2,1)}, bf16[512,1024]{1,0:T(8,128)(2,1)}, u32[]{:S(2)}, u32[]{:S(2)}) collective-permute-start(bf16[512,1024]{1,0:T(8,128)(2,1)} %get-tuple-element.147), channel_id=1, source_target_pairs={{0,4},{4,0},{8,12},{12,8},{16,20},{20,16},{24,28},{28,24},{1,5},{5... | collective-permute-start | bytes 3145736 | tf_op jit(solution)/shard_map/ppermute | solution.py:748
  440.2 7.1 %copy-start.12 = (bf16[1024,1024]{1,0:T(8,128)(2,1)S(1)}, bf16[1024,1024]{1,0:T(8,128)(2,1)}, u32[]{:S(2)}) copy-start(bf16[1024,1024]{1,0:T(8,128)(2,1)} %copy-done.11) | copy-start | bytes 6291460
  440.2 24.1 %all-to-all-start.8 = ((bf16[4,128,1024]{2,1,0:T(8,128)(2,1)}), bf16[4,128,1024]{2,1,0:T(8,128)(2,1)}, u32[]{:S(2)}, u32[]{:S(2)}) async-start(bf16[4,128,1024]{2,1,0:T(8,128)(2,1)} %bitcast.222), calls=%async_computation.9 | async-start | bytes 2097152 | tf_op jit(solution)/shard_map/all_to_all | solution.py:763
  448.2 10.3 %collective-permute-start.24 = (bf16[128,1024]{1,0:T(8,128)(2,1)}, bf16[128,1024]{1,0:T(8,128)(2,1)}, u32[]{:S(2)}, u32[]{:S(2)}) collective-permute-start(bf16[128,1024]{1,0:T(8,128)(2,1)} %get-tuple-element.324), channel_id=1, source_target_pairs={{0,1},{1,2},{2,3},{3,0},{4,5},{5,6},{6,7},{7,4},{8,9},{9,10},{10,1... | collective-permute-start | bytes 786440 | tf_op jit(solution)/shard_map/ppermute | solution.py:733
  450.5 13.9 %collective-permute-start.25 = (bf16[128,1024]{1,0:T(8,128)(2,1)}, bf16[128,1024]{1,0:T(8,128)(2,1)}, u32[]{:S(2)}, u32[]{:S(2)}) collective-permute-start(bf16[128,1024]{1,0:T(8,128)(2,1)} %get-tuple-element.323), channel_id=1, source_target_pairs={{0,3},{1,0},{2,1},{3,2},{4,7},{5,4},{6,5},{7,6},{8,11},{9,8},{10,9... | collective-permute-start | bytes 786440 | tf_op jit(solution)/shard_map/ppermute | solution.py:734
  466.4 15.5 %collective-permute-start.26 = (bf16[128,1024]{1,0:T(8,128)(2,1)}, bf16[128,1024]{1,0:T(8,128)(2,1)S(1)}, u32[]{:S(2)}, u32[]{:S(2)}) collective-permute-start(bf16[128,1024]{1,0:T(8,128)(2,1)} %get-tuple-element.328), channel_id=1, source_target_pairs={{0,1},{1,2},{2,3},{3,0},{4,5},{5,6},{6,7},{7,4},{8,9},{9,10},{10,1... | collective-permute-start | bytes 786440 | tf_op jit(solution)/shard_map/ppermute | solution.py:733
  466.7 15.2 %collective-permute-start.27 = (bf16[128,1024]{1,0:T(8,128)(2,1)}, bf16[128,1024]{1,0:T(8,128)(2,1)S(1)}, u32[]{:S(2)}, u32[]{:S(2)}) collective-permute-start(bf16[128,1024]{1,0:T(8,128)(2,1)} %get-tuple-element.327), channel_id=1, source_target_pairs={{0,3},{1,0},{2,1},{3,2},{4,7},{5,4},{6,5},{7,6},{8,11},{9,8},{10,9... | collective-permute-start | bytes 786440 | tf_op jit(solution)/shard_map/ppermute | solution.py:734
  471.2 10.7 %all-to-all-start.9 = ((f32[4,1,8448]{2,1,0:T(1,128)}), f32[4,1,8448]{2,1,0:T(1,128)S(1)}, u32[]{:S(2)}, u32[]{:S(2)}) async-start(f32[4,1,8448]{2,1,0:T(1,128)} %broadcast_in_dim.152), calls=%async_computation.10 | async-start | bytes 270336 | tf_op jit(solution)/shard_map/all_to_all | solution.py:1066
  474.5 12.1 %copy-start.21 = (bf16[1024,256]{1,0:T(8,128)(2,1)S(1)}, bf16[1024,256]{1,0:T(8,128)(2,1)}, u32[]{:S(2)}) copy-start(bf16[1024,256]{1,0:T(8,128)(2,1)} %refs_1_.1) | copy-start | bytes 1572868
  476.0 10.8 %copy-start.76 = (bf16[256]{0:T(256)(128)(2,1)S(1)}, bf16[256]{0:T(256)(128)(2,1)}, u32[]{:S(2)}) copy-start(bf16[256]{0:T(256)(128)(2,1)} %param.23) | copy-start | bytes 1540
  483.1 29.8 %all-to-all-start.10 = ((bf16[4,128,1024]{2,1,0:T(8,128)(2,1)}), bf16[4,128,1024]{2,1,0:T(8,128)(2,1)S(1)}, u32[]{:S(2)}, u32[]{:S(2)}) async-start(bf16[4,128,1024]{2,1,0:T(8,128)(2,1)} %broadcast_in_dim.150), calls=%async_computation.11 | async-start | bytes 2097152 | tf_op jit(solution)/shard_map/all_to_all | solution.py:772
  495.4 17.6 %copy-start.57 = (f32[4,1,8448]{2,1,0:T(1,128)S(1)}, f32[4,1,8448]{2,1,0:T(1,128)}, u32[]{:S(2)}) copy-start(f32[4,1,8448]{2,1,0:T(1,128)} %copy-done.56) | copy-start | bytes 405508
  497.6 21.6 %copy-start.63 = (bf16[10,1024]{1,0:T(8,128)(2,1)S(1)}, bf16[10,1024]{1,0:T(8,128)(2,1)}, u32[]{:S(2)}) copy-start(bf16[10,1024]{1,0:T(8,128)(2,1)} %param.35) | copy-start | bytes 61444
  497.6 7.7 %collective-permute-start.28 = (bf16[128,1024]{1,0:T(8,128)(2,1)}, bf16[128,1024]{1,0:T(8,128)(2,1)S(1)}, u32[]{:S(2)}, u32[]{:S(2)}) collective-permute-start(bf16[128,1024]{1,0:T(8,128)(2,1)} %get-tuple-element.326), channel_id=1, source_target_pairs={{0,1},{1,2},{2,3},{3,0},{4,5},{5,6},{6,7},{7,4},{8,9},{9,10},{10,1... | collective-permute-start | bytes 786440 | tf_op jit(solution)/shard_map/ppermute | solution.py:733
  499.3 13.6 %collective-permute-start.29 = (bf16[128,1024]{1,0:T(8,128)(2,1)}, bf16[128,1024]{1,0:T(8,128)(2,1)S(1)}, u32[]{:S(2)}, u32[]{:S(2)}) collective-permute-start(bf16[128,1024]{1,0:T(8,128)(2,1)} %get-tuple-element.325), channel_id=1, source_target_pairs={{0,3},{1,0},{2,1},{3,2},{4,7},{5,4},{6,5},{7,6},{8,11},{9,8},{10,9... | collective-permute-start | bytes 786440 | tf_op jit(solution)/shard_map/ppermute | solution.py:734
  505.2 13.9 %copy-start.36 = (bf16[128,1024]{1,0:T(8,128)(2,1)}, bf16[128,1024]{1,0:T(8,128)(2,1)S(1)}, u32[]{:S(2)}) copy-start(bf16[128,1024]{1,0:T(8,128)(2,1)S(1)} %collective-permute-done.28.up) | copy-start | bytes 786436
  514.0 16.0 %all-to-all-start.11 = ((f32[8,1,3072]{2,1,0:T(1,128)}), f32[8,1,3072]{2,1,0:T(1,128)S(1)}, u32[]{:S(2)}, u32[]{:S(2)}) async-start(f32[8,1,3072]{2,1,0:T(1,128)} %broadcast_in_dim.155), calls=%async_computation.12 | async-start | bytes 196608 | tf_op jit(solution)/shard_map/all_to_all | solution.py:691
  519.1 12.9 %collective-permute-start.30 = (bf16[512,1024]{1,0:T(8,128)(2,1)S(1)}, bf16[512,1024]{1,0:T(8,128)(2,1)}, u32[]{:S(2)}, u32[]{:S(2)}) collective-permute-start(bf16[512,1024]{1,0:T(8,128)(2,1)S(1)} %bitcast.213), channel_id=1, source_target_pairs={{0,4},{4,0},{8,12},{12,8},{16,20},{20,16},{24,28},{28,24},{1,5},{5... | collective-permute-start | bytes 3145736 | tf_op jit(solution)/shard_map/ppermute | solution.py:748
  (59 other events, 159.9 us)
Sparse Core Ops, SparseCore 0:
  75.1 45.0 all-gather.1
  271.4 82.9 all-reduce.4
  357.4 43.8 reduce-scatter.1

commit v3 on v2

--- a/solution.py
+++ b/solution.py
@@ -58,48 +58,65 @@
     rank = meta[DOCS - 1]
     first = base + rank * chunk
     last = base + (count // chunk - 1) * (chunk * group) + rank * chunk + chunk - 1
-    return first, last, document_start(meta, first), document_start(meta, last)
+    return document_start(meta, first), document_start(meta, last)
 
 
 def one_row(rows, columns):
     return lax.broadcasted_iota(jnp.int32, (rows, columns), 0) == 0
 
 
-def over_keys(bounds, keys, block):
-    first, last, low, low_last = bounds
+def by_rank(meta, group, first, second, work):
+    if group != 2:
+        work(first, second)
+        return
+
+    @pl.when(meta[DOCS - 1] == 0)
+    def _():
+        work(first, second)
+
+    @pl.when(meta[DOCS - 1] == 1)
+    def _():
+        work(second, first)
+
+
+def over_keys(bounds, base, tile, group, keys, block):
+    low, low_last = bounds
 
     def step(number, _):
-        clear = (number * keys >= low_last) & ((number + 1) * keys - 1 <= first)
+        clear = number * keys >= low_last
 
         @pl.when(clear)
         def _():
-            block(number, False)
+            block(number * keys, keys, 0, False)
 
         @pl.when(jnp.logical_not(clear))
         def _():
-            block(number, True)
+            block(number * keys, keys, 0, True)
 
         return 0
 
-    lax.fori_loop(low // keys, last // keys + 1, step, 0)
-
-
-def allowed(meta, number, keys, places):
-    key = number * keys + lax.broadcasted_iota(jnp.int32, (keys, 1), 0)
+    lax.fori_loop(low // keys, base // keys, step, 0)
+    for stair in range(tile // LANES):
+        block(base + stair * LANES * group, LANES * group, stair * LANES, True)
+
+
+def allowed(meta, start, count, places):
+    key = start + lax.broadcasted_iota(jnp.int32, (count, 1), 0)
     return (key <= places) & (key >= document_start(meta, places))
 
 
 def forward_kernel(
-    meta, query, key, value, pre_key, pre_value,
+    meta, query, own, other, pre_key, pre_value,
     out_low, out_full, log_total,
-    key_rows, value_ones, accum, peak,
-    *, tile, keys, prefix, chunk, group,
+    key_rows, value_ones, accum, peak, norm,
+    *, tile, keys, prefix, chunk, group, length, width,
 ):
-    sources, size, length = key.shape
-    blocks, _, width = query.shape
+    sources, size, whole = own.shape
+    blocks = query.shape[0]
     per = width // tile
     scale = size**-0.5
     padded = pre_key.shape[1]
+    kept = slice(whole - length, whole)
 
     def extended(values, count, total):
         ones = jnp.where(one_row(PAD, count), 1.0, 0.0).astype(BF16)
@@ -111,13 +128,21 @@
         wide = values.astype(F32)
         return jnp.max(jnp.sum(wide * wide, 0, keepdims=True), 1, keepdims=True)
 
-    def prepare(source, most):
-        rows = pl.ds(pl.multiple_of(source * length, length), length)
-        key_rows[rows, :] = extended(key[source], length, LANES).astype(F32).T.astype(BF16)
-        value_ones[:, rows] = extended(value[source], length, size + PAD)
-        return jnp.maximum(most, longest(key[source]))
-
-    most = jnp.sqrt(lax.fori_loop(0, sources, prepare, longest(pre_key[...])))
+    norm[...] = jnp.broadcast_to(longest(pre_key[...]), norm.shape)
+
+    def fill(key, value):
+        def prepare(source, _):
+            rows = pl.ds(pl.multiple_of(source * length, length), length)
+            found = key[source, :, kept]
+            key_rows[rows, :] = extended(found, length, LANES).astype(F32).T.astype(BF16)
+            value_ones[:, rows] = extended(value[source, :, kept], length, size + PAD)
+            norm[...] = jnp.maximum(norm[...], longest(found))
+            return 0
+
+        lax.fori_loop(0, sources, prepare, 0)
+
+    by_rank(meta, group, own, other, fill)
+    most = jnp.sqrt(norm[0:1, 0:1])
     pre_key_ones = extended(pre_key[...], padded, LANES)
     pre_value_ones = extended(pre_value[...], padded, size + PAD)
     pre_row = lax.broadcasted_iota(jnp.int32, (padded, tile), 0)
@@ -144,14 +169,14 @@
         weights = jnp.where(pre_row < prefix, jnp.exp(contract(pre_key_ones, shifted, 0, 0)), 0.0)
         accum[...] = contract(pre_value_ones, weights.astype(BF16), 1, 0)
 
-        def block(number, masked):
-            rows = pl.ds(pl.multiple_of(number * keys, keys), keys)
-            weights = jnp.exp(contract(key_rows[rows, :], shifted, 1, 0))
+        def block(start, count, lane, masked):
+            rows = pl.ds(pl.multiple_of(start, LANES), count)
+            weights = jnp.exp(contract(key_rows[rows, :], shifted[:, lane:], 1, 0))
             if masked:
-                weights = jnp.where(allowed(meta, number, keys, places), weights, 0.0)
-            accum[...] += contract(value_ones[:, rows], weights.astype(BF16), 1, 0)
-
-        over_keys(bounds, keys, block)
+                weights = jnp.where(allowed(meta, start, count, places[:, lane:]), weights, 0.0)
+            accum[:, lane:] += contract(value_ones[:, rows], weights.astype(BF16), 1, 0)
+
+        over_keys(bounds, base, tile, group, keys, block)
         peak[...] = limit
 
         @pl.when(jnp.min(accum[size : size + 1, :]) < WEAK)
@@ -169,16 +194,14 @@
             accum[...] = jnp.zeros(accum.shape, F32)
             fold(contract(pre_key[...], plain, 0, 0), pre_row < prefix, pre_value_ones)
 
-            def slow(number, masked):
+            def step(number, _):
                 rows = pl.ds(pl.multiple_of(number * keys, keys), keys)
                 scores = contract(key_rows[rows, :][:, :size], plain, 1, 0)
-                fold(scores, allowed(meta, number, keys, places), value_ones[:, rows])
-
-            def step(number, _):
-                slow(number, True)
+                mask = allowed(meta, number * keys, keys, places)
+                fold(scores, mask, value_ones[:, rows])
                 return 0
 
-            lax.fori_loop(bounds[2] // keys, bounds[1] // keys + 1, step, 0)
+            lax.fori_loop(bounds[0] // keys, (base + tile * group - 1) // keys + 1, step, 0)
 
         total = accum[size : size + 1, :]
         result = accum[:size, :] / total
@@ -192,12 +215,16 @@
     lax.fori_loop(0, blocks * per, query_tile, 0)
 
 
-def attend_forward(meta, query, key, value, pre_key, pre_value, tile, keys, prefix, chunk, group):
-    sources, size, length = key.shape
-    count = query.shape[0] * query.shape[2]
+def attend_forward(
+    meta, query, own, other, pre_key, pre_value,
+    tile, keys, prefix, chunk, group, length, width,
+):
+    sources, size, _ = own.shape
+    count = query.shape[0] * width
     return pl.pallas_call(
         functools.partial(
-            forward_kernel, tile=tile, keys=keys, prefix=prefix, chunk=chunk, group=group
+            forward_kernel, tile=tile, keys=keys, prefix=prefix, chunk=chunk, group=group,
+            length=length, width=width,
         ),
         out_shape=(
             jax.ShapeDtypeStruct((count // LANES, size, LANES), BF16),
@@ -211,11 +238,12 @@
             pltpu.VMEM((size + PAD, sources * length), BF16),
             pltpu.VMEM((size + PAD, tile), F32),
             pltpu.VMEM((1, tile), F32),
+            pltpu.VMEM((8, LANES), F32),
         ],
         compiler_params=pltpu.CompilerParams(vmem_limit_bytes=48 * 2**20),
         cost_estimate=work(count, sources * length, 2),
         name="attend_forward",
-    )(meta, query, key, value, pre_key, pre_value)
+    )(meta, query, own, other, pre_key, pre_value)
 
 
 def in_three(values):
@@ -227,13 +255,14 @@
 
 
 def backward_kernel(
-    meta, query, key, value, pre_key, pre_value, grad_out, out_full, log_total,
+    meta, query, own, other, pre_key, pre_value, grad_out, out_full, log_total,
     grad_query, grad_keep, grad_send, grad_prefix,
     key_rows, value_rows, key_columns, sums, query_sum,
-    *, tile, keys, prefix, chunk, group,
+    *, tile, keys, prefix, chunk, group, length, width,
 ):
-    sources, size, length = key.shape
-    blocks, _, width = query.shape
+    sources, size, whole = own.shape
+    blocks = query.shape[0]
+    kept = slice(whole - length, whole)
     per = width // tile
     scale = size**-0.5
     count = tile // LANES
@@ -245,15 +274,19 @@
         )
         return jnp.concatenate([values.astype(F32), ones], 0)
 
-    def prepare(source, _):
-        rows = pl.ds(pl.multiple_of(source * length, length), length)
-        key_rows[rows, :] = extended(key[source]).T.astype(BF16)
-        value_rows[rows, :] = extended(value[source]).T.astype(BF16)
-        key_columns[:, rows] = key[source]
-        sums[rows, :] = jnp.zeros((length, LANES), F32)
-        return 0
-
-    lax.fori_loop(0, sources, prepare, 0)
+    def fill(key, value):
+        def prepare(source, _):
+            rows = pl.ds(pl.multiple_of(source * length, length), length)
+            found = key[source, :, kept]
+            key_rows[rows, :] = extended(found).T.astype(BF16)
+            value_rows[rows, :] = extended(value[source, :, kept]).T.astype(BF16)
+            key_columns[:, rows] = found
+            sums[rows, :] = jnp.zeros((length, LANES), F32)
+            return 0
+
+        lax.fori_loop(0, sources, prepare, 0)
+
+    by_rank(meta, group, own, other, fill)
     grad_prefix[...] = jnp.zeros(grad_prefix.shape, F32)
     pre_row = lax.broadcasted_iota(jnp.int32, (pre_key.shape[0], tile), 0)
 
@@ -285,17 +318,19 @@
         grad_prefix[1] += contract(probs.astype(BF16), grad, 1, 1)
         query_sum[...] = contract(pre_key[...], slope, 0, 0)
 
-        def block(number, masked):
-            rows = pl.ds(pl.multiple_of(number * keys, keys), keys)
-            probs = jnp.exp(contract(key_rows[rows, :], scaled_less, 1, 0))
+        def block(start, count, lane, masked):
+            rows = pl.ds(pl.multiple_of(start, LANES), count)
+            probs = jnp.exp(contract(key_rows[rows, :], scaled_less[:, lane:], 1, 0))
             if masked:
-                probs = jnp.where(allowed(meta, number, keys, places), probs, 0.0)
-            slope = (probs * contract(value_rows[rows, :], grad_less, 1, 0)).astype(BF16)
+                probs = jnp.where(allowed(meta, start, count, places[:, lane:]), probs, 0.0)
+            slope = probs * contract(value_rows[rows, :], grad_less[:, lane:], 1, 0)
+            slope = slope.astype(BF16)
             both = jnp.concatenate([probs.astype(BF16), slope], 1)
-            sums[rows, :] += contract(both, pair, 1, 1)
-            query_sum[...] += contract(key_columns[:, rows], slope, 1, 0)
-
-        over_keys(bounds, keys, block)
+            ends = jnp.concatenate([pair[:, lane:tile], pair[:, tile + lane :]], 1) if lane else pair
+            sums[rows, :] += contract(both, ends, 1, 1)
+            query_sum[:, lane:] += contract(key_columns[:, rows], slope, 1, 0)
+
+        over_keys(bounds, base, tile, group, keys, block)
         grad_query[source, :, columns] = (query_sum[...] * scale).astype(BF16)
         return 0
 
@@ -326,18 +361,20 @@
 
 
 def attend_backward(
-    meta, query, key, value, pre_key, pre_value, grad_out, out_full, log_total,
-    tile, keys, prefix, chunk, group,
+    meta, query, own, other, pre_key, pre_value, grad_out, out_full, log_total,
+    tile, keys, prefix, chunk, group, length, width,
 ):
-    sources, size, length = key.shape
+    sources, size, _ = own.shape
+    pair = jax.ShapeDtypeStruct((sources, size, length), BF16)
     return pl.pallas_call(
         functools.partial(
-            backward_kernel, tile=tile, keys=keys, prefix=prefix, chunk=chunk, group=group
+            backward_kernel, tile=tile, keys=keys, prefix=prefix, chunk=chunk, group=group,
+            length=length, width=width,
         ),
         out_shape=(
-            jax.ShapeDtypeStruct(query.shape, BF16),
-            jax.ShapeDtypeStruct(key.shape, BF16),
-            jax.ShapeDtypeStruct(key.shape, BF16),
+            jax.ShapeDtypeStruct((query.shape[0], size, width), BF16),
+            pair,
+            pair,
             jax.ShapeDtypeStruct((2,) + pre_key.shape, F32),
         ),
         in_specs=[SM] + [VM] * 8,
@@ -350,9 +387,9 @@
             pltpu.VMEM((size, tile), F32),
         ],
         compiler_params=pltpu.CompilerParams(vmem_limit_bytes=56 * 2**20),
-        cost_estimate=work(query.shape[0] * query.shape[2], sources * length, 5),
+        cost_estimate=work(query.shape[0] * width, sources * length, 5),
         name="attend_backward",
-    )(meta, query, key, value, pre_key, pre_value, grad_out, out_full, log_total)
+    )(meta, query, own, other, pre_key, pre_value, grad_out, out_full, log_total)
 
 
 def turn_kernel(*refs):
@@ -367,7 +404,7 @@
         out_shape=tuple(jax.ShapeDtypeStruct(a.shape[::-1], BF16) for a in arrays),
         in_specs=[VM] * len(arrays),
         out_specs=(VM,) * len(arrays),
-        compiler_params=pltpu.CompilerParams(vmem_limit_bytes=32 * 2**20),
+        compiler_params=pltpu.CompilerParams(vmem_limit_bytes=8 * 2**20),
         name="turned",
     )(*arrays)
 
@@ -409,22 +446,33 @@
         ),
         in_specs=[VM] * 4,
         out_specs=(VM, VM, VM),
-        compiler_params=pltpu.CompilerParams(vmem_limit_bytes=40 * 2**20),
+        compiler_params=pltpu.CompilerParams(vmem_limit_bytes=20 * 2**20),
         name="project",
     )(rows, columns, weight, bias)
 
 
 def unproject_kernel(
-    spot, flat, weight, rows, stats, columns, own_grad,
-    part, row_sums, sums, head_sums,
-    *, step,
+    spot, came, weight, rows, stats, columns, own_grad,
+    flat, part, row_sums, sums, head_sums,
+    *, heads, size, step,
 ):
+    length = rows.shape[1]
+    half = step // 2
+    past = length // 2
     gain = columns[:, 0:1]
     sums[...] = jnp.zeros(sums.shape, F32)
     head_sums[...] = jnp.zeros(head_sums.shape, F32)
-    for piece in range(rows.shape[1] // step):
+    for piece in range(length // step):
         lanes = slice(piece * step, (piece + 1) * step)
-        grads = flat[:, lanes]
+        place = slice(piece * half, (piece + 1) * half)
+        pair = slice(past + piece * step, past + (piece + 1) * step)
+        pieces = []
+        for head in range(heads):
+            first, second = 2 * head, 2 * head + 1
+            pieces.append(jnp.concatenate([came[first, :, place], came[second, :, place]], 1))
+            pieces += [came[first, :, pair], came[second, :, pair]]
+        grads = jnp.concatenate(pieces, 0)
+        flat[:, lanes] = grads
         head_sums[...] += jnp.sum(grads.astype(F32), 1, keepdims=True)
         back = contract(weight[...], grads, 1, 0)
         part[:, lanes] = back.astype(BF16)
@@ -441,24 +489,26 @@
         sums[:, 1:2] += jnp.sum(back, 1, keepdims=True)
 
 
-def unproject(spot, flat, weight, rows, stats, columns, own_grad, step):
+def unproject(spot, came, weight, rows, stats, columns, own_grad, heads, size, step):
     width, length = rows.shape
+    mixed = 3 * heads * size
     return pl.pallas_call(
-        functools.partial(unproject_kernel, step=step),
+        functools.partial(unproject_kernel, heads=heads, size=size, step=step),
         out_shape=(
+            jax.ShapeDtypeStruct((mixed, length), BF16),
             jax.ShapeDtypeStruct((width, length), BF16),
             jax.ShapeDtypeStruct((2, length), F32),
             jax.ShapeDtypeStruct((width, 2), F32),
-            jax.ShapeDtypeStruct((flat.shape[0], 1), F32),
+            jax.ShapeDtypeStruct((mixed, 1), F32),
         ),
         in_specs=[SM] + [VM] * 6,
-        out_specs=(VM,) * 4,
-        compiler_params=pltpu.CompilerParams(vmem_limit_bytes=40 * 2**20),
+        out_specs=(VM,) * 5,
+        compiler_params=pltpu.CompilerParams(vmem_limit_bytes=20 * 2**20),
         cost_estimate=pl.CostEstimate(
-            flops=4 * flat.shape[0] * width * length, bytes_accessed=2**23, transcendentals=0
+            flops=4 * mixed * width * length, bytes_accessed=2**23, transcendentals=0
         ),
         name="unproject",
-    )(spot, flat, weight, rows, stats, columns, own_grad)
+    )(spot, came, weight, rows, stats, columns, own_grad)
 
 
 def finish_kernel(up, down, own_up, own_down, rows, gain, stats, row_sums, grad):
@@ -479,7 +529,7 @@
         out_shape=jax.ShapeDtypeStruct(rows.shape[::-1], BF16),
         in_specs=[VM] * 8,
         out_specs=VM,
-        compiler_params=pltpu.CompilerParams(vmem_limit_bytes=32 * 2**20),
+        compiler_params=pltpu.CompilerParams(vmem_limit_bytes=8 * 2**20),
         name="finish",
     )(up, down, own_up, own_down, rows, gain, stats, row_sums)
 
@@ -524,7 +574,7 @@
             whole((inner, 1)),
         ],
         out_specs=(block(inner), block(inner), block(width)),
-        compiler_params=pltpu.CompilerParams(vmem_limit_bytes=32 * 2**20),
+        compiler_params=pltpu.CompilerParams(vmem_limit_bytes=28 * 2**20),
         cost_estimate=pl.CostEstimate(
             flops=6 * blocks * width * inner * count, bytes_accessed=2**24, transcendentals=0
         ),
@@ -532,14 +582,9 @@
     )(rows, grads, up_turned, up, down, bias)
 
 
-def feed_rest_kernel(
-    spot, rows, grads, hidden, grad_pre, down_turned, middle, columns,
-    mine, other, bias, out,
-    *, square,
-):
+def feed_weights_kernel(rows, grads, hidden, grad_pre, grad_down, grad_up, bias, *, square):
     blocks, width, count = rows.shape
     inner = hidden.shape[1]
-    features = out.shape[2]
 
     def lanes(n):
         return slice(n * count, (n + 1) * count)
@@ -552,69 +597,167 @@
             turned = jnp.concatenate([second(n, tile) for n in range(blocks)], 1)
             target[:, tile] = contract(whole, turned, 1, 1).astype(BF16)
 
-    def down(target):
-        weights(target, lambda n: hidden[n], lambda n, tile: grads[tile, lanes(n)], width)
-
-    def up(target):
-        if square:
-            weights(target, lambda n: rows[n], lambda n, tile: grad_pre[n, tile], inner)
-        else:
-            weights(target, lambda n: grad_pre[n], lambda n, tile: rows[n, tile], width)
-
-    down(mine)
-    up(other)
+    weights(grad_down, lambda n: hidden[n], lambda n, tile: grads[tile, lanes(n)], width)
+    if square:
+        weights(grad_up, lambda n: rows[n], lambda n, tile: grad_pre[n, tile], inner)
+    else:
+        weights(grad_up, lambda n: grad_pre[n], lambda n, tile: rows[n, tile], width)
     bias[...] = sum(jnp.sum(grad_pre[n].astype(F32), 1, keepdims=True) for n in range(blocks))
-    for n in range(blocks):
-        result = contract(down_turned[...], hidden[n], 1, 0)
-
-        def put(values):
-            for block in range(out.shape[0]):
-                out[block, n] = values[block * features : (block + 1) * features].astype(BF16)
-
-        put(result)
-
-        @pl.when(spot[0] == n)
-        def _():
-            put(result + middle[...] + columns[:, 5:6])
-
-
-def feed_rest(spot, rows, grads, hidden, grad_pre, down_turned, middle, columns):
+
+
+def feed_weights(rows, grads, hidden, grad_pre):
     blocks, width, count = rows.shape
     inner = hidden.shape[1]
     return pl.pallas_call(
-        functools.partial(feed_rest_kernel, square=inner == width),
+        functools.partial(feed_weights_kernel, square=inner == width),
         out_shape=(
             jax.ShapeDtypeStruct((inner, width), BF16),
             jax.ShapeDtypeStruct((inner, width), BF16),
             jax.ShapeDtypeStruct((inner, 1), F32),
-            jax.ShapeDtypeStruct((blocks, blocks, width // blocks, count), BF16),
-        ),
-        in_specs=[SM] + [VM] * 7,
+        ),
+        in_specs=[VM] * 4,
+        out_specs=(VM,) * 3,
+        compiler_params=pltpu.CompilerParams(vmem_limit_bytes=14 * 2**20),
+        cost_estimate=pl.CostEstimate(
+            flops=4 * blocks * width * inner * count, bytes_accessed=2**24, transcendentals=0
+        ),
+        name="feed_weights",
+    )(rows, grads, hidden, grad_pre)
+
+
+def feed_out_kernel(spot, hidden, down_turned, middle, columns, out):
+    features = out.shape[2]
+    for n in range(hidden.shape[0]):
+        result = contract(down_turned[...], hidden[n], 1, 0)
+
+        def put(values):
+            for block in range(out.shape[0]):
+                out[block, n] = values[block * features : (block + 1) * features].astype(BF16)
+
+        put(result)
+
+        @pl.when(spot[0] == n)
+        def _():
+            put(result + middle[...] + columns[:, 5:6])
+
+
+def feed_out(spot, hidden, down_turned, middle, columns):
+    blocks, inner, count = hidden.shape
+    width = middle.shape[0]
+    return pl.pallas_call(
+        feed_out_kernel,
+        out_shape=jax.ShapeDtypeStruct((blocks, blocks, width // blocks, count), BF16),
+        in_specs=[SM] + [VM] * 4,
+        out_specs=VM,
+        compiler_params=pltpu.CompilerParams(vmem_limit_bytes=8 * 2**20),
+        cost_estimate=pl.CostEstimate(
+            flops=2 * blocks * width * inner * count, bytes_accessed=2**23, transcendentals=0
+        ),
+        name="feed_out",
+    )(spot, hidden, down_turned, middle, columns)
+
+
+def enter_kernel(
+    spot, came, weight, tokens, columns, attended, middle, normed, inverse, low, *, heads
+):
+    size, half = came.shape[1:]
+    count = 2 * half
+    tensors = came.shape[0] // (2 * heads)
+    for block in range(tensors):
+        for head in range(heads):
+            row = (block * heads + head) * size
+            for rank in range(2):
+                attended[row : row + size, rank * half : (rank + 1) * half] = came[
+                    (2 * head + rank) * tensors + block
+                ]
+    branch = contract(attended[...], weight[...], 0, 0).T
+    lanes = pl.ds(pl.multiple_of(spot[0] * count, count), count)
+    values = tokens[:, lanes].astype(F32) + branch + columns[:, 4:5]
+    middle[...] = values
+    centered = values - jnp.mean(values, 0, keepdims=True)
+    scale = lax.rsqrt(jnp.mean(centered * centered, 0, keepdims=True) + EPS)
+    inverse[...] = scale
+    centered = centered * scale
+    normed[...] = centered
+    low[...] = (centered * columns[:, 2:3] + columns[:, 3:4]).astype(BF16)
+
+
+def enter(spot, came, weight, tokens, columns, heads):
+    width, count = tokens.shape[0], 2 * came.shape[2]
+    return pl.pallas_call(
+        functools.partial(enter_kernel, heads=heads),
+        out_shape=(
+            jax.ShapeDtypeStruct((width, count), BF16),
+            jax.ShapeDtypeStruct((width, count), F32),
+            jax.ShapeDtypeStruct((width, count), F32),
+            jax.ShapeDtypeStruct((1, count), F32),
+            jax.ShapeDtypeStruct((width, count), BF16),
+        ),
+        in_specs=[SM] + [VM] * 4,
+        out_specs=(VM,) * 5,
+        compiler_params=pltpu.CompilerParams(vmem_limit_bytes=12 * 2**20),
+        name="enter",
+    )(spot, came, weight, tokens, columns)
+
+
+def leave_kernel(
+    spot, up, down, own_up, own_down, normed, inverse, grads, weight, columns,
+    middle, branch, sums, sent,
+    *, heads,
+):
+    size, half = sent.shape[1:]
+    count = 2 * half
+    tensors = sent.shape[0] // (2 * heads)
+    total = jnp.concatenate(
+        [
+            up[...].astype(F32) + own_up[...].astype(F32),
+            down[...].astype(F32) + own_down[...].astype(F32),
+        ],
+        0,
+    )
+    scaled = total * columns[:, 2:3]
+    first = jnp.mean(scaled, 0, keepdims=True)
+    second = jnp.mean(scaled * normed[...], 0, keepdims=True)
+    lanes = pl.ds(pl.multiple_of(spot[0] * count, count), count)
+    result = grads[:, lanes].astype(F32) + inverse[...] * (
+        scaled - first - normed[...] * second
+    )
+    middle[...] = result
+    low = result.astype(BF16)
+    branch[...] = low
+    back = contract(weight[...], low, 1, 0).astype(BF16)
+    for block in range(tensors):
+        for head in range(heads):
+            row = (block * heads + head) * size
+            for rank in range(2):
+                sent[(2 * head + rank) * tensors + block] = back[
+                    row : row + size, rank * half : (rank + 1) * half
+                ]
+    sums[:, 0:1] = jnp.sum(total * normed[...], 1, keepdims=True)
+    sums[:, 1:2] = jnp.sum(total, 1, keepdims=True)
+    sums[:, 2:3] = jnp.sum(result, 1, keepdims=True)
+
+
+def leave(spot, terms, normed, inverse, grads, weight, columns, heads, size):
+    width, count = normed.shape
+    blocks = width // size
+    return pl.pallas_call(
+        functools.partial(leave_kernel, heads=heads),
+        out_shape=(
+            jax.ShapeDtypeStruct((width, count), F32),
+            jax.ShapeDtypeStruct((width, count), BF16),
+            jax.ShapeDtypeStruct((width, 3), F32),
+            jax.ShapeDtypeStruct((2 * blocks, size, count // 2), BF16),
+        ),
+        in_specs=[SM] + [VM] * 9,
         out_specs=(VM,) * 4,
-        compiler_params=pltpu.CompilerParams(vmem_limit_bytes=48 * 2**20),
-        cost_estimate=pl.CostEstimate(
-            flops=6 * blocks * width * inner * count, bytes_accessed=2**24, transcendentals=0
-        ),
-        name="feed_rest",
-    )(spot, rows, grads, hidden, grad_pre, down_turned, middle, columns)
-
-
-def rest_kernel(spot, came, full, out, flat, mine, other, *, heads, size, step):
-    width, length = full.shape
-    half = step // 2
-    past = length // 2
-    for piece in range(length // step):
-        lanes = slice(piece * step, (piece + 1) * step)
-        place = slice(piece * half, (piece + 1) * half)
-        pair = slice(past + piece * step, past + (piece + 1) * step)
-        for head in range(heads):
-            first, second = 2 * head, 2 * head + 1
-            row = 3 * size * head
-            flat[row : row + size, lanes] = jnp.concatenate(
-                [came[first, :, place], came[second, :, place]], 1
-            )
-            flat[row + size : row + 2 * size, lanes] = came[first, :, pair]
-            flat[row + 2 * size : row + 3 * size, lanes] = came[second, :, pair]
+        compiler_params=pltpu.CompilerParams(vmem_limit_bytes=12 * 2**20),
+        name="leave",
+    )(spot, *terms, normed, inverse, grads, weight, columns)
+
+
+def rest_kernel(spot, flat, full, out, mine, other):
+    width = full.shape[0]
     split = mine.shape[0]
     step = min(256, width)
     for start in range(0, width, step):
@@ -634,22 +777,19 @@
             other[:, tile] = first
 
 
-def rest_halves(spot, came, full, out, heads, size, step):
-    width, length = full.shape
-    rows = 3 * heads * size
-    half = (rows + out.shape[0]) // 2
+def rest_halves(spot, flat, full, out):
+    half = (flat.shape[0] + out.shape[0]) // 2
     return pl.pallas_call(
-        functools.partial(rest_kernel, heads=heads, size=size, step=step),
-        out_shape=(
-            jax.ShapeDtypeStruct((rows, length), BF16),
-            jax.ShapeDtypeStruct((half, width), BF16),
-            jax.ShapeDtypeStruct((half, width), BF16),
-        ),
+        rest_kernel,
+        out_shape=(jax.ShapeDtypeStruct((half, full.shape[0]), BF16),) * 2,
         in_specs=[SM] + [VM] * 3,
-        out_specs=(VM,) * 3,
-        compiler_params=pltpu.CompilerParams(vmem_limit_bytes=32 * 2**20),
+        out_specs=(VM, VM),
+        compiler_params=pltpu.CompilerParams(vmem_limit_bytes=8 * 2**20),
+        cost_estimate=pl.CostEstimate(
+            flops=2 * flat.shape[0] * full.size, bytes_accessed=2**23, transcendentals=0
+        ),
         name="rest_halves",
-    )(spot, came, full, out)
+    )(spot, flat, full, out)
 
 
 def rest_whole_kernel(spot, half, other, mixed, out):
@@ -680,9 +820,45 @@
         ),
         in_specs=[SM, VM, VM],
         out_specs=(VM, VM),
-        compiler_params=pltpu.CompilerParams(vmem_limit_bytes=32 * 2**20),
+        compiler_params=pltpu.CompilerParams(vmem_limit_bytes=8 * 2**20),
         name="rest_whole",
     )(spot, half, other)
+
+
+def prefix_kernel(total, hidden, embed, weight, grad_embed, grad_weight, grad_bias):
+    rows = hidden.shape[0]
+    pre = total[...] * (1.0 - hidden[...] * hidden[...])
+    grad_bias[...] = jnp.sum(pre, 0, keepdims=True)
+
+    def exact(first, second, dims):
+        return lax.dot_general(
+            first, second, ((dims[:1], dims[1:]), ((), ())),
+            preferred_element_type=F32, precision=HIGHEST,
+        )
+
+    wide = embed[...].astype(F32)
+    grad_weight[...] = exact(wide, pre, (0, 0))
+    grad_embed[...] = exact(pre, weight[...].astype(F32), (1, 1))[:rows]
+
+
+def prefix_back(total, hidden, embed, weight):
+    rows, width = embed.shape
+    extra = -rows % 8
+    total, hidden = [jnp.pad(a, ((0, extra), (0, 0))) for a in (total, hidden)]
+    embed = jnp.pad(embed, ((0, extra), (0, 0)))
+    grad_embed, grad_weight, grad_bias = pl.pallas_call(
+        prefix_kernel,
+        out_shape=(
+            jax.ShapeDtypeStruct((rows + extra, width), F32),
+            jax.ShapeDtypeStruct(weight.shape, F32),
+            jax.ShapeDtypeStruct((1, weight.shape[1]), F32),
+        ),
+        in_specs=[VM] * 4,
+        out_specs=(VM,) * 3,
+        compiler_params=pltpu.CompilerParams(vmem_limit_bytes=12 * 2**20),
+        name="prefix_back",
+    )(total, hidden, embed, weight)
+    return grad_embed[:rows], grad_weight, grad_bias[0]
 
 
 def spread(values, axis):
@@ -753,19 +929,31 @@
     return [[2 * chip + core for chip in range(chips)] for core in range(2)]
 
 
-def core_sum(mine, other):
-    return (mine.astype(F32) + swapped(other).astype(F32)).astype(BF16)
-
-
-def chip_parts(half):
-    chips = lax.axis_size("seq") // 2
+def chip_parts_direct(half):
+    count = lax.axis_size("seq")
+    chips = count // 2
+    chip = lax.axis_index("seq") // 2
     blocks = half.reshape(chips, half.shape[0] // chips, half.shape[1])
-    return lax.all_to_all(blocks, "seq", 0, 0, axis_index_groups=chip_groups(), tiled=True)
+    total = lax.dynamic_index_in_dim(blocks, chip, 0, keepdims=False)
+    parts = [total]
+    for step in range(1, chips):
+        block = lax.dynamic_index_in_dim(blocks, (chip + step) % chips, 0, keepdims=False)
+        parts.append(lax.ppermute(block, "seq", ring("seq", 2 * step)))
+    return parts
+
+
+def owned_direct(values, axis):
+    count, place = lax.axis_size(axis), lax.axis_index(axis)
+    parts = [lax.dynamic_index_in_dim(values, place, 0, keepdims=False)]
+    for step in range(1, count):
+        block = lax.dynamic_index_in_dim(values, (place + step) % count, 0, keepdims=False)
+        parts.append(lax.ppermute(block, axis, ring(axis, step)))
+    return parts
 
 
 def chip_copies(parts):
-    part = jnp.sum(parts.astype(F32), 0).astype(BF16)
-    return jnp.broadcast_to(part[None], parts.shape)
+    part = sum(part.astype(F32) for part in parts).astype(BF16)
+    return jnp.broadcast_to(part[None], (len(parts),) + part.shape)
 
 
 def chip_gather(copies):
@@ -849,7 +1037,7 @@
     tokens_head = rows // group
     query_width = max(tokens_head, LANES)
     forward_tile = min(512, query_width)
-    backward_tile = min(256, query_width)
+    backward_tile = min(512, query_width)
     forward_keys, backward_keys = 1024, 1024
     both = ("seq", "tensor")
     paired = group == 2 and chunk == LANES
@@ -874,11 +1062,9 @@
     columns = vectors.transpose(0, 2, 1).reshape(width, 6).astype(F32)
     out_share = w_out.reshape(seqs, heads * size // seqs, width)
     out_share = lax.dynamic_index_in_dim(out_share, place, 0, keepdims=False)
-    gain2, shift2, bias_out = [columns[:, i : i + 1] for i in (2, 3, 4)]
     core = place % 2
     spot = jnp.stack([slot, core]).astype(jnp.int32)
 
-    embed_float = prefix_embed.astype(F32)
     prefix_hidden = jnp.tanh(
         jnp.dot(prefix_embed, reparam_in, preferred_element_type=F32)
         + reparam_in_bias.astype(F32)
@@ -915,41 +1101,44 @@
         sent = jnp.concatenate([query_part, pair_part], 2)
     out_share = spread_direct(after(out_share, sent), "tensor")
     came = lax.all_to_all(sent, "seq", 0, 0, tiled=True)
-    out_share = jnp.broadcast_to(out_share[None], (seqs,) + out_share.shape)
     came, out_share = lax.optimization_barrier((came, out_share))
-    out_share = lax.all_to_all(out_share, "seq", 0, 0, tiled=True)
-    w_out_full = out_share.transpose(1, 0, 2, 3).reshape(width, width)
-    query, pair = came[:, :, :tokens_head], came[:, :, tokens_head:]
-    query = regrouped(query, query_width)
-    pair = group_gather(pair, group)
+    w_out_full = lax.all_gather(out_share, "seq")
+    w_out_full = w_out_full.transpose(1, 0, 2, 3).reshape(width, width)
     if group == 2:
-        key, value = pair[0], pair[1]
+        query, own, other = came, came, swapped(came)
     else:
-        pair = pair.transpose(1, 2, 0, 3).reshape(seqs, size, 2, rows)
-        key, value = pair[:, :, 0], pair[:, :, 1]
+        query, pair = came[:, :, :tokens_head], came[:, :, tokens_head:]
+        query = regrouped(query, query_width)
+        pair = group_gather(pair, group).transpose(1, 2, 0, 3).reshape(seqs, size, 2, rows)
+        own, other = pair[:, :, 0], pair[:, :, 1]
     full_grad = lax.all_gather(after(own_grads, full_tokens), "tensor", axis=0, tiled=True)
     out_low, out_full, log_total = attend_forward(
-        meta, query, key, value, pre_key.T, pre_value.T,
-        forward_tile, forward_keys, prefix, chunk, group,
-    )
-    out_low, full_grad, late_up, late_down = lax.optimization_barrier(
-        (out_low, full_grad, w_up, w_down)
-    )
+        meta, query, own, other, pre_key.T, pre_value.T,
+        forward_tile, forward_keys, prefix, chunk, group, rows, query_width,
+    )
+    out_low, full_grad, late_up, late_down, late_qkv = lax.optimization_barrier(
+        (out_low, full_grad, w_up, w_down, w_qkv)
+    )
+    late_flat = late_qkv.reshape(width, heads * 3 * size)
 
     came = lax.all_to_all(regrouped(out_low, chunk), both, 0, 0, tiled=True)
-    came, up_turned, down_turned, w_out_full = lax.optimization_barrier(
-        (came, late_up.T, late_down.T, w_out_full)
-    )
-    came = came.reshape(heads, group, tensors, size, chunk).transpose(2, 0, 3, 1, 4)
-    attended = came.reshape(width, own_rows)
-    branch = contract(w_out_full, attended, 0, 0)
-    own_block = lax.dynamic_slice_in_dim(full_tokens, slot * own_rows, own_rows, 1)
-    middle = own_block.astype(F32) + branch + bias_out
-    mean2 = jnp.mean(middle, 0, keepdims=True)
-    centered = middle - mean2
-    inverse2 = lax.rsqrt(jnp.mean(centered * centered, 0, keepdims=True) + EPS)
-    normed2 = centered * inverse2
-    out2 = (normed2 * gain2 + shift2).astype(BF16)
+    came, up_turned, down_turned, late_flat, w_out_full = lax.optimization_barrier(
+        (came, late_up.T, late_down.T, late_flat, w_out_full)
+    )
+    if paired:
+        attended, middle, normed2, inverse2, out2 = enter(
+            spot, came, w_out_full, full_tokens, columns, heads
+        )
+    else:
+        came = came.reshape(heads, group, tensors, size, chunk).transpose(2, 0, 3, 1, 4)
+        attended = came.reshape(width, own_rows)
+        branch = contract(w_out_full, attended, 0, 0)
+        own_block = lax.dynamic_slice_in_dim(full_tokens, slot * own_rows, own_rows, 1)
+        middle = own_block.astype(F32) + branch + columns[:, 4:5]
+        centered = middle - jnp.mean(middle, 0, keepdims=True)
+        inverse2 = lax.rsqrt(jnp.mean(centered * centered, 0, keepdims=True) + EPS)
+        normed2 = centered * inverse2
+        out2 = (normed2 * columns[:, 2:3] + columns[:, 3:4]).astype(BF16)
 
     full2 = ring_gather(out2, "tensor")
     hidden, grad_pre, part = feed(
@@ -957,35 +1146,36 @@
     )
 
     def weights_here(_):
-        return feed_rest(
-            spot, full2, full_grad, hidden, grad_pre, down_turned, middle, columns
+        return feed_weights(full2, full_grad, hidden, grad_pre)
+
+    def out_here(state):
+        return state, feed_out(spot, hidden, down_turned, middle, columns)
+
+    terms, (weights, mlp_out) = ring_terms(part, "tensor", (weights_here, out_here))
+    grad_w_down, grad_w_up, grad_b_up = weights
+    feed_sums = lax.psum((grad_w_down, grad_w_up), "seq")
+
+    if paired:
+        grad_middle, grad_branch, token_sums, sent = leave(
+            spot, terms, normed2, inverse2, full_grad, w_out_full, columns, heads, size
         )
-
-    terms, (grad_w_down, grad_w_up, grad_b_up, mlp_out) = ring_terms(
-        part, "tensor", (weights_here,)
-    )
-    feed_sums = lax.psum((grad_w_down, grad_w_up), "seq")
-    up, down, own_up, own_down = [a.astype(F32) for a in terms]
-    grad_normed2 = jnp.concatenate([up + own_up, down + own_down], 0)
-
-    scaled = grad_normed2 * gain2
-    first = jnp.mean(scaled, 0, keepdims=True)
-    second = jnp.mean(scaled * normed2, 0, keepdims=True)
-    own_grad = lax.dynamic_slice_in_dim(full_grad, slot * own_rows, own_rows, 1)
-    grad_middle = own_grad.astype(F32) + inverse2 * (scaled - first - normed2 * second)
-    grad_branch = grad_middle.astype(BF16)
-    grad_attended = contract(w_out_full, grad_branch, 1, 0).astype(BF16)
-    sent = grad_attended.reshape(tensors, heads, size, group, chunk).transpose(1, 3, 0, 2, 4)
-    came = lax.all_to_all(sent.reshape(seqs * tensors, size, chunk), both, 0, 0, tiled=True)
+    else:
+        up, down, own_up, own_down = [a.astype(F32) for a in terms]
+        grad_normed2 = jnp.concatenate([up + own_up, down + own_down], 0)
+        scaled = grad_normed2 * columns[:, 2:3]
+        first = jnp.mean(scaled, 0, keepdims=True)
+        second = jnp.mean(scaled * normed2, 0, keepdims=True)
+        own_grad = lax.dynamic_slice_in_dim(full_grad, slot * own_rows, own_rows, 1)
+        grad_middle = own_grad.astype(F32) + inverse2 * (scaled - first - normed2 * second)
+        grad_branch = grad_middle.astype(BF16)
+        token_sums = [grad_normed2 * normed2, grad_normed2, grad_middle]
+        token_sums = jnp.stack([jnp.sum(a, 1) for a in token_sums], 1)
+        sent = contract(w_out_full, grad_branch, 1, 0).astype(BF16)
+        sent = sent.reshape(tensors, heads, size, group, chunk).transpose(1, 3, 0, 2, 4)
+        sent = sent.reshape(seqs * tensors, size, chunk)
+    came = lax.all_to_all(sent, both, 0, 0, tiled=True)
     grad_out = regrouped(came, LANES)
 
-    token_sums = jnp.stack(
-        [
-            jnp.sum(grad_normed2 * normed2, 1),
-            jnp.sum(grad_normed2, 1),
-            jnp.sum(grad_middle, 1),
-        ]
-    )
     grad_w_out = contract(attended, grad_branch, 1, 1).astype(BF16)
     grad_out, mlp_out, grad_w_out = lax.optimization_barrier((grad_out, mlp_out, grad_w_out))
     output_act = lax.all_to_all(mlp_out, "tensor", 0, 0, tiled=True)
@@ -993,8 +1183,8 @@
 
     levels = log_total.reshape(-1, 1, backward_tile)
     grad_query, grad_keep, grad_send, grad_prefix = attend_backward(
-        meta, query, key, value, pre_key[:PAD], pre_value[:PAD], grad_out, out_full, levels,
-        backward_tile, backward_keys, prefix, chunk, group,
+        meta, query, own, other, pre_key[:PAD], pre_value[:PAD], grad_out, out_full, levels,
+        backward_tile, backward_keys, prefix, chunk, group, rows, query_width,
     )
     if group == 2:
         grad_share = (grad_keep.astype(F32) + swapped(grad_send).astype(F32)).astype(BF16)
@@ -1013,11 +1203,14 @@
     came = lax.all_to_all(sent, "seq", 0, 0, tiled=True)
     output_act = jnp.sum(output_act.astype(F32), 0).astype(BF16)
     output_act = output_act.transpose(0, 2, 1).reshape(rows, features)
-    came, output_act, grad_w_out = lax.optimization_barrier((came, output_act, grad_w_out))
+    out_w_down = feed_sums[0].astype(F32)
+    out_w_up = (feed_sums[1] if inner == width else feed_sums[1].T).astype(F32)
+    came, output_act, grad_w_out, out_w_down, out_w_up = lax.optimization_barrier(
+        (came, output_act, grad_w_out, out_w_down, out_w_up)
+    )
     if paired:
-        grad_flat, mine, other = rest_halves(spot, came, full1, grad_w_out, heads, size, own_rows)
-        grad_part, row_sums, sums1, head_sums = unproject(
-            spot, grad_flat, w_flat, full_tokens, stats, columns, grad_middle, own_rows
+        grad_flat, grad_part, row_sums, sums1, head_sums = unproject(
+            spot, came, late_flat, full_tokens, stats, columns, grad_middle, heads, size, own_rows
         )
     else:
         query_part = came[:, :, :tokens_head].reshape(heads, group, size, tensors, chunk)
@@ -1026,12 +1219,7 @@
         pair_part = pair_part.reshape(heads, group, size, 2 * tokens_head).transpose(0, 2, 1, 3)
         pair_part = pair_part.reshape(heads, size, 2, rows).transpose(0, 2, 1, 3)
         grad_flat = jnp.concatenate([query_part, pair_part], 1).reshape(heads * 3 * size, rows)
-        grad_w_qkv = contract(grad_flat, full1, 1, 1).astype(BF16)
-        rest = jnp.concatenate([grad_w_qkv, grad_w_out], 0)
-        halves = rest.reshape(2, rest.shape[0] // 2, width)
-        mine = lax.dynamic_index_in_dim(halves, core, 0, keepdims=False)
-        other = lax.dynamic_index_in_dim(halves, 1 - core, 0, keepdims=False)
-        back = contract(w_flat, grad_flat, 1, 0)
+        back = contract(late_flat, grad_flat, 1, 0)
         normed1 = (full_tokens.astype(F32) - stats[0]) * stats[1]
         scaled = back * columns[:, 0:1]
         row_sums = jnp.stack([jnp.sum(scaled, 0), jnp.sum(scaled * normed1, 0)])
@@ -1042,15 +1230,12 @@
         own_part = own_part + grad_middle / (own_inverse * columns[:, 0:1])
         back = lax.dynamic_update_slice_in_dim(back, own_part, slot * own_rows, 1)
         grad_part = back.astype(BF16)
-    rest_half = core_sum(mine, other)
-    grad_part, rest_half = lax.optimization_barrier((grad_part, rest_half))
-
     prefix_low = came[:, :, 3 * tokens_head : 3 * tokens_head + 2 * PAD].astype(F32)
     prefix_low = jnp.sum(prefix_low.reshape(heads, group, size, 2, PAD), 1)[..., :prefix]
     prefix_low = prefix_low.transpose(3, 0, 2, 1).reshape(prefix, heads, 2 * size).astype(BF16)
     prefix_grad = prefix_low.astype(F32)
     hidden_part = jnp.einsum("phe,ahe->pa", prefix_low, reparam_out, preferred_element_type=F32)
-    owned = jnp.concatenate([sums1.T, token_sums], 0)
+    owned = jnp.concatenate([sums1, token_sums], 1).T
     owned = owned.reshape(-1, tensors, features).transpose(1, 0, 2).reshape(tensors, -1)
     shared = jnp.concatenate([row_sums.reshape(-1), hidden_part.reshape(-1)])
     shared = jnp.broadcast_to(shared[None], (tensors, shared.shape[0]))
@@ -1059,31 +1244,40 @@
     grad_b_down = jnp.sum(out_grad.astype(F32), 0)
     head_sums = head_sums.reshape(heads, 3, size)
 
-    def rest_parts(_):
-        return chip_parts(rest_half)
-
-    def small_here(parts):
-        return chip_copies(parts), lax.all_to_all(small, "tensor", 0, 0, tiled=True)
-
-    def rest_back(state):
-        return chip_gather(state[0]), state[1]
-
-    last_terms, (rest_half, small) = ring_terms(
+    def halves_here(_):
+        if paired:
+            return rest_halves(spot, grad_flat, full1, grad_w_out)
+        grad_w_qkv = contract(grad_flat, full1, 1, 1).astype(BF16)
+        rest = jnp.concatenate([grad_w_qkv, grad_w_out], 0)
+        halves = rest.reshape(2, rest.shape[0] // 2, width)
+        mine = lax.dynamic_index_in_dim(halves, core, 0, keepdims=False)
+        other = lax.dynamic_index_in_dim(halves, 1 - core, 0, keepdims=False)
+        return mine, other
+
+    def small_here(state):
+        return state[0], swapped(state[1]), owned_direct(small, "tensor")
+
+    def parts_here(state):
+        half = (state[0].astype(F32) + state[1].astype(F32)).astype(BF16)
+        sums = sum(state[2])[0]
+        late = jnp.concatenate(
+            [
+                sums[: 5 * features],
+                grad_b_down,
+                grad_b_up.reshape(-1),
+                head_sums[:, 0].reshape(-1),
+                head_sums[:, 2].reshape(-1),
+            ]
+        )
+        return chip_parts_direct(half), sums, spread(late[None], "seq")
+
+    last_terms, (rest_parts, small, late) = ring_terms(
         grad_part.reshape(tensors, features, rows),
         "tensor",
-        (rest_parts, small_here) + (lambda state: state,) * (tensors - 4) + (rest_back,),
-    )
-    small = jnp.sum(small, 0)[0]
-    late = jnp.concatenate(
-        [
-            small[: 5 * features],
-            grad_b_down,
-            grad_b_up.reshape(-1),
-            head_sums[:, 0].reshape(-1),
-            head_sums[:, 2].reshape(-1),
-        ]
-    )
-    late = small_sum(late[None], "seq")[0]
+        (halves_here, small_here) + (lambda state: state,) * (tensors - 4) + (parts_here,),
+    )
+    rest_half = chip_gather(chip_copies(rest_parts))
+    late = jnp.sum(late, 0)[0]
     row_sums = small[5 * features : 5 * features + 2 * rows]
     hidden_grad = small[5 * features + 2 * rows :].reshape(prefix_hidden.shape)
     input_grad = finish(
@@ -1098,9 +1292,6 @@
         out_w_qkv, out_w_out = rest[:mixed_rows], rest[mixed_rows:]
     out_w_qkv = out_w_qkv.reshape(heads, 3 * size, width).transpose(2, 0, 1)
     out_w_out = out_w_out.reshape(heads, size, width)
-    out_w_down = feed_sums[0].astype(F32)
-    out_w_up = (feed_sums[1] if inner == width else feed_sums[1].T).astype(F32)
-
     out_ln1_gain, out_ln1_bias, out_ln2_gain, out_ln2_bias, out_b_out, out_b_down = [
         late[i * features : (i + 1) * features] for i in range(6)
     ]
@@ -1111,11 +1302,8 @@
 
     grad_reparam_out = jnp.einsum("pa,phe->ahe", prefix_hidden, prefix_grad, precision=HIGHEST)
     grad_reparam_out_bias = jnp.sum(prefix_grad, 0)
-    grad_prefix_pre = hidden_grad * (1.0 - prefix_hidden * prefix_hidden)
-    grad_reparam_in_bias = jnp.sum(grad_prefix_pre, 0)
-    grad_reparam_in = jnp.einsum("pd,pa->da", embed_float, grad_prefix_pre, precision=HIGHEST)
-    grad_prefix_embed = jnp.einsum(
-        "pa,da->pd", grad_prefix_pre, reparam_in.astype(F32), precision=HIGHEST
+    grad_prefix_embed, grad_reparam_in, grad_reparam_in_bias = prefix_back(
+        hidden_grad, prefix_hidden, prefix_embed, reparam_in
     )
     return (
         output_act,

time: 553 us -> 506 us (0.915)
  starting transfers between devices: 116 us -> 83.8 us
  local copies, waits for them, and re-layouts: 101 us -> 72.2 us
  blocking collectives: 0 us -> 26.4 us
  other arithmetic: 44 us -> 26.2 us
  Pallas kernels: 132 us -> 145 us
  matrix products: 12.6 us -> 6.4 us
    all_to_all x0 -> x2, blocking collectives: none -> 26.4 us  [the longest x1 15.3 us: chip_gather(): lax.all_to_all(copies, 'seq', 0, 0, axis_index_groups=chip_groups(), tile...]
    all_to_all x5 -> x1, starting transfers between devices: 24.5 us -> 4.39 us  [on_device(): came = lax.all_to_all(sent, both, 0, 0, tiled=True)]
    ppermute x6, waiting for transfers between devices: 16.9 us -> 4.21 us  [ring_terms(): up = lax.ppermute(up, axis, ring(axis, 1))]
    ppermute x0 -> x6, waiting for transfers between devices: none -> 12.3 us  [the longest x3 12.3 us: owned_direct(): parts.append(lax.ppermute(block, axis, ring(axis, step)))]
    ppermute x6, waiting for transfers between devices: 20.7 us -> 10.6 us  [ring_terms(): down = lax.ppermute(down, axis, ring(axis, -1))]
    ppermute x6, waiting for transfers between devices: 17.7 us -> 26.8 us  [ring_gather(): down = lax.ppermute(down, axis, ring(axis, -1))]
    pallas_call x1, Pallas kernels: 25.5 us -> 32.8 us  [attend_forward(): pl.pallas_call(functools.partial(forward_kernel, tile=tile, keys=keys, pr...]
    reshape x4 -> x0, local copies, waits for them, and re-layouts: 7.17 us -> none  [the longest x2 4.05 us: on_device(): grad_attended.reshape(tensors, heads, size, group, chunk)]
  transfers between devices with their start and end apart: 46 -> 48, of which waited for: 27 -> 26; matrix products, arithmetic and copies ran while one was open for 18% -> 10% of each run, Pallas kernels for 19% -> 24%
where the time goes in v3:
time: 506 us; the launch traced here: 497 us
  Pallas kernels  145 us (29%)
  waiting for transfers between devices  121 us (24%)
  starting transfers between devices  83.8 us (17%)
  local copies, waits for them, and re-layouts  72.2 us (14%)
  blocking collectives  26.4 us (5%)
  other arithmetic  26.2 us (5%)
  between operations  15.7 us (3%)
  matrix products  6.4 us (1%)
    pallas_call x1, Pallas kernels, attend_backward(): pl.pallas_call(functools.partial(backward_kernel, tile=tile, keys=keys, p...  60 us
    unnamed x204, local copies, waits for them, and re-layouts  43.7 us
    pallas_call x1, Pallas kernels, attend_forward(): pl.pallas_call(functools.partial(forward_kernel, tile=tile, keys=keys, pr...  32.8 us
    ppermute x6, waiting for transfers between devices, ring_gather(): down = lax.ppermute(down, axis, ring(axis, -1))  26.8 us
    ppermute x6, waiting for transfers between devices, ring_gather(): up = lax.ppermute(up, axis, ring(axis, 1))  24.6 us
    ppermute x6, starting transfers between devices, ring_terms(): down = lax.ppermute(down, axis, ring(axis, -1))  16.1 us
    all_to_all x1, blocking collectives, chip_gather(): lax.all_to_all(copies, 'seq', 0, 0, axis_index_groups=chip_groups(), tile...  15.3 us
    ppermute x3, waiting for transfers between devices, owned_direct(): parts.append(lax.ppermute(block, axis, ring(axis, step)))  12.3 us
  transfers between devices with their start and end apart: 48, of which 26 were waited for; matrix products, arithmetic and copies ran while one was open for 10% of the time, Pallas kernels for 24%

profile of v3, /device:TPU:1, one launch (start us, length us, event | category | flops | bytes accessed | tf_op | source)
XLA Modules:
  0.0 496.9 jit_solution(7743500836870743375)
XLA Ops:
  11.4 2.1 collective-permute-start
  13.6 2.0 collective-permute-start.2
  16.3 3.3 all-to-all-start
  21.9 5.2 %collective-permute-done.2 = bf16[128,1024]{1,0:T(8,128)(2,1)} collective-permute-done((bf16[128,1024]{1,0:T(8,128)(2,1)}, bf16[128,1024]{1,0:T(8,128)(2,1)}, u32[]{:S(2)}, u32[]{:S(2)}) %collective-permute-start.2) | collective-permute-done | bytes 262176 | tf_op jit(solution)/shard_map/ppermute | solution.py:889
  30.2 6.7 %all-to-all-start.1 = ((s32[8,4,128]{2,1,0:T(4,128)}), s32[8,4,128]{2,1,0:T(4,128)S(1)}, u32[]{:S(2)}, u32[]{:S(2)}) async-start(s32[8,4,128]{2,1,0:T(4,128)} %broadcast_in_dim_broadcast_in_dim_broadcast_in_dim.2), calls=%async_computation.1 | async-start | bytes 32768 | tf_op jit(solution)/shard_map/all_to_all | solution.py:867
  36.9 2.9 collective-permute-done.3
  39.8 3.3 collective-permute-start.5
  43.1 5.9 %collective-permute-done.4 = bf16[128,1024]{1,0:T(8,128)(2,1)S(1)} collective-permute-done((bf16[128,1024]{1,0:T(8,128)(2,1)S(1)}, bf16[128,1024]{1,0:T(8,128)(2,1)S(1)}, u32[]{:S(2)}, u32[]{:S(2)}) %collective-permute-start.4) | collective-permute-done | bytes 262176 | tf_op jit(solution)/shard_map/ppermute | solution.py:888
  49.0 3.2 collective-permute-done.5
  56.9 3.2 project.1
  62.5 6.3 %all-to-all-start.2 = ((bf16[8,64,1536]{2,1,0:T(8,128)(2,1)}), bf16[8,64,1536]{2,1,0:T(8,128)(2,1)}, u32[]{:S(2)}, u32[]{:S(2)}) async-start(bf16[8,64,1536]{2,1,0:T(8,128)(2,1)} %copy-done.27), calls=%async_computation.2 | async-start | bytes 3145728 | tf_op jit(solution)/shard_map/all_to_all | solution.py:1103
  69.0 2.2 collective-permute-start.7
  71.2 2.3 collective-permute-start.8
  73.5 2.5 collective-permute-done.6
  76.1 5.0 %collective-permute-done.7 = bf16[32,1024]{1,0:T(8,128)(2,1)S(1)} collective-permute-done((bf16[32,1024]{1,0:T(8,128)(2,1)S(1)}, bf16[32,1024]{1,0:T(8,128)(2,1)S(1)}, u32[]{:S(2)}, u32[]{:S(2)}) %collective-permute-start.7) | collective-permute-done | bytes 65568 | tf_op jit(solution)/shard_map/ppermute | solution.py:969
  81.1 5.3 %all-to-all-done.2.query.own = bf16[8,64,1536]{2,1,0:T(8,128)(2,1)} async-done(((bf16[8,64,1536]{2,1,0:T(8,128)(2,1)}), bf16[8,64,1536]{2,1,0:T(8,128)(2,1)}, u32[]{:S(2)}, u32[]{:S(2)}) %all-to-all-start.2) | async-done | bytes 1572896 | tf_op jit(solution)/shard_map/all_to_all | solution.py:1103
  86.4 3.6 collective-permute-start.9
  91.3 2.2 collective-permute-done.9.other
  93.4 32.8 %attend_forward.1 = (bf16[32,64,128]{2,1,0:T(8,128)(2,1)S(1)}, f32[32,64,128]{2,1,0:T(8,128)S(1)}, f32[8,1,512]{2,1,0:T(1,128)S(1)}) custom-call(s32[5]{0:T(128)S(1)} %pad_add_fusion.meta, bf16[8,64,1536]{2,1,0:T(8,128)(2,1)} %all-to-all-done.2.query.own, bf16[8,64,1536]{2,1,0:T(8,128)(2,1)} %all-to-all-done.2.query.own, ...), custom_call_target="tpu_custom_call" | custom-call | flops 17179869184 | bytes 8388608 | tf_op jit(solution)/shard_map/attend_forward/pallas_call | solution.py:224
  128.0 2.9 all-to-all-start.3
  131.5 2.5 copy.142
  134.0 3.9 copy.143
  139.8 6.4 %all-to-all-done.3.came = bf16[32,64,128]{2,1,0:T(8,128)(2,1)S(1)} async-done(((bf16[32,64,128]{2,1,0:T(8,128)(2,1)}), bf16[32,64,128]{2,1,0:T(8,128)(2,1)S(1)}, u32[]{:S(2)}, u32[]{:S(2)}) %all-to-all-start.3) | async-done | bytes 524320 | tf_op jit(solution)/shard_map/all_to_all | solution.py:1124
  154.2 3.2 collective-permute-start.11
  157.6 5.6 %collective-permute-done.10 = bf16[512,256]{1,0:T(8,128)(2,1)S(1)} collective-permute-done((bf16[512,256]{1,0:T(8,128)(2,1)}, bf16[512,256]{1,0:T(8,128)(2,1)S(1)}, u32[]{:S(2)}, u32[]{:S(2)}) %collective-permute-start.10) | collective-permute-done | bytes 262176 | tf_op jit(solution)/shard_map/ppermute | solution.py:888
  163.2 4.4 collective-permute-done.11
  168.5 6.0 %collective-permute-done.12 = bf16[512,256]{1,0:T(8,128)(2,1)S(1)} collective-permute-done((bf16[512,256]{1,0:T(8,128)(2,1)S(1)}, bf16[512,256]{1,0:T(8,128)(2,1)S(1)}, u32[]{:S(2)}, u32[]{:S(2)}) %collective-permute-start.12) | collective-permute-done | bytes 262176 | tf_op jit(solution)/shard_map/ppermute | solution.py:888
  174.5 5.6 %collective-permute-done.13 = bf16[512,256]{1,0:T(8,128)(2,1)S(1)} collective-permute-done((bf16[512,256]{1,0:T(8,128)(2,1)S(1)}, bf16[512,256]{1,0:T(8,128)(2,1)S(1)}, u32[]{:S(2)}, u32[]{:S(2)}) %collective-permute-start.13) | collective-permute-done | bytes 262176 | tf_op jit(solution)/shard_map/ppermute | solution.py:889
  180.1 5.6 %collective-permute-done.14 = bf16[512,256]{1,0:T(8,128)(2,1)S(1)} collective-permute-done((bf16[512,256]{1,0:T(8,128)(2,1)S(1)}, bf16[512,256]{1,0:T(8,128)(2,1)S(1)}, u32[]{:S(2)}, u32[]{:S(2)}) %collective-permute-start.14) | collective-permute-done | bytes 262176 | tf_op jit(solution)/shard_map/ppermute | solution.py:888
  185.8 5.5 %collective-permute-done.15 = bf16[512,256]{1,0:T(8,128)(2,1)S(1)} collective-permute-done((bf16[512,256]{1,0:T(8,128)(2,1)S(1)}, bf16[512,256]{1,0:T(8,128)(2,1)S(1)}, u32[]{:S(2)}, u32[]{:S(2)}) %collective-permute-start.15) | collective-permute-done | bytes 262176 | tf_op jit(solution)/shard_map/ppermute | solution.py:889
  194.0 11.9 %feed.1 = (bf16[4,1024,256]{2,1,0:T(8,128)(2,1)S(1)}, bf16[4,1024,256]{2,1,0:T(8,128)(2,1)S(1)}, bf16[4,1024,256]{2,1,0:T(8,128)(2,1)S(1)}) custom-call(bf16[4,1024,256]{2,1,0:T(8,128)(2,1)S(1)} %bitcast_dynamic-update-slice_fusion.2.rows, bf16[1024,1024]{1,0:T(8,128)(2,1)S(1)} %copy-done.17, bf16[1024,1024]{1,0:T(8,128)(2,1)S(1)} %bitcast.207, ...), custom_call_target="tpu_custom_call" | custom-call | flops 6442450944 | bytes 16777216 | tf_op jit(solution)/shard_map/feed/pallas_call | solution.py:560
  207.2 3.0 collective-permute-start.17
  210.2 4.5 feed_weights.1
  222.3 2.9 collective-permute-start.19
  229.6 7.1 %feed_out.1 = bf16[4,4,256,256]{3,2,1,0:T(8,128)(2,1)} custom-call(s32[2]{0:T(128)S(1)} %pad_add_fusion.1.spot, bf16[4,1024,256]{2,1,0:T(8,128)(2,1)S(1)} %copy-done.60, bf16[1024,1024]{1,0:T(8,128)(2,1)S(1)} %bitcast.206, f32[1024,256]{1,0:T(8,128)S(1)} %copy-done.54, f32[1024,6]{1,0:T(8,128)S(1)} %bitcast.196), custom_call_target="tpu_custom_call" | custom-call | flops 2147483648 | bytes 8388608 | tf_op jit(solution)/shard_map/feed_out/pallas_call | solution.py:647
  239.5 2.1 collective-permute-start.21
  241.5 4.2 collective-permute-done.20.up
  245.7 7.0 %collective-permute-done.21.down = bf16[512,256]{1,0:T(8,128)(2,1)S(1)} collective-permute-done((bf16[512,256]{1,0:T(8,128)(2,1)S(1)}, bf16[512,256]{1,0:T(8,128)(2,1)S(1)}, u32[]{:S(2)}, u32[]{:S(2)}) %collective-permute-start.21) | collective-permute-done | bytes 262176 | tf_op jit(solution)/shard_map/ppermute | solution.py:910
  255.3 2.0 leave.1
  259.9 4.4 all-to-all-start.4
  264.9 3.1 convolution_convert_fusion
  268.0 11.5 %all-to-all-done.4.grad_out = bf16[32,64,128]{2,1,0:T(8,128)(2,1)S(1)} async-done(((bf16[32,64,128]{2,1,0:T(8,128)(2,1)}), bf16[32,64,128]{2,1,0:T(8,128)(2,1)S(1)}, u32[]{:S(2)}, u32[]{:S(2)}) %all-to-all-start.4) | async-done | bytes 524320 | tf_op jit(solution)/shard_map/all_to_all | solution.py:1176
  280.4 4.5 all-to-all-start.5
  285.4 60.0 %attend_backward.1 = (bf16[8,64,512]{2,1,0:T(8,128)(2,1)}, bf16[8,64,1024]{2,1,0:T(8,128)(2,1)}, bf16[8,64,1024]{2,1,0:T(8,128)(2,1)}, f32[2,16,64]{2,1,0:T(8,128)}) custom-call(s32[5]{0:T(128)} %copy-done.58, bf16[8,64,1536]{2,1,0:T(8,128)(2,1)} %all-to-all-done.2.query.own, bf16[8,64,1536]{2,1,0:T(8,128)(2,1)} %all-to-all-done.2.query.own, ...), custom_call_target="tpu_custom_call" | custom-call | flops 42949672960 | bytes 8388608 | tf_op jit(solution)/shard_map/attend_backward/pallas_call | solution.py:369
  346.3 2.0 collective-permute-done.22
  351.3 4.7 all-to-all-start.6
  357.8 4.2 convert_element_type.234
  362.1 2.5 convert_element_type.235
  364.5 2.2 reduce_sum.74
  368.1 6.8 %all-to-all-done.6.came = bf16[8,64,1664]{2,1,0:T(8,128)(2,1)} async-done(((bf16[8,64,1664]{2,1,0:T(8,128)(2,1)}), bf16[8,64,1664]{2,1,0:T(8,128)(2,1)}, u32[]{:S(2)}, u32[]{:S(2)}) %all-to-all-start.6) | async-done | bytes 1703968 | tf_op jit(solution)/shard_map/all_to_all | solution.py:1203
  378.5 6.3 %unproject.1 = (bf16[768,1024]{1,0:T(8,128)(2,1)S(1)}, bf16[1024,1024]{1,0:T(8,128)(2,1)S(1)}, f32[2,1024]{1,0:T(2,128)S(1)}, f32[1024,2]{1,0:T(8,128)S(1)}, f32[768,1]{1,0:T(8,128)S(1)}) custom-call(s32[2]{0:T(128)S(1)} %pad_add_fusion.1.spot, bf16[8,64,1664]{2,1,0:T(8,128)(2,1)} %all-to-all-done.6.came, bf16[1024,768]{1,0:T(8,128)(2,1)S(1)} %copy-done.28, ...), custom_call_target="tpu_custom_call" | custom-call | flops 3221225472 | bytes 8388608 | tf_op jit(solution)/shard_map/unproject/pallas_call | solution.py:495
  389.8 2.1 dynamic-slice_bitcast_fusion
  396.8 5.8 %rest_halves.1 = (bf16[512,1024]{1,0:T(8,128)(2,1)S(1)}, bf16[512,1024]{1,0:T(8,128)(2,1)}) custom-call(s32[2]{0:T(128)S(1)} %pad_add_fusion.1.spot, bf16[768,1024]{1,0:T(8,128)(2,1)S(1)} %copy-done.62, bf16[1024,1024]{1,0:T(8,128)(2,1)S(1)} %copy-done.52, bf16[256,1024]{1,0:T(8,128)(2,1)S(1)} %copy-done.57), custom_call_target="tpu_custom_call" | custom-call | flops 1610612736 | bytes 8388608 | tf_op jit(solution)/shard_map/rest_halves/pallas_call | solution.py:782
  405.5 2.2 collective-permute-start.27
  409.3 2.7 collective-permute-start.26
  415.3 9.5 %collective-permute-done.28 = f32[1,8448]{1,0:T(1,128)S(1)} collective-permute-done((f32[1,8448]{1,0:T(1,128)}, f32[1,8448]{1,0:T(1,128)S(1)}, u32[]{:S(2)}, u32[]{:S(2)}) %collective-permute-start.28) | collective-permute-done | bytes 33824 | tf_op jit(solution)/shard_map/ppermute | solution.py:950
  425.0 2.8 collective-permute-done.30
  431.4 3.3 collective-permute-start.33
  437.2 3.5 collective-permute-start.32
  440.8 11.1 %all_to_all.45 = f32[8,1,3072]{2,1,0:T(1,128)} all-to-all(f32[8,1,3072]{2,1,0:T(1,128)S(1)} %broadcast_in_dim.138), channel_id=1, replica_groups=mesh['seq'=8,'tensor'=4] {'seq'}, dimensions={0} | all-to-all | bytes 196608 | tf_op jit(solution)/shard_map/all_to_all | solution.py:867
  452.3 15.3 %all_to_all.46 = bf16[4,128,1024]{2,1,0:T(8,128)(2,1)S(1)} all-to-all(bf16[4,128,1024]{2,1,0:T(8,128)(2,1)S(1)} %broadcast_in_dim.141), channel_id=1, replica_groups={{0,8,16,24},{4,12,20,28},{1,9,17,25},{5,13,21,29},{2,10,18,26},{6,14,22..., dimensions={0} | all-to-all | bytes 2097152 | tf_op jit(solution)/shard_map/all_to_all | solution.py:960
  467.7 2.3 collective-permute-start.36
  476.6 4.3 prefix_back.1
  486.4 3.5 rest_whole.1
  (382 shorter events, 104.4 us)
Async XLA Ops:
  7.2 61.7 %copy-start = (bf16[4,64,1024]{2,1,0:T(8,128)(2,1)S(1)}, bf16[4,64,1024]{2,1,0:T(8,128)(2,1)}, u32[]{:S(2)}) copy-start(bf16[4,64,1024]{2,1,0:T(8,128)(2,1)} %param.27) | copy-start | bytes 1572868
  11.4 10.4 %collective-permute-start = (bf16[128,1024]{1,0:T(8,128)(2,1)}, bf16[128,1024]{1,0:T(8,128)(2,1)S(1)}, u32[]{:S(2)}, u32[]{:S(2)}) collective-permute-start(bf16[128,1024]{1,0:T(8,128)(2,1)} %get-tuple-element.368), channel_id=1, source_target_pairs={{0,1},{1,2},{2,3},{3,0},{4,5},{5,6},{6,7},{7,4},{8,9},{9,10},{10,1... | collective-permute-start | bytes 786440 | tf_op jit(solution)/shard_map/ppermute | solution.py:888
  13.6 13.5 %collective-permute-start.2 = (bf16[128,1024]{1,0:T(8,128)(2,1)}, bf16[128,1024]{1,0:T(8,128)(2,1)}, u32[]{:S(2)}, u32[]{:S(2)}) collective-permute-start(bf16[128,1024]{1,0:T(8,128)(2,1)} %get-tuple-element.367), channel_id=1, source_target_pairs={{0,3},{1,0},{2,1},{3,2},{4,7},{5,4},{6,5},{7,6},{8,11},{9,8},{10,9... | collective-permute-start | bytes 786440 | tf_op jit(solution)/shard_map/ppermute | solution.py:889
  16.3 13.2 %all-to-all-start = ((bf16[4,6,256]{2,1,0:T(8,128)(2,1)}), bf16[4,6,256]{2,1,0:T(8,128)(2,1)S(1)}, u32[]{:S(2)}, u32[]{:S(2)}) async-start(bf16[4,6,256]{2,1,0:T(8,128)(2,1)} %broadcast_in_dim.111), calls=%async_computation | async-start | bytes 32768 | tf_op jit(solution)/shard_map/all_to_all | solution.py:867
  20.2 33.0 %copy-start.88 = (bf16[4,128]{1,0:T(4,128)(2,1)S(1)}, bf16[4,128]{1,0:T(4,128)(2,1)}, u32[]{:S(2)}) copy-start(bf16[4,128]{1,0:T(4,128)(2,1)} %param.26) | copy-start | bytes 3076
  21.9 15.0 %collective-permute-start.1 = (bf16[128,1024]{1,0:T(8,128)(2,1)S(1)}, bf16[128,1024]{1,0:T(8,128)(2,1)S(1)}, u32[]{:S(2)}, u32[]{:S(2)}) collective-permute-start(bf16[128,1024]{1,0:T(8,128)(2,1)S(1)} %collective-permute-done), channel_id=1, source_target_pairs={{0,1},{1,2},{2,3},{3,0},{4,5},{5,6},{6,7},{7,4},{8,9},{9,10},{10,1... | collective-permute-start | bytes 786440 | tf_op jit(solution)/shard_map/ppermute | solution.py:888
  27.1 12.7 %collective-permute-start.3 = (bf16[128,1024]{1,0:T(8,128)(2,1)}, bf16[128,1024]{1,0:T(8,128)(2,1)S(1)}, u32[]{:S(2)}, u32[]{:S(2)}) collective-permute-start(bf16[128,1024]{1,0:T(8,128)(2,1)} %collective-permute-done.2), channel_id=1, source_target_pairs={{0,3},{1,0},{2,1},{3,2},{4,7},{5,4},{6,5},{7,6},{8,11},{9,8},{10,9... | collective-permute-start | bytes 786440 | tf_op jit(solution)/shard_map/ppermute | solution.py:889
  30.2 12.9 %all-to-all-start.1 = ((s32[8,4,128]{2,1,0:T(4,128)}), s32[8,4,128]{2,1,0:T(4,128)S(1)}, u32[]{:S(2)}, u32[]{:S(2)}) async-start(s32[8,4,128]{2,1,0:T(4,128)} %broadcast_in_dim_broadcast_in_dim_broadcast_in_dim.2), calls=%async_computation.1 | async-start | bytes 32768 | tf_op jit(solution)/shard_map/all_to_all | solution.py:867
  36.9 91.1 %all-gather.4.cloned.1.call-start = ((), (), s32[]{:S(2)}) async-start(), calls=%async_computation.10 | async-start | bytes 2621440 | tf_op jit(solution)/shard_map/all_gather | solution.py:1114
  39.8 9.2 %collective-permute-start.4 = (bf16[128,1024]{1,0:T(8,128)(2,1)S(1)}, bf16[128,1024]{1,0:T(8,128)(2,1)S(1)}, u32[]{:S(2)}, u32[]{:S(2)}) collective-permute-start(bf16[128,1024]{1,0:T(8,128)(2,1)S(1)} %collective-permute-done.1), channel_id=1, source_target_pairs={{0,1},{1,2},{2,3},{3,0},{4,5},{5,6},{6,7},{7,4},{8,9},{9,10},{10,1... | collective-permute-start | bytes 786440 | tf_op jit(solution)/shard_map/ppermute | solution.py:888
  39.8 12.4 %collective-permute-start.5 = (bf16[128,1024]{1,0:T(8,128)(2,1)S(1)}, bf16[128,1024]{1,0:T(8,128)(2,1)}, u32[]{:S(2)}, u32[]{:S(2)}) collective-permute-start(bf16[128,1024]{1,0:T(8,128)(2,1)S(1)} %collective-permute-done.3), channel_id=1, source_target_pairs={{0,3},{1,0},{2,1},{3,2},{4,7},{5,4},{6,5},{7,6},{8,11},{9,8},{10,9... | collective-permute-start | bytes 786440 | tf_op jit(solution)/shard_map/ppermute | solution.py:889
  62.5 27.5 %copy-start.89 = (bf16[4,128]{1,0:T(4,128)(2,1)S(1)}, bf16[4,128]{1,0:T(4,128)(2,1)}, u32[]{:S(2)}) copy-start(bf16[4,128]{1,0:T(4,128)(2,1)} %param.39) | copy-start | bytes 3076
  62.5 27.5 %copy-start.90 = (bf16[512]{0:T(512)(128)(2,1)S(1)}, bf16[512]{0:T(512)(128)(2,1)}, u32[]{:S(2)}) copy-start(bf16[512]{0:T(512)(128)(2,1)} %param.37) | copy-start | bytes 3076
  62.5 27.6 %copy-start.9 = (bf16[1024,512]{1,0:T(8,128)(2,1)S(1)}, bf16[1024,512]{1,0:T(8,128)(2,1)}, u32[]{:S(2)}) copy-start(bf16[1024,512]{1,0:T(8,128)(2,1)} %weight.1) | copy-start | bytes 3145732
  62.5 27.6 %copy-start.78 = (bf16[10,1024]{1,0:T(8,128)(2,1)S(1)}, bf16[10,1024]{1,0:T(8,128)(2,1)}, u32[]{:S(2)}) copy-start(bf16[10,1024]{1,0:T(8,128)(2,1)} %param.35) | copy-start | bytes 61444
  62.5 27.9 %copy-start.66 = (bf16[512,4,128]{2,1,0:T(4,128)(2,1)S(1)}, bf16[512,4,128]{2,1,0:T(4,128)(2,1)}, u32[]{:S(2)}) copy-start(bf16[512,4,128]{2,1,0:T(4,128)(2,1)} %param.38) | copy-start | bytes 1572868
  62.5 23.9 %all-to-all-start.2 = ((bf16[8,64,1536]{2,1,0:T(8,128)(2,1)}), bf16[8,64,1536]{2,1,0:T(8,128)(2,1)}, u32[]{:S(2)}, u32[]{:S(2)}) async-start(bf16[8,64,1536]{2,1,0:T(8,128)(2,1)} %copy-done.27), calls=%async_computation.2 | async-start | bytes 3145728 | tf_op jit(solution)/shard_map/all_to_all | solution.py:1103
  68.9 22.2 %copy-start.82 = (s32[8,4,128]{2,1,0:T(4,128)S(1)}, s32[8,4,128]{2,1,0:T(4,128)}, u32[]{:S(2)}) copy-start(s32[8,4,128]{2,1,0:T(4,128)} %copy-done.81) | copy-start | bytes 49156
  68.9 69.1 %all-gather.6.cloned.1.call-start = ((), (), s32[]{:S(2)}) async-start(), calls=%async_computation.12 | async-start | bytes 2359296 | tf_op jit(solution)/shard_map/all_gather | solution.py:1105
  68.9 7.1 %collective-permute-start.6 = (bf16[32,1024]{1,0:T(8,128)(2,1)S(1)}, bf16[32,1024]{1,0:T(8,128)(2,1)S(1)}, u32[]{:S(2)}, u32[]{:S(2)}) collective-permute-start(bf16[32,1024]{1,0:T(8,128)(2,1)S(1)} %dynamic-slice_bitcast_fusion.20), channel_id=1, source_target_pairs={{0,1},{1,2},{2,3},{3,0},{4,5},{5,6},{6,7},{7,4},{8,9},{9,10},{10,1... | collective-permute-start | bytes 196616 | tf_op jit(solution)/shard_map/ppermute | solution.py:969
  69.0 12.1 %collective-permute-start.7 = (bf16[32,1024]{1,0:T(8,128)(2,1)S(1)}, bf16[32,1024]{1,0:T(8,128)(2,1)S(1)}, u32[]{:S(2)}, u32[]{:S(2)}) collective-permute-start(bf16[32,1024]{1,0:T(8,128)(2,1)S(1)} %dynamic-slice_bitcast_fusion.20), channel_id=1, source_target_pairs={{0,2},{1,3},{2,0},{3,1},{4,6},{5,7},{6,4},{7,5},{8,10},{9,11},{10,... | collective-permute-start | bytes 196616 | tf_op jit(solution)/shard_map/ppermute | solution.py:969
  71.2 9.9 %collective-permute-start.8 = (bf16[32,1024]{1,0:T(8,128)(2,1)S(1)}, bf16[32,1024]{1,0:T(8,128)(2,1)S(1)}, u32[]{:S(2)}, u32[]{:S(2)}) collective-permute-start(bf16[32,1024]{1,0:T(8,128)(2,1)S(1)} %dynamic-slice_bitcast_fusion.20), channel_id=1, source_target_pairs={{0,3},{1,0},{2,1},{3,2},{4,7},{5,4},{6,5},{7,6},{8,11},{9,8},{10,9... | collective-permute-start | bytes 196616 | tf_op jit(solution)/shard_map/ppermute | solution.py:969
  86.4 7.0 %collective-permute-start.9 = (bf16[8,64,1536]{2,1,0:T(8,128)(2,1)}, bf16[8,64,1536]{2,1,0:T(8,128)(2,1)}, u32[]{:S(2)}, u32[]{:S(2)}) collective-permute-start(bf16[8,64,1536]{2,1,0:T(8,128)(2,1)} %all-to-all-done.2.query.own), channel_id=1, source_target_pairs={{0,4},{4,0},{8,12},{12,8},{16,20},{20,16},{24,28},{28,24},{1,5},{5... | collective-permute-start | bytes 4718600 | tf_op jit(solution)/shard_map/ppermute | solution.py:924
  91.3 34.9 %copy-start.58 = (s32[5]{0:T(128)}, s32[5]{0:T(128)S(1)}, u32[]{:S(2)}) copy-start(s32[5]{0:T(128)S(1)} %pad_add_fusion.meta) | copy-start | bytes 64
  93.4 38.1 %copy-start.14 = (bf16[1024,1024]{1,0:T(8,128)(2,1)S(1)}, bf16[1024,1024]{1,0:T(8,128)(2,1)}, u32[]{:S(2)}) copy-start(bf16[1024,1024]{1,0:T(8,128)(2,1)} %up.1) | copy-start | bytes 6291460
  128.0 18.2 %all-to-all-start.3 = ((bf16[32,64,128]{2,1,0:T(8,128)(2,1)}), bf16[32,64,128]{2,1,0:T(8,128)(2,1)S(1)}, u32[]{:S(2)}, u32[]{:S(2)}) async-start(bf16[32,64,128]{2,1,0:T(8,128)(2,1)} %copy-done.41), calls=%async_computation.3 | async-start | bytes 1048576 | tf_op jit(solution)/shard_map/all_to_all | solution.py:1124
  130.9 220.4 %all-reduce.8.cloned.1.call-start = ((), (), s32[]{:S(2)}) async-start(), calls=%async_computation.13 | async-start | bytes 8388608 | tf_op jit(solution)/shard_map/psum | solution.py:1156
  131.5 263.7 %copy-start.49 = (s32[2]{0:T(128)}, s32[2]{0:T(128)S(1)}, u32[]{:S(2)}) copy-start(s32[2]{0:T(128)S(1)} %pad_add_fusion.1.spot) | copy-start | bytes 28
  153.1 10.1 %collective-permute-start.10 = (bf16[512,256]{1,0:T(8,128)(2,1)}, bf16[512,256]{1,0:T(8,128)(2,1)S(1)}, u32[]{:S(2)}, u32[]{:S(2)}) collective-permute-start(bf16[512,256]{1,0:T(8,128)(2,1)} %get-tuple-element.366), channel_id=1, source_target_pairs={{0,1},{1,2},{2,3},{3,0},{4,5},{5,6},{6,7},{7,4},{8,9},{9,10},{10,1... | collective-permute-start | bytes 786440 | tf_op jit(solution)/shard_map/ppermute | solution.py:888
  154.2 13.4 %collective-permute-start.11 = (bf16[512,256]{1,0:T(8,128)(2,1)}, bf16[512,256]{1,0:T(8,128)(2,1)S(1)}, u32[]{:S(2)}, u32[]{:S(2)}) collective-permute-start(bf16[512,256]{1,0:T(8,128)(2,1)} %get-tuple-element.365), channel_id=1, source_target_pairs={{0,3},{1,0},{2,1},{3,2},{4,7},{5,4},{6,5},{7,6},{8,11},{9,8},{10,9... | collective-permute-start | bytes 786440 | tf_op jit(solution)/shard_map/ppermute | solution.py:889
  157.4 33.9 %copy-start.17 = (bf16[1024,1024]{1,0:T(8,128)(2,1)S(1)}, bf16[1024,1024]{1,0:T(8,128)(2,1)}, u32[]{:S(2)}) copy-start(bf16[1024,1024]{1,0:T(8,128)(2,1)} %all-gather.4.cloned.1.call-done.grads) | copy-start | bytes 6291460
  157.6 33.8 %copy-start.15 = (bf16[1024,1024]{1,0:T(8,128)(2,1)S(1)}, bf16[1024,1024]{1,0:T(8,128)(2,1)}, u32[]{:S(2)}) copy-start(bf16[1024,1024]{1,0:T(8,128)(2,1)} %up.1) | copy-start | bytes 6291460
  157.6 33.8 %copy-start.16 = (bf16[1024,1024]{1,0:T(8,128)(2,1)S(1)}, bf16[1024,1024]{1,0:T(8,128)(2,1)}, u32[]{:S(2)}) copy-start(bf16[1024,1024]{1,0:T(8,128)(2,1)} %down.1) | copy-start | bytes 6291460
  163.2 11.3 %collective-permute-start.12 = (bf16[512,256]{1,0:T(8,128)(2,1)S(1)}, bf16[512,256]{1,0:T(8,128)(2,1)S(1)}, u32[]{:S(2)}, u32[]{:S(2)}) collective-permute-start(bf16[512,256]{1,0:T(8,128)(2,1)S(1)} %collective-permute-done.10), channel_id=1, source_target_pairs={{0,1},{1,2},{2,3},{3,0},{4,5},{5,6},{6,7},{7,4},{8,9},{9,10},{10,1... | collective-permute-start | bytes 786440 | tf_op jit(solution)/shard_map/ppermute | solution.py:888
  167.6 12.5 %collective-permute-start.13 = (bf16[512,256]{1,0:T(8,128)(2,1)S(1)}, bf16[512,256]{1,0:T(8,128)(2,1)S(1)}, u32[]{:S(2)}, u32[]{:S(2)}) collective-permute-start(bf16[512,256]{1,0:T(8,128)(2,1)S(1)} %collective-permute-done.11), channel_id=1, source_target_pairs={{0,3},{1,0},{2,1},{3,2},{4,7},{5,4},{6,5},{7,6},{8,11},{9,8},{10,9... | collective-permute-start | bytes 786440 | tf_op jit(solution)/shard_map/ppermute | solution.py:889
  174.5 11.3 %collective-permute-start.14 = (bf16[512,256]{1,0:T(8,128)(2,1)S(1)}, bf16[512,256]{1,0:T(8,128)(2,1)S(1)}, u32[]{:S(2)}, u32[]{:S(2)}) collective-permute-start(bf16[512,256]{1,0:T(8,128)(2,1)S(1)} %collective-permute-done.12), channel_id=1, source_target_pairs={{0,1},{1,2},{2,3},{3,0},{4,5},{5,6},{6,7},{7,4},{8,9},{9,10},{10,1... | collective-permute-start | bytes 786440 | tf_op jit(solution)/shard_map/ppermute | solution.py:888
  180.1 11.2 %collective-permute-start.15 = (bf16[512,256]{1,0:T(8,128)(2,1)S(1)}, bf16[512,256]{1,0:T(8,128)(2,1)S(1)}, u32[]{:S(2)}, u32[]{:S(2)}) collective-permute-start(bf16[512,256]{1,0:T(8,128)(2,1)S(1)} %collective-permute-done.13), channel_id=1, source_target_pairs={{0,3},{1,0},{2,1},{3,2},{4,7},{5,4},{6,5},{7,6},{8,11},{9,8},{10,9... | collective-permute-start | bytes 786440 | tf_op jit(solution)/shard_map/ppermute | solution.py:889
  206.9 10.5 %collective-permute-start.16 = (bf16[512,256]{1,0:T(8,128)(2,1)S(1)}, bf16[512,256]{1,0:T(8,128)(2,1)S(1)}, u32[]{:S(2)}, u32[]{:S(2)}) collective-permute-start(bf16[512,256]{1,0:T(8,128)(2,1)S(1)} %get-tuple-element.356), channel_id=1, source_target_pairs={{0,1},{1,2},{2,3},{3,0},{4,5},{5,6},{6,7},{7,4},{8,9},{9,10},{10,1... | collective-permute-start | bytes 786440 | tf_op jit(solution)/shard_map/ppermute | solution.py:909
  207.2 12.7 %collective-permute-start.17 = (bf16[512,256]{1,0:T(8,128)(2,1)S(1)}, bf16[512,256]{1,0:T(8,128)(2,1)S(1)}, u32[]{:S(2)}, u32[]{:S(2)}) collective-permute-start(bf16[512,256]{1,0:T(8,128)(2,1)S(1)} %get-tuple-element.355), channel_id=1, source_target_pairs={{0,3},{1,0},{2,1},{3,2},{4,7},{5,4},{6,5},{7,6},{8,11},{9,8},{10,9... | collective-permute-start | bytes 786440 | tf_op jit(solution)/shard_map/ppermute | solution.py:910
  221.9 14.9 %collective-permute-start.18 = (bf16[512,256]{1,0:T(8,128)(2,1)S(1)}, bf16[512,256]{1,0:T(8,128)(2,1)}, u32[]{:S(2)}, u32[]{:S(2)}) collective-permute-start(bf16[512,256]{1,0:T(8,128)(2,1)S(1)} %get-tuple-element.360), channel_id=1, source_target_pairs={{0,1},{1,2},{2,3},{3,0},{4,5},{5,6},{6,7},{7,4},{8,9},{9,10},{10,1... | collective-permute-start | bytes 786440 | tf_op jit(solution)/shard_map/ppermute | solution.py:909
  222.3 14.5 %collective-permute-start.19 = (bf16[512,256]{1,0:T(8,128)(2,1)S(1)}, bf16[512,256]{1,0:T(8,128)(2,1)}, u32[]{:S(2)}, u32[]{:S(2)}) collective-permute-start(bf16[512,256]{1,0:T(8,128)(2,1)S(1)} %get-tuple-element.359), channel_id=1, source_target_pairs={{0,3},{1,0},{2,1},{3,2},{4,7},{5,4},{6,5},{7,6},{8,11},{9,8},{10,9... | collective-permute-start | bytes 786440 | tf_op jit(solution)/shard_map/ppermute | solution.py:910
  238.2 7.5 %collective-permute-start.20 = (bf16[512,256]{1,0:T(8,128)(2,1)S(1)}, bf16[512,256]{1,0:T(8,128)(2,1)S(1)}, u32[]{:S(2)}, u32[]{:S(2)}) collective-permute-start(bf16[512,256]{1,0:T(8,128)(2,1)S(1)} %get-tuple-element.358), channel_id=1, source_target_pairs={{0,1},{1,2},{2,3},{3,0},{4,5},{5,6},{6,7},{7,4},{8,9},{9,10},{10,1... | collective-permute-start | bytes 786440 | tf_op jit(solution)/shard_map/ppermute | solution.py:909
  239.5 13.2 %collective-permute-start.21 = (bf16[512,256]{1,0:T(8,128)(2,1)S(1)}, bf16[512,256]{1,0:T(8,128)(2,1)S(1)}, u32[]{:S(2)}, u32[]{:S(2)}) collective-permute-start(bf16[512,256]{1,0:T(8,128)(2,1)S(1)} %get-tuple-element.357), channel_id=1, source_target_pairs={{0,3},{1,0},{2,1},{3,2},{4,7},{5,4},{6,5},{7,6},{8,11},{9,8},{10,9... | collective-permute-start | bytes 786440 | tf_op jit(solution)/shard_map/ppermute | solution.py:910
  259.9 19.7 %all-to-all-start.4 = ((bf16[32,64,128]{2,1,0:T(8,128)(2,1)}), bf16[32,64,128]{2,1,0:T(8,128)(2,1)S(1)}, u32[]{:S(2)}, u32[]{:S(2)}) async-start(bf16[32,64,128]{2,1,0:T(8,128)(2,1)} %copy-done.42), calls=%async_computation.4 | async-start | bytes 1048576 | tf_op jit(solution)/shard_map/all_to_all | solution.py:1176
  280.4 71.0 %all-to-all-start.5 = ((bf16[4,4,256,256]{3,2,1,0:T(8,128)(2,1)}), bf16[4,4,256,256]{3,2,1,0:T(8,128)(2,1)}, u32[]{:S(2)}, u32[]{:S(2)}) async-start(bf16[4,4,256,256]{3,2,1,0:T(8,128)(2,1)} %feed_out.1), calls=%async_computation.5 | async-start | bytes 4194304 | tf_op jit(solution)/shard_map/all_to_all | solution.py:1181
  284.8 83.3 %reduce-scatter.2.cloned.1.call-start = ((), (), s32[]{:S(2)}) async-start(), calls=%async_computation.11 | async-start | bytes 2621440 | tf_op jit(solution)/shard_map/reduce_scatter | solution.py:1182
  345.4 2.9 collective-permute-start.22
  351.3 23.6 %all-to-all-start.6 = ((bf16[8,64,1664]{2,1,0:T(8,128)(2,1)}), bf16[8,64,1664]{2,1,0:T(8,128)(2,1)}, u32[]{:S(2)}, u32[]{:S(2)}) async-start(bf16[8,64,1664]{2,1,0:T(8,128)(2,1)} %pad_maximum_fusion), calls=%async_computation.6 | async-start | bytes 3407872 | tf_op jit(solution)/shard_map/all_to_all | solution.py:1203
  391.9 11.7 %collective-permute-start.23 = (bf16[128,1024]{1,0:T(8,128)(2,1)S(1)}, bf16[128,1024]{1,0:T(8,128)(2,1)S(1)}, u32[]{:S(2)}, u32[]{:S(2)}) collective-permute-start(bf16[128,1024]{1,0:T(8,128)(2,1)S(1)} %get-tuple-element.348), channel_id=1, source_target_pairs={{0,1},{1,2},{2,3},{3,0},{4,5},{5,6},{6,7},{7,4},{8,9},{9,10},{10,1... | collective-permute-start | bytes 786440 | tf_op jit(solution)/shard_map/ppermute | solution.py:909
  393.2 12.3 %collective-permute-start.24 = (bf16[128,1024]{1,0:T(8,128)(2,1)S(1)}, bf16[128,1024]{1,0:T(8,128)(2,1)S(1)}, u32[]{:S(2)}, u32[]{:S(2)}) collective-permute-start(bf16[128,1024]{1,0:T(8,128)(2,1)S(1)} %get-tuple-element.347), channel_id=1, source_target_pairs={{0,3},{1,0},{2,1},{3,2},{4,7},{5,4},{6,5},{7,6},{8,11},{9,8},{10,9... | collective-permute-start | bytes 786440 | tf_op jit(solution)/shard_map/ppermute | solution.py:910
  405.5 22.2 %collective-permute-start.27 = (bf16[512,1024]{1,0:T(8,128)(2,1)}, bf16[512,1024]{1,0:T(8,128)(2,1)}, u32[]{:S(2)}, u32[]{:S(2)}) collective-permute-start(bf16[512,1024]{1,0:T(8,128)(2,1)} %get-tuple-element.194), channel_id=1, source_target_pairs={{0,4},{4,0},{8,12},{12,8},{16,20},{20,16},{24,28},{28,24},{1,5},{5... | collective-permute-start | bytes 3145736 | tf_op jit(solution)/shard_map/ppermute | solution.py:924
  408.8 19.0 %collective-permute-start.25 = (bf16[128,1024]{1,0:T(8,128)(2,1)}, bf16[128,1024]{1,0:T(8,128)(2,1)}, u32[]{:S(2)}, u32[]{:S(2)}) collective-permute-start(bf16[128,1024]{1,0:T(8,128)(2,1)} %get-tuple-element.352), channel_id=1, source_target_pairs={{0,1},{1,2},{2,3},{3,0},{4,5},{5,6},{6,7},{7,4},{8,9},{9,10},{10,1... | collective-permute-start | bytes 786440 | tf_op jit(solution)/shard_map/ppermute | solution.py:909
  409.3 18.5 %collective-permute-start.26 = (bf16[128,1024]{1,0:T(8,128)(2,1)}, bf16[128,1024]{1,0:T(8,128)(2,1)}, u32[]{:S(2)}, u32[]{:S(2)}) collective-permute-start(bf16[128,1024]{1,0:T(8,128)(2,1)} %get-tuple-element.351), channel_id=1, source_target_pairs={{0,3},{1,0},{2,1},{3,2},{4,7},{5,4},{6,5},{7,6},{8,11},{9,8},{10,9... | collective-permute-start | bytes 786440 | tf_op jit(solution)/shard_map/ppermute | solution.py:910
  412.8 12.0 %collective-permute-start.28 = (f32[1,8448]{1,0:T(1,128)}, f32[1,8448]{1,0:T(1,128)S(1)}, u32[]{:S(2)}, u32[]{:S(2)}) collective-permute-start(f32[1,8448]{1,0:T(1,128)} %get-tuple-element.371), channel_id=1, source_target_pairs={{0,1},{1,2},{2,3},{3,0},{4,5},{5,6},{6,7},{7,4},{8,9},{9,10},{10,1... | collective-permute-start | bytes 101384 | tf_op jit(solution)/shard_map/ppermute | solution.py:950
  413.7 11.3 %collective-permute-start.29 = (f32[1,8448]{1,0:T(1,128)}, f32[1,8448]{1,0:T(1,128)S(1)}, u32[]{:S(2)}, u32[]{:S(2)}) collective-permute-start(f32[1,8448]{1,0:T(1,128)} %get-tuple-element.370), channel_id=1, source_target_pairs={{0,2},{1,3},{2,0},{3,1},{4,6},{5,7},{6,4},{7,5},{8,10},{9,11},{10,... | collective-permute-start | bytes 101384 | tf_op jit(solution)/shard_map/ppermute | solution.py:950
  424.8 3.0 collective-permute-start.30
  431.4 20.6 %collective-permute-start.33 = (bf16[128,1024]{1,0:T(8,128)(2,1)S(1)}, bf16[128,1024]{1,0:T(8,128)(2,1)S(1)}, u32[]{:S(2)}, u32[]{:S(2)}) collective-permute-start(bf16[128,1024]{1,0:T(8,128)(2,1)S(1)} %get-tuple-element.363), channel_id=1, source_target_pairs={{0,8},{4,12},{8,16},{12,20},{16,24},{20,28},{24,0},{28,4},{1,9},{5... | collective-permute-start | bytes 786440 | tf_op jit(solution)/shard_map/ppermute | solution.py:941
  434.6 17.3 %collective-permute-start.34 = (bf16[128,1024]{1,0:T(8,128)(2,1)S(1)}, bf16[128,1024]{1,0:T(8,128)(2,1)S(1)}, u32[]{:S(2)}, u32[]{:S(2)}) collective-permute-start(bf16[128,1024]{1,0:T(8,128)(2,1)S(1)} %get-tuple-element.362), channel_id=1, source_target_pairs={{0,16},{4,20},{8,24},{12,28},{16,0},{20,4},{24,8},{28,12},{1,17},{... | collective-permute-start | bytes 786440 | tf_op jit(solution)/shard_map/ppermute | solution.py:941
  434.7 17.2 %collective-permute-start.35 = (bf16[128,1024]{1,0:T(8,128)(2,1)S(1)}, bf16[128,1024]{1,0:T(8,128)(2,1)S(1)}, u32[]{:S(2)}, u32[]{:S(2)}) collective-permute-start(bf16[128,1024]{1,0:T(8,128)(2,1)S(1)} %get-tuple-element.361), channel_id=1, source_target_pairs={{0,24},{4,28},{8,0},{12,4},{16,8},{20,12},{24,16},{28,20},{1,25},{... | collective-permute-start | bytes 786440 | tf_op jit(solution)/shard_map/ppermute | solution.py:941
  437.1 14.8 %collective-permute-start.31 = (bf16[128,1024]{1,0:T(8,128)(2,1)S(1)}, bf16[128,1024]{1,0:T(8,128)(2,1)S(1)}, u32[]{:S(2)}, u32[]{:S(2)}) collective-permute-start(bf16[128,1024]{1,0:T(8,128)(2,1)S(1)} %get-tuple-element.350), channel_id=1, source_target_pairs={{0,1},{1,2},{2,3},{3,0},{4,5},{5,6},{6,7},{7,4},{8,9},{9,10},{10,1... | collective-permute-start | bytes 786440 | tf_op jit(solution)/shard_map/ppermute | solution.py:909
  437.2 14.8 %collective-permute-start.32 = (bf16[128,1024]{1,0:T(8,128)(2,1)S(1)}, bf16[128,1024]{1,0:T(8,128)(2,1)S(1)}, u32[]{:S(2)}, u32[]{:S(2)}) collective-permute-start(bf16[128,1024]{1,0:T(8,128)(2,1)S(1)} %get-tuple-element.349), channel_id=1, source_target_pairs={{0,3},{1,0},{2,1},{3,2},{4,7},{5,4},{6,5},{7,6},{8,11},{9,8},{10,9... | collective-permute-start | bytes 786440 | tf_op jit(solution)/shard_map/ppermute | solution.py:910
  452.0 18.0 %copy-start.69 = (f32[10,512]{1,0:T(8,128)S(1)}, f32[10,512]{1,0:T(8,128)}, u32[]{:S(2)}) copy-start(f32[10,512]{1,0:T(8,128)} %copy-done.68) | copy-start | bytes 61444
  452.0 18.0 %copy-start.79 = (bf16[10,1024]{1,0:T(8,128)(2,1)S(1)}, bf16[10,1024]{1,0:T(8,128)(2,1)}, u32[]{:S(2)}) copy-start(bf16[10,1024]{1,0:T(8,128)(2,1)} %param.35) | copy-start | bytes 61444
  467.7 18.1 %collective-permute-start.36 = (bf16[512,1024]{1,0:T(8,128)(2,1)S(1)}, bf16[512,1024]{1,0:T(8,128)(2,1)}, u32[]{:S(2)}, u32[]{:S(2)}) collective-permute-start(bf16[512,1024]{1,0:T(8,128)(2,1)S(1)} %bitcast.201), channel_id=1, source_target_pairs={{0,4},{4,0},{8,12},{12,8},{16,20},{20,16},{24,28},{28,24},{1,5},{5... | collective-permute-start | bytes 3145736 | tf_op jit(solution)/shard_map/ppermute | solution.py:924
  (82 other events, 393.3 us)
Sparse Core Ops, SparseCore 0:
  53.3 52.8 all-gather.3
  108.7 27.8 all-gather.5
  236.9 83.4 all-reduce.7
  322.7 45.4 reduce-scatter.1

commit v4 on v3

--- a/solution.py
+++ b/solution.py
@@ -240,7 +240,7 @@
             pltpu.VMEM((1, tile), F32),
             pltpu.VMEM((8, LANES), F32),
         ],
-        compiler_params=pltpu.CompilerParams(vmem_limit_bytes=48 * 2**20),
+        compiler_params=pltpu.CompilerParams(vmem_limit_bytes=26 * 2**20),
         cost_estimate=work(count, sources * length, 2),
         name="attend_forward",
     )(meta, query, own, other, pre_key, pre_value)
@@ -386,10 +386,18 @@
             pltpu.VMEM((sources * length, LANES), F32),
             pltpu.VMEM((size, tile), F32),
         ],
-        compiler_params=pltpu.CompilerParams(vmem_limit_bytes=56 * 2**20),
+        compiler_params=pltpu.CompilerParams(vmem_limit_bytes=34 * 2**20),
         cost_estimate=work(query.shape[0] * width, sources * length, 5),
         name="attend_backward",
     )(meta, query, own, other, pre_key, pre_value, grad_out, out_full, log_total)
+
+
+def as_rows(columns):
+    lane = lax.broadcasted_iota(jnp.int32, (columns[0].shape[0], LANES), 1)
+    wide = jnp.zeros(lane.shape, F32)
+    for number, column in enumerate(columns):
+        wide = jnp.where(lane == number, column, wide)
+    return wide.T[:8]
 
 
 def turn_kernel(*refs):
@@ -452,16 +460,17 @@
 
 
 def unproject_kernel(
-    spot, came, weight, rows, stats, columns, own_grad,
-    flat, part, row_sums, sums, head_sums,
-    *, heads, size, step,
+    spot, came, weight, rows, stats, columns, own_grad, token_rows, reparam,
+    flat, part, first_up, first_down, head_row, prefix_low, *rest,
+    heads, size, step,
 ):
-    length = rows.shape[1]
+    *small, totals = rest
+    width, length = rows.shape
     half = step // 2
     past = length // 2
     gain = columns[:, 0:1]
-    sums[...] = jnp.zeros(sums.shape, F32)
-    head_sums[...] = jnp.zeros(head_sums.shape, F32)
+    row_sums = []
+    sums = [0.0, 0.0, 0.0]
     for piece in range(length // step):
         lanes = slice(piece * step, (piece + 1) * step)
         place = slice(piece * half, (piece + 1) * half)
@@ -473,7 +482,6 @@
             pieces += [came[first, :, pair], came[second, :, pair]]
         grads = jnp.concatenate(pieces, 0)
         flat[:, lanes] = grads
-        head_sums[...] += jnp.sum(grads.astype(F32), 1, keepdims=True)
         back = contract(weight[...], grads, 1, 0)
         part[:, lanes] = back.astype(BF16)
 
@@ -483,32 +491,150 @@
 
         normed = (rows[:, lanes].astype(F32) - stats[0:1, lanes]) * stats[1:2, lanes]
         scaled = back * gain
-        row_sums[0:1, lanes] = jnp.sum(scaled, 0, keepdims=True)
-        row_sums[1:2, lanes] = jnp.sum(scaled * normed, 0, keepdims=True)
-        sums[:, 0:1] += jnp.sum(back * normed, 1, keepdims=True)
-        sums[:, 1:2] += jnp.sum(back, 1, keepdims=True)
-
-
-def unproject(spot, came, weight, rows, stats, columns, own_grad, heads, size, step):
+        row_sums.append(
+            [jnp.sum(values, 0, keepdims=True) for values in (scaled, scaled * normed)]
+        )
+        for number, values in enumerate((back * normed, back, grads.astype(F32))):
+            sums[number] += jnp.sum(values, 1, keepdims=True)
+    count = first_up.shape[0]
+    blocks = width // (2 * count)
+    for block in range(blocks):
+        row = 2 * count * block
+
+        @pl.when(lax.rem(spot[0] + blocks - 1, blocks) == block)
+        def _():
+            first_up[...] = part[row : row + count]
+
+        @pl.when(lax.rem(spot[0] + 1, blocks) == block)
+        def _():
+            first_down[...] = part[row + count : row + 2 * count]
+
+    head_row[...] = as_rows(sums[2:])[:1]
+    totals[...] = as_rows(sums[:2])
+    found = []
+    for head in range(heads):
+        both = came[2 * head, :, 3 * past :].astype(F32) + came[2 * head + 1, :, 3 * past :].astype(F32)
+        both = both.T
+        found += [both[:PAD], both[PAD : 2 * PAD]]
+    low = jnp.concatenate(found, 1).astype(BF16)
+    prefix_low[...] = low
+    hidden = contract(low, reparam[...], 1, 1)
+    features = 2 * count
+    for number, target in enumerate(small):
+        start = pl.multiple_of(lax.rem(spot[0] + number, blocks) * features, features)
+        target[0:2] = totals[0:2, pl.ds(start, features)]
+        target[2:5] = token_rows[0:3, pl.ds(start, features)]
+        target[5:8] = jnp.zeros((3, features), F32)
+        for which in range(2):
+            for piece in range(blocks):
+                row = 8 + which * blocks + piece
+                target[row : row + 1] = row_sums[piece][which]
+        for piece in range(hidden.shape[1] // features):
+            row = 8 + 2 * blocks + piece * PAD
+            target[row : row + PAD] = hidden[:, piece * features : (piece + 1) * features]
+
+
+def unproject(spot, came, weight, rows, stats, columns, own_grad, token_rows, reparam, heads, size, step):
     width, length = rows.shape
+    blocks = length // step
+    features = width // blocks
     mixed = 3 * heads * size
+    small = 8 + 2 * blocks + reparam.shape[0] // features * PAD
+    first = jax.ShapeDtypeStruct((features // 2, length), BF16)
     return pl.pallas_call(
         functools.partial(unproject_kernel, heads=heads, size=size, step=step),
         out_shape=(
             jax.ShapeDtypeStruct((mixed, length), BF16),
             jax.ShapeDtypeStruct((width, length), BF16),
-            jax.ShapeDtypeStruct((2, length), F32),
-            jax.ShapeDtypeStruct((width, 2), F32),
-            jax.ShapeDtypeStruct((mixed, 1), F32),
-        ),
-        in_specs=[SM] + [VM] * 6,
-        out_specs=(VM,) * 5,
+            first,
+            first,
+            jax.ShapeDtypeStruct((1, mixed), F32),
+            jax.ShapeDtypeStruct((PAD, 2 * heads * size), BF16),
+        )
+        + (jax.ShapeDtypeStruct((small, features), F32),) * blocks,
+        in_specs=[SM] + [VM] * 8,
+        out_specs=(VM,) * (6 + blocks),
+        scratch_shapes=[pltpu.VMEM((8, width), F32)],
         compiler_params=pltpu.CompilerParams(vmem_limit_bytes=20 * 2**20),
         cost_estimate=pl.CostEstimate(
             flops=4 * mixed * width * length, bytes_accessed=2**23, transcendentals=0
         ),
         name="unproject",
-    )(spot, came, weight, rows, stats, columns, own_grad)
+    )(spot, came, weight, rows, stats, columns, own_grad, token_rows, reparam)
+
+
+def small_kernel(*refs, blocks, width, hidden_rows):
+    pieces = refs[:blocks]
+    down_row, up_row, head_row, row_sums, hidden, late = refs[blocks:]
+    total = sum(piece[...] for piece in pieces)
+    features = total.shape[1]
+    for which in range(2):
+        for piece in range(blocks):
+            row = 8 + which * blocks + piece
+            lanes = slice(piece * features, (piece + 1) * features)
+            row_sums[which : which + 1, lanes] = total[row : row + 1] / width
+    for piece in range(hidden.shape[1] // features):
+        row = 8 + 2 * blocks + piece * PAD
+        hidden[:, piece * features : (piece + 1) * features] = total[row : row + PAD]
+    late[...] = jnp.zeros(late.shape, F32)
+    late[0:5] = total[0:5]
+    late[5:6] = down_row[...]
+    row = 6
+    for source in (up_row, head_row):
+        for piece in range(source.shape[1] // features):
+            late[row : row + 1] = source[:, piece * features : (piece + 1) * features]
+            row += 1
+
+
+def small_totals(pieces, down_row, up_row, head_row, rows, hidden_width, width):
+    features = pieces[0].shape[1]
+    late = 6 + (up_row.shape[1] + head_row.shape[1]) // features
+    return pl.pallas_call(
+        functools.partial(
+            small_kernel, blocks=len(pieces), width=width, hidden_rows=hidden_width
+        ),
+        out_shape=(
+            jax.ShapeDtypeStruct((2, rows), F32),
+            jax.ShapeDtypeStruct((PAD, hidden_width), F32),
+            jax.ShapeDtypeStruct((-(-late // 8) * 8, features), F32),
+        ),
+        in_specs=[VM] * (len(pieces) + 3),
+        out_specs=(VM,) * 3,
+        compiler_params=pltpu.CompilerParams(vmem_limit_bytes=8 * 2**20),
+        name="small_totals",
+    )(*pieces, down_row, up_row, head_row)
+
+
+def late_kernel(parts, vectors, up, pairs, *, heads, size):
+    total = sum(parts[n] for n in range(parts.shape[0]))
+    features = total.shape[1]
+    vectors[...] = total[:8]
+    count = up.shape[1] // features
+    up[...] = jnp.concatenate([total[6 + n : 7 + n] for n in range(count)], 1)
+    mixed = 3 * heads * size
+    row = jnp.concatenate(
+        [total[6 + count + n : 7 + count + n] for n in range(mixed // features)], 1
+    )
+    for head in range(heads):
+        start = 3 * size * head
+        pairs[head : head + 1] = jnp.concatenate(
+            [row[:, start : start + size], row[:, start + 2 * size : start + 3 * size]], 1
+        )
+
+
+def late_totals(parts, inner, heads, size):
+    return pl.pallas_call(
+        functools.partial(late_kernel, heads=heads, size=size),
+        out_shape=(
+            jax.ShapeDtypeStruct((8, parts.shape[2]), F32),
+            jax.ShapeDtypeStruct((1, inner), F32),
+            jax.ShapeDtypeStruct((heads, 2 * size), F32),
+        ),
+        in_specs=[VM],
+        out_specs=(VM,) * 3,
+        compiler_params=pltpu.CompilerParams(vmem_limit_bytes=8 * 2**20),
+        name="late_totals",
+    )(parts)
 
 
 def finish_kernel(up, down, own_up, own_down, rows, gain, stats, row_sums, grad):
@@ -602,7 +728,8 @@
         weights(grad_up, lambda n: rows[n], lambda n, tile: grad_pre[n, tile], inner)
     else:
         weights(grad_up, lambda n: grad_pre[n], lambda n, tile: rows[n, tile], width)
-    bias[...] = sum(jnp.sum(grad_pre[n].astype(F32), 1, keepdims=True) for n in range(blocks))
+    total = sum(jnp.sum(grad_pre[n].astype(F32), 1, keepdims=True) for n in range(blocks))
+    bias[...] = as_rows([total])[:1]
 
 
 def feed_weights(rows, grads, hidden, grad_pre):
@@ -613,7 +740,7 @@
         out_shape=(
             jax.ShapeDtypeStruct((inner, width), BF16),
             jax.ShapeDtypeStruct((inner, width), BF16),
-            jax.ShapeDtypeStruct((inner, 1), F32),
+            jax.ShapeDtypeStruct((1, inner), F32),
         ),
         in_specs=[VM] * 4,
         out_specs=(VM,) * 3,
@@ -733,9 +860,9 @@
                 sent[(2 * head + rank) * tensors + block] = back[
                     row : row + size, rank * half : (rank + 1) * half
                 ]
-    sums[:, 0:1] = jnp.sum(total * normed[...], 1, keepdims=True)
-    sums[:, 1:2] = jnp.sum(total, 1, keepdims=True)
-    sums[:, 2:3] = jnp.sum(result, 1, keepdims=True)
+    sums[...] = as_rows(
+        [jnp.sum(values, 1, keepdims=True) for values in (total * normed[...], total, result)]
+    )
 
 
 def leave(spot, terms, normed, inverse, grads, weight, columns, heads, size):
@@ -746,7 +873,7 @@
         out_shape=(
             jax.ShapeDtypeStruct((width, count), F32),
             jax.ShapeDtypeStruct((width, count), BF16),
-            jax.ShapeDtypeStruct((width, 3), F32),
+            jax.ShapeDtypeStruct((8, width), F32),
             jax.ShapeDtypeStruct((2 * blocks, size, count // 2), BF16),
         ),
         in_specs=[SM] + [VM] * 9,
@@ -792,28 +919,29 @@
     )(spot, flat, full, out)
 
 
-def rest_whole_kernel(spot, half, other, mixed, out):
-    rows = half.shape[0]
-    extra = mixed.shape[0] - rows
-
-    def write(first, second):
-        mixed[:rows] = first[...].astype(F32)
-        mixed[rows:] = second[:extra].astype(F32)
-        out[...] = second[extra:].astype(F32)
-
-    @pl.when(spot[1] == 0)
-    def _():
-        write(half, other)
-
-    @pl.when(spot[1] == 1)
-    def _():
-        write(other, half)
-
-
-def rest_whole(spot, half, other, rows):
+def rest_whole_kernel(spot, half, other, mixed, out, *, chips):
+    step = half.shape[0] // chips
+    edge = mixed.shape[0] // step
+    for piece in range(chips):
+        owner = lax.rem(spot[2] + chips - piece, chips)
+        rows = slice(piece * step, (piece + 1) * step)
+        for source, core in ((half, spot[1]), (other, 1 - spot[1])):
+            block = core * chips + owner
+            values = source[rows].astype(F32)
+
+            @pl.when(block < edge)
+            def _():
+                mixed[pl.ds(pl.multiple_of(jnp.minimum(block, edge - 1) * step, step), step)] = values
+
+            @pl.when(block >= edge)
+            def _():
+                out[pl.ds(pl.multiple_of(jnp.maximum(block - edge, 0) * step, step), step)] = values
+
+
+def rest_whole(spot, half, other, rows, chips):
     width = half.shape[1]
     return pl.pallas_call(
-        rest_whole_kernel,
+        functools.partial(rest_whole_kernel, chips=chips),
         out_shape=(
             jax.ShapeDtypeStruct((rows, width), F32),
             jax.ShapeDtypeStruct((2 * half.shape[0] - rows, width), F32),
@@ -825,8 +953,9 @@
     )(spot, half, other)
 
 
-def prefix_kernel(total, hidden, embed, weight, grad_embed, grad_weight, grad_bias):
-    rows = hidden.shape[0]
+def prefix_kernel(
+    total, hidden, embed, weight, low, grad_embed, grad_weight, grad_bias, grad_out, grad_out_bias
+):
     pre = total[...] * (1.0 - hidden[...] * hidden[...])
     grad_bias[...] = jnp.sum(pre, 0, keepdims=True)
 
@@ -836,29 +965,40 @@
             preferred_element_type=F32, precision=HIGHEST,
         )
 
-    wide = embed[...].astype(F32)
-    grad_weight[...] = exact(wide, pre, (0, 0))
-    grad_embed[...] = exact(pre, weight[...].astype(F32), (1, 1))[:rows]
-
-
-def prefix_back(total, hidden, embed, weight):
+    grad_weight[...] = exact(embed[...].astype(F32), pre, (0, 0))
+    grad_embed[...] = exact(pre, weight[...].astype(F32), (1, 1))
+    wide = low[...].astype(F32)
+    result = exact(hidden[...], wide, (0, 0))
+    sums = jnp.sum(wide, 0, keepdims=True)
+    each = grad_out.shape[2]
+    for head in range(grad_out.shape[1]):
+        lanes = slice(head * each, (head + 1) * each)
+        grad_out[:, head, :] = result[:, lanes]
+        grad_out_bias[head : head + 1] = sums[:, lanes]
+
+
+def prefix_back(total, hidden, embed, weight, low, heads):
     rows, width = embed.shape
-    extra = -rows % 8
-    total, hidden = [jnp.pad(a, ((0, extra), (0, 0))) for a in (total, hidden)]
+    extra = PAD - rows
+    hidden = jnp.pad(hidden, ((0, extra), (0, 0)))
     embed = jnp.pad(embed, ((0, extra), (0, 0)))
-    grad_embed, grad_weight, grad_bias = pl.pallas_call(
+    inner = weight.shape[1]
+    each = low.shape[1] // heads
+    grad_embed, grad_weight, grad_bias, grad_out, grad_out_bias = pl.pallas_call(
         prefix_kernel,
         out_shape=(
-            jax.ShapeDtypeStruct((rows + extra, width), F32),
+            jax.ShapeDtypeStruct((PAD, width), F32),
             jax.ShapeDtypeStruct(weight.shape, F32),
-            jax.ShapeDtypeStruct((1, weight.shape[1]), F32),
-        ),
-        in_specs=[VM] * 4,
-        out_specs=(VM,) * 3,
-        compiler_params=pltpu.CompilerParams(vmem_limit_bytes=12 * 2**20),
+            jax.ShapeDtypeStruct((1, inner), F32),
+            jax.ShapeDtypeStruct((inner, heads, each), F32),
+            jax.ShapeDtypeStruct((heads, each), F32),
+        ),
+        in_specs=[VM] * 5,
+        out_specs=(VM,) * 5,
+        compiler_params=pltpu.CompilerParams(vmem_limit_bytes=16 * 2**20),
         name="prefix_back",
-    )(total, hidden, embed, weight)
-    return grad_embed[:rows], grad_weight, grad_bias[0]
+    )(total, hidden, embed, weight, low)
+    return grad_embed[:rows], grad_weight, grad_bias[0], grad_out, grad_out_bias
 
 
 def spread(values, axis):
@@ -895,7 +1035,7 @@
     return (out, results) if beside else out
 
 
-def ring_terms(blocks, axis, beside=()):
+def ring_terms(blocks, axis, beside=(), first=None):
     count, place = lax.axis_size(axis), lax.axis_index(axis)
     half = blocks.shape[1] // 2
 
@@ -903,7 +1043,7 @@
         block = lax.dynamic_index_in_dim(blocks, (place + offset) % count, 0, keepdims=False)
         return block[half:] if upper else block[:half]
 
-    up, down = own(-1, False), own(1, True)
+    up, down = first or (own(-1, False), own(1, True))
     state = None
     for step in range(1, count):
         up = lax.ppermute(up, axis, ring(axis, 1))
@@ -924,12 +1064,7 @@
     return lax.ppermute(values, "seq", pairs)
 
 
-def chip_groups():
-    chips = lax.axis_size("seq") // 2
-    return [[2 * chip + core for chip in range(chips)] for core in range(2)]
-
-
-def chip_parts_direct(half):
+def chip_parts(half):
     count = lax.axis_size("seq")
     chips = count // 2
     chip = lax.axis_index("seq") // 2
@@ -951,14 +1086,10 @@
     return parts
 
 
-def chip_copies(parts):
+def chip_gather(parts):
     part = sum(part.astype(F32) for part in parts).astype(BF16)
-    return jnp.broadcast_to(part[None], (len(parts),) + part.shape)
-
-
-def chip_gather(copies):
-    half = lax.all_to_all(copies, "seq", 0, 0, axis_index_groups=chip_groups(), tiled=True)
-    return half.reshape(-1, half.shape[2])
+    behind = [lax.ppermute(part, "seq", ring("seq", 2 * step)) for step in range(1, len(parts))]
+    return jnp.concatenate([part] + behind, 0)
 
 
 def spread_direct(values, axis):
@@ -972,11 +1103,19 @@
 
 
 def core_gather(half):
-    core = lax.axis_index("seq") % 2
-    other = swapped(half)
+    core, chip = lax.axis_index("seq") % 2, lax.axis_index("seq") // 2
+    chips = lax.axis_size("seq") // 2
+    order = (chip - jnp.arange(chips)) % chips
+
+    def sorted_parts(values):
+        parts = values.reshape(chips, -1, values.shape[1])
+        picked = [lax.dynamic_index_in_dim(parts, order[n], 0) for n in range(chips)]
+        return jnp.concatenate(picked, 0).reshape(values.shape)
+
+    half, other = sorted_parts(half), sorted_parts(swapped(half))
     first = jnp.where(core == 0, half, other)
     second = jnp.where(core == 0, other, half)
-    return first, second
+    return jnp.concatenate([first, second], 0)
 
 
 def regrouped(values, width):
@@ -1063,7 +1202,7 @@
     out_share = w_out.reshape(seqs, heads * size // seqs, width)
     out_share = lax.dynamic_index_in_dim(out_share, place, 0, keepdims=False)
     core = place % 2
-    spot = jnp.stack([slot, core]).astype(jnp.int32)
+    spot = jnp.stack([slot, core, place // 2]).astype(jnp.int32)
 
     prefix_hidden = jnp.tanh(
         jnp.dot(prefix_embed, reparam_in, preferred_element_type=F32)
@@ -1209,9 +1348,12 @@
         (came, output_act, grad_w_out, out_w_down, out_w_up)
     )
     if paired:
-        grad_flat, grad_part, row_sums, sums1, head_sums = unproject(
-            spot, came, late_flat, full_tokens, stats, columns, grad_middle, heads, size, own_rows
+        grad_flat, grad_part, first_up, first_down, head_row, prefix_low, *small = unproject(
+            spot, came, late_flat, full_tokens, stats, columns, grad_middle, token_sums,
+            reparam_out.reshape(reparam_out.shape[0], -1), heads, size, own_rows,
         )
+        first_blocks = first_up, first_down
+        mine, other = rest_halves(spot, grad_flat, full1, grad_w_out)
     else:
         query_part = came[:, :, :tokens_head].reshape(heads, group, size, tensors, chunk)
         query_part = query_part.transpose(0, 2, 3, 1, 4).reshape(heads, 1, size, rows)
@@ -1230,81 +1372,93 @@
         own_part = own_part + grad_middle / (own_inverse * columns[:, 0:1])
         back = lax.dynamic_update_slice_in_dim(back, own_part, slot * own_rows, 1)
         grad_part = back.astype(BF16)
-    prefix_low = came[:, :, 3 * tokens_head : 3 * tokens_head + 2 * PAD].astype(F32)
-    prefix_low = jnp.sum(prefix_low.reshape(heads, group, size, 2, PAD), 1)[..., :prefix]
-    prefix_low = prefix_low.transpose(3, 0, 2, 1).reshape(prefix, heads, 2 * size).astype(BF16)
-    prefix_grad = prefix_low.astype(F32)
-    hidden_part = jnp.einsum("phe,ahe->pa", prefix_low, reparam_out, preferred_element_type=F32)
-    owned = jnp.concatenate([sums1, token_sums], 1).T
-    owned = owned.reshape(-1, tensors, features).transpose(1, 0, 2).reshape(tensors, -1)
-    shared = jnp.concatenate([row_sums.reshape(-1), hidden_part.reshape(-1)])
-    shared = jnp.broadcast_to(shared[None], (tensors, shared.shape[0]))
-    small = jnp.concatenate([owned, shared], 1)[:, None, :]
-
-    grad_b_down = jnp.sum(out_grad.astype(F32), 0)
-    head_sums = head_sums.reshape(heads, 3, size)
-
-    def halves_here(_):
-        if paired:
-            return rest_halves(spot, grad_flat, full1, grad_w_out)
+        first_blocks = None
         grad_w_qkv = contract(grad_flat, full1, 1, 1).astype(BF16)
         rest = jnp.concatenate([grad_w_qkv, grad_w_out], 0)
         halves = rest.reshape(2, rest.shape[0] // 2, width)
         mine = lax.dynamic_index_in_dim(halves, core, 0, keepdims=False)
         other = lax.dynamic_index_in_dim(halves, 1 - core, 0, keepdims=False)
-        return mine, other
-
-    def small_here(state):
-        return state[0], swapped(state[1]), owned_direct(small, "tensor")
+
+    if not paired:
+        prefix_low = came[:, :, 3 * tokens_head : 3 * tokens_head + 2 * PAD].astype(F32)
+        prefix_low = jnp.sum(prefix_low.reshape(heads, group, size, 2, PAD), 1)
+        prefix_low = prefix_low.transpose(3, 0, 2, 1).reshape(PAD, -1).astype(BF16)
+        hidden_part = contract(prefix_low, reparam_out.reshape(reparam_out.shape[0], -1), 1, 1)
+        owned = jnp.concatenate([sums1.T, token_sums.T], 0)
+        owned = owned.reshape(-1, tensors, features).transpose(1, 0, 2).reshape(tensors, -1)
+        shared = jnp.concatenate([row_sums.reshape(-1), hidden_part.reshape(-1)])
+        shared = jnp.broadcast_to(shared[None], (tensors, shared.shape[0]))
+        small = jnp.concatenate([owned, shared], 1)[:, None, :]
+
+    grad_b_down = jnp.sum(out_grad.astype(F32), 0)
+
+    def small_here(_):
+        if not paired:
+            return swapped(other), owned_direct(small, "tensor")
+        pieces = [small[0]]
+        for step in range(1, tensors):
+            pieces.append(lax.ppermute(small[step], "tensor", ring("tensor", step)))
+        return swapped(other), pieces
 
     def parts_here(state):
-        half = (state[0].astype(F32) + state[1].astype(F32)).astype(BF16)
-        sums = sum(state[2])[0]
-        late = jnp.concatenate(
-            [
-                sums[: 5 * features],
-                grad_b_down,
-                grad_b_up.reshape(-1),
-                head_sums[:, 0].reshape(-1),
-                head_sums[:, 2].reshape(-1),
-            ]
-        )
-        return chip_parts_direct(half), sums, spread(late[None], "seq")
-
-    last_terms, (rest_parts, small, late) = ring_terms(
+        half = (mine.astype(F32) + state[0].astype(F32)).astype(BF16)
+        if paired:
+            sums = small_totals(
+                state[1], grad_b_down[None], grad_b_up, head_row, rows,
+                prefix_hidden.shape[1], width,
+            )
+            return chip_parts(half), sums
+        sums = sum(state[1])[0]
+        after_rows = 5 * features + 2 * rows
+        row_means = sums[5 * features : after_rows].reshape(2, rows) / width
+        hidden = sums[after_rows:].reshape(PAD, -1)
+        mixed_sums = head_sums.reshape(heads, 3, size)
+        late = [sums[: 5 * features], grad_b_down, grad_b_up[0]]
+        late += [mixed_sums[:, 0].reshape(-1), mixed_sums[:, 2].reshape(-1)]
+        return chip_parts(half), (row_means, hidden, jnp.concatenate(late)[None])
+
+    def gather_here(state):
+        return chip_gather(state[0]), state[1], spread(state[1][2], "seq")
+
+    last_terms, (rest_half, (row_means, hidden_grad, _), late) = ring_terms(
         grad_part.reshape(tensors, features, rows),
         "tensor",
-        (halves_here, small_here) + (lambda state: state,) * (tensors - 4) + (parts_here,),
-    )
-    rest_half = chip_gather(chip_copies(rest_parts))
-    late = jnp.sum(late, 0)[0]
-    row_sums = small[5 * features : 5 * features + 2 * rows]
-    hidden_grad = small[5 * features + 2 * rows :].reshape(prefix_hidden.shape)
+        (small_here, parts_here) + (lambda state: state,) * (tensors - 4) + (gather_here,),
+        first_blocks,
+    )
     input_grad = finish(
-        *last_terms, own_tokens, ln1_gain.astype(F32)[:, None], stats,
-        row_sums.reshape(2, rows) / width,
+        *last_terms, own_tokens, ln1_gain.astype(F32)[:, None], stats, row_means,
     )
     mixed_rows = heads * 3 * size
     if paired:
-        out_w_qkv, out_w_out = rest_whole(spot, rest_half, swapped(rest_half), mixed_rows)
+        out_w_qkv, out_w_out = rest_whole(
+            spot, rest_half, swapped(rest_half), mixed_rows, seqs // 2
+        )
     else:
-        rest = jnp.concatenate(core_gather(rest_half), 0).astype(F32)
+        rest = core_gather(rest_half).astype(F32)
         out_w_qkv, out_w_out = rest[:mixed_rows], rest[mixed_rows:]
     out_w_qkv = out_w_qkv.reshape(heads, 3 * size, width).transpose(2, 0, 1)
     out_w_out = out_w_out.reshape(heads, size, width)
+    if paired:
+        vectors, out_b_up, out_b_qv = late_totals(late, inner, heads, size)
+        out_b_up = out_b_up[0]
+    else:
+        late = jnp.sum(late, 0)[0]
+        vectors = late[: 6 * features].reshape(6, features)
+        out_b_up = late[6 * features : 6 * features + inner]
+        pair_sums = late[6 * features + inner :].reshape(2, heads, size)
+        out_b_qv = jnp.concatenate([pair_sums[0], pair_sums[1]], 1)
     out_ln1_gain, out_ln1_bias, out_ln2_gain, out_ln2_bias, out_b_out, out_b_down = [
-        late[i * features : (i + 1) * features] for i in range(6)
+        vectors[i] for i in range(6)
     ]
-    late = late[6 * features :]
-    out_b_up = late[:inner]
-    pair_sums = late[inner:].reshape(2, heads, size)
-    out_b_qv = jnp.concatenate([pair_sums[0], pair_sums[1]], 1)
-
-    grad_reparam_out = jnp.einsum("pa,phe->ahe", prefix_hidden, prefix_grad, precision=HIGHEST)
-    grad_reparam_out_bias = jnp.sum(prefix_grad, 0)
-    grad_prefix_embed, grad_reparam_in, grad_reparam_in_bias = prefix_back(
-        hidden_grad, prefix_hidden, prefix_embed, reparam_in
-    )
+
+    (
+        grad_prefix_embed,
+        grad_reparam_in,
+        grad_reparam_in_bias,
+        grad_reparam_out,
+        grad_reparam_out_bias,
+    ) = prefix_back(hidden_grad, prefix_hidden, prefix_embed, reparam_in, prefix_low, heads)
     return (
         output_act,
         input_grad,

time: 506 us -> 484 us (0.957)
  blocking collectives: 26.4 us -> 0 us
  starting transfers between devices: 83.8 us -> 97.3 us
  local copies, waits for them, and re-layouts: 72.2 us -> 60.8 us
  waiting for transfers between devices: 121 us -> 129 us
  other arithmetic: 26.2 us -> 20.8 us
    all_to_all x2 -> x0, blocking collectives: 26.4 us -> none  [the longest x1 15.3 us: chip_gather(): lax.all_to_all(copies, 'seq', 0, 0, axis_index_groups=chip_groups(), tile...]
    ppermute x6 -> x9, waiting for transfers between devices: 12.3 us -> 20 us  [the longest x3 13.3 us: small_here(): pieces.append(lax.ppermute(small[step], 'tensor', ring('tensor', step)))]
    all_to_all x2 -> x3, starting transfers between devices: 9.95 us -> 17.2 us  [spread(): return lax.all_to_all(copies, axis, 0, 0, tiled=True)]
    unnamed x204 -> x179, local copies, waits for them, and re-layouts: 43.7 us -> 36.7 us
  transfers between devices with their start and end apart: 48 -> 52, of which waited for: 26 -> 28; matrix products, arithmetic and copies ran while one was open for 10% -> 9% of each run, Pallas kernels for 24% -> 25%
where the time goes in v4:
time: 484 us; the launch traced here: 475 us
  Pallas kernels  148 us (31%)
  waiting for transfers between devices  129 us (27%)
  starting transfers between devices  97.3 us (20%)
  local copies, waits for them, and re-layouts  60.8 us (13%)
  other arithmetic  20.8 us (4%)
  between operations  15.5 us (3%)
    pallas_call x1, Pallas kernels, attend_backward(): pl.pallas_call(functools.partial(backward_kernel, tile=tile, keys=keys, p...  58.9 us
    unnamed x179, local copies, waits for them, and re-layouts  36.7 us
    pallas_call x1, Pallas kernels, attend_forward(): pl.pallas_call(functools.partial(forward_kernel, tile=tile, keys=keys, pr...  32.7 us
    ppermute x6, waiting for transfers between devices, ring_gather(): down = lax.ppermute(down, axis, ring(axis, -1))  26.8 us
    ppermute x6, waiting for transfers between devices, ring_gather(): up = lax.ppermute(up, axis, ring(axis, 1))  24.6 us
    all_to_all x3, starting transfers between devices, spread(): return lax.all_to_all(copies, axis, 0, 0, tiled=True)  17.2 us
    ppermute x6, starting transfers between devices, ring_terms(): down = lax.ppermute(down, axis, ring(axis, -1))  13.4 us
    ppermute x3, waiting for transfers between devices, small_here(): pieces.append(lax.ppermute(small[step], 'tensor', ring('tensor', step)))  13.3 us
  transfers between devices with their start and end apart: 52, of which 28 were waited for; matrix products, arithmetic and copies ran while one was open for 9% of the time, Pallas kernels for 25%

profile of v4, /device:TPU:1, one launch (start us, length us, event | category | flops | bytes accessed | tf_op | source)
XLA Modules:
  0.0 475.0 jit_solution(8983303924002658922)
XLA Ops:
  11.4 2.1 collective-permute-start
  13.5 2.0 collective-permute-start.2
  16.3 3.3 all-to-all-start
  21.8 5.2 %collective-permute-done.2 = bf16[128,1024]{1,0:T(8,128)(2,1)} collective-permute-done((bf16[128,1024]{1,0:T(8,128)(2,1)}, bf16[128,1024]{1,0:T(8,128)(2,1)}, u32[]{:S(2)}, u32[]{:S(2)}) %collective-permute-start.2) | collective-permute-done | bytes 262176 | tf_op jit(solution)/shard_map/ppermute | solution.py:1029
  30.2 6.7 %all-to-all-start.1 = ((s32[8,4,128]{2,1,0:T(4,128)}), s32[8,4,128]{2,1,0:T(4,128)S(1)}, u32[]{:S(2)}, u32[]{:S(2)}) async-start(s32[8,4,128]{2,1,0:T(4,128)} %broadcast_in_dim_broadcast_in_dim_broadcast_in_dim.2), calls=%async_computation.1 | async-start | bytes 32768 | tf_op jit(solution)/shard_map/all_to_all | solution.py:1007
  36.9 2.9 collective-permute-done.3
  39.7 3.3 collective-permute-start.5
  43.1 5.9 %collective-permute-done.4 = bf16[128,1024]{1,0:T(8,128)(2,1)S(1)} collective-permute-done((bf16[128,1024]{1,0:T(8,128)(2,1)S(1)}, bf16[128,1024]{1,0:T(8,128)(2,1)S(1)}, u32[]{:S(2)}, u32[]{:S(2)}) %collective-permute-start.4) | collective-permute-done | bytes 262176 | tf_op jit(solution)/shard_map/ppermute | solution.py:1028
  49.0 3.2 collective-permute-done.5
  56.9 3.2 project.1
  63.1 6.3 %all-to-all-start.2 = ((bf16[8,64,1536]{2,1,0:T(8,128)(2,1)}), bf16[8,64,1536]{2,1,0:T(8,128)(2,1)}, u32[]{:S(2)}, u32[]{:S(2)}) async-start(bf16[8,64,1536]{2,1,0:T(8,128)(2,1)} %copy-done.25), calls=%async_computation.2 | async-start | bytes 3145728 | tf_op jit(solution)/shard_map/all_to_all | solution.py:1242
  69.6 2.2 collective-permute-start.7
  71.7 2.3 collective-permute-start.8
  74.1 2.5 collective-permute-done.6
  76.6 4.8 %collective-permute-done.7 = bf16[32,1024]{1,0:T(8,128)(2,1)S(1)} collective-permute-done((bf16[32,1024]{1,0:T(8,128)(2,1)S(1)}, bf16[32,1024]{1,0:T(8,128)(2,1)S(1)}, u32[]{:S(2)}, u32[]{:S(2)}) %collective-permute-start.7) | collective-permute-done | bytes 65568 | tf_op jit(solution)/shard_map/ppermute | solution.py:1100
  81.5 5.5 %all-to-all-done.2.query.own = bf16[8,64,1536]{2,1,0:T(8,128)(2,1)} async-done(((bf16[8,64,1536]{2,1,0:T(8,128)(2,1)}), bf16[8,64,1536]{2,1,0:T(8,128)(2,1)}, u32[]{:S(2)}, u32[]{:S(2)}) %all-to-all-start.2) | async-done | bytes 1572896 | tf_op jit(solution)/shard_map/all_to_all | solution.py:1242
  87.0 3.6 collective-permute-start.9
  91.8 2.2 collective-permute-done.9.other
  94.0 32.7 %attend_forward.1 = (bf16[32,64,128]{2,1,0:T(8,128)(2,1)S(1)}, f32[32,64,128]{2,1,0:T(8,128)S(1)}, f32[8,1,512]{2,1,0:T(1,128)S(1)}) custom-call(s32[5]{0:T(128)S(1)} %pad_add_fusion.meta, bf16[8,64,1536]{2,1,0:T(8,128)(2,1)} %all-to-all-done.2.query.own, bf16[8,64,1536]{2,1,0:T(8,128)(2,1)} %all-to-all-done.2.query.own, ...), custom_call_target="tpu_custom_call" | custom-call | flops 17179869184 | bytes 8388608 | tf_op jit(solution)/shard_map/attend_forward/pallas_call | solution.py:224
  128.5 2.9 all-to-all-start.3
  132.1 2.5 copy.93
  134.6 3.9 copy.94
  140.3 6.4 %all-to-all-done.3.came = bf16[32,64,128]{2,1,0:T(8,128)(2,1)S(1)} async-done(((bf16[32,64,128]{2,1,0:T(8,128)(2,1)}), bf16[32,64,128]{2,1,0:T(8,128)(2,1)S(1)}, u32[]{:S(2)}, u32[]{:S(2)}) %all-to-all-start.3) | async-done | bytes 524320 | tf_op jit(solution)/shard_map/all_to_all | solution.py:1263
  154.8 3.2 collective-permute-start.11
  158.2 5.6 %collective-permute-done.10 = bf16[512,256]{1,0:T(8,128)(2,1)S(1)} collective-permute-done((bf16[512,256]{1,0:T(8,128)(2,1)}, bf16[512,256]{1,0:T(8,128)(2,1)S(1)}, u32[]{:S(2)}, u32[]{:S(2)}) %collective-permute-start.10) | collective-permute-done | bytes 262176 | tf_op jit(solution)/shard_map/ppermute | solution.py:1028
  163.8 4.4 collective-permute-done.11
  169.1 6.0 %collective-permute-done.12 = bf16[512,256]{1,0:T(8,128)(2,1)S(1)} collective-permute-done((bf16[512,256]{1,0:T(8,128)(2,1)S(1)}, bf16[512,256]{1,0:T(8,128)(2,1)S(1)}, u32[]{:S(2)}, u32[]{:S(2)}) %collective-permute-start.12) | collective-permute-done | bytes 262176 | tf_op jit(solution)/shard_map/ppermute | solution.py:1028
  175.1 5.6 %collective-permute-done.13 = bf16[512,256]{1,0:T(8,128)(2,1)S(1)} collective-permute-done((bf16[512,256]{1,0:T(8,128)(2,1)S(1)}, bf16[512,256]{1,0:T(8,128)(2,1)S(1)}, u32[]{:S(2)}, u32[]{:S(2)}) %collective-permute-start.13) | collective-permute-done | bytes 262176 | tf_op jit(solution)/shard_map/ppermute | solution.py:1029
  180.7 5.6 %collective-permute-done.14 = bf16[512,256]{1,0:T(8,128)(2,1)S(1)} collective-permute-done((bf16[512,256]{1,0:T(8,128)(2,1)S(1)}, bf16[512,256]{1,0:T(8,128)(2,1)S(1)}, u32[]{:S(2)}, u32[]{:S(2)}) %collective-permute-start.14) | collective-permute-done | bytes 262176 | tf_op jit(solution)/shard_map/ppermute | solution.py:1028
  186.4 5.5 %collective-permute-done.15 = bf16[512,256]{1,0:T(8,128)(2,1)S(1)} collective-permute-done((bf16[512,256]{1,0:T(8,128)(2,1)S(1)}, bf16[512,256]{1,0:T(8,128)(2,1)S(1)}, u32[]{:S(2)}, u32[]{:S(2)}) %collective-permute-start.15) | collective-permute-done | bytes 262176 | tf_op jit(solution)/shard_map/ppermute | solution.py:1029
  194.6 11.9 %feed.1 = (bf16[4,1024,256]{2,1,0:T(8,128)(2,1)S(1)}, bf16[4,1024,256]{2,1,0:T(8,128)(2,1)S(1)}, bf16[4,1024,256]{2,1,0:T(8,128)(2,1)S(1)}) custom-call(bf16[4,1024,256]{2,1,0:T(8,128)(2,1)S(1)} %bitcast_dynamic-update-slice_fusion.2.rows, bf16[1024,1024]{1,0:T(8,128)(2,1)S(1)} %copy-done.15, bf16[1024,1024]{1,0:T(8,128)(2,1)S(1)} %bitcast.175, ...), custom_call_target="tpu_custom_call" | custom-call | flops 6442450944 | bytes 16777216 | tf_op jit(solution)/shard_map/feed/pallas_call | solution.py:686
  207.7 3.0 collective-permute-start.17
  210.7 4.5 feed_weights.1
  217.9 2.5 collective-permute-done.17
  222.7 2.9 collective-permute-start.19
  230.1 7.1 %feed_out.1 = bf16[4,4,256,256]{3,2,1,0:T(8,128)(2,1)} custom-call(s32[3]{0:T(128)S(1)} %pad_add_fusion.1.spot, bf16[4,1024,256]{2,1,0:T(8,128)(2,1)S(1)} %copy-done.55, bf16[1024,1024]{1,0:T(8,128)(2,1)S(1)} %bitcast.174, f32[1024,256]{1,0:T(8,128)S(1)} %copy-done.48, f32[1024,6]{1,0:T(8,128)S(1)} %bitcast.169), custom_call_target="tpu_custom_call" | custom-call | flops 2147483648 | bytes 8388608 | tf_op jit(solution)/shard_map/feed_out/pallas_call | solution.py:774
  239.7 2.2 collective-permute-start.21
  241.9 4.2 collective-permute-done.20.up
  246.1 6.8 %collective-permute-done.21.down = bf16[512,256]{1,0:T(8,128)(2,1)S(1)} collective-permute-done((bf16[512,256]{1,0:T(8,128)(2,1)S(1)}, bf16[512,256]{1,0:T(8,128)(2,1)S(1)}, u32[]{:S(2)}, u32[]{:S(2)}) %collective-permute-start.21) | collective-permute-done | bytes 262176 | tf_op jit(solution)/shard_map/ppermute | solution.py:1050
  259.8 4.5 all-to-all-start.4
  264.4 3.2 convolution_convert_fusion
  267.6 12.1 %all-to-all-done.4.grad_out = bf16[32,64,128]{2,1,0:T(8,128)(2,1)S(1)} async-done(((bf16[32,64,128]{2,1,0:T(8,128)(2,1)}), bf16[32,64,128]{2,1,0:T(8,128)(2,1)S(1)}, u32[]{:S(2)}, u32[]{:S(2)}) %all-to-all-start.4) | async-done | bytes 524320 | tf_op jit(solution)/shard_map/all_to_all | solution.py:1315
  279.6 4.5 all-to-all-start.5
  285.9 58.9 %attend_backward.1 = (bf16[8,64,512]{2,1,0:T(8,128)(2,1)S(1)}, bf16[8,64,1024]{2,1,0:T(8,128)(2,1)S(1)}, bf16[8,64,1024]{2,1,0:T(8,128)(2,1)}, f32[2,16,64]{2,1,0:T(8,128)S(1)}) custom-call(s32[5]{0:T(128)S(1)} %pad_add_fusion.meta, bf16[8,64,1536]{2,1,0:T(8,128)(2,1)} %all-to-all-done.2.query.own, bf16[8,64,1536]{2,1,0:T(8,128)(2,1)} %all-to-all-done.2.query.own, ...), custom_call_target="tpu_custom_call" | custom-call | flops 42949672960 | bytes 8388608 | tf_op jit(solution)/shard_map/attend_backward/pallas_call | solution.py:369
  345.0 2.8 collective-permute-done.22
  351.7 4.7 all-to-all-start.6
  358.1 4.3 convert_element_type.216
  362.4 2.5 convert_element_type.217
  364.9 3.0 reduce_sum.41
  367.8 2.0 copy.98
  369.9 5.4 %all-to-all-done.6.came = bf16[8,64,1664]{2,1,0:T(8,128)(2,1)} async-done(((bf16[8,64,1664]{2,1,0:T(8,128)(2,1)}), bf16[8,64,1664]{2,1,0:T(8,128)(2,1)}, u32[]{:S(2)}, u32[]{:S(2)}) %all-to-all-start.6) | async-done | bytes 1703968 | tf_op jit(solution)/shard_map/all_to_all | solution.py:1342
  378.0 7.9 %unproject.1 = (bf16[768,1024]{1,0:T(8,128)(2,1)S(1)}, bf16[1024,1024]{1,0:T(8,128)(2,1)S(1)}, bf16[128,1024]{1,0:T(8,128)(2,1)}, bf16[128,1024]{1,0:T(8,128)(2,...) custom-call(s32[3]{0:T(128)S(1)} %pad_add_fusion.1.spot, ...), custom_call_target="tpu_custom_call" | custom-call | flops 3221225472 | bytes 8388608 | tf_op jit(solution)/shard_map/unproject/pallas_call | solution.py:544
  385.9 4.8 %rest_halves.1 = (bf16[512,1024]{1,0:T(8,128)(2,1)S(1)}, bf16[512,1024]{1,0:T(8,128)(2,1)S(1)}) custom-call(s32[3]{0:T(128)S(1)} %pad_add_fusion.1.spot, bf16[768,1024]{1,0:T(8,128)(2,1)S(1)} %get-tuple-element.203.flat, bf16[1024,1024]{1,0:T(8,128)(2,1)S(1)} %copy-done.46, bf16[256,1024]{1,0:T(8,128)(2,1)S(1)} %copy-done.51), custom_call_target="tpu_custom_call" | custom-call | flops 1610612736 | bytes 8388608 | tf_op jit(solution)/shard_map/rest_halves/pallas_call | solution.py:909
  390.7 3.6 collective-permute-start.25
  399.2 11.7 %collective-permute-done.26.refs_1_ = f32[48,256]{1,0:T(8,128)S(1)} collective-permute-done((f32[48,256]{1,0:T(8,128)S(1)}, f32[48,256]{1,0:T(8,128)S(1)}, u32[]{:S(2)}, u32[]{:S(2)}) %collective-permute-start.26) | collective-permute-done | bytes 49184 | tf_op jit(solution)/shard_map/ppermute | solution.py:1400
  417.2 2.0 collective-permute-start.33
  419.6 3.2 collective-permute-start.30
  422.9 6.7 %collective-permute-done.32 = bf16[128,1024]{1,0:T(8,128)(2,1)S(1)} collective-permute-done((bf16[128,1024]{1,0:T(8,128)(2,1)S(1)}, bf16[128,1024]{1,0:T(8,128)(2,1)S(1)}, u32[]{:S(2)}, u32[]{:S(2)}) %collective-permute-start.32) | collective-permute-done | bytes 262176 | tf_op jit(solution)/shard_map/ppermute | solution.py:1076
  431.2 2.3 collective-permute-start.38
  434.5 4.9 %collective-permute-start.34 = (bf16[128,1024]{1,0:T(8,128)(2,1)}, bf16[128,1024]{1,0:T(8,128)(2,1)S(1)}, u32[]{:S(2)}, u32[]{:S(2)}) collective-permute-start(bf16[128,1024]{1,0:T(8,128)(2,1)} %get-tuple-element.258), channel_id=1, source_target_pairs={{0,1},{1,2},{2,3},{3,0},{4,5},{5,6},{6,7},{7,4},{8,9},{9,10},{10,1... | collective-permute-start | bytes 786440 | tf_op jit(solution)/shard_map/ppermute | solution.py:1049
  440.3 7.3 %all-to-all-start.7 = ((f32[8,16,256]{2,1,0:T(8,128)}), f32[8,16,256]{2,1,0:T(8,128)S(1)}, u32[]{:S(2)}, u32[]{:S(2)}) async-start(f32[8,16,256]{2,1,0:T(8,128)} %broadcast_in_dim.129), calls=%async_computation.8 | async-start | bytes 262144 | tf_op jit(solution)/shard_map/all_to_all | solution.py:1007
  455.1 5.7 %prefix_back.1 = (f32[16,1024]{1,0:T(8,128)}, f32[1024,512]{1,0:T(8,128)}, f32[1,512]{1,0:T(1,128)}, f32[512,4,128]{2,1,0:T(4,128)}, f32[4,128]{1,0:T(4,128)}) custom-call(f32[16,512]{1,0:T(8,128)S(1)} %get-tuple-element.246.total, f32[16,512]{1,0:T(8,128)S(1)} %pad.18.hidden, bf16[16,1024]{1,0:T(8,128)(2,1)S(1)} %pad.19.embed, ...), custom_call_target="tpu_custom_call" | custom-call | tf_op jit(solution)/shard_map/prefix_back/pallas_call | solution.py:987
  461.5 2.2 finish.1
  464.4 3.7 rest_whole.1
  (330 shorter events, 89.1 us)
Async XLA Ops:
  7.2 62.3 %copy-start = (bf16[4,64,1024]{2,1,0:T(8,128)(2,1)S(1)}, bf16[4,64,1024]{2,1,0:T(8,128)(2,1)}, u32[]{:S(2)}) copy-start(bf16[4,64,1024]{2,1,0:T(8,128)(2,1)} %param.27) | copy-start | bytes 1572868
  11.4 10.4 %collective-permute-start = (bf16[128,1024]{1,0:T(8,128)(2,1)}, bf16[128,1024]{1,0:T(8,128)(2,1)S(1)}, u32[]{:S(2)}, u32[]{:S(2)}) collective-permute-start(bf16[128,1024]{1,0:T(8,128)(2,1)} %get-tuple-element.276), channel_id=1, source_target_pairs={{0,1},{1,2},{2,3},{3,0},{4,5},{5,6},{6,7},{7,4},{8,9},{9,10},{10,1... | collective-permute-start | bytes 786440 | tf_op jit(solution)/shard_map/ppermute | solution.py:1028
  13.5 13.5 %collective-permute-start.2 = (bf16[128,1024]{1,0:T(8,128)(2,1)}, bf16[128,1024]{1,0:T(8,128)(2,1)}, u32[]{:S(2)}, u32[]{:S(2)}) collective-permute-start(bf16[128,1024]{1,0:T(8,128)(2,1)} %get-tuple-element.275), channel_id=1, source_target_pairs={{0,3},{1,0},{2,1},{3,2},{4,7},{5,4},{6,5},{7,6},{8,11},{9,8},{10,9... | collective-permute-start | bytes 786440 | tf_op jit(solution)/shard_map/ppermute | solution.py:1029
  16.3 13.2 %all-to-all-start = ((bf16[4,6,256]{2,1,0:T(8,128)(2,1)}), bf16[4,6,256]{2,1,0:T(8,128)(2,1)S(1)}, u32[]{:S(2)}, u32[]{:S(2)}) async-start(bf16[4,6,256]{2,1,0:T(8,128)(2,1)} %broadcast_in_dim.102), calls=%async_computation | async-start | bytes 32768 | tf_op jit(solution)/shard_map/all_to_all | solution.py:1007
  20.2 33.0 %copy-start.79 = (bf16[4,128]{1,0:T(4,128)(2,1)S(1)}, bf16[4,128]{1,0:T(4,128)(2,1)}, u32[]{:S(2)}) copy-start(bf16[4,128]{1,0:T(4,128)(2,1)} %param.26) | copy-start | bytes 3076
  21.8 15.0 %collective-permute-start.1 = (bf16[128,1024]{1,0:T(8,128)(2,1)S(1)}, bf16[128,1024]{1,0:T(8,128)(2,1)S(1)}, u32[]{:S(2)}, u32[]{:S(2)}) collective-permute-start(bf16[128,1024]{1,0:T(8,128)(2,1)S(1)} %collective-permute-done), channel_id=1, source_target_pairs={{0,1},{1,2},{2,3},{3,0},{4,5},{5,6},{6,7},{7,4},{8,9},{9,10},{10,1... | collective-permute-start | bytes 786440 | tf_op jit(solution)/shard_map/ppermute | solution.py:1028
  27.1 12.7 %collective-permute-start.3 = (bf16[128,1024]{1,0:T(8,128)(2,1)}, bf16[128,1024]{1,0:T(8,128)(2,1)S(1)}, u32[]{:S(2)}, u32[]{:S(2)}) collective-permute-start(bf16[128,1024]{1,0:T(8,128)(2,1)} %collective-permute-done.2), channel_id=1, source_target_pairs={{0,3},{1,0},{2,1},{3,2},{4,7},{5,4},{6,5},{7,6},{8,11},{9,8},{10,9... | collective-permute-start | bytes 786440 | tf_op jit(solution)/shard_map/ppermute | solution.py:1029
  30.2 12.9 %all-to-all-start.1 = ((s32[8,4,128]{2,1,0:T(4,128)}), s32[8,4,128]{2,1,0:T(4,128)S(1)}, u32[]{:S(2)}, u32[]{:S(2)}) async-start(s32[8,4,128]{2,1,0:T(4,128)} %broadcast_in_dim_broadcast_in_dim_broadcast_in_dim.2), calls=%async_computation.1 | async-start | bytes 32768 | tf_op jit(solution)/shard_map/all_to_all | solution.py:1007
  36.9 91.7 %all-gather.4.cloned.1.call-start = ((), (), s32[]{:S(2)}) async-start(), calls=%async_computation.9 | async-start | bytes 2621440 | tf_op jit(solution)/shard_map/all_gather | solution.py:1253
  39.7 9.2 %collective-permute-start.4 = (bf16[128,1024]{1,0:T(8,128)(2,1)S(1)}, bf16[128,1024]{1,0:T(8,128)(2,1)S(1)}, u32[]{:S(2)}, u32[]{:S(2)}) collective-permute-start(bf16[128,1024]{1,0:T(8,128)(2,1)S(1)} %collective-permute-done.1), channel_id=1, source_target_pairs={{0,1},{1,2},{2,3},{3,0},{4,5},{5,6},{6,7},{7,4},{8,9},{9,10},{10,1... | collective-permute-start | bytes 786440 | tf_op jit(solution)/shard_map/ppermute | solution.py:1028
  39.7 12.4 %collective-permute-start.5 = (bf16[128,1024]{1,0:T(8,128)(2,1)S(1)}, bf16[128,1024]{1,0:T(8,128)(2,1)}, u32[]{:S(2)}, u32[]{:S(2)}) collective-permute-start(bf16[128,1024]{1,0:T(8,128)(2,1)S(1)} %collective-permute-done.3), channel_id=1, source_target_pairs={{0,3},{1,0},{2,1},{3,2},{4,7},{5,4},{6,5},{7,6},{8,11},{9,8},{10,9... | collective-permute-start | bytes 786440 | tf_op jit(solution)/shard_map/ppermute | solution.py:1029
  63.1 27.5 %copy-start.80 = (bf16[4,128]{1,0:T(4,128)(2,1)S(1)}, bf16[4,128]{1,0:T(4,128)(2,1)}, u32[]{:S(2)}) copy-start(bf16[4,128]{1,0:T(4,128)(2,1)} %param.39) | copy-start | bytes 3076
  63.1 27.5 %copy-start.81 = (bf16[512]{0:T(512)(128)(2,1)S(1)}, bf16[512]{0:T(512)(128)(2,1)}, u32[]{:S(2)}) copy-start(bf16[512]{0:T(512)(128)(2,1)} %param.37) | copy-start | bytes 3076
  63.1 27.6 %copy-start.9 = (bf16[1024,512]{1,0:T(8,128)(2,1)S(1)}, bf16[1024,512]{1,0:T(8,128)(2,1)}, u32[]{:S(2)}) copy-start(bf16[1024,512]{1,0:T(8,128)(2,1)} %weight.1) | copy-start | bytes 3145732
  63.1 27.6 %copy-start.73 = (bf16[10,1024]{1,0:T(8,128)(2,1)S(1)}, bf16[10,1024]{1,0:T(8,128)(2,1)}, u32[]{:S(2)}) copy-start(bf16[10,1024]{1,0:T(8,128)(2,1)} %param.35) | copy-start | bytes 61444
  63.1 27.9 %copy-start.59 = (bf16[512,4,128]{2,1,0:T(4,128)(2,1)S(1)}, bf16[512,4,128]{2,1,0:T(4,128)(2,1)}, u32[]{:S(2)}) copy-start(bf16[512,4,128]{2,1,0:T(4,128)(2,1)} %param.38) | copy-start | bytes 1572868
  63.1 23.9 %all-to-all-start.2 = ((bf16[8,64,1536]{2,1,0:T(8,128)(2,1)}), bf16[8,64,1536]{2,1,0:T(8,128)(2,1)}, u32[]{:S(2)}, u32[]{:S(2)}) async-start(bf16[8,64,1536]{2,1,0:T(8,128)(2,1)} %copy-done.25), calls=%async_computation.2 | async-start | bytes 3145728 | tf_op jit(solution)/shard_map/all_to_all | solution.py:1242
  69.5 69.1 %all-gather.6.cloned.1.call-start = ((), (), s32[]{:S(2)}) async-start(), calls=%async_computation.11 | async-start | bytes 2359296 | tf_op jit(solution)/shard_map/all_gather | solution.py:1244
  69.5 7.1 %collective-permute-start.6 = (bf16[32,1024]{1,0:T(8,128)(2,1)S(1)}, bf16[32,1024]{1,0:T(8,128)(2,1)S(1)}, u32[]{:S(2)}, u32[]{:S(2)}) collective-permute-start(bf16[32,1024]{1,0:T(8,128)(2,1)S(1)} %dynamic-slice_bitcast_fusion.18), channel_id=1, source_target_pairs={{0,1},{1,2},{2,3},{3,0},{4,5},{5,6},{6,7},{7,4},{8,9},{9,10},{10,1... | collective-permute-start | bytes 196616 | tf_op jit(solution)/shard_map/ppermute | solution.py:1100
  69.6 11.9 %collective-permute-start.7 = (bf16[32,1024]{1,0:T(8,128)(2,1)S(1)}, bf16[32,1024]{1,0:T(8,128)(2,1)S(1)}, u32[]{:S(2)}, u32[]{:S(2)}) collective-permute-start(bf16[32,1024]{1,0:T(8,128)(2,1)S(1)} %dynamic-slice_bitcast_fusion.18), channel_id=1, source_target_pairs={{0,2},{1,3},{2,0},{3,1},{4,6},{5,7},{6,4},{7,5},{8,10},{9,11},{10,... | collective-permute-start | bytes 196616 | tf_op jit(solution)/shard_map/ppermute | solution.py:1100
  71.7 9.7 %collective-permute-start.8 = (bf16[32,1024]{1,0:T(8,128)(2,1)S(1)}, bf16[32,1024]{1,0:T(8,128)(2,1)S(1)}, u32[]{:S(2)}, u32[]{:S(2)}) collective-permute-start(bf16[32,1024]{1,0:T(8,128)(2,1)S(1)} %dynamic-slice_bitcast_fusion.18), channel_id=1, source_target_pairs={{0,3},{1,0},{2,1},{3,2},{4,7},{5,4},{6,5},{7,6},{8,11},{9,8},{10,9... | collective-permute-start | bytes 196616 | tf_op jit(solution)/shard_map/ppermute | solution.py:1100
  87.0 7.0 %collective-permute-start.9 = (bf16[8,64,1536]{2,1,0:T(8,128)(2,1)}, bf16[8,64,1536]{2,1,0:T(8,128)(2,1)}, u32[]{:S(2)}, u32[]{:S(2)}) collective-permute-start(bf16[8,64,1536]{2,1,0:T(8,128)(2,1)} %all-to-all-done.2.query.own), channel_id=1, source_target_pairs={{0,4},{4,0},{8,12},{12,8},{16,20},{20,16},{24,28},{28,24},{1,5},{5... | collective-permute-start | bytes 4718600 | tf_op jit(solution)/shard_map/ppermute | solution.py:1064
  94.0 38.1 %copy-start.12 = (bf16[1024,1024]{1,0:T(8,128)(2,1)S(1)}, bf16[1024,1024]{1,0:T(8,128)(2,1)}, u32[]{:S(2)}) copy-start(bf16[1024,1024]{1,0:T(8,128)(2,1)} %up.1) | copy-start | bytes 6291460
  128.5 18.2 %all-to-all-start.3 = ((bf16[32,64,128]{2,1,0:T(8,128)(2,1)}), bf16[32,64,128]{2,1,0:T(8,128)(2,1)S(1)}, u32[]{:S(2)}, u32[]{:S(2)}) async-start(bf16[32,64,128]{2,1,0:T(8,128)(2,1)} %copy-done.35), calls=%async_computation.3 | async-start | bytes 1048576 | tf_op jit(solution)/shard_map/all_to_all | solution.py:1263
  131.5 220.2 %all-reduce.7.cloned.1.call-start = ((), (), s32[]{:S(2)}) async-start(), calls=%async_computation.12 | async-start | bytes 8388608 | tf_op jit(solution)/shard_map/psum | solution.py:1295
  132.1 253.8 %copy-start.43 = (s32[3]{0:T(128)}, s32[3]{0:T(128)S(1)}, u32[]{:S(2)}) copy-start(s32[3]{0:T(128)S(1)} %pad_add_fusion.1.spot) | copy-start | bytes 40
  153.7 10.1 %collective-permute-start.10 = (bf16[512,256]{1,0:T(8,128)(2,1)}, bf16[512,256]{1,0:T(8,128)(2,1)S(1)}, u32[]{:S(2)}, u32[]{:S(2)}) collective-permute-start(bf16[512,256]{1,0:T(8,128)(2,1)} %get-tuple-element.274), channel_id=1, source_target_pairs={{0,1},{1,2},{2,3},{3,0},{4,5},{5,6},{6,7},{7,4},{8,9},{9,10},{10,1... | collective-permute-start | bytes 786440 | tf_op jit(solution)/shard_map/ppermute | solution.py:1028
  154.8 13.4 %collective-permute-start.11 = (bf16[512,256]{1,0:T(8,128)(2,1)}, bf16[512,256]{1,0:T(8,128)(2,1)S(1)}, u32[]{:S(2)}, u32[]{:S(2)}) collective-permute-start(bf16[512,256]{1,0:T(8,128)(2,1)} %get-tuple-element.273), channel_id=1, source_target_pairs={{0,3},{1,0},{2,1},{3,2},{4,7},{5,4},{6,5},{7,6},{8,11},{9,8},{10,9... | collective-permute-start | bytes 786440 | tf_op jit(solution)/shard_map/ppermute | solution.py:1029
  158.0 33.9 %copy-start.15 = (bf16[1024,1024]{1,0:T(8,128)(2,1)S(1)}, bf16[1024,1024]{1,0:T(8,128)(2,1)}, u32[]{:S(2)}) copy-start(bf16[1024,1024]{1,0:T(8,128)(2,1)} %all-gather.4.cloned.1.call-done.grads) | copy-start | bytes 6291460
  158.1 33.8 %copy-start.13 = (bf16[1024,1024]{1,0:T(8,128)(2,1)S(1)}, bf16[1024,1024]{1,0:T(8,128)(2,1)}, u32[]{:S(2)}) copy-start(bf16[1024,1024]{1,0:T(8,128)(2,1)} %up.1) | copy-start | bytes 6291460
  158.2 33.8 %copy-start.14 = (bf16[1024,1024]{1,0:T(8,128)(2,1)S(1)}, bf16[1024,1024]{1,0:T(8,128)(2,1)}, u32[]{:S(2)}) copy-start(bf16[1024,1024]{1,0:T(8,128)(2,1)} %down.1) | copy-start | bytes 6291460
  163.8 11.3 %collective-permute-start.12 = (bf16[512,256]{1,0:T(8,128)(2,1)S(1)}, bf16[512,256]{1,0:T(8,128)(2,1)S(1)}, u32[]{:S(2)}, u32[]{:S(2)}) collective-permute-start(bf16[512,256]{1,0:T(8,128)(2,1)S(1)} %collective-permute-done.10), channel_id=1, source_target_pairs={{0,1},{1,2},{2,3},{3,0},{4,5},{5,6},{6,7},{7,4},{8,9},{9,10},{10,1... | collective-permute-start | bytes 786440 | tf_op jit(solution)/shard_map/ppermute | solution.py:1028
  168.2 12.5 %collective-permute-start.13 = (bf16[512,256]{1,0:T(8,128)(2,1)S(1)}, bf16[512,256]{1,0:T(8,128)(2,1)S(1)}, u32[]{:S(2)}, u32[]{:S(2)}) collective-permute-start(bf16[512,256]{1,0:T(8,128)(2,1)S(1)} %collective-permute-done.11), channel_id=1, source_target_pairs={{0,3},{1,0},{2,1},{3,2},{4,7},{5,4},{6,5},{7,6},{8,11},{9,8},{10,9... | collective-permute-start | bytes 786440 | tf_op jit(solution)/shard_map/ppermute | solution.py:1029
  175.1 11.3 %collective-permute-start.14 = (bf16[512,256]{1,0:T(8,128)(2,1)S(1)}, bf16[512,256]{1,0:T(8,128)(2,1)S(1)}, u32[]{:S(2)}, u32[]{:S(2)}) collective-permute-start(bf16[512,256]{1,0:T(8,128)(2,1)S(1)} %collective-permute-done.12), channel_id=1, source_target_pairs={{0,1},{1,2},{2,3},{3,0},{4,5},{5,6},{6,7},{7,4},{8,9},{9,10},{10,1... | collective-permute-start | bytes 786440 | tf_op jit(solution)/shard_map/ppermute | solution.py:1028
  180.7 11.2 %collective-permute-start.15 = (bf16[512,256]{1,0:T(8,128)(2,1)S(1)}, bf16[512,256]{1,0:T(8,128)(2,1)S(1)}, u32[]{:S(2)}, u32[]{:S(2)}) collective-permute-start(bf16[512,256]{1,0:T(8,128)(2,1)S(1)} %collective-permute-done.13), channel_id=1, source_target_pairs={{0,3},{1,0},{2,1},{3,2},{4,7},{5,4},{6,5},{7,6},{8,11},{9,8},{10,9... | collective-permute-start | bytes 786440 | tf_op jit(solution)/shard_map/ppermute | solution.py:1029
  207.4 10.5 %collective-permute-start.16 = (bf16[512,256]{1,0:T(8,128)(2,1)S(1)}, bf16[512,256]{1,0:T(8,128)(2,1)S(1)}, u32[]{:S(2)}, u32[]{:S(2)}) collective-permute-start(bf16[512,256]{1,0:T(8,128)(2,1)S(1)} %get-tuple-element.264), channel_id=1, source_target_pairs={{0,1},{1,2},{2,3},{3,0},{4,5},{5,6},{6,7},{7,4},{8,9},{9,10},{10,1... | collective-permute-start | bytes 786440 | tf_op jit(solution)/shard_map/ppermute | solution.py:1049
  207.7 12.7 %collective-permute-start.17 = (bf16[512,256]{1,0:T(8,128)(2,1)S(1)}, bf16[512,256]{1,0:T(8,128)(2,1)S(1)}, u32[]{:S(2)}, u32[]{:S(2)}) collective-permute-start(bf16[512,256]{1,0:T(8,128)(2,1)S(1)} %get-tuple-element.263), channel_id=1, source_target_pairs={{0,3},{1,0},{2,1},{3,2},{4,7},{5,4},{6,5},{7,6},{8,11},{9,8},{10,9... | collective-permute-start | bytes 786440 | tf_op jit(solution)/shard_map/ppermute | solution.py:1050
  222.4 14.9 %collective-permute-start.18 = (bf16[512,256]{1,0:T(8,128)(2,1)S(1)}, bf16[512,256]{1,0:T(8,128)(2,1)S(1)}, u32[]{:S(2)}, u32[]{:S(2)}) collective-permute-start(bf16[512,256]{1,0:T(8,128)(2,1)S(1)} %get-tuple-element.268), channel_id=1, source_target_pairs={{0,1},{1,2},{2,3},{3,0},{4,5},{5,6},{6,7},{7,4},{8,9},{9,10},{10,1... | collective-permute-start | bytes 786440 | tf_op jit(solution)/shard_map/ppermute | solution.py:1049
  222.7 14.5 %collective-permute-start.19 = (bf16[512,256]{1,0:T(8,128)(2,1)S(1)}, bf16[512,256]{1,0:T(8,128)(2,1)S(1)}, u32[]{:S(2)}, u32[]{:S(2)}) collective-permute-start(bf16[512,256]{1,0:T(8,128)(2,1)S(1)} %get-tuple-element.267), channel_id=1, source_target_pairs={{0,3},{1,0},{2,1},{3,2},{4,7},{5,4},{6,5},{7,6},{8,11},{9,8},{10,9... | collective-permute-start | bytes 786440 | tf_op jit(solution)/shard_map/ppermute | solution.py:1050
  238.5 7.5 %collective-permute-start.20 = (bf16[512,256]{1,0:T(8,128)(2,1)S(1)}, bf16[512,256]{1,0:T(8,128)(2,1)S(1)}, u32[]{:S(2)}, u32[]{:S(2)}) collective-permute-start(bf16[512,256]{1,0:T(8,128)(2,1)S(1)} %get-tuple-element.266), channel_id=1, source_target_pairs={{0,1},{1,2},{2,3},{3,0},{4,5},{5,6},{6,7},{7,4},{8,9},{9,10},{10,1... | collective-permute-start | bytes 786440 | tf_op jit(solution)/shard_map/ppermute | solution.py:1049
  239.7 13.1 %collective-permute-start.21 = (bf16[512,256]{1,0:T(8,128)(2,1)S(1)}, bf16[512,256]{1,0:T(8,128)(2,1)S(1)}, u32[]{:S(2)}, u32[]{:S(2)}) collective-permute-start(bf16[512,256]{1,0:T(8,128)(2,1)S(1)} %get-tuple-element.265), channel_id=1, source_target_pairs={{0,3},{1,0},{2,1},{3,2},{4,7},{5,4},{6,5},{7,6},{8,11},{9,8},{10,9... | collective-permute-start | bytes 786440 | tf_op jit(solution)/shard_map/ppermute | solution.py:1050
  259.8 19.8 %all-to-all-start.4 = ((bf16[32,64,128]{2,1,0:T(8,128)(2,1)}), bf16[32,64,128]{2,1,0:T(8,128)(2,1)S(1)}, u32[]{:S(2)}, u32[]{:S(2)}) async-start(bf16[32,64,128]{2,1,0:T(8,128)(2,1)} %copy-done.36), calls=%async_computation.4 | async-start | bytes 1048576 | tf_op jit(solution)/shard_map/all_to_all | solution.py:1315
  279.6 72.1 %all-to-all-start.5 = ((bf16[4,4,256,256]{3,2,1,0:T(8,128)(2,1)}), bf16[4,4,256,256]{3,2,1,0:T(8,128)(2,1)}, u32[]{:S(2)}, u32[]{:S(2)}) async-start(bf16[4,4,256,256]{3,2,1,0:T(8,128)(2,1)} %feed_out.1), calls=%async_computation.5 | async-start | bytes 4194304 | tf_op jit(solution)/shard_map/all_to_all | solution.py:1320
  284.1 85.8 %reduce-scatter.2.cloned.1.call-start = ((), (), s32[]{:S(2)}) async-start(), calls=%async_computation.10 | async-start | bytes 2621440 | tf_op jit(solution)/shard_map/reduce_scatter | solution.py:1321
  344.8 2.9 collective-permute-start.22
  351.7 23.6 %all-to-all-start.6 = ((bf16[8,64,1664]{2,1,0:T(8,128)(2,1)}), bf16[8,64,1664]{2,1,0:T(8,128)(2,1)}, u32[]{:S(2)}, u32[]{:S(2)}) async-start(bf16[8,64,1664]{2,1,0:T(8,128)(2,1)} %pad_maximum_fusion), calls=%async_computation.6 | async-start | bytes 3407872 | tf_op jit(solution)/shard_map/all_to_all | solution.py:1342
  390.7 23.2 %collective-permute-start.25 = (bf16[512,1024]{1,0:T(8,128)(2,1)S(1)}, bf16[512,1024]{1,0:T(8,128)(2,1)}, u32[]{:S(2)}, u32[]{:S(2)}) collective-permute-start(bf16[512,1024]{1,0:T(8,128)(2,1)S(1)} %get-tuple-element.206), channel_id=1, source_target_pairs={{0,4},{4,0},{8,12},{12,8},{16,20},{20,16},{24,28},{28,24},{1,5},{5... | collective-permute-start | bytes 3145736 | tf_op jit(solution)/shard_map/ppermute | solution.py:1064
  394.3 19.5 %collective-permute-start.23 = (bf16[128,1024]{1,0:T(8,128)(2,1)}, bf16[128,1024]{1,0:T(8,128)(2,1)S(1)}, u32[]{:S(2)}, u32[]{:S(2)}) collective-permute-start(bf16[128,1024]{1,0:T(8,128)(2,1)} %get-tuple-element.201), channel_id=1, source_target_pairs={{0,1},{1,2},{2,3},{3,0},{4,5},{5,6},{6,7},{7,4},{8,9},{9,10},{10,1... | collective-permute-start | bytes 786440 | tf_op jit(solution)/shard_map/ppermute | solution.py:1049
  395.7 18.2 %collective-permute-start.24 = (bf16[128,1024]{1,0:T(8,128)(2,1)}, bf16[128,1024]{1,0:T(8,128)(2,1)S(1)}, u32[]{:S(2)}, u32[]{:S(2)}) collective-permute-start(bf16[128,1024]{1,0:T(8,128)(2,1)} %get-tuple-element.202), channel_id=1, source_target_pairs={{0,3},{1,0},{2,1},{3,2},{4,7},{5,4},{6,5},{7,6},{8,11},{9,8},{10,9... | collective-permute-start | bytes 786440 | tf_op jit(solution)/shard_map/ppermute | solution.py:1050
  397.6 13.3 %collective-permute-start.26 = (f32[48,256]{1,0:T(8,128)S(1)}, f32[48,256]{1,0:T(8,128)S(1)}, u32[]{:S(2)}, u32[]{:S(2)}) collective-permute-start(f32[48,256]{1,0:T(8,128)S(1)} %get-tuple-element.208), channel_id=1, source_target_pairs={{0,1},{1,2},{2,3},{3,0},{4,5},{5,6},{6,7},{7,4},{8,9},{9,10},{10,1... | collective-permute-start | bytes 147464 | tf_op jit(solution)/shard_map/ppermute | solution.py:1400
  397.6 15.8 %collective-permute-start.27 = (f32[48,256]{1,0:T(8,128)S(1)}, f32[48,256]{1,0:T(8,128)S(1)}, u32[]{:S(2)}, u32[]{:S(2)}) collective-permute-start(f32[48,256]{1,0:T(8,128)S(1)} %get-tuple-element.209), channel_id=1, source_target_pairs={{0,2},{1,3},{2,0},{3,1},{4,6},{5,7},{6,4},{7,5},{8,10},{9,11},{10,... | collective-permute-start | bytes 147464 | tf_op jit(solution)/shard_map/ppermute | solution.py:1400
  410.9 2.9 collective-permute-start.28
  416.5 6.4 %collective-permute-start.31 = (bf16[128,1024]{1,0:T(8,128)(2,1)S(1)}, bf16[128,1024]{1,0:T(8,128)(2,1)S(1)}, u32[]{:S(2)}, u32[]{:S(2)}) collective-permute-start(bf16[128,1024]{1,0:T(8,128)(2,1)S(1)} %get-tuple-element.271), channel_id=1, source_target_pairs={{0,8},{4,12},{8,16},{12,20},{16,24},{20,28},{24,0},{28,4},{1,9},{5... | collective-permute-start | bytes 786440 | tf_op jit(solution)/shard_map/ppermute | solution.py:1076
  416.6 13.0 %collective-permute-start.32 = (bf16[128,1024]{1,0:T(8,128)(2,1)S(1)}, bf16[128,1024]{1,0:T(8,128)(2,1)S(1)}, u32[]{:S(2)}, u32[]{:S(2)}) collective-permute-start(bf16[128,1024]{1,0:T(8,128)(2,1)S(1)} %get-tuple-element.270), channel_id=1, source_target_pairs={{0,16},{4,20},{8,24},{12,28},{16,0},{20,4},{24,8},{28,12},{1,17},{... | collective-permute-start | bytes 786440 | tf_op jit(solution)/shard_map/ppermute | solution.py:1076
  417.2 12.4 %collective-permute-start.33 = (bf16[128,1024]{1,0:T(8,128)(2,1)S(1)}, bf16[128,1024]{1,0:T(8,128)(2,1)S(1)}, u32[]{:S(2)}, u32[]{:S(2)}) collective-permute-start(bf16[128,1024]{1,0:T(8,128)(2,1)S(1)} %get-tuple-element.269), channel_id=1, source_target_pairs={{0,24},{4,28},{8,0},{12,4},{16,8},{20,12},{24,16},{28,20},{1,25},{... | collective-permute-start | bytes 786440 | tf_op jit(solution)/shard_map/ppermute | solution.py:1076
  419.4 10.2 %collective-permute-start.29 = (bf16[128,1024]{1,0:T(8,128)(2,1)S(1)}, bf16[128,1024]{1,0:T(8,128)(2,1)S(1)}, u32[]{:S(2)}, u32[]{:S(2)}) collective-permute-start(bf16[128,1024]{1,0:T(8,128)(2,1)S(1)} %get-tuple-element.260), channel_id=1, source_target_pairs={{0,1},{1,2},{2,3},{3,0},{4,5},{5,6},{6,7},{7,4},{8,9},{9,10},{10,1... | collective-permute-start | bytes 786440 | tf_op jit(solution)/shard_map/ppermute | solution.py:1049
  419.6 10.1 %collective-permute-start.30 = (bf16[128,1024]{1,0:T(8,128)(2,1)S(1)}, bf16[128,1024]{1,0:T(8,128)(2,1)S(1)}, u32[]{:S(2)}, u32[]{:S(2)}) collective-permute-start(bf16[128,1024]{1,0:T(8,128)(2,1)S(1)} %get-tuple-element.259), channel_id=1, source_target_pairs={{0,3},{1,0},{2,1},{3,2},{4,7},{5,4},{6,5},{7,6},{8,11},{9,8},{10,9... | collective-permute-start | bytes 786440 | tf_op jit(solution)/shard_map/ppermute | solution.py:1050
  429.9 17.7 %collective-permute-start.36 = (bf16[128,1024]{1,0:T(8,128)(2,1)S(1)}, bf16[128,1024]{1,0:T(8,128)(2,1)S(1)}, u32[]{:S(2)}, u32[]{:S(2)}) collective-permute-start(bf16[128,1024]{1,0:T(8,128)(2,1)S(1)} %add_convert_fusion.2), channel_id=1, source_target_pairs={{0,8},{4,12},{8,16},{12,20},{16,24},{20,28},{24,0},{28,4},{1,9},{5... | collective-permute-start | bytes 786440 | tf_op jit(solution)/shard_map/ppermute | solution.py:1091
  430.3 17.3 %collective-permute-start.37 = (bf16[128,1024]{1,0:T(8,128)(2,1)S(1)}, bf16[128,1024]{1,0:T(8,128)(2,1)S(1)}, u32[]{:S(2)}, u32[]{:S(2)}) collective-permute-start(bf16[128,1024]{1,0:T(8,128)(2,1)S(1)} %add_convert_fusion.2), channel_id=1, source_target_pairs={{0,16},{4,20},{8,24},{12,28},{16,0},{20,4},{24,8},{28,12},{1,17},{... | collective-permute-start | bytes 786440 | tf_op jit(solution)/shard_map/ppermute | solution.py:1091
  431.2 17.8 %collective-permute-start.38 = (bf16[128,1024]{1,0:T(8,128)(2,1)S(1)}, bf16[128,1024]{1,0:T(8,128)(2,1)}, u32[]{:S(2)}, u32[]{:S(2)}) collective-permute-start(bf16[128,1024]{1,0:T(8,128)(2,1)S(1)} %add_convert_fusion.2), channel_id=1, source_target_pairs={{0,24},{4,28},{8,0},{12,4},{16,8},{20,12},{24,16},{28,20},{1,25},{... | collective-permute-start | bytes 786440 | tf_op jit(solution)/shard_map/ppermute | solution.py:1091
  434.5 17.8 %collective-permute-start.34 = (bf16[128,1024]{1,0:T(8,128)(2,1)}, bf16[128,1024]{1,0:T(8,128)(2,1)S(1)}, u32[]{:S(2)}, u32[]{:S(2)}) collective-permute-start(bf16[128,1024]{1,0:T(8,128)(2,1)} %get-tuple-element.258), channel_id=1, source_target_pairs={{0,1},{1,2},{2,3},{3,0},{4,5},{5,6},{6,7},{7,4},{8,9},{9,10},{10,1... | collective-permute-start | bytes 786440 | tf_op jit(solution)/shard_map/ppermute | solution.py:1049
  439.4 12.9 %collective-permute-start.35 = (bf16[128,1024]{1,0:T(8,128)(2,1)}, bf16[128,1024]{1,0:T(8,128)(2,1)}, u32[]{:S(2)}, u32[]{:S(2)}) collective-permute-start(bf16[128,1024]{1,0:T(8,128)(2,1)} %get-tuple-element.257), channel_id=1, source_target_pairs={{0,3},{1,0},{2,1},{3,2},{4,7},{5,4},{6,5},{7,6},{8,11},{9,8},{10,9... | collective-permute-start | bytes 786440 | tf_op jit(solution)/shard_map/ppermute | solution.py:1050
  440.3 12.0 %all-to-all-start.7 = ((f32[8,16,256]{2,1,0:T(8,128)}), f32[8,16,256]{2,1,0:T(8,128)S(1)}, u32[]{:S(2)}, u32[]{:S(2)}) async-start(f32[8,16,256]{2,1,0:T(8,128)} %broadcast_in_dim.129), calls=%async_computation.8 | async-start | bytes 262144 | tf_op jit(solution)/shard_map/all_to_all | solution.py:1007
  452.3 12.1 %collective-permute-start.39 = (bf16[512,1024]{1,0:T(8,128)(2,1)S(1)}, bf16[512,1024]{1,0:T(8,128)(2,1)}, u32[]{:S(2)}, u32[]{:S(2)}) collective-permute-start(bf16[512,1024]{1,0:T(8,128)(2,1)S(1)} %pad_maximum_fusion.1.half), channel_id=1, source_target_pairs={{0,4},{4,0},{8,12},{12,8},{16,20},{20,16},{24,28},{28,24},{1,5},{5... | collective-permute-start | bytes 3145736 | tf_op jit(solution)/shard_map/ppermute | solution.py:1064
  (77 other events, 447.0 us)
Sparse Core Ops, SparseCore 0:
  53.3 52.8 all-gather.3
  108.6 27.1 all-gather.5
  237.4 83.1 all-reduce.6
  322.9 44.4 reduce-scatter.1

commit v5 on v4

--- a/solution.py
+++ b/solution.py
@@ -461,10 +461,9 @@
 
 def unproject_kernel(
     spot, came, weight, rows, stats, columns, own_grad, token_rows, reparam,
-    flat, part, first_up, first_down, head_row, prefix_low, *rest,
-    heads, size, step,
+    flat, part, first_up, first_down, head_row, prefix_low, small, totals,
+    *, heads, size, step,
 ):
-    *small, totals = rest
     width, length = rows.shape
     half = step // 2
     past = length // 2
@@ -518,12 +517,17 @@
         found += [both[:PAD], both[PAD : 2 * PAD]]
     low = jnp.concatenate(found, 1).astype(BF16)
     prefix_low[...] = low
-    hidden = contract(low, reparam[...], 1, 1)
+    each = 2 * size
+    hidden = sum(
+        contract(low[:, head * each : (head + 1) * each], reparam[:, head, :], 1, 1)
+        for head in range(heads)
+    )
     features = 2 * count
-    for number, target in enumerate(small):
-        start = pl.multiple_of(lax.rem(spot[0] + number, blocks) * features, features)
-        target[0:2] = totals[0:2, pl.ds(start, features)]
-        target[2:5] = token_rows[0:3, pl.ds(start, features)]
+    for number in range(blocks):
+        spread_over = slice(number * features, (number + 1) * features)
+        target = small.at[number]
+        target[0:2] = totals[0:2, spread_over]
+        target[2:5] = token_rows[0:3, spread_over]
         target[5:8] = jnp.zeros((3, features), F32)
         for which in range(2):
             for piece in range(blocks):
@@ -550,10 +554,10 @@
             first,
             jax.ShapeDtypeStruct((1, mixed), F32),
             jax.ShapeDtypeStruct((PAD, 2 * heads * size), BF16),
-        )
-        + (jax.ShapeDtypeStruct((small, features), F32),) * blocks,
+            jax.ShapeDtypeStruct((blocks, small, features), F32),
+        ),
         in_specs=[SM] + [VM] * 8,
-        out_specs=(VM,) * (6 + blocks),
+        out_specs=(VM,) * 7,
         scratch_shapes=[pltpu.VMEM((8, width), F32)],
         compiler_params=pltpu.CompilerParams(vmem_limit_bytes=20 * 2**20),
         cost_estimate=pl.CostEstimate(
@@ -563,10 +567,9 @@
     )(spot, came, weight, rows, stats, columns, own_grad, token_rows, reparam)
 
 
-def small_kernel(*refs, blocks, width, hidden_rows):
-    pieces = refs[:blocks]
-    down_row, up_row, head_row, row_sums, hidden, late = refs[blocks:]
-    total = sum(piece[...] for piece in pieces)
+def small_kernel(parts, down_row, up_row, head_row, row_sums, hidden, late, *, width):
+    blocks = parts.shape[0]
+    total = sum(parts[n] for n in range(blocks))
     features = total.shape[1]
     for which in range(2):
         for piece in range(blocks):
@@ -586,23 +589,21 @@
             row += 1
 
 
-def small_totals(pieces, down_row, up_row, head_row, rows, hidden_width, width):
-    features = pieces[0].shape[1]
+def small_totals(parts, down_row, up_row, head_row, rows, hidden_width, width):
+    features = parts.shape[2]
     late = 6 + (up_row.shape[1] + head_row.shape[1]) // features
     return pl.pallas_call(
-        functools.partial(
-            small_kernel, blocks=len(pieces), width=width, hidden_rows=hidden_width
-        ),
+        functools.partial(small_kernel, width=width),
         out_shape=(
             jax.ShapeDtypeStruct((2, rows), F32),
             jax.ShapeDtypeStruct((PAD, hidden_width), F32),
             jax.ShapeDtypeStruct((-(-late // 8) * 8, features), F32),
         ),
-        in_specs=[VM] * (len(pieces) + 3),
+        in_specs=[VM] * 4,
         out_specs=(VM,) * 3,
         compiler_params=pltpu.CompilerParams(vmem_limit_bytes=8 * 2**20),
         name="small_totals",
-    )(*pieces, down_row, up_row, head_row)
+    )(parts, down_row, up_row, head_row)
 
 
 def late_kernel(parts, vectors, up, pairs, *, heads, size):
@@ -660,132 +661,164 @@
     )(up, down, own_up, own_down, rows, gain, stats, row_sums)
 
 
-def feed_kernel(rows, grads, up_turned, up, down, bias, hidden, grad_pre, part):
-    pre = contract(up_turned[...], rows[0], 1, 0) + bias[...]
+def ring_lanes(slot, step, blocks, count):
+    half = count // 2
+    below = lax.rem(slot + blocks - step, blocks) * count
+    above = lax.rem(slot + step, blocks) * count + half
+    if half % LANES == 0:
+        below, above = pl.multiple_of(below, half), pl.multiple_of(above, half)
+    return pl.ds(below, half), pl.ds(above, half)
+
+
+def feed_kernel(
+    rows_up, rows_down, given, up_turned, up, down, bias,
+    rows, hidden, grad_pre, part_up, part_down,
+):
+    half = rows_up.shape[1]
+    both = jnp.concatenate([rows_up[...], rows_down[...]], 1)
+    rows[...] = both
+    pre = contract(up_turned[...], both, 1, 0) + bias[...]
     act, pull = jax.vjp(gelu_tanh, pre)
-    hidden[0] = act.astype(BF16)
-    given = grads[...] if len(grads.shape) == 2 else grads[0]
-    low = pull(contract(down[...], given, 1, 0))[0].astype(BF16)
-    grad_pre[0] = low
-    part[0] = contract(up[...], low, 1, 0).astype(BF16)
-
-
-def feed(rows, grads, up_turned, up, down, bias):
-    blocks, width, count = rows.shape
+    hidden[...] = act.astype(BF16)
+    low = pull(contract(down[...], given[...], 1, 0))[0].astype(BF16)
+    grad_pre[...] = low
+    part = contract(up[...], low, 1, 0).astype(BF16)
+    part_up[...] = part[:, :half]
+    part_down[...] = part[:, half:]
+
+
+def feed(rows_up, rows_down, given, up_turned, up, down, bias):
+    width, half = rows_up.shape
     inner = down.shape[0]
-
-    def whole(shape):
-        return pl.BlockSpec(shape, lambda i: (0,) * len(shape), pipeline_mode=pl.Buffered(1))
-
-    def block(size):
-        return pl.BlockSpec((1, size, count), lambda i: (i, 0, 0))
-
-    if count % LANES:
-        grads = grads.reshape(width, blocks, count).transpose(1, 0, 2)
-
+    count = 2 * half
     return pl.pallas_call(
         feed_kernel,
-        grid=(blocks,),
         out_shape=(
-            jax.ShapeDtypeStruct((blocks, inner, count), BF16),
-            jax.ShapeDtypeStruct((blocks, inner, count), BF16),
-            jax.ShapeDtypeStruct((blocks, width, count), BF16),
-        ),
-        in_specs=[
-            block(width),
-            block(width) if count % LANES else pl.BlockSpec((width, count), lambda i: (0, i)),
-            whole((inner, width)),
-            whole((width, inner)),
-            whole((inner, width)),
-            whole((inner, 1)),
-        ],
-        out_specs=(block(inner), block(inner), block(width)),
-        compiler_params=pltpu.CompilerParams(vmem_limit_bytes=28 * 2**20),
+            jax.ShapeDtypeStruct((width, count), BF16),
+            jax.ShapeDtypeStruct((inner, count), BF16),
+            jax.ShapeDtypeStruct((inner, count), BF16),
+            jax.ShapeDtypeStruct((width, half), BF16),
+            jax.ShapeDtypeStruct((width, half), BF16),
+        ),
+        in_specs=[VM] * 7,
+        out_specs=(VM,) * 5,
+        compiler_params=pltpu.CompilerParams(vmem_limit_bytes=12 * 2**20),
         cost_estimate=pl.CostEstimate(
-            flops=6 * blocks * width * inner * count, bytes_accessed=2**24, transcendentals=0
+            flops=6 * width * inner * count, bytes_accessed=2**22, transcendentals=0
         ),
         name="feed",
-    )(rows, grads, up_turned, up, down, bias)
-
-
-def feed_weights_kernel(rows, grads, hidden, grad_pre, grad_down, grad_up, bias, *, square):
-    blocks, width, count = rows.shape
-    inner = hidden.shape[1]
-
-    def lanes(n):
-        return slice(n * count, (n + 1) * count)
-
-    def weights(target, first, second, columns):
-        step = min(256, columns)
-        whole = jnp.concatenate([first(n) for n in range(blocks)], 1)
-        for start in range(0, columns, step):
+    )(rows_up, rows_down, given, up_turned, up, down, bias)
+
+
+def given_kernel(spot, grads, *given):
+    blocks = len(given)
+    count = given[0].shape[1]
+    for step, target in enumerate(given):
+        lanes = ring_lanes(spot[0], step, blocks, count)
+        target[...] = jnp.concatenate([grads[:, spread] for spread in lanes], 1)
+
+
+def given_grads(spot, grads, blocks):
+    width, length = grads.shape
+    count = length // blocks
+    if count // 2 % LANES:
+        found = []
+        for step in range(blocks):
+            below = (spot[0] - step) % blocks * count
+            above = (spot[0] + step) % blocks * count + count // 2
+            halves = [lax.dynamic_slice_in_dim(grads, at, count // 2, 1) for at in (below, above)]
+            found.append(jnp.concatenate(halves, 1))
+        return found
+    return pl.pallas_call(
+        given_kernel,
+        out_shape=(jax.ShapeDtypeStruct((width, count), BF16),) * blocks,
+        in_specs=[SM, VM],
+        out_specs=(VM,) * blocks,
+        compiler_params=pltpu.CompilerParams(vmem_limit_bytes=8 * 2**20),
+        name="given_grads",
+    )(spot, grads)
+
+
+def feed_weights_kernel(*refs, blocks, square):
+    rows, grads, hidden, grad_pre = [refs[n * blocks : (n + 1) * blocks] for n in range(4)]
+    grad_down, grad_up, bias = refs[4 * blocks :]
+
+    def weights(target, first, second):
+        step = min(256, second[0].shape[0])
+        whole = jnp.concatenate([ref[...] for ref in first], 1)
+        for start in range(0, second[0].shape[0], step):
             tile = slice(start, start + step)
-            turned = jnp.concatenate([second(n, tile) for n in range(blocks)], 1)
+            turned = jnp.concatenate([ref[tile] for ref in second], 1)
             target[:, tile] = contract(whole, turned, 1, 1).astype(BF16)
 
-    weights(grad_down, lambda n: hidden[n], lambda n, tile: grads[tile, lanes(n)], width)
+    weights(grad_down, hidden, grads)
     if square:
-        weights(grad_up, lambda n: rows[n], lambda n, tile: grad_pre[n, tile], inner)
+        weights(grad_up, rows, grad_pre)
     else:
-        weights(grad_up, lambda n: grad_pre[n], lambda n, tile: rows[n, tile], width)
-    total = sum(jnp.sum(grad_pre[n].astype(F32), 1, keepdims=True) for n in range(blocks))
+        weights(grad_up, grad_pre, rows)
+    total = sum(jnp.sum(ref[...].astype(F32), 1, keepdims=True) for ref in grad_pre)
     bias[...] = as_rows([total])[:1]
 
 
 def feed_weights(rows, grads, hidden, grad_pre):
-    blocks, width, count = rows.shape
-    inner = hidden.shape[1]
+    blocks = len(rows)
+    width, count = rows[0].shape
+    inner = hidden[0].shape[0]
     return pl.pallas_call(
-        functools.partial(feed_weights_kernel, square=inner == width),
+        functools.partial(feed_weights_kernel, blocks=blocks, square=inner == width),
         out_shape=(
             jax.ShapeDtypeStruct((inner, width), BF16),
             jax.ShapeDtypeStruct((inner, width), BF16),
             jax.ShapeDtypeStruct((1, inner), F32),
         ),
-        in_specs=[VM] * 4,
+        in_specs=[VM] * (4 * blocks),
         out_specs=(VM,) * 3,
         compiler_params=pltpu.CompilerParams(vmem_limit_bytes=14 * 2**20),
         cost_estimate=pl.CostEstimate(
             flops=4 * blocks * width * inner * count, bytes_accessed=2**24, transcendentals=0
         ),
         name="feed_weights",
-    )(rows, grads, hidden, grad_pre)
-
-
-def feed_out_kernel(spot, hidden, down_turned, middle, columns, out):
-    features = out.shape[2]
-    for n in range(hidden.shape[0]):
-        result = contract(down_turned[...], hidden[n], 1, 0)
-
-        def put(values):
-            for block in range(out.shape[0]):
-                out[block, n] = values[block * features : (block + 1) * features].astype(BF16)
-
-        put(result)
-
-        @pl.when(spot[0] == n)
-        def _():
-            put(result + middle[...] + columns[:, 5:6])
+    )(*rows, *grads, *hidden, *grad_pre)
+
+
+def feed_out_kernel(spot, *refs, blocks):
+    hidden = refs[:blocks]
+    down_turned, middle, columns, out = refs[blocks:]
+    features, half = out.shape[2:]
+    for step, source in enumerate(hidden):
+        result = contract(down_turned[...], source[...], 1, 0)
+        if step == 0:
+            result = result + middle[...] + columns[:, 5:6]
+        result = result.astype(BF16)
+        below = lax.rem(spot[0] + blocks - step, blocks)
+        above = lax.rem(spot[0] + step, blocks)
+        for block in range(blocks):
+            piece = result[block * features : (block + 1) * features]
+            out[block, 2 * below] = piece[:, :half]
+            out[block, 2 * above + 1] = piece[:, half:]
 
 
 def feed_out(spot, hidden, down_turned, middle, columns):
-    blocks, inner, count = hidden.shape
+    blocks = len(hidden)
+    inner, count = hidden[0].shape
     width = middle.shape[0]
     return pl.pallas_call(
-        feed_out_kernel,
-        out_shape=jax.ShapeDtypeStruct((blocks, blocks, width // blocks, count), BF16),
-        in_specs=[SM] + [VM] * 4,
+        functools.partial(feed_out_kernel, blocks=blocks),
+        out_shape=jax.ShapeDtypeStruct((blocks, 2 * blocks, width // blocks, count // 2), BF16),
+        in_specs=[SM] + [VM] * (blocks + 3),
         out_specs=VM,
         compiler_params=pltpu.CompilerParams(vmem_limit_bytes=8 * 2**20),
         cost_estimate=pl.CostEstimate(
             flops=2 * blocks * width * inner * count, bytes_accessed=2**23, transcendentals=0
         ),
         name="feed_out",
-    )(spot, hidden, down_turned, middle, columns)
+    )(spot, *hidden, down_turned, middle, columns)
 
 
 def enter_kernel(
-    spot, came, weight, tokens, columns, attended, middle, normed, inverse, low, *, heads
+    spot, came, weight, tokens, columns,
+    attended, middle, normed, inverse, low_up, low_down,
+    *, heads,
 ):
     size, half = came.shape[1:]
     count = 2 * half
@@ -806,7 +839,9 @@
     inverse[...] = scale
     centered = centered * scale
     normed[...] = centered
-    low[...] = (centered * columns[:, 2:3] + columns[:, 3:4]).astype(BF16)
+    low = (centered * columns[:, 2:3] + columns[:, 3:4]).astype(BF16)
+    low_up[...] = low[:, :half]
+    low_down[...] = low[:, half:]
 
 
 def enter(spot, came, weight, tokens, columns, heads):
@@ -818,10 +853,11 @@
             jax.ShapeDtypeStruct((width, count), F32),
             jax.ShapeDtypeStruct((width, count), F32),
             jax.ShapeDtypeStruct((1, count), F32),
-            jax.ShapeDtypeStruct((width, count), BF16),
+            jax.ShapeDtypeStruct((width, count // 2), BF16),
+            jax.ShapeDtypeStruct((width, count // 2), BF16),
         ),
         in_specs=[SM] + [VM] * 4,
-        out_specs=(VM,) * 5,
+        out_specs=(VM,) * 6,
         compiler_params=pltpu.CompilerParams(vmem_limit_bytes=12 * 2**20),
         name="enter",
     )(spot, came, weight, tokens, columns)
@@ -840,7 +876,7 @@
             up[...].astype(F32) + own_up[...].astype(F32),
             down[...].astype(F32) + own_down[...].astype(F32),
         ],
-        0,
+        1,
     )
     scaled = total * columns[:, 2:3]
     first = jnp.mean(scaled, 0, keepdims=True)
@@ -996,6 +1032,7 @@
         in_specs=[VM] * 5,
         out_specs=(VM,) * 5,
         compiler_params=pltpu.CompilerParams(vmem_limit_bytes=16 * 2**20),
+        cost_estimate=pl.CostEstimate(flops=2**31, bytes_accessed=2**22, transcendentals=0),
         name="prefix_back",
     )(total, hidden, embed, weight, low)
     return grad_embed[:rows], grad_weight, grad_bias[0], grad_out, grad_out_bias
@@ -1035,15 +1072,21 @@
     return (out, results) if beside else out
 
 
-def ring_terms(blocks, axis, beside=(), first=None):
+def half_blocks(blocks, axis):
     count, place = lax.axis_size(axis), lax.axis_index(axis)
     half = blocks.shape[1] // 2
 
-    def own(offset, upper):
-        block = lax.dynamic_index_in_dim(blocks, (place + offset) % count, 0, keepdims=False)
+    def own(step, upper):
+        at = place + step if upper else place - step
+        block = lax.dynamic_index_in_dim(blocks, at % count, 0, keepdims=False)
         return block[half:] if upper else block[:half]
 
-    up, down = first or (own(-1, False), own(1, True))
+    return own
+
+
+def ring_terms(own, axis, beside=(), first=None):
+    count = lax.axis_size(axis)
+    up, down = first or (own(1, False), own(1, True))
     state = None
     for step in range(1, count):
         up = lax.ppermute(up, axis, ring(axis, 1))
@@ -1052,8 +1095,8 @@
             state = beside[step - 1](state)
             up, down, state = lax.optimization_barrier((up, down, state))
         if step < count - 1:
-            up = (up.astype(F32) + own(-1 - step, False).astype(F32)).astype(BF16)
-            down = (down.astype(F32) + own(1 + step, True).astype(F32)).astype(BF16)
+            up = (up.astype(F32) + own(step + 1, False).astype(F32)).astype(BF16)
+            down = (down.astype(F32) + own(step + 1, True).astype(F32)).astype(BF16)
     for other in beside[count - 1 :]:
         state = other(state)
     return (up, down, own(0, False), own(0, True)), state
@@ -1074,15 +1117,6 @@
     for step in range(1, chips):
         block = lax.dynamic_index_in_dim(blocks, (chip + step) % chips, 0, keepdims=False)
         parts.append(lax.ppermute(block, "seq", ring("seq", 2 * step)))
-    return parts
-
-
-def owned_direct(values, axis):
-    count, place = lax.axis_size(axis), lax.axis_index(axis)
-    parts = [lax.dynamic_index_in_dim(values, place, 0, keepdims=False)]
-    for step in range(1, count):
-        block = lax.dynamic_index_in_dim(values, (place + step) % count, 0, keepdims=False)
-        parts.append(lax.ppermute(block, axis, ring(axis, step)))
     return parts
 
 
@@ -1258,14 +1292,15 @@
     out_low, full_grad, late_up, late_down, late_qkv = lax.optimization_barrier(
         (out_low, full_grad, w_up, w_down, w_qkv)
     )
-    late_flat = late_qkv.reshape(width, heads * 3 * size)
+    late_qkv = late_qkv.transpose(1, 2, 0).reshape(heads * 3 * size, width)
+    up_turned, down_turned, late_flat = turned(late_up, late_down, late_qkv)
 
     came = lax.all_to_all(regrouped(out_low, chunk), both, 0, 0, tiled=True)
     came, up_turned, down_turned, late_flat, w_out_full = lax.optimization_barrier(
-        (came, late_up.T, late_down.T, late_flat, w_out_full)
+        (came, up_turned, down_turned, late_flat, w_out_full)
     )
     if paired:
-        attended, middle, normed2, inverse2, out2 = enter(
+        attended, middle, normed2, inverse2, ring_up, ring_down = enter(
             spot, came, w_out_full, full_tokens, columns, heads
         )
     else:
@@ -1278,19 +1313,35 @@
         inverse2 = lax.rsqrt(jnp.mean(centered * centered, 0, keepdims=True) + EPS)
         normed2 = centered * inverse2
         out2 = (normed2 * columns[:, 2:3] + columns[:, 3:4]).astype(BF16)
-
-    full2 = ring_gather(out2, "tensor")
-    hidden, grad_pre, part = feed(
-        full2, full_grad, up_turned, w_up, w_down, b_up.astype(F32)[:, None]
-    )
+        ring_up, ring_down = out2[:, : own_rows // 2], out2[:, own_rows // 2 :]
+
+    bias_up = b_up.astype(F32)[:, None]
+    given = given_grads(spot, full_grad, tensors)
+    results = []
+    for step in range(tensors):
+        def block(up=ring_up, down=ring_down, step=step):
+            return feed(up, down, given[step], up_turned, w_up, w_down, bias_up)
+
+        if step < tensors - 1:
+            ring_up = lax.ppermute(ring_up, "tensor", ring("tensor", 1))
+            ring_down = lax.ppermute(ring_down, "tensor", ring("tensor", -1))
+            ring_up, ring_down, result = lax.optimization_barrier((ring_up, ring_down, block()))
+        else:
+            result = block()
+        results.append(result)
+    blocks, hidden, grad_pre, parts_up, parts_down = zip(*results)
 
     def weights_here(_):
-        return feed_weights(full2, full_grad, hidden, grad_pre)
+        return feed_weights(blocks, given, hidden, grad_pre)
 
     def out_here(state):
         return state, feed_out(spot, hidden, down_turned, middle, columns)
 
-    terms, (weights, mlp_out) = ring_terms(part, "tensor", (weights_here, out_here))
+    terms, (weights, mlp_out) = ring_terms(
+        lambda step, upper: (parts_down if upper else parts_up)[step],
+        "tensor",
+        (weights_here, out_here),
+    )
     grad_w_down, grad_w_up, grad_b_up = weights
     feed_sums = lax.psum((grad_w_down, grad_w_up), "seq")
 
@@ -1300,7 +1351,7 @@
         )
     else:
         up, down, own_up, own_down = [a.astype(F32) for a in terms]
-        grad_normed2 = jnp.concatenate([up + own_up, down + own_down], 0)
+        grad_normed2 = jnp.concatenate([up + own_up, down + own_down], 1)
         scaled = grad_normed2 * columns[:, 2:3]
         first = jnp.mean(scaled, 0, keepdims=True)
         second = jnp.mean(scaled * normed2, 0, keepdims=True)
@@ -1348,9 +1399,9 @@
         (came, output_act, grad_w_out, out_w_down, out_w_up)
     )
     if paired:
-        grad_flat, grad_part, first_up, first_down, head_row, prefix_low, *small = unproject(
+        grad_flat, grad_part, first_up, first_down, head_row, prefix_low, small = unproject(
             spot, came, late_flat, full_tokens, stats, columns, grad_middle, token_sums,
-            reparam_out.reshape(reparam_out.shape[0], -1), heads, size, own_rows,
+            reparam_out, heads, size, own_rows,
         )
         first_blocks = first_up, first_down
         mine, other = rest_halves(spot, grad_flat, full1, grad_w_out)
@@ -1392,38 +1443,37 @@
 
     grad_b_down = jnp.sum(out_grad.astype(F32), 0)
 
-    def small_here(_):
-        if not paired:
-            return swapped(other), owned_direct(small, "tensor")
-        pieces = [small[0]]
-        for step in range(1, tensors):
-            pieces.append(lax.ppermute(small[step], "tensor", ring("tensor", step)))
-        return swapped(other), pieces
-
-    def parts_here(state):
-        half = (mine.astype(F32) + state[0].astype(F32)).astype(BF16)
+    def halves_here(_):
+        return (mine.astype(F32) + swapped(other).astype(F32)).astype(BF16)
+
+    def parts_here(half):
+        return chip_parts(half), lax.all_to_all(small, "tensor", 0, 0, tiled=True)
+
+    def totals(parts):
         if paired:
-            sums = small_totals(
-                state[1], grad_b_down[None], grad_b_up, head_row, rows,
-                prefix_hidden.shape[1], width,
+            return small_totals(
+                parts, grad_b_down[None], grad_b_up, head_row, rows, prefix_hidden.shape[1], width
             )
-            return chip_parts(half), sums
-        sums = sum(state[1])[0]
+        sums = jnp.sum(parts, 0)[0]
         after_rows = 5 * features + 2 * rows
         row_means = sums[5 * features : after_rows].reshape(2, rows) / width
         hidden = sums[after_rows:].reshape(PAD, -1)
         mixed_sums = head_sums.reshape(heads, 3, size)
         late = [sums[: 5 * features], grad_b_down, grad_b_up[0]]
         late += [mixed_sums[:, 0].reshape(-1), mixed_sums[:, 2].reshape(-1)]
-        return chip_parts(half), (row_means, hidden, jnp.concatenate(late)[None])
+        return row_means, hidden, jnp.concatenate(late)[None]
 
     def gather_here(state):
-        return chip_gather(state[0]), state[1], spread(state[1][2], "seq")
-
-    last_terms, (rest_half, (row_means, hidden_grad, _), late) = ring_terms(
-        grad_part.reshape(tensors, features, rows),
+        row_means, hidden_grad, late = totals(state[1])
+        prefix_grads = prefix_back(
+            hidden_grad, prefix_hidden, prefix_embed, reparam_in, prefix_low, heads
+        )
+        return chip_gather(state[0]), row_means, spread(late, "seq"), prefix_grads
+
+    last_terms, (rest_half, row_means, late, prefix_grads) = ring_terms(
+        half_blocks(grad_part.reshape(tensors, features, rows), "tensor"),
         "tensor",
-        (small_here, parts_here) + (lambda state: state,) * (tensors - 4) + (gather_here,),
+        (halves_here, parts_here) + (lambda state: state,) * (tensors - 4) + (gather_here,),
         first_blocks,
     )
     input_grad = finish(
@@ -1452,13 +1502,6 @@
         vectors[i] for i in range(6)
     ]
 
-    (
-        grad_prefix_embed,
-        grad_reparam_in,
-        grad_reparam_in_bias,
-        grad_reparam_out,
-        grad_reparam_out_bias,
-    ) = prefix_back(hidden_grad, prefix_hidden, prefix_embed, reparam_in, prefix_low, heads)
     return (
         output_act,
         input_grad,
@@ -1474,11 +1517,7 @@
         out_b_up,
         out_w_down,
         out_b_down,
-        grad_prefix_embed,
-        grad_reparam_in,
-        grad_reparam_in_bias,
-        grad_reparam_out,
-        grad_reparam_out_bias,
+        *prefix_grads,
     )
 
 

time: 484 us -> 473 us (0.977)
  waiting for transfers between devices: 129 us -> 96 us
  local copies, waits for them, and re-layouts: 60.8 us -> 69.5 us
  other arithmetic: 20.8 us -> 28.2 us
    unnamed x179 -> x198, local copies, waits for them, and re-layouts: 36.7 us -> 54 us
    ppermute x6 -> x3, waiting for transfers between devices: 24.6 us -> 7.5 us  [ring_gather(): up = lax.ppermute(up, axis, ring(axis, 1))]
    ppermute x6 -> x3, waiting for transfers between devices: 26.8 us -> 11.3 us  [ring_gather(): down = lax.ppermute(down, axis, ring(axis, -1))]
    optimization_barrier x3 -> x0, local copies, waits for them, and re-layouts: 8.04 us -> none  [the longest x2 6.47 us: on_device(): lax.optimization_barrier((out_low, full_grad, w_up, w_down, w_qkv))]
    ppermute x3 -> x6, starting transfers between devices: 2.95 us -> 9.79 us  [the longest x3 7.18 us: on_device(): ring_down = lax.ppermute(ring_down, 'tensor', ring('tensor', -1))]
    ppermute x6, waiting for transfers between devices: 9.3 us -> 15.8 us  [ring_terms(): down = lax.ppermute(down, axis, ring(axis, -1))]
    ppermute x6, starting transfers between devices: 8.19 us -> 3.32 us  [ring_terms(): up = lax.ppermute(up, axis, ring(axis, 1))]
    convert_element_type x5 -> x7, other arithmetic: 5.45 us -> 10.2 us  [the longest x4 6.04 us: ring_terms(): down = (down.astype(F32) + own(step + 1, True).astype(F32)).astype(BF16)]
  transfers between devices with their start and end apart: 52 -> 50, of which waited for: 28 -> 26; matrix products, arithmetic and copies ran while one was open for 9% -> 9% of each run, Pallas kernels for 25% -> 28%
where the time goes in v5:
time: 473 us; the launch traced here: 463 us
  Pallas kernels  147 us (31%)
  starting transfers between devices  102 us (22%)
  waiting for transfers between devices  96 us (20%)
  local copies, waits for them, and re-layouts  69.5 us (15%)
  other arithmetic  28.2 us (6%)
  between operations  15.4 us (3%)
  matrix products  4.92 us (1%)
    pallas_call x1, Pallas kernels, attend_backward(): pl.pallas_call(functools.partial(backward_kernel, tile=tile, keys=keys, p...  57.8 us
    unnamed x198, local copies, waits for them, and re-layouts  54 us
    pallas_call x1, Pallas kernels, attend_forward(): pl.pallas_call(functools.partial(forward_kernel, tile=tile, keys=keys, pr...  31.8 us
    ppermute x6, waiting for transfers between devices, ring_terms(): down = lax.ppermute(down, axis, ring(axis, -1))  15.8 us
    ppermute x6, starting transfers between devices, ring_terms(): down = lax.ppermute(down, axis, ring(axis, -1))  15.5 us
    all_to_all x3, starting transfers between devices, spread(): return lax.all_to_all(copies, axis, 0, 0, tiled=True)  14.6 us
    pallas_call x4, Pallas kernels, feed(): pl.pallas_call(feed_kernel, out_shape=(jax.ShapeDtypeStruct((width, count...  13.7 us
    all_to_all x2, waiting for transfers between devices, on_device(): came = lax.all_to_all(sent, 'seq', 0, 0, tiled=True)  12.8 us
  transfers between devices with their start and end apart: 50, of which 26 were waited for; matrix products, arithmetic and copies ran while one was open for 9% of the time, Pallas kernels for 28%

profile of v5, /device:TPU:1, one launch (start us, length us, event | category | flops | bytes accessed | tf_op | source)
XLA Modules:
  0.0 463.3 jit_solution(17851580917448656549)
XLA Ops:
  11.4 2.1 collective-permute-start
  13.5 2.0 collective-permute-start.2
  16.3 3.3 all-to-all-start
  21.9 5.2 %collective-permute-done.2 = bf16[128,1024]{1,0:T(8,128)(2,1)} collective-permute-done((bf16[128,1024]{1,0:T(8,128)(2,1)}, bf16[128,1024]{1,0:T(8,128)(2,1)}, u32[]{:S(2)}, u32[]{:S(2)}) %collective-permute-start.2) | collective-permute-done | bytes 262176 | tf_op jit(solution)/shard_map/ppermute | solution.py:1066
  30.2 6.7 %all-to-all-start.1 = ((s32[8,4,128]{2,1,0:T(4,128)}), s32[8,4,128]{2,1,0:T(4,128)S(1)}, u32[]{:S(2)}, u32[]{:S(2)}) async-start(s32[8,4,128]{2,1,0:T(4,128)} %broadcast_in_dim_broadcast_in_dim_broadcast_in_dim.2), calls=%async_computation.1 | async-start | bytes 32768 | tf_op jit(solution)/shard_map/all_to_all | solution.py:1044
  36.9 2.9 collective-permute-done.3
  39.8 3.3 collective-permute-start.5
  43.1 5.9 %collective-permute-done.4 = bf16[128,1024]{1,0:T(8,128)(2,1)S(1)} collective-permute-done((bf16[128,1024]{1,0:T(8,128)(2,1)S(1)}, bf16[128,1024]{1,0:T(8,128)(2,1)S(1)}, u32[]{:S(2)}, u32[]{:S(2)}) %collective-permute-start.4) | collective-permute-done | bytes 262176 | tf_op jit(solution)/shard_map/ppermute | solution.py:1065
  49.0 3.2 collective-permute-done.5
  56.9 3.2 project.1
  62.5 5.9 %all-to-all-start.2 = ((bf16[8,64,1536]{2,1,0:T(8,128)(2,1)}), bf16[8,64,1536]{2,1,0:T(8,128)(2,1)S(1)}, u32[]{:S(2)}, u32[]{:S(2)}) async-start(bf16[8,64,1536]{2,1,0:T(8,128)(2,1)} %copy-done.25), calls=%async_computation.2 | async-start | bytes 3145728 | tf_op jit(solution)/shard_map/all_to_all | solution.py:1276
  68.5 2.2 collective-permute-start.7
  70.7 2.3 collective-permute-start.8
  73.0 2.6 collective-permute-done.6
  75.6 4.1 collective-permute-done.7
  79.7 6.2 %all-to-all-done.2.query.own = bf16[8,64,1536]{2,1,0:T(8,128)(2,1)S(1)} async-done(((bf16[8,64,1536]{2,1,0:T(8,128)(2,1)}), bf16[8,64,1536]{2,1,0:T(8,128)(2,1)S(1)}, u32[]{:S(2)}, u32[]{:S(2)}) %all-to-all-start.2) | async-done | bytes 1572896 | tf_op jit(solution)/shard_map/all_to_all | solution.py:1276
  86.0 3.5 collective-permute-start.9
  94.0 31.8 %attend_forward.1 = (bf16[32,64,128]{2,1,0:T(8,128)(2,1)S(1)}, f32[32,64,128]{2,1,0:T(8,128)S(1)}, f32[8,1,512]{2,1,0:T(1,128)S(1)}) custom-call(s32[5]{0:T(128)S(1)} %pad_add_fusion.meta, bf16[8,64,1536]{2,1,0:T(8,128)(2,1)S(1)} %copy-done.23, bf16[8,64,1536]{2,1,0:T(8,128)(2,1)S(1)} %copy-done.23, bf16[8,64,1536]{2,1,0:T(8,128)(2,1)} %collective-permute-done.9.other, ...), custom_call_target="tpu_custom_call" | custom-call | flops 17179869184 | bytes 8388608 | tf_op jit(solution)/shard_map/attend_forward/pallas_call | solution.py:224
  127.6 3.0 all-to-all-start.3
  139.7 3.2 copy.90
  142.9 3.0 all-to-all-done.3.came
  149.1 2.6 enter.1
  154.4 3.3 collective-permute-start.11
  162.7 3.9 feed.4
  166.9 2.3 collective-permute-start.12
  170.1 3.9 feed.5
  174.5 8.2 %collective-permute-done.13.rows_down = bf16[1024,128]{1,0:T(8,128)(2,1)S(1)} collective-permute-done((bf16[1024,128]{1,0:T(8,128)(2,1)}, bf16[1024,128]{1,0:T(8,128)(2,1)S(1)}, u32[]{:S(2)}, u32[]{:S(2)}) %collective-permute-start.13) | collective-permute-done | bytes 262176 | tf_op jit(solution)/shard_map/ppermute | solution.py:1327
  183.0 3.0 collective-permute-start.17
  186.0 3.4 collective-permute-start.15
  189.4 2.9 feed.6
  195.7 2.9 feed.7
  199.4 4.5 feed_weights.1
  209.1 2.2 collective-permute-start.19
  217.8 4.2 feed_out.1
  224.1 3.3 collective-permute-start.21
  228.5 2.3 collective-permute-done.21.down
  230.8 5.8 %collective-permute-done.20.up = bf16[1024,128]{1,0:T(8,128)(2,1)S(1)} collective-permute-done((bf16[1024,128]{1,0:T(8,128)(2,1)S(1)}, bf16[1024,128]{1,0:T(8,128)(2,1)S(1)}, u32[]{:S(2)}, u32[]{:S(2)}) %collective-permute-start.20) | collective-permute-done | bytes 262176 | tf_op jit(solution)/shard_map/ppermute | solution.py:1092
  242.9 9.3 %all-to-all-start.4 = ((bf16[32,64,128]{2,1,0:T(8,128)(2,1)}), bf16[32,64,128]{2,1,0:T(8,128)(2,1)S(1)}, u32[]{:S(2)}, u32[]{:S(2)}) async-start(bf16[32,64,128]{2,1,0:T(8,128)(2,1)} %copy-done.38), calls=%async_computation.4 | async-start | bytes 1048576 | tf_op jit(solution)/shard_map/all_to_all | solution.py:1366
  252.3 3.1 convolution_convert_fusion
  255.5 12.2 %all-to-all-done.4.grad_out = bf16[32,64,128]{2,1,0:T(8,128)(2,1)S(1)} async-done(((bf16[32,64,128]{2,1,0:T(8,128)(2,1)}), bf16[32,64,128]{2,1,0:T(8,128)(2,1)S(1)}, u32[]{:S(2)}, u32[]{:S(2)}) %all-to-all-start.4) | async-done | bytes 524320 | tf_op jit(solution)/shard_map/all_to_all | solution.py:1366
  267.7 4.7 %all-to-all-start.5 = ((bf16[4,8,256,128]{3,2,1,0:T(8,128)(2,1)}), bf16[4,8,256,128]{3,2,1,0:T(8,128)(2,1)}, u32[]{:S(2)}, u32[]{:S(2)}) async-start(bf16[4,8,256,128]{3,2,1,0:T(8,128)(2,1)} %feed_out.1), calls=%async_computation.5 | async-start | bytes 4194304 | tf_op jit(solution)/shard_map/all_to_all | solution.py:1371
  275.0 57.8 %attend_backward.1 = (bf16[8,64,512]{2,1,0:T(8,128)(2,1)S(1)}, bf16[8,64,1024]{2,1,0:T(8,128)(2,1)S(1)}, bf16[8,64,1024]{2,1,0:T(8,128)(2,1)}, f32[2,16,64]{2,1,0:T(8,128)S(1)}) custom-call(s32[5]{0:T(128)S(1)} %pad_add_fusion.meta, bf16[8,64,1536]{2,1,0:T(8,128)(2,1)S(1)} %copy-done.24, bf16[8,64,1536]{2,1,0:T(8,128)(2,1)S(1)} %copy-done.24, ...), custom_call_target="tpu_custom_call" | custom-call | flops 42949672960 | bytes 8388608 | tf_op jit(solution)/shard_map/attend_backward/pallas_call | solution.py:369
  333.9 2.8 collective-permute-done.22
  339.7 4.3 all-to-all-start.6
  344.0 4.2 convert_element_type.200
  348.2 2.5 convert_element_type.201
  350.7 3.0 reduce_sum.41
  353.7 2.0 copy.96
  356.4 6.5 %all-to-all-done.6.came = bf16[8,64,1664]{2,1,0:T(8,128)(2,1)} async-done(((bf16[8,64,1664]{2,1,0:T(8,128)(2,1)}), bf16[8,64,1664]{2,1,0:T(8,128)(2,1)}, u32[]{:S(2)}, u32[]{:S(2)}) %all-to-all-start.6) | async-done | bytes 1703968 | tf_op jit(solution)/shard_map/all_to_all | solution.py:1393
  365.6 8.9 %unproject.1 = (bf16[768,1024]{1,0:T(8,128)(2,1)S(1)}, bf16[1024,1024]{1,0:T(8,128)(2,1)S(1)}, bf16[128,1024]{1,0:T(8,128)(2,1)S(1)}, bf16[128,1024]{1,0:T(8,128...) custom-call(s32[3]{0:T(128)S(1)} %pad_add_fusion.1.spot, ...), custom_call_target="tpu_custom_call" | custom-call | flops 3221225472 | bytes 8388608 | tf_op jit(solution)/shard_map/unproject/pallas_call | solution.py:548
  374.5 4.8 %rest_halves.1 = (bf16[512,1024]{1,0:T(8,128)(2,1)S(1)}, bf16[512,1024]{1,0:T(8,128)(2,1)S(1)}) custom-call(s32[3]{0:T(128)S(1)} %pad_add_fusion.1.spot, bf16[768,1024]{1,0:T(8,128)(2,1)S(1)} %get-tuple-element.290.flat, bf16[1024,1024]{1,0:T(8,128)(2,1)S(1)} %copy-done.55, bf16[256,1024]{1,0:T(8,128)(2,1)S(1)} %copy-done.66), custom_call_target="tpu_custom_call" | custom-call | flops 1610612736 | bytes 8388608 | tf_op jit(solution)/shard_map/rest_halves/pallas_call | solution.py:945
  380.3 3.6 collective-permute-start.25
  387.2 3.4 all-to-all-start.7
  391.5 2.1 add_convert_fusion
  393.9 4.7 %collective-permute-done.24 = bf16[128,1024]{1,0:T(8,128)(2,1)} collective-permute-done((bf16[128,1024]{1,0:T(8,128)(2,1)S(1)}, bf16[128,1024]{1,0:T(8,128)(2,1)}, u32[]{:S(2)}, u32[]{:S(2)}) %collective-permute-start.24) | collective-permute-done | bytes 262176 | tf_op jit(solution)/shard_map/ppermute | solution.py:1093
  400.1 2.0 collective-permute-start.30
  407.5 5.5 %collective-permute-done.29 = bf16[128,1024]{1,0:T(8,128)(2,1)} collective-permute-done((bf16[128,1024]{1,0:T(8,128)(2,1)}, bf16[128,1024]{1,0:T(8,128)(2,1)}, u32[]{:S(2)}, u32[]{:S(2)}) %collective-permute-start.29) | collective-permute-done | bytes 262176 | tf_op jit(solution)/shard_map/ppermute | solution.py:1119
  413.0 7.0 %collective-permute-done.27 = bf16[128,1024]{1,0:T(8,128)(2,1)} collective-permute-done((bf16[128,1024]{1,0:T(8,128)(2,1)}, bf16[128,1024]{1,0:T(8,128)(2,1)}, u32[]{:S(2)}, u32[]{:S(2)}) %collective-permute-start.27) | collective-permute-done | bytes 262176 | tf_op jit(solution)/shard_map/ppermute | solution.py:1093
  420.0 2.0 add_convert_fusion.2
  423.2 2.4 collective-permute-start.35
  426.3 4.7 %all-to-all-start.8 = ((f32[8,16,256]{2,1,0:T(8,128)}), f32[8,16,256]{2,1,0:T(8,128)S(1)}, u32[]{:S(2)}, u32[]{:S(2)}) async-start(f32[8,16,256]{2,1,0:T(8,128)} %broadcast_in_dim.97), calls=%async_computation.9 | async-start | bytes 262144 | tf_op jit(solution)/shard_map/all_to_all | solution.py:1044
  432.8 3.2 collective-permute-start.32
  437.3 5.7 %prefix_back.1 = (f32[16,1024]{1,0:T(8,128)}, f32[1024,512]{1,0:T(8,128)}, f32[1,512]{1,0:T(1,128)}, f32[512,4,128]{2,1,0:T(4,128)}, f32[4,128]{1,0:T(4,128)}) custom-call(f32[16,512]{1,0:T(8,128)S(1)} %get-tuple-element.311.total, f32[16,512]{1,0:T(8,128)S(1)} %pad.18.hidden, bf16[16,1024]{1,0:T(8,128)(2,1)S(1)} %pad.19.embed, ...), custom_call_target="tpu_custom_call" | custom-call | flops 2147483648 | bytes 4194304 | tf_op jit(solution)/shard_map/prefix_back/pallas_call | solution.py:1023
  453.4 3.0 rest_whole.1
  (339 shorter events, 108.5 us)
Async XLA Ops:
  7.2 61.2 %copy-start = (bf16[4,64,1024]{2,1,0:T(8,128)(2,1)S(1)}, bf16[4,64,1024]{2,1,0:T(8,128)(2,1)}, u32[]{:S(2)}) copy-start(bf16[4,64,1024]{2,1,0:T(8,128)(2,1)} %param.27) | copy-start | bytes 1572868
  11.4 10.4 %collective-permute-start = (bf16[128,1024]{1,0:T(8,128)(2,1)}, bf16[128,1024]{1,0:T(8,128)(2,1)S(1)}, u32[]{:S(2)}, u32[]{:S(2)}) collective-permute-start(bf16[128,1024]{1,0:T(8,128)(2,1)} %get-tuple-element.348), channel_id=1, source_target_pairs={{0,1},{1,2},{2,3},{3,0},{4,5},{5,6},{6,7},{7,4},{8,9},{9,10},{10,1... | collective-permute-start | bytes 786440 | tf_op jit(solution)/shard_map/ppermute | solution.py:1065
  13.5 13.5 %collective-permute-start.2 = (bf16[128,1024]{1,0:T(8,128)(2,1)}, bf16[128,1024]{1,0:T(8,128)(2,1)}, u32[]{:S(2)}, u32[]{:S(2)}) collective-permute-start(bf16[128,1024]{1,0:T(8,128)(2,1)} %get-tuple-element.347), channel_id=1, source_target_pairs={{0,3},{1,0},{2,1},{3,2},{4,7},{5,4},{6,5},{7,6},{8,11},{9,8},{10,9... | collective-permute-start | bytes 786440 | tf_op jit(solution)/shard_map/ppermute | solution.py:1066
  16.3 13.2 %all-to-all-start = ((bf16[4,6,256]{2,1,0:T(8,128)(2,1)}), bf16[4,6,256]{2,1,0:T(8,128)(2,1)S(1)}, u32[]{:S(2)}, u32[]{:S(2)}) async-start(bf16[4,6,256]{2,1,0:T(8,128)(2,1)} %broadcast_in_dim.78), calls=%async_computation | async-start | bytes 32768 | tf_op jit(solution)/shard_map/all_to_all | solution.py:1044
  20.2 33.0 %copy-start.89 = (bf16[4,128]{1,0:T(4,128)(2,1)S(1)}, bf16[4,128]{1,0:T(4,128)(2,1)}, u32[]{:S(2)}) copy-start(bf16[4,128]{1,0:T(4,128)(2,1)} %param.26) | copy-start | bytes 3076
  21.9 15.0 %collective-permute-start.1 = (bf16[128,1024]{1,0:T(8,128)(2,1)S(1)}, bf16[128,1024]{1,0:T(8,128)(2,1)S(1)}, u32[]{:S(2)}, u32[]{:S(2)}) collective-permute-start(bf16[128,1024]{1,0:T(8,128)(2,1)S(1)} %collective-permute-done), channel_id=1, source_target_pairs={{0,1},{1,2},{2,3},{3,0},{4,5},{5,6},{6,7},{7,4},{8,9},{9,10},{10,1... | collective-permute-start | bytes 786440 | tf_op jit(solution)/shard_map/ppermute | solution.py:1065
  27.1 12.7 %collective-permute-start.3 = (bf16[128,1024]{1,0:T(8,128)(2,1)}, bf16[128,1024]{1,0:T(8,128)(2,1)S(1)}, u32[]{:S(2)}, u32[]{:S(2)}) collective-permute-start(bf16[128,1024]{1,0:T(8,128)(2,1)} %collective-permute-done.2), channel_id=1, source_target_pairs={{0,3},{1,0},{2,1},{3,2},{4,7},{5,4},{6,5},{7,6},{8,11},{9,8},{10,9... | collective-permute-start | bytes 786440 | tf_op jit(solution)/shard_map/ppermute | solution.py:1066
  30.2 12.9 %all-to-all-start.1 = ((s32[8,4,128]{2,1,0:T(4,128)}), s32[8,4,128]{2,1,0:T(4,128)S(1)}, u32[]{:S(2)}, u32[]{:S(2)}) async-start(s32[8,4,128]{2,1,0:T(4,128)} %broadcast_in_dim_broadcast_in_dim_broadcast_in_dim.2), calls=%async_computation.1 | async-start | bytes 32768 | tf_op jit(solution)/shard_map/all_to_all | solution.py:1044
  36.9 90.7 %all-gather.4.cloned.1.call-start = ((), (), s32[]{:S(2)}) async-start(), calls=%async_computation.10 | async-start | bytes 2621440 | tf_op jit(solution)/shard_map/all_gather | solution.py:1287
  39.7 9.2 %collective-permute-start.4 = (bf16[128,1024]{1,0:T(8,128)(2,1)S(1)}, bf16[128,1024]{1,0:T(8,128)(2,1)S(1)}, u32[]{:S(2)}, u32[]{:S(2)}) collective-permute-start(bf16[128,1024]{1,0:T(8,128)(2,1)S(1)} %collective-permute-done.1), channel_id=1, source_target_pairs={{0,1},{1,2},{2,3},{3,0},{4,5},{5,6},{6,7},{7,4},{8,9},{9,10},{10,1... | collective-permute-start | bytes 786440 | tf_op jit(solution)/shard_map/ppermute | solution.py:1065
  39.8 12.4 %collective-permute-start.5 = (bf16[128,1024]{1,0:T(8,128)(2,1)S(1)}, bf16[128,1024]{1,0:T(8,128)(2,1)}, u32[]{:S(2)}, u32[]{:S(2)}) collective-permute-start(bf16[128,1024]{1,0:T(8,128)(2,1)S(1)} %collective-permute-done.3), channel_id=1, source_target_pairs={{0,3},{1,0},{2,1},{3,2},{4,7},{5,4},{6,5},{7,6},{8,11},{9,8},{10,9... | collective-permute-start | bytes 786440 | tf_op jit(solution)/shard_map/ppermute | solution.py:1066
  62.5 26.9 %copy-start.90 = (bf16[4,128]{1,0:T(4,128)(2,1)S(1)}, bf16[4,128]{1,0:T(4,128)(2,1)}, u32[]{:S(2)}) copy-start(bf16[4,128]{1,0:T(4,128)(2,1)} %param.39) | copy-start | bytes 3076
  62.5 26.9 %copy-start.91 = (bf16[512]{0:T(512)(128)(2,1)S(1)}, bf16[512]{0:T(512)(128)(2,1)}, u32[]{:S(2)}) copy-start(bf16[512]{0:T(512)(128)(2,1)} %param.37) | copy-start | bytes 3076
  62.5 27.0 %copy-start.85 = (bf16[10,1024]{1,0:T(8,128)(2,1)S(1)}, bf16[10,1024]{1,0:T(8,128)(2,1)}, u32[]{:S(2)}) copy-start(bf16[10,1024]{1,0:T(8,128)(2,1)} %param.35) | copy-start | bytes 61444
  62.5 28.5 %copy-start.33 = (bf16[512,4,128]{2,1,0:T(4,128)(2,1)S(1)}, bf16[512,4,128]{2,1,0:T(4,128)(2,1)}, u32[]{:S(2)}) copy-start(bf16[512,4,128]{2,1,0:T(4,128)(2,1)} %reparam.1) | copy-start | bytes 1572868
  62.5 23.4 %all-to-all-start.2 = ((bf16[8,64,1536]{2,1,0:T(8,128)(2,1)}), bf16[8,64,1536]{2,1,0:T(8,128)(2,1)S(1)}, u32[]{:S(2)}, u32[]{:S(2)}) async-start(bf16[8,64,1536]{2,1,0:T(8,128)(2,1)} %copy-done.25), calls=%async_computation.2 | async-start | bytes 3145728 | tf_op jit(solution)/shard_map/all_to_all | solution.py:1276
  68.4 71.3 %all-gather.6.cloned.1.call-start = ((), (), s32[]{:S(2)}) async-start(), calls=%async_computation.12 | async-start | bytes 2359296 | tf_op jit(solution)/shard_map/all_gather | solution.py:1278
  68.4 7.2 %collective-permute-start.6 = (bf16[32,1024]{1,0:T(8,128)(2,1)S(1)}, bf16[32,1024]{1,0:T(8,128)(2,1)S(1)}, u32[]{:S(2)}, u32[]{:S(2)}) collective-permute-start(bf16[32,1024]{1,0:T(8,128)(2,1)S(1)} %dynamic-slice_bitcast_fusion.10), channel_id=1, source_target_pairs={{0,1},{1,2},{2,3},{3,0},{4,5},{5,6},{6,7},{7,4},{8,9},{9,10},{10,1... | collective-permute-start | bytes 196616 | tf_op jit(solution)/shard_map/ppermute | solution.py:1134
  68.5 11.2 %collective-permute-start.7 = (bf16[32,1024]{1,0:T(8,128)(2,1)S(1)}, bf16[32,1024]{1,0:T(8,128)(2,1)S(1)}, u32[]{:S(2)}, u32[]{:S(2)}) collective-permute-start(bf16[32,1024]{1,0:T(8,128)(2,1)S(1)} %dynamic-slice_bitcast_fusion.10), channel_id=1, source_target_pairs={{0,2},{1,3},{2,0},{3,1},{4,6},{5,7},{6,4},{7,5},{8,10},{9,11},{10,... | collective-permute-start | bytes 196616 | tf_op jit(solution)/shard_map/ppermute | solution.py:1134
  70.7 9.0 %collective-permute-start.8 = (bf16[32,1024]{1,0:T(8,128)(2,1)S(1)}, bf16[32,1024]{1,0:T(8,128)(2,1)S(1)}, u32[]{:S(2)}, u32[]{:S(2)}) collective-permute-start(bf16[32,1024]{1,0:T(8,128)(2,1)S(1)} %dynamic-slice_bitcast_fusion.10), channel_id=1, source_target_pairs={{0,3},{1,0},{2,1},{3,2},{4,7},{5,4},{6,5},{7,6},{8,11},{9,8},{10,9... | collective-permute-start | bytes 196616 | tf_op jit(solution)/shard_map/ppermute | solution.py:1134
  86.0 6.6 %collective-permute-start.9 = (bf16[8,64,1536]{2,1,0:T(8,128)(2,1)S(1)}, bf16[8,64,1536]{2,1,0:T(8,128)(2,1)}, u32[]{:S(2)}, u32[]{:S(2)}) collective-permute-start(bf16[8,64,1536]{2,1,0:T(8,128)(2,1)S(1)} %all-to-all-done.2.query.own), channel_id=1, source_target_pairs={{0,4},{4,0},{8,12},{12,8},{16,20},{20,16},{24,28},{28,24},{1,5},{5... | collective-permute-start | bytes 4718600 | tf_op jit(solution)/shard_map/ppermute | solution.py:1107
  94.0 37.2 %copy-start.2 = (bf16[1024,1024]{1,0:T(8,128)(2,1)S(1)}, bf16[1024,1024]{1,0:T(8,128)(2,1)}, u32[]{:S(2)}) copy-start(bf16[1024,1024]{1,0:T(8,128)(2,1)} %up.7) | copy-start | bytes 6291460
  127.6 18.3 %all-to-all-start.3 = ((bf16[32,64,128]{2,1,0:T(8,128)(2,1)}), bf16[32,64,128]{2,1,0:T(8,128)(2,1)S(1)}, u32[]{:S(2)}, u32[]{:S(2)}) async-start(bf16[32,64,128]{2,1,0:T(8,128)(2,1)} %copy-done.37), calls=%async_computation.3 | async-start | bytes 1048576 | tf_op jit(solution)/shard_map/all_to_all | solution.py:1298
  130.6 209.1 %all-reduce.7.cloned.1.call-start = ((), (), s32[]{:S(2)}) async-start(), calls=%async_computation.13 | async-start | bytes 8388608 | tf_op jit(solution)/shard_map/psum | solution.py:1346
  154.4 12.3 %collective-permute-start.10 = (bf16[1024,128]{1,0:T(8,128)(2,1)}, bf16[1024,128]{1,0:T(8,128)(2,1)}, u32[]{:S(2)}, u32[]{:S(2)}) collective-permute-start(bf16[1024,128]{1,0:T(8,128)(2,1)} %get-tuple-element.200.rows_up), channel_id=1, source_target_pairs={{0,1},{1,2},{2,3},{3,0},{4,5},{5,6},{6,7},{7,4},{8,9},{9,10},{10,1... | collective-permute-start | bytes 786440 | tf_op jit(solution)/shard_map/ppermute | solution.py:1326
  154.4 12.4 %collective-permute-start.11 = (bf16[1024,128]{1,0:T(8,128)(2,1)}, bf16[1024,128]{1,0:T(8,128)(2,1)}, u32[]{:S(2)}, u32[]{:S(2)}) collective-permute-start(bf16[1024,128]{1,0:T(8,128)(2,1)} %get-tuple-element.201.rows_down), channel_id=1, source_target_pairs={{0,3},{1,0},{2,1},{3,2},{4,7},{5,4},{6,5},{7,6},{8,11},{9,8},{10,9... | collective-permute-start | bytes 786440 | tf_op jit(solution)/shard_map/ppermute | solution.py:1327
  166.7 32.7 %copy-start.64 = (bf16[1024,256]{1,0:T(8,128)(2,1)}, bf16[1024,256]{1,0:T(8,128)(2,1)S(1)}, u32[]{:S(2)}) copy-start(bf16[1024,256]{1,0:T(8,128)(2,1)S(1)} %get-tuple-element.235.refs_8_.refs_0_) | copy-start | bytes 1572868
  166.9 7.6 %collective-permute-start.12 = (bf16[1024,128]{1,0:T(8,128)(2,1)}, bf16[1024,128]{1,0:T(8,128)(2,1)S(1)}, u32[]{:S(2)}, u32[]{:S(2)}) collective-permute-start(bf16[1024,128]{1,0:T(8,128)(2,1)} %collective-permute-done.10.rows_up), channel_id=1, source_target_pairs={{0,1},{1,2},{2,3},{3,0},{4,5},{5,6},{6,7},{7,4},{8,9},{9,10},{10,1... | collective-permute-start | bytes 786440 | tf_op jit(solution)/shard_map/ppermute | solution.py:1326
  169.2 13.5 %collective-permute-start.13 = (bf16[1024,128]{1,0:T(8,128)(2,1)}, bf16[1024,128]{1,0:T(8,128)(2,1)S(1)}, u32[]{:S(2)}, u32[]{:S(2)}) collective-permute-start(bf16[1024,128]{1,0:T(8,128)(2,1)} %collective-permute-done.11.rows_down), channel_id=1, source_target_pairs={{0,3},{1,0},{2,1},{3,2},{4,7},{5,4},{6,5},{7,6},{8,11},{9,8},{10,9... | collective-permute-start | bytes 786440 | tf_op jit(solution)/shard_map/ppermute | solution.py:1327
  174.1 25.2 %copy-start.67 = (bf16[1024,256]{1,0:T(8,128)(2,1)}, bf16[1024,256]{1,0:T(8,128)(2,1)S(1)}, u32[]{:S(2)}) copy-start(bf16[1024,256]{1,0:T(8,128)(2,1)S(1)} %get-tuple-element.236.refs_9_.refs_1_) | copy-start | bytes 1572868
  182.7 11.0 %collective-permute-start.16 = (bf16[1024,128]{1,0:T(8,128)(2,1)S(1)}, bf16[1024,128]{1,0:T(8,128)(2,1)S(1)}, u32[]{:S(2)}, u32[]{:S(2)}) collective-permute-start(bf16[1024,128]{1,0:T(8,128)(2,1)S(1)} %collective-permute-done.12.rows_up), channel_id=1, source_target_pairs={{0,1},{1,2},{2,3},{3,0},{4,5},{5,6},{6,7},{7,4},{8,9},{9,10},{10,1... | collective-permute-start | bytes 786440 | tf_op jit(solution)/shard_map/ppermute | solution.py:1326
  183.0 12.7 %collective-permute-start.17 = (bf16[1024,128]{1,0:T(8,128)(2,1)S(1)}, bf16[1024,128]{1,0:T(8,128)(2,1)S(1)}, u32[]{:S(2)}, u32[]{:S(2)}) collective-permute-start(bf16[1024,128]{1,0:T(8,128)(2,1)S(1)} %collective-permute-done.13.rows_down), channel_id=1, source_target_pairs={{0,3},{1,0},{2,1},{3,2},{4,7},{5,4},{6,5},{7,6},{8,11},{9,8},{10,9... | collective-permute-start | bytes 786440 | tf_op jit(solution)/shard_map/ppermute | solution.py:1327
  186.0 20.7 %collective-permute-start.14 = (bf16[1024,128]{1,0:T(8,128)(2,1)S(1)}, bf16[1024,128]{1,0:T(8,128)(2,1)S(1)}, u32[]{:S(2)}, u32[]{:S(2)}) collective-permute-start(bf16[1024,128]{1,0:T(8,128)(2,1)S(1)} %get-tuple-element.218), channel_id=1, source_target_pairs={{0,1},{1,2},{2,3},{3,0},{4,5},{5,6},{6,7},{7,4},{8,9},{9,10},{10,1... | collective-permute-start | bytes 786440 | tf_op jit(solution)/shard_map/ppermute | solution.py:1092
  186.0 20.9 %collective-permute-start.15 = (bf16[1024,128]{1,0:T(8,128)(2,1)S(1)}, bf16[1024,128]{1,0:T(8,128)(2,1)S(1)}, u32[]{:S(2)}, u32[]{:S(2)}) collective-permute-start(bf16[1024,128]{1,0:T(8,128)(2,1)S(1)} %get-tuple-element.219), channel_id=1, source_target_pairs={{0,3},{1,0},{2,1},{3,2},{4,7},{5,4},{6,5},{7,6},{8,11},{9,8},{10,9... | collective-permute-start | bytes 786440 | tf_op jit(solution)/shard_map/ppermute | solution.py:1093
  199.4 13.0 %copy-start.57 = (bf16[1024,1024]{1,0:T(8,128)(2,1)S(1)}, bf16[1024,1024]{1,0:T(8,128)(2,1)}, u32[]{:S(2)}) copy-start(bf16[1024,1024]{1,0:T(8,128)(2,1)} %copy-done.56) | copy-start | bytes 6291460
  209.1 12.9 %collective-permute-start.19 = (bf16[1024,128]{1,0:T(8,128)(2,1)S(1)}, bf16[1024,128]{1,0:T(8,128)(2,1)}, u32[]{:S(2)}, u32[]{:S(2)}) collective-permute-start(bf16[1024,128]{1,0:T(8,128)(2,1)S(1)} %add_convert_fusion.5), channel_id=1, source_target_pairs={{0,3},{1,0},{2,1},{3,2},{4,7},{5,4},{6,5},{7,6},{8,11},{9,8},{10,9... | collective-permute-start | bytes 786440 | tf_op jit(solution)/shard_map/ppermute | solution.py:1093
  212.3 10.2 %collective-permute-start.18 = (bf16[1024,128]{1,0:T(8,128)(2,1)S(1)}, bf16[1024,128]{1,0:T(8,128)(2,1)}, u32[]{:S(2)}, u32[]{:S(2)}) collective-permute-start(bf16[1024,128]{1,0:T(8,128)(2,1)S(1)} %add_convert_fusion.6), channel_id=1, source_target_pairs={{0,1},{1,2},{2,3},{3,0},{4,5},{5,6},{6,7},{7,4},{8,9},{9,10},{10,1... | collective-permute-start | bytes 786440 | tf_op jit(solution)/shard_map/ppermute | solution.py:1092
  222.0 14.6 %copy-start.8 = (bf16[4,8,32,1024]{3,2,1,0:T(8,128)(2,1)S(1)}, bf16[4,8,32,1024]{3,2,1,0:T(8,128)(2,1)}, u32[]{:S(2)}) copy-start(bf16[4,8,32,1024]{3,2,1,0:T(8,128)(2,1)} %copy.90) | copy-start | bytes 6291460
  222.6 14.0 %copy-start.32 = (f32[1024,256]{1,0:T(8,128)S(1)}, f32[1024,256]{1,0:T(8,128)}, u32[]{:S(2)}) copy-start(f32[1024,256]{1,0:T(8,128)} %copy-done.31) | copy-start | bytes 3145732
  224.1 6.7 %collective-permute-start.21 = (bf16[1024,128]{1,0:T(8,128)(2,1)S(1)}, bf16[1024,128]{1,0:T(8,128)(2,1)S(1)}, u32[]{:S(2)}, u32[]{:S(2)}) collective-permute-start(bf16[1024,128]{1,0:T(8,128)(2,1)S(1)} %add_convert_fusion.3), channel_id=1, source_target_pairs={{0,3},{1,0},{2,1},{3,2},{4,7},{5,4},{6,5},{7,6},{8,11},{9,8},{10,9... | collective-permute-start | bytes 786440 | tf_op jit(solution)/shard_map/ppermute | solution.py:1093
  228.4 8.1 %collective-permute-start.20 = (bf16[1024,128]{1,0:T(8,128)(2,1)S(1)}, bf16[1024,128]{1,0:T(8,128)(2,1)S(1)}, u32[]{:S(2)}, u32[]{:S(2)}) collective-permute-start(bf16[1024,128]{1,0:T(8,128)(2,1)S(1)} %add_convert_fusion.4), channel_id=1, source_target_pairs={{0,1},{1,2},{2,3},{3,0},{4,5},{5,6},{6,7},{7,4},{8,9},{9,10},{10,1... | collective-permute-start | bytes 786440 | tf_op jit(solution)/shard_map/ppermute | solution.py:1092
  242.9 24.7 %all-to-all-start.4 = ((bf16[32,64,128]{2,1,0:T(8,128)(2,1)}), bf16[32,64,128]{2,1,0:T(8,128)(2,1)S(1)}, u32[]{:S(2)}, u32[]{:S(2)}) async-start(bf16[32,64,128]{2,1,0:T(8,128)(2,1)} %copy-done.38), calls=%async_computation.4 | async-start | bytes 1048576 | tf_op jit(solution)/shard_map/all_to_all | solution.py:1366
  267.7 72.0 %all-to-all-start.5 = ((bf16[4,8,256,128]{3,2,1,0:T(8,128)(2,1)}), bf16[4,8,256,128]{3,2,1,0:T(8,128)(2,1)}, u32[]{:S(2)}, u32[]{:S(2)}) async-start(bf16[4,8,256,128]{3,2,1,0:T(8,128)(2,1)} %feed_out.1), calls=%async_computation.5 | async-start | bytes 4194304 | tf_op jit(solution)/shard_map/all_to_all | solution.py:1371
  272.3 84.1 %reduce-scatter.2.cloned.1.call-start = ((), (), s32[]{:S(2)}) async-start(), calls=%async_computation.11 | async-start | bytes 2621440 | tf_op jit(solution)/shard_map/reduce_scatter | solution.py:1372
  333.8 2.9 collective-permute-start.22
  339.7 23.3 %all-to-all-start.6 = ((bf16[8,64,1664]{2,1,0:T(8,128)(2,1)}), bf16[8,64,1664]{2,1,0:T(8,128)(2,1)}, u32[]{:S(2)}, u32[]{:S(2)}) async-start(bf16[8,64,1664]{2,1,0:T(8,128)(2,1)} %pad_maximum_fusion), calls=%async_computation.6 | async-start | bytes 3407872 | tf_op jit(solution)/shard_map/all_to_all | solution.py:1393
  380.3 10.2 %collective-permute-start.25 = (bf16[512,1024]{1,0:T(8,128)(2,1)S(1)}, bf16[512,1024]{1,0:T(8,128)(2,1)S(1)}, u32[]{:S(2)}, u32[]{:S(2)}) collective-permute-start(bf16[512,1024]{1,0:T(8,128)(2,1)S(1)} %get-tuple-element.294), channel_id=1, source_target_pairs={{0,4},{4,0},{8,12},{12,8},{16,20},{20,16},{24,28},{28,24},{1,5},{5... | collective-permute-start | bytes 3145736 | tf_op jit(solution)/shard_map/ppermute | solution.py:1107
  383.9 10.0 %collective-permute-start.23 = (bf16[128,1024]{1,0:T(8,128)(2,1)}, bf16[128,1024]{1,0:T(8,128)(2,1)S(1)}, u32[]{:S(2)}, u32[]{:S(2)}) collective-permute-start(bf16[128,1024]{1,0:T(8,128)(2,1)} %copy-done.73), channel_id=1, source_target_pairs={{0,1},{1,2},{2,3},{3,0},{4,5},{5,6},{6,7},{7,4},{8,9},{9,10},{10,1... | collective-permute-start | bytes 786440 | tf_op jit(solution)/shard_map/ppermute | solution.py:1092
  385.2 13.4 %collective-permute-start.24 = (bf16[128,1024]{1,0:T(8,128)(2,1)S(1)}, bf16[128,1024]{1,0:T(8,128)(2,1)}, u32[]{:S(2)}, u32[]{:S(2)}) collective-permute-start(bf16[128,1024]{1,0:T(8,128)(2,1)S(1)} %get-tuple-element.289), channel_id=1, source_target_pairs={{0,3},{1,0},{2,1},{3,2},{4,7},{5,4},{6,5},{7,6},{8,11},{9,8},{10,9... | collective-permute-start | bytes 786440 | tf_op jit(solution)/shard_map/ppermute | solution.py:1093
  387.2 20.3 %all-to-all-start.7 = ((f32[4,48,256]{2,1,0:T(8,128)}), f32[4,48,256]{2,1,0:T(8,128)S(1)}, u32[]{:S(2)}, u32[]{:S(2)}) async-start(f32[4,48,256]{2,1,0:T(8,128)} %get-tuple-element.299), calls=%async_computation.8 | async-start | bytes 393216 | tf_op jit(solution)/shard_map/all_to_all | solution.py:1450
  393.6 13.7 %copy-start.21 = (bf16[1024,256]{1,0:T(8,128)(2,1)S(1)}, bf16[1024,256]{1,0:T(8,128)(2,1)}, u32[]{:S(2)}) copy-start(bf16[1024,256]{1,0:T(8,128)(2,1)} %refs_1_.1) | copy-start | bytes 1572868
  399.5 8.0 %collective-permute-start.28 = (bf16[128,1024]{1,0:T(8,128)(2,1)}, bf16[128,1024]{1,0:T(8,128)(2,1)}, u32[]{:S(2)}, u32[]{:S(2)}) collective-permute-start(bf16[128,1024]{1,0:T(8,128)(2,1)} %get-tuple-element.345), channel_id=1, source_target_pairs={{0,8},{4,12},{8,16},{12,20},{16,24},{20,28},{24,0},{28,4},{1,9},{5... | collective-permute-start | bytes 786440 | tf_op jit(solution)/shard_map/ppermute | solution.py:1119
  399.7 13.4 %collective-permute-start.29 = (bf16[128,1024]{1,0:T(8,128)(2,1)}, bf16[128,1024]{1,0:T(8,128)(2,1)}, u32[]{:S(2)}, u32[]{:S(2)}) collective-permute-start(bf16[128,1024]{1,0:T(8,128)(2,1)} %get-tuple-element.344), channel_id=1, source_target_pairs={{0,16},{4,20},{8,24},{12,28},{16,0},{20,4},{24,8},{28,12},{1,17},{... | collective-permute-start | bytes 786440 | tf_op jit(solution)/shard_map/ppermute | solution.py:1119
  400.1 12.9 %collective-permute-start.30 = (bf16[128,1024]{1,0:T(8,128)(2,1)}, bf16[128,1024]{1,0:T(8,128)(2,1)}, u32[]{:S(2)}, u32[]{:S(2)}) collective-permute-start(bf16[128,1024]{1,0:T(8,128)(2,1)} %get-tuple-element.343), channel_id=1, source_target_pairs={{0,24},{4,28},{8,0},{12,4},{16,8},{20,12},{24,16},{28,20},{1,25},{... | collective-permute-start | bytes 786440 | tf_op jit(solution)/shard_map/ppermute | solution.py:1119
  404.1 32.0 %copy-start.75 = (bf16[16,512]{1,0:T(8,128)(2,1)S(1)}, bf16[16,512]{1,0:T(8,128)(2,1)}, u32[]{:S(2)}) copy-start(bf16[16,512]{1,0:T(8,128)(2,1)} %copy-done.74) | copy-start | bytes 49156
  404.1 9.0 %collective-permute-start.26 = (bf16[128,1024]{1,0:T(8,128)(2,1)}, bf16[128,1024]{1,0:T(8,128)(2,1)}, u32[]{:S(2)}, u32[]{:S(2)}) collective-permute-start(bf16[128,1024]{1,0:T(8,128)(2,1)} %get-tuple-element.342), channel_id=1, source_target_pairs={{0,1},{1,2},{2,3},{3,0},{4,5},{5,6},{6,7},{7,4},{8,9},{9,10},{10,1... | collective-permute-start | bytes 786440 | tf_op jit(solution)/shard_map/ppermute | solution.py:1092
  405.9 14.1 %collective-permute-start.27 = (bf16[128,1024]{1,0:T(8,128)(2,1)}, bf16[128,1024]{1,0:T(8,128)(2,1)}, u32[]{:S(2)}, u32[]{:S(2)}) collective-permute-start(bf16[128,1024]{1,0:T(8,128)(2,1)} %get-tuple-element.341), channel_id=1, source_target_pairs={{0,3},{1,0},{2,1},{3,2},{4,7},{5,4},{6,5},{7,6},{8,11},{9,8},{10,9... | collective-permute-start | bytes 786440 | tf_op jit(solution)/shard_map/ppermute | solution.py:1093
  422.0 21.0 %collective-permute-start.33 = (bf16[128,1024]{1,0:T(8,128)(2,1)}, bf16[128,1024]{1,0:T(8,128)(2,1)}, u32[]{:S(2)}, u32[]{:S(2)}) collective-permute-start(bf16[128,1024]{1,0:T(8,128)(2,1)} %add_convert_fusion.2), channel_id=1, source_target_pairs={{0,8},{4,12},{8,16},{12,20},{16,24},{20,28},{24,0},{28,4},{1,9},{5... | collective-permute-start | bytes 786440 | tf_op jit(solution)/shard_map/ppermute | solution.py:1125
  422.0 21.0 %collective-permute-start.34 = (bf16[128,1024]{1,0:T(8,128)(2,1)}, bf16[128,1024]{1,0:T(8,128)(2,1)}, u32[]{:S(2)}, u32[]{:S(2)}) collective-permute-start(bf16[128,1024]{1,0:T(8,128)(2,1)} %add_convert_fusion.2), channel_id=1, source_target_pairs={{0,16},{4,20},{8,24},{12,28},{16,0},{20,4},{24,8},{28,12},{1,17},{... | collective-permute-start | bytes 786440 | tf_op jit(solution)/shard_map/ppermute | solution.py:1125
  423.2 19.8 %collective-permute-start.35 = (bf16[128,1024]{1,0:T(8,128)(2,1)}, bf16[128,1024]{1,0:T(8,128)(2,1)}, u32[]{:S(2)}, u32[]{:S(2)}) collective-permute-start(bf16[128,1024]{1,0:T(8,128)(2,1)} %add_convert_fusion.2), channel_id=1, source_target_pairs={{0,24},{4,28},{8,0},{12,4},{16,8},{20,12},{24,16},{28,20},{1,25},{... | collective-permute-start | bytes 786440 | tf_op jit(solution)/shard_map/ppermute | solution.py:1125
  426.3 18.1 %all-to-all-start.8 = ((f32[8,16,256]{2,1,0:T(8,128)}), f32[8,16,256]{2,1,0:T(8,128)S(1)}, u32[]{:S(2)}, u32[]{:S(2)}) async-start(f32[8,16,256]{2,1,0:T(8,128)} %broadcast_in_dim.97), calls=%async_computation.9 | async-start | bytes 262144 | tf_op jit(solution)/shard_map/all_to_all | solution.py:1044
  432.8 11.5 %collective-permute-start.31 = (bf16[128,1024]{1,0:T(8,128)(2,1)}, bf16[128,1024]{1,0:T(8,128)(2,1)S(1)}, u32[]{:S(2)}, u32[]{:S(2)}) collective-permute-start(bf16[128,1024]{1,0:T(8,128)(2,1)} %get-tuple-element.340), channel_id=1, source_target_pairs={{0,1},{1,2},{2,3},{3,0},{4,5},{5,6},{6,7},{7,4},{8,9},{9,10},{10,1... | collective-permute-start | bytes 786440 | tf_op jit(solution)/shard_map/ppermute | solution.py:1092
  432.8 13.1 %collective-permute-start.32 = (bf16[128,1024]{1,0:T(8,128)(2,1)S(1)}, bf16[128,1024]{1,0:T(8,128)(2,1)S(1)}, u32[]{:S(2)}, u32[]{:S(2)}) collective-permute-start(bf16[128,1024]{1,0:T(8,128)(2,1)S(1)} %get-tuple-element.339), channel_id=1, source_target_pairs={{0,3},{1,0},{2,1},{3,2},{4,7},{5,4},{6,5},{7,6},{8,11},{9,8},{10,9... | collective-permute-start | bytes 786440 | tf_op jit(solution)/shard_map/ppermute | solution.py:1093
  446.6 6.8 %collective-permute-start.36 = (bf16[512,1024]{1,0:T(8,128)(2,1)S(1)}, bf16[512,1024]{1,0:T(8,128)(2,1)S(1)}, u32[]{:S(2)}, u32[]{:S(2)}) collective-permute-start(bf16[512,1024]{1,0:T(8,128)(2,1)S(1)} %pad_maximum_fusion.1.half), channel_id=1, source_target_pairs={{0,4},{4,0},{8,12},{12,8},{16,20},{20,16},{24,28},{28,24},{1,5},{5... | collective-permute-start | bytes 3145736 | tf_op jit(solution)/shard_map/ppermute | solution.py:1107
  (85 other events, 303.2 us)
Sparse Core Ops, SparseCore 0:
  53.3 52.8 all-gather.3
  108.7 28.7 all-gather.5
  222.7 87.1 all-reduce.6
  312.7 43.6 reduce-scatter.1
